TPU v7x, 32 devices: a whole 2x2x4 slice. The times are simulated.
32 devices in a mesh: dp: 8 (over z, y), mp: 4 (over x, core).
Axes of the slice: x: 2, y: 2, z: 4, core: 2. Of those that a mesh axis runs over, the one named last changes fastest.
Arguments:
- tokens: bfloat16 [8192, 1024], P(('dp', 'mp')), may hold values from -6 to 6
- cotangent: bfloat16 [8192, 1024], P(('dp', 'mp')), may hold values from -6 to 6
- segments: int32 [8192], P('dp'), may hold values from 0 to 21, as said below
- lengths: int32 [8, 21], P('dp'), may hold values from 0 to 1024, as said below
- scale_levels: int32 [8], P('dp'), may hold values from 0 to 3
- first_gain: float32 [1024], replicated, may hold values from 0.5 to 1.5
- first_shift: float32 [1024], replicated, may hold values from -3 to 3
- input_weight: bfloat16 [3, 1024, 1024], P(None, None, 'mp'), may hold values from -0.1875 to 0.1875
- input_bias: float32 [2, 1024], P(None, 'mp'), may hold values from -3 to 3
- output_weight: bfloat16 [1024, 1024], P('mp'), may hold values from -0.75 to 0.75
- output_bias: float32 [1024], replicated, may hold values from -3 to 3
- second_gain: float32 [1024], replicated, may hold values from 0.5 to 1.5
- second_shift: float32 [1024], replicated, may hold values from -3 to 3
- expand_weight: bfloat16 [1024, 4096], P(None, 'mp'), may hold values from -0.1875 to 0.1875
- expand_bias: float32 [4096], P('mp'), may hold values from -3 to 3
- reduce_weight: bfloat16 [4096, 1024], P('mp'), may hold values from -0.09375 to 0.09375
- reduce_bias: float32 [1024], replicated, may hold values from -3 to 3
Outputs:
- block_output: bfloat16 [8192, 1024], P(('dp', 'mp'))
- input_gradient: float32 [8192, 1024], P(('dp', 'mp'))
- first_gain_gradient: float32 [1024], replicated
- first_shift_gradient: float32 [1024], replicated
- input_weight_gradient: float32 [3, 1024, 1024], P(None, None, 'mp')
- input_bias_gradient: float32 [2, 1024], P(None, 'mp')
- output_weight_gradient: float32 [1024, 1024], P('mp')
- output_bias_gradient: float32 [1024], replicated
- second_gain_gradient: float32 [1024], replicated
- second_shift_gradient: float32 [1024], replicated
- expand_weight_gradient: float32 [1024, 4096], P(None, 'mp')
- expand_bias_gradient: float32 [4096], P('mp')
- reduce_weight_gradient: float32 [4096, 1024], P('mp')
- reduce_bias_gradient: float32 [1024], replicated
Inputs may be any that keep to these rules, and one draw needn't show every extreme that they name: In each group, slot 0 holds one scene, the next slots hold chips of exactly 49 patches, the rest hold 0; a group's lengths sum to more than 975 and to 1024 at most. Items take consecutive rows in slot order from the group's first row, each as many as its length; rows past the sum of the group's lengths carry 21 (padding); segments agree with lengths.
All inputs are finite; a program needn't handle non-finite values.
Results may differ from a plain program's by a relative error of at most 0.017.
Values may be sent and summed in bfloat16 or wider, within the bound.
No kernel may reach another device: no remote copies, remote signals or barrier semaphores. Data moves between devices by JAX's collectives and lax.ppermute only.
A program may use at most 128 MiB of HBM per device.

v0:
```python
from functools import partial

import jax
import jax.numpy as jnp
from jax import lax
from jax.sharding import PartitionSpec as P

HD = 64


EPSILON = 1e-06
EXCLUDED = -1e30


def row_contract(left_side, right_side):
    return lax.dot_general(
        left_side, right_side, (((0,), (0,)), ((), ())), preferred_element_type=jnp.float32
    )


def column_contract(left_side, right_side):
    return lax.dot_general(
        left_side, right_side, (((1,), (1,)), ((), ())), preferred_element_type=jnp.float32
    )


def normalize(values):
    center = values - jnp.mean(values, -1, keepdims=True)
    inverse = lax.rsqrt(jnp.mean(center * center, -1, keepdims=True) + EPSILON)
    return (center * inverse, inverse)


def normalize_back(upstream, normed, inverse, gain):
    scaled = upstream * gain
    return inverse * (
        scaled
        - jnp.mean(scaled, -1, keepdims=True)
        - normed * jnp.mean(scaled * normed, -1, keepdims=True)
    )


def position_rows(own_items, item_lengths, level, first_row, width):
    slot_count = item_lengths.shape[0]
    item_ends = jnp.cumsum(item_lengths)
    starts = item_ends - item_lengths
    slot_index = lax.broadcasted_iota(jnp.int32, (1, slot_count), 1)
    start_row = jnp.sum(jnp.where(own_items[:, None] == slot_index, starts[None, :], 0), 1)
    row_index = first_row + jnp.arange(own_items.shape[0], dtype=jnp.int32)
    valid_rows = (own_items < slot_count).astype(jnp.float32)
    level_ratio = jnp.exp2(level.astype(jnp.float32) - 2.0)
    places = (row_index - start_row).astype(jnp.float32) * level_ratio
    half_width = width // 2
    frequency = jnp.exp(-jnp.log(10000.0) * jnp.arange(half_width, dtype=jnp.float32) / half_width)
    angles = places[:, None] * frequency[None, :]
    return (
        jnp.concatenate([jnp.sin(angles), jnp.cos(angles)], 1) * valid_rows[:, None],
        valid_rows,
    )


def to_blocks(array, block_rows):
    return array.reshape((array.shape[0] // block_rows, block_rows) + array.shape[1:])


def attend_forward(query_rows, key_rows, value_rows, segments, block_rows):
    group_rows, head_count, head_size = query_rows.shape
    score_scale = head_size ** (-0.5)

    def forward_block(inputs):
        query_block, item_block = inputs
        scores = (
            jnp.einsum("bhe,khe->hbk", query_block, key_rows, preferred_element_type=jnp.float32)
            * score_scale
        )
        same_item = item_block[None, :, None] == segments[None, None, :]
        scores = jnp.where(same_item, scores, EXCLUDED)
        row_max = jnp.max(scores, -1, keepdims=True)
        exp_scores = jnp.exp(scores - row_max)
        row_total = jnp.sum(exp_scores, -1, keepdims=True)
        prob_low = (exp_scores / row_total).astype(jnp.bfloat16)
        attended = jnp.einsum(
            "hbk,khe->bhe", prob_low, value_rows, preferred_element_type=jnp.float32
        )
        return (attended, row_max[..., 0] + jnp.log(row_total[..., 0]))

    attended, log_totals = lax.map(
        forward_block, (to_blocks(query_rows, block_rows), to_blocks(segments, block_rows))
    )
    return (attended.reshape(group_rows, head_count * head_size), log_totals)


def attend_back(query_rows, key_rows, value_rows, head_grads, log_totals, segments, block_rows):
    group_rows, head_count, head_size = query_rows.shape
    score_scale = head_size ** (-0.5)

    def backward_block(running, inputs):
        key_sum, value_sum = running
        query_block, item_block, log_block, grad_block = inputs
        scores = (
            jnp.einsum("bhe,khe->hbk", query_block, key_rows, preferred_element_type=jnp.float32)
            * score_scale
        )
        same_item = item_block[None, :, None] == segments[None, None, :]
        prob_full = jnp.where(same_item, jnp.exp(scores - log_block[:, :, None]), 0.0)
        prob_low = prob_full.astype(jnp.bfloat16)
        value_sum = value_sum + jnp.einsum(
            "hbk,bhe->khe", prob_low, grad_block, preferred_element_type=jnp.float32
        )
        prob_grad = jnp.einsum(
            "bhe,khe->hbk", grad_block, value_rows, preferred_element_type=jnp.float32
        )
        center = jnp.sum(prob_grad * prob_full, -1, keepdims=True)
        score_grad = (prob_full * (prob_grad - center)).astype(jnp.bfloat16)
        query_grad = (
            jnp.einsum("hbk,khe->bhe", score_grad, key_rows, preferred_element_type=jnp.float32)
            * score_scale
        )
        key_sum = (
            key_sum
            + jnp.einsum(
                "hbk,bhe->khe", score_grad, query_block, preferred_element_type=jnp.float32
            )
            * score_scale
        )
        return ((key_sum, value_sum), query_grad)

    zero_grads = jnp.zeros((group_rows, head_count, head_size), jnp.float32)
    (key_sum, value_sum), query_grads = lax.scan(
        backward_block,
        (zero_grads, zero_grads),
        (
            to_blocks(query_rows, block_rows),
            to_blocks(segments, block_rows),
            log_totals,
            to_blocks(head_grads, block_rows),
        ),
    )
    return (query_grads.reshape(group_rows, head_count, head_size), key_sum, value_sum)


def per_device(
    tokens,
    cotangent,
    segments,
    lengths,
    scale_levels,
    first_gain,
    first_shift,
    input_weight,
    input_bias,
    output_weight,
    output_bias,
    second_gain,
    second_shift,
    expand_weight,
    expand_bias,
    reduce_weight,
    reduce_bias,
):
    own_count = tokens.shape[0]
    first_row = lax.axis_index("mp") * own_count
    group_rows = segments.shape[0]
    block_rows = min(512, group_rows)
    local_width = input_weight.shape[2]
    head_count = local_width // HD
    own_items = lax.dynamic_slice_in_dim(segments, first_row, own_count)
    positions, valid_rows = position_rows(
        own_items, lengths[0], scale_levels[0], first_row, tokens.shape[1]
    )
    group_patches = jnp.sum(lengths).astype(jnp.float32)
    residual = tokens.astype(jnp.float32) + positions
    normed_one, inverse_one = normalize(residual)
    attn_input = (normed_one * first_gain + first_shift).astype(jnp.bfloat16)
    attn_rows = lax.all_gather(attn_input, "mp", axis=0, tiled=True)
    projected = jnp.einsum(
        "rd,tde->tre", attn_rows, input_weight, preferred_element_type=jnp.float32
    )
    bias_rows = jnp.stack([input_bias[0], jnp.zeros_like(input_bias[0]), input_bias[1]])
    qkv_rows = (
        (projected + bias_rows[:, None, :])
        .astype(jnp.bfloat16)
        .reshape(3, group_rows, head_count, HD)
    )
    query_rows, key_rows, value_rows = (qkv_rows[0], qkv_rows[1], qkv_rows[2])
    attended, log_totals = attend_forward(query_rows, key_rows, value_rows, segments, block_rows)
    heads_out = attended.astype(jnp.bfloat16)
    attn_sum = lax.psum_scatter(
        jnp.dot(heads_out, output_weight, preferred_element_type=jnp.float32),
        "mp",
        scatter_dimension=0,
        tiled=True,
    )
    hidden_res = residual + attn_sum + output_bias
    normed_two, inverse_two = normalize(hidden_res)
    mlp_input = (normed_two * second_gain + second_shift).astype(jnp.bfloat16)
    mlp_rows = lax.all_gather(mlp_input, "mp", axis=0, tiled=True)
    pre_act = jnp.dot(mlp_rows, expand_weight, preferred_element_type=jnp.float32) + expand_bias
    activated = jax.nn.gelu(pre_act, approximate=False).astype(jnp.bfloat16)
    mlp_sum = lax.psum_scatter(
        jnp.dot(activated, reduce_weight, preferred_element_type=jnp.float32).astype(jnp.bfloat16),
        "mp",
        scatter_dimension=0,
        tiled=True,
    ).astype(jnp.float32)
    block_output = (hidden_res + mlp_sum + reduce_bias).astype(jnp.bfloat16)
    grad_out = cotangent.astype(jnp.float32) * valid_rows[:, None]
    grad_all = lax.all_gather(grad_out.astype(jnp.bfloat16), "mp", axis=0, tiled=True)
    reduce_grad = row_contract(activated, grad_all)
    reduce_bias_part = jnp.sum(grad_out, 0)
    act_grad = column_contract(grad_all, reduce_weight)
    _, gelu_back = jax.vjp(partial(jax.nn.gelu, approximate=False), pre_act)
    pre_grad = gelu_back(act_grad)[0].astype(jnp.bfloat16)
    expand_grad = row_contract(mlp_rows, pre_grad)
    expand_bias_grad = jnp.sum(pre_grad, 0, dtype=jnp.float32)
    normed_grad_two = lax.psum_scatter(
        column_contract(pre_grad, expand_weight), "mp", scatter_dimension=0, tiled=True
    )
    gain_two_part = jnp.sum(normed_grad_two * normed_two, 0)
    shift_two_part = jnp.sum(normed_grad_two, 0)
    residual_grad = grad_out + normalize_back(normed_grad_two, normed_two, inverse_two, second_gain)
    branch_grad = residual_grad.astype(jnp.bfloat16)
    out_bias_part = jnp.sum(branch_grad, 0, dtype=jnp.float32)
    branch_all = lax.all_gather(branch_grad, "mp", axis=0, tiled=True)
    output_grad = row_contract(heads_out, branch_all)
    head_grads = column_contract(branch_all, output_weight).astype(jnp.bfloat16)
    query_grad, key_grad, value_grad = attend_back(
        query_rows,
        key_rows,
        value_rows,
        head_grads.reshape(group_rows, head_count, HD),
        log_totals,
        segments,
        block_rows,
    )
    qkv_grad = (
        jnp.stack([query_grad, key_grad, value_grad])
        .astype(jnp.bfloat16)
        .reshape(3, group_rows, local_width)
    )
    qv_grad = jnp.stack(
        [jnp.sum(qkv_grad[0], 0, dtype=jnp.float32), jnp.sum(qkv_grad[2], 0, dtype=jnp.float32)]
    )
    input_grad = jnp.einsum("rd,tre->tde", attn_rows, qkv_grad, preferred_element_type=jnp.float32)
    normed_grad_one = lax.psum_scatter(
        jnp.einsum("tre,tde->rd", qkv_grad, input_weight, preferred_element_type=jnp.float32),
        "mp",
        scatter_dimension=0,
        tiled=True,
    )
    gain_one_part = jnp.sum(normed_grad_one * normed_one, 0)
    shift_one_part = jnp.sum(normed_grad_one, 0)
    input_gradient = residual_grad + normalize_back(
        normed_grad_one, normed_one, inverse_one, first_gain
    )
    gain_one, shift_one, gain_two, shift_two, out_bias_sum, reduce_bias_sum = lax.psum(
        (
            gain_one_part,
            shift_one_part,
            gain_two_part,
            shift_two_part,
            out_bias_part,
            reduce_bias_part,
        ),
        ("dp", "mp"),
    )
    (
        input_total,
        qv_total,
        output_total,
        expand_total,
        expand_bias_total,
        reduce_total,
        total_patches,
    ) = (
        lax.psum(input_grad.astype(jnp.bfloat16), "dp").astype(jnp.float32),
        lax.psum(qv_grad.astype(jnp.bfloat16), "dp").astype(jnp.float32),
        lax.psum(output_grad.astype(jnp.bfloat16), "dp").astype(jnp.float32),
        lax.psum(expand_grad.astype(jnp.bfloat16), "dp").astype(jnp.float32),
        lax.psum(expand_bias_grad.astype(jnp.bfloat16), "dp").astype(jnp.float32),
        lax.psum(reduce_grad.astype(jnp.bfloat16), "dp").astype(jnp.float32),
        lax.psum(group_patches.astype(jnp.bfloat16), "dp").astype(jnp.float32),
    )
    factor = lax.rsqrt(total_patches)
    return (
        block_output,
        input_gradient,
        gain_one * factor,
        shift_one * factor,
        input_total * factor,
        qv_total * factor,
        output_total * factor,
        out_bias_sum * factor,
        gain_two * factor,
        shift_two * factor,
        expand_total * factor,
        expand_bias_total * factor,
        reduce_total * factor,
        reduce_bias_sum * factor,
    )


def solution(mesh):
    placed = (
        P(("dp", "mp"), None),
        P(("dp", "mp"), None),
        P("dp"),
        P("dp", None),
        P("dp"),
        P(),
        P(),
        P(None, None, "mp"),
        P(None, "mp"),
        P("mp", None),
        P(),
        P(),
        P(),
        P(None, "mp"),
        P("mp"),
        P("mp", None),
        P(),
    )
    return jax.shard_map(
        per_device,
        mesh=mesh,
        in_specs=placed,
        out_specs=(
            P(("dp", "mp"), None),
            P(("dp", "mp"), None),
            P(),
            P(),
            P(None, None, "mp"),
            P(None, "mp"),
            P("mp", None),
            P(),
            P(),
            P(),
            P(None, "mp"),
            P("mp"),
            P("mp", None),
            P(),
        ),
        check_vma=False,
    )
```

profile of v0, /device:TPU:0, one launch (start us, length us, event | category | flops | bytes accessed | tf_op | source)
XLA Modules:
  0.0 652.6 jit_solution(4002657279944057823)
XLA Ops:
  11.1 1.9 multiply_sine_fusion
  13.0 2.3 fusion.69
  17.6 25.2 %all-gather.5.cloned.1.call-done = bf16[1024,1024]{1,0:T(8,128)(2,1)} async-done(((bf16[256,1024]{1,0:T(8,128)(2,1)}), bf16[1024,1024]{1,0:T(8,128)(2,1)}) %all-gather.5.cloned.1.call-update) | async-done | bytes 2097168 | tf_op jit(solution)/shard_map/all_gather | solution.py:174
  42.8 3.9 fusion.54
  50.8 16.5 %while.27 = (s32[]{:T(128)}, bf16[2,512,4,64]{1,3,2,0:T(8,128)(2,1)}, f32[2,4,512]{2,1,0:T(4,128)S(1)}, s32[2,512]{1,0:T(2,128)S(1)}, s32[1024]{0:T(1024)S(1)}, ...) while((s32[]{:T(128)}, ...), condition=%wide.region_7.8_spmd, body=%wide.region_4.7_spmd.sunk | while | flops 562558976 | bytes 35465416 | solution.py:86
  52.9 2.3 fusion.125
  55.2 3.0 fusion.126
  61.1 2.3 fusion.125
  63.5 3.0 fusion.126
  69.8 3.8 fusion.74
  73.7 44.7 %reduce-scatter.5.cloned.1.call-done = f32[256,1024]{1,0:T(8,128)} async-done(((f32[1024,1024]{1,0:T(8,128)}), f32[256,1024]{1,0:T(8,128)}) %reduce-scatter.5.cloned.1.call-update) | async-done | bytes 1048592 | tf_op jit(solution)/shard_map/reduce_scatter | solution.py:187
  123.3 21.6 %all-gather.7.cloned.1.call-done = bf16[1024,1024]{1,0:T(8,128)(2,1)} async-done(((bf16[256,1024]{1,0:T(8,128)(2,1)}), bf16[1024,1024]{1,0:T(8,128)(2,1)}) %all-gather.7.cloned.1.call-update) | async-done | bytes 2097168 | tf_op jit(solution)/shard_map/all_gather | solution.py:196
  144.9 6.6 %fusion.75 = f32[1024,1024]{1,0:T(8,128)} fusion(bf16[1024,1024]{1,0:T(8,128)(2,1)} %all-gather.7.cloned.1.call-done, bf16[1024,1024]{1,0:T(8,128)(2,1)} %param.34), kind=kOutput, calls=%fused_computation.144 | convolution fusion | flops 2147483648 | bytes 8388608 | tf_op jit(solution)/shard_map/dot_general | solution.py:197
  151.5 18.0 %all-gather.9.cloned.1.call-done = bf16[1024,1024]{1,0:T(8,128)(2,1)} async-done(((bf16[256,1024]{1,0:T(8,128)(2,1)}), bf16[1024,1024]{1,0:T(8,128)(2,1)}) %all-gather.9.cloned.1.call-update) | async-done | bytes 2097168 | tf_op jit(solution)/shard_map/all_gather | solution.py:207
  169.5 14.8 %fusion.65 = (bf16[1024]{0:T(1024)(128)(2,1)S(1)}, bf16[1024,1024]{1,0:T(8,128)(2,1)S(1)}, f32[1024,1024]{1,0:T(8,128)}) fusion(f32[1024,1024]{1,0:T(8,128)} %fusion.75, f32[1024]{0:T(1024)S(1)} %copy-done.37, bf16[1024,1024]{1,0:T(8,128)(2,1)} %all-gather.9.cloned.1.call-done, bf16[1024,1024]{1,0:T(8,128)(2,1)S(1)} %copy-done), kind=kOutput, calls=%fused_computation.136 | convolution fusion | flops 2225077248 | bytes 14686208 | tf_op jit(solution)/shard_map/dot_general | solution.py:22
  185.6 4.3 fusion.76
  190.0 4.6 multiply_convert_fusion.1
  195.9 3.7 convolution_convert_fusion.2
  199.7 35.0 %reduce-scatter.9.cloned.1.call-done = f32[256,1024]{1,0:T(8,128)} async-done(((f32[1024,1024]{1,0:T(8,128)}), f32[256,1024]{1,0:T(8,128)}) %reduce-scatter.9.cloned.1.call-update) | async-done | bytes 1048592 | tf_op jit(solution)/shard_map/reduce_scatter | solution.py:215
  234.7 2.0 multiply_reduce_fusion.1
  236.7 32.1 %reduce-scatter.7.cloned.1.call-done = bf16[256,1024]{1,0:T(8,128)(2,1)} async-done(((bf16[1024,1024]{1,0:T(8,128)(2,1)}), bf16[256,1024]{1,0:T(8,128)(2,1)}) %reduce-scatter.7.cloned.1.call-update) | async-done | bytes 524304 | tf_op jit(solution)/shard_map/reduce_scatter | solution.py:199
  268.9 3.3 convert_reduce_fusion
  272.4 6.1 convolution_convert_fusion.1
  278.5 3.8 convolution_convert_fusion
  282.3 12.6 %all-gather.11.cloned.1.call-done = bf16[1024,1024]{1,0:T(8,128)(2,1)} async-done(((bf16[256,1024]{1,0:T(8,128)(2,1)}), bf16[1024,1024]{1,0:T(8,128)(2,1)}) %all-gather.11.cloned.1.call-update) | async-done | bytes 2097168 | tf_op jit(solution)/shard_map/all_gather | solution.py:223
  294.9 3.1 convolution_convert_fusion.4
  298.0 2.8 reshape.231
  300.8 2.3 copy.57
  303.9 24.2 %while.28 = (s32[]{:T(128)}, f32[1024,4,64]{0,2,1:T(8,128)S(1)}, f32[1024,4,64]{0,2,1:T(8,128)}, bf16[2,512,4,64]{1,3,2,0:T(8,128)(2,1)}, bf16[2,512,4,64]{1,3,2...) while((s32[]{:T(128)}, f32[1024,4,64]{0,2,1:T(8,128)S(1)}, ...), condition=%wide.region_17.18_spmd.clone, body=%wide.region_15.17_spmd.clone.sunk | while | flops 1375598592 | bytes 87099704 | solution.py:128
  305.6 2.2 fusion.138
  307.8 3.3 multiply_reduce_fusion.10
  311.1 2.4 multiply_convert_fusion.3
  317.8 2.2 fusion.138
  320.0 3.3 multiply_reduce_fusion.10
  323.3 2.4 multiply_convert_fusion.3
  332.5 3.1 convolution_convert_fusion.3
  335.6 4.6 fusion.57
  340.2 5.2 convolution_bitcast_fusion
  347.0 23.0 %all-reduce.1 = (bf16[]{:T(256)}, bf16[2,256]{1,0:T(2,128)(2,1)S(1)}, bf16[1024]{0:T(1024)(128)(2,1)S(1)}) all-reduce(bf16[]{:T(256)S(6)} %convert_element_type.148, bf16[2,256]{1,0:T(2,128)(2,1)S(1)} %pad_maximum_fusion.4, bf16[1024]{0:T(1024)(128)(2,1)S(1)} %get-tuple-element.315), channel_id=1, replica_groups=mesh['dp'=8,'mp'=4] {'dp'}, use_global_device_ids=true, to_apply=%region_24.25 | all-reduce | flops 1537 | bytes 6148 | tf_op jit(solution)/shard_map/psum | solution.py:281
  371.8 179.3 %all-reduce.5.cloned.1.call-done = (bf16[3,1024,256]{1,2,0:T(8,128)(2,1)}, bf16[256,1024]{1,0:T(8,128)(2,1)}, bf16[1024,1024]{1,0:T(8,128)(2,1)}, bf16[1024,1024]{1,0:T(8,128)(2,1)}) async-done(((bf16[3,1024,256]{1,2,0:T(8,128)(2,1)}, bf16[256,1024]{1,0:T(8,128)(2,1)}, bf16[1024,1024]{1,0:T(8,128)(2,1)}, bf16[1024,1024]{1,0:T(8,128)(2,1)}), (bf16[3,1024,256]{1,2,0:T(8,128)(2,1)}, ...) | async-done | bytes 6291472 | tf_op jit(solution)/shard_map/psum | solution.py:275
  551.1 3.5 convert_multiply_fusion.2
  554.6 3.7 copy.63
  559.4 3.0 convert_multiply_fusion.1
  562.4 2.6 convert_multiply_fusion
  565.0 32.3 %reduce-scatter.11.cloned.1.call-done = f32[256,1024]{1,0:T(8,128)} async-done(((f32[1024,1024]{1,0:T(8,128)}), f32[256,1024]{1,0:T(8,128)}) %reduce-scatter.11.cloned.1.call-update) | async-done | bytes 1048592 | tf_op jit(solution)/shard_map/reduce_scatter | solution.py:244
  597.3 2.0 multiply_reduce_fusion.2
  599.3 39.7 %all-reduce = (f32[1024]{0:T(1024)S(1)}, f32[1024]{0:T(1024)S(1)}, f32[1024]{0:T(1024)S(1)}, f32[1024]{0:T(1024)S(1)}, f32[1024]{0:T(1024)S(1)}, /*index=5*/f32[1024]{0:T(1024)S(1)}) all-reduce(f32[1024]{0:T(1024)S(1)} %get-tuple-element.258, f32[1024]{0:T(1024)S(1)} %get-tuple-element.263, ...), channel_id=1, replica_groups=mesh['dp'=8,'mp'=4] {'dp','mp'}, use_global_device_ids=true, to_apply=%region_22.23 | all-reduce | flops 6144 | bytes 49152 | tf_op jit(solution)/shard_map/psum | solution.py:255
  642.6 3.2 multiply_add_fusion
  (191 shorter events, 45.6 us)
Async XLA Ops:
  7.2 162.3 %copy-start = (bf16[1024,1024]{1,0:T(8,128)(2,1)S(1)}, bf16[1024,1024]{1,0:T(8,128)(2,1)}, u32[]{:S(2)}) copy-start(bf16[1024,1024]{1,0:T(8,128)(2,1)} %param.36) | copy-start | bytes 6291460
  7.2 10.2 %copy-start.24 = (s32[1024]{0:T(1024)S(1)}, s32[1024]{0:T(1024)}, u32[]{:S(2)}) copy-start(s32[1024]{0:T(1024)} %param.23) | copy-start | bytes 12292
  7.2 9.1 %copy-start.26 = (f32[1024]{0:T(1024)S(1)}, f32[1024]{0:T(1024)}, u32[]{:S(2)}) copy-start(f32[1024]{0:T(1024)} %param.26) | copy-start | bytes 12292
  7.2 9.1 %copy-start.34 = (f32[1024]{0:T(1024)S(1)}, f32[1024]{0:T(1024)}, u32[]{:S(2)}) copy-start(f32[1024]{0:T(1024)} %param.27) | copy-start | bytes 12292
  7.2 10.3 %copy-start.39 = (f32[2,256]{1,0:T(2,128)S(1)}, f32[2,256]{1,0:T(2,128)}, u32[]{:S(2)}) copy-start(f32[2,256]{1,0:T(2,128)} %param.29) | copy-start | bytes 6148
  7.2 35.6 %all-gather.5.cloned.1.call-start = ((), (), s32[]{:S(2)}) async-start(), calls=%async_computation.4 | async-start | bytes 2621440 | tf_op jit(solution)/shard_map/all_gather | solution.py:174
  11.0 4.3 copy-start.32
  15.3 27.5 %copy-start.28 = (f32[256]{0:T(256)}, f32[256]{0:T(256)S(1)}, u32[]{:S(2)}) copy-start(f32[256]{0:T(256)S(1)} %broadcast_multiply_fusion.11) | copy-start | bytes 3076
  16.3 26.5 %copy-start.30 = (f32[256]{0:T(256)}, f32[256]{0:T(256)S(1)}, u32[]{:S(2)}) copy-start(f32[256]{0:T(256)S(1)} %add_rsqrt_fusion.1) | copy-start | bytes 3076
  17.4 101.0 %reduce-scatter.5.cloned.1.call-start = ((), (), s32[]{:S(2)}) async-start(), calls=%async_computation.5 | async-start | bytes 5242880 | tf_op jit(solution)/shard_map/reduce_scatter | solution.py:187
  52.9 2.4 copy-start.5
  52.9 2.4 copy-start.18
  61.1 2.4 copy-start.5
  61.1 2.4 copy-start.18
  73.6 44.8 %copy-start.35 = (f32[1024]{0:T(1024)S(1)}, f32[1024]{0:T(1024)}, u32[]{:S(2)}) copy-start(f32[1024]{0:T(1024)} %param.31) | copy-start | bytes 12292
  73.6 47.5 %copy-start.25 = (f32[1024]{0:T(1024)S(1)}, f32[1024]{0:T(1024)}, u32[]{:S(2)}) copy-start(f32[1024]{0:T(1024)} %param.32) | copy-start | bytes 12292
  73.6 47.5 %copy-start.36 = (f32[1024]{0:T(1024)S(1)}, f32[1024]{0:T(1024)}, u32[]{:S(2)}) copy-start(f32[1024]{0:T(1024)} %param.33) | copy-start | bytes 12292
  73.6 71.3 %all-gather.7.cloned.1.call-start = ((), (), s32[]{:S(2)}) async-start(), calls=%async_computation.6 | async-start | bytes 2621440 | tf_op jit(solution)/shard_map/all_gather | solution.py:196
  122.2 47.3 %all-gather.9.cloned.1.call-start = ((), (), s32[]{:S(2)}) async-start(), calls=%async_computation.8 | async-start | bytes 2621440 | tf_op jit(solution)/shard_map/all_gather | solution.py:207
  122.8 46.7 %copy-start.37 = (f32[1024]{0:T(1024)S(1)}, f32[1024]{0:T(1024)}, u32[]{:S(2)}) copy-start(f32[1024]{0:T(1024)} %param.35) | copy-start | bytes 12292
  122.8 111.9 %reduce-scatter.9.cloned.1.call-start = ((), (), s32[]{:S(2)}) async-start(), calls=%async_computation.9 | async-start | bytes 5242880 | tf_op jit(solution)/shard_map/reduce_scatter | solution.py:215
  169.5 16.1 %copy-start.40 = (bf16[1024,1024]{1,0:T(8,128)(2,1)S(1)}, bf16[1024,1024]{1,0:T(8,128)(2,1)}, u32[]{:S(2)}) copy-start(bf16[1024,1024]{1,0:T(8,128)(2,1)} %param.34) | copy-start | bytes 6291460
  190.0 78.9 %reduce-scatter.7.cloned.1.call-start = ((), (), s32[]{:S(2)}) async-start(), calls=%async_computation.7 | async-start | bytes 2621440 | tf_op jit(solution)/shard_map/reduce_scatter | solution.py:199
  199.6 69.3 %copy-start.4 = (f32[256,1024]{1,0:T(8,128)S(1)}, f32[256,1024]{1,0:T(8,128)}, u32[]{:S(2)}) copy-start(f32[256,1024]{1,0:T(8,128)} %copy-done.3) | copy-start | bytes 3145732
  199.6 69.3 %copy-start.17 = (bf16[256,1024]{1,0:T(8,128)(2,1)S(1)}, bf16[256,1024]{1,0:T(8,128)(2,1)}, u32[]{:S(2)}) copy-start(bf16[256,1024]{1,0:T(8,128)(2,1)} %param.22) | copy-start | bytes 1572868
  199.6 69.3 %copy-start.33 = (f32[256]{0:T(256)S(1)}, f32[256]{0:T(256)}, u32[]{:S(2)}) copy-start(f32[256]{0:T(256)} %copy-done.32) | copy-start | bytes 3076
  199.6 69.3 %copy-start.38 = (f32[1024]{0:T(1024)S(1)}, f32[1024]{0:T(1024)}, u32[]{:S(2)}) copy-start(f32[1024]{0:T(1024)} %param.37) | copy-start | bytes 12292
  199.6 95.3 %all-gather.11.cloned.1.call-start = ((), (), s32[]{:S(2)}) async-start(), calls=%async_computation.10 | async-start | bytes 2621440 | tf_op jit(solution)/shard_map/all_gather | solution.py:223
  272.2 278.9 %all-reduce.5.cloned.1.call-start = ((), (), s32[]{:S(2)}) async-start(), calls=%async_computation.12 | async-start | bytes 12582912 | tf_op jit(solution)/shard_map/psum | solution.py:275
  272.4 6.1 copy-start.16
  272.4 6.1 copy-start.41
  278.5 16.4 %copy-start.22 = (bf16[256,1024]{1,0:T(8,128)(2,1)S(1)}, bf16[256,1024]{1,0:T(8,128)(2,1)}, u32[]{:S(2)}) copy-start(bf16[256,1024]{1,0:T(8,128)(2,1)} %param.30) | copy-start | bytes 1572868
  282.3 21.6 %copy-start.6 = (bf16[1024,4,64]{0,2,1:T(8,128)(2,1)S(1)}, bf16[1024,4,64]{0,2,1:T(8,128)(2,1)}, u32[]{:S(2)}) copy-start(bf16[1024,4,64]{0,2,1:T(8,128)(2,1)} %get-tuple-element.557) | copy-start | bytes 1572868
  304.3 1.4 copy-start.20
  307.8 3.3 copy-start.21
  311.1 2.4 copy-start.8
  316.4 1.4 copy-start.20
  320.0 3.3 copy-start.21
  323.3 2.4 copy-start.8
  328.1 4.4 copy-start.12
  340.2 257.1 %reduce-scatter.11.cloned.1.call-start = ((), (), s32[]{:S(2)}) async-start(), calls=%async_computation.11 | async-start | bytes 5242880 | tf_op jit(solution)/shard_map/reduce_scatter | solution.py:244
  554.6 3.7 copy-start.23
  554.6 4.8 copy-start.14
  558.3 4.1 copy-start.13
  562.4 34.9 %copy-start.27 = (f32[1024]{0:T(1024)S(1)}, f32[1024]{0:T(1024)}, u32[]{:S(2)}) copy-start(f32[1024]{0:T(1024)} %param.26) | copy-start | bytes 12292
  562.4 34.9 %copy-start.29 = (f32[256]{0:T(256)S(1)}, f32[256]{0:T(256)}, u32[]{:S(2)}) copy-start(f32[256]{0:T(256)} %copy-done.28) | copy-start | bytes 3076
  562.4 34.9 %copy-start.31 = (f32[256]{0:T(256)S(1)}, f32[256]{0:T(256)}, u32[]{:S(2)}) copy-start(f32[256]{0:T(256)} %copy-done.30) | copy-start | bytes 3076
  562.4 83.4 %copy-start.1 = (bf16[1024,1024]{1,0:T(8,128)(2,1)S(1)}, bf16[1024,1024]{1,0:T(8,128)(2,1)}, u32[]{:S(2)}) copy-start(bf16[1024,1024]{1,0:T(8,128)(2,1)} %param.36) | copy-start | bytes 6291460
  (12 other events, 12.8 us)
Sparse Core Ops, SparseCore 0:
  17.5 25.2 all-gather.4
  73.8 44.5 reduce-scatter.4
  122.3 22.5 all-gather.6
  146.9 22.5 all-gather.8
  190.1 44.5 reduce-scatter.8
  237.6 31.1 reduce-scatter.6
  272.3 22.5 all-gather.10
  340.3 210.7 all-reduce.4
  553.6 43.6 reduce-scatter.10
where the time goes:
time: 662 us; the launch traced here: 653 us
  waiting for transfers between devices  401 us (61%)
  matrix products  90.5 us (14%)
  blocking collectives  62.7 us (9%)
  other arithmetic  54.2 us (8%)
  local copies, waits for them, and re-layouts  25.6 us (4%)
  between operations  16.7 us (3%)
    psum x1, waiting for transfers between devices, per_device(): lax.psum(input_grad.astype(jnp.bfloat16), 'dp').astype(jnp.float32)  179 us
    reduce_scatter x1, waiting for transfers between devices, per_device(): lax.psum_scatter(jnp.dot(heads_out, output_weight, preferred_element_type...  44.7 us
    psum x1, blocking collectives, per_device(): lax.psum((gain_one_part, shift_one_part, gain_two_part, shift_two_part, o...  39.7 us
    reduce_scatter x1, waiting for transfers between devices, per_device(): lax.psum_scatter(column_contract(pre_grad, expand_weight), 'mp', scatter_...  35 us
    reduce_scatter x1, waiting for transfers between devices, per_device(): lax.psum_scatter(jnp.einsum('tre,tde->rd', qkv_grad, input_weight, prefer...  32.3 us
    reduce_scatter x1, waiting for transfers between devices, per_device(): lax.psum_scatter(jnp.dot(activated, reduce_weight, preferred_element_type...  32.1 us
    all_gather x1, waiting for transfers between devices, per_device(): attn_rows = lax.all_gather(attn_input, 'mp', axis=0, tiled=True)  25.2 us
    psum x1, blocking collectives, per_device(): lax.psum(group_patches.astype(jnp.bfloat16), 'dp').astype(jnp.float32)  23 us
  transfers between devices with their start and end apart: 9, of which 9 were waited for; matrix products, arithmetic and copies ran while one was open for 7% of the time, Pallas kernels for 0%

commit v1 on v0

v1 whole, which is shorter than its diff:
```python
import jax
import jax.numpy as jnp
from jax import lax
from jax.sharding import PartitionSpec as P

HD = 64
EPSILON = 1e-06
EXCLUDED = -1e30
F32 = jnp.float32
BF16 = jnp.bfloat16


def row_contract(left_side, right_side):
    return lax.dot_general(
        left_side, right_side, (((0,), (0,)), ((), ())), preferred_element_type=F32
    )


def column_contract(left_side, right_side):
    return lax.dot_general(
        left_side, right_side, (((1,), (1,)), ((), ())), preferred_element_type=F32
    )


def normalize(values):
    center = values - jnp.mean(values, -1, keepdims=True)
    inverse = lax.rsqrt(jnp.mean(center * center, -1, keepdims=True) + EPSILON)
    return (center * inverse, inverse)


def normalize_back(upstream, normed, inverse, gain):
    scaled = upstream * gain
    return inverse * (
        scaled
        - jnp.mean(scaled, -1, keepdims=True)
        - normed * jnp.mean(scaled * normed, -1, keepdims=True)
    )


def position_rows(own_items, item_lengths, level, first_row, width):
    slot_count = item_lengths.shape[0]
    item_ends = jnp.cumsum(item_lengths)
    starts = item_ends - item_lengths
    slot_index = lax.broadcasted_iota(jnp.int32, (1, slot_count), 1)
    start_row = jnp.sum(jnp.where(own_items[:, None] == slot_index, starts[None, :], 0), 1)
    row_index = first_row + jnp.arange(own_items.shape[0], dtype=jnp.int32)
    valid_rows = (own_items < slot_count).astype(F32)
    level_ratio = jnp.exp2(level.astype(F32) - 2.0)
    places = (row_index - start_row).astype(F32) * level_ratio
    half_width = width // 2
    frequency = jnp.exp(-jnp.log(10000.0) * jnp.arange(half_width, dtype=F32) / half_width)
    angles = places[:, None] * frequency[None, :]
    return (
        jnp.concatenate([jnp.sin(angles), jnp.cos(angles)], 1) * valid_rows[:, None],
        valid_rows,
    )


def bits_of(size):
    bits = []
    step = 1
    while step < size:
        bits.append(step)
        step *= 2
    return bits


def swap(array, axis, size, bit):
    return lax.ppermute(array, axis, [(i, i ^ bit) for i in range(size)])


def gather_rows(own, count):
    blocks = {0: own}
    for bit in reversed(bits_of(count)):
        blocks.update(
            {j | bit: swap(rows, "mp", count, bit) for j, rows in list(blocks.items())}
        )
    return [blocks[j] for j in range(count)]


def scatter_rows(blocks, count):
    held = {j: block for j, block in enumerate(blocks)}
    for bit in bits_of(count):
        arrived = {
            j ^ bit: swap(held[j].astype(BF16), "mp", count, bit)
            for j in held
            if j & bit
        }
        held = {j: held[j].astype(F32) + arrived[j].astype(F32) for j in arrived}
    return held[0]


def row_blocks(array, count):
    size = array.shape[0] // count
    return [array[j * size : (j + 1) * size] for j in range(count)]


def dp_sum(parts, count, index, axis):
    held = parts
    for bit in bits_of(count):
        half = held.shape[axis] // 2
        high = jnp.where((index & bit) != 0, 1, 0)
        keep = lax.dynamic_slice_in_dim(held, high * half, half, axis)
        send = lax.dynamic_slice_in_dim(held, (1 - high) * half, half, axis)
        held = keep.astype(F32) + swap(send.astype(BF16), "dp", count, bit).astype(F32)
    held = held.astype(BF16)
    for bit in reversed(bits_of(count)):
        other = swap(held, "dp", count, bit)
        high = (index & bit) != 0
        held = jnp.where(
            high, jnp.concatenate([other, held], axis), jnp.concatenate([held, other], axis)
        )
    return held


def butterfly(values, sizes):
    for axis, size in sizes:
        for bit in bits_of(size):
            values = values + swap(values, axis, size, bit)
    return values


def attend_forward(query_rows, key_rows, value_rows, segments):
    score_scale = query_rows.shape[2] ** (-0.5)
    scores = (
        jnp.einsum("bhe,khe->hbk", query_rows, key_rows, preferred_element_type=F32) * score_scale
    )
    same_item = segments[None, :, None] == segments[None, None, :]
    scores = jnp.where(same_item, scores, EXCLUDED)
    row_max = jnp.max(scores, -1, keepdims=True)
    exp_scores = jnp.exp(scores - row_max)
    row_total = jnp.sum(exp_scores, -1, keepdims=True)
    prob_low = (exp_scores / row_total).astype(BF16)
    attended = jnp.einsum("hbk,khe->bhe", prob_low, value_rows, preferred_element_type=F32)
    return (attended, row_max[..., 0] + jnp.log(row_total[..., 0]))


def attend_back(query_rows, key_rows, value_rows, head_grads, log_totals, segments):
    score_scale = query_rows.shape[2] ** (-0.5)
    scores = (
        jnp.einsum("bhe,khe->hbk", query_rows, key_rows, preferred_element_type=F32) * score_scale
    )
    same_item = segments[None, :, None] == segments[None, None, :]
    prob_full = jnp.where(same_item, jnp.exp(scores - log_totals[:, :, None]), 0.0)
    prob_low = prob_full.astype(BF16)
    value_sum = jnp.einsum("hbk,bhe->khe", prob_low, head_grads, preferred_element_type=F32)
    prob_grad = jnp.einsum("bhe,khe->hbk", head_grads, value_rows, preferred_element_type=F32)
    center = jnp.sum(prob_grad * prob_full, -1, keepdims=True)
    score_grad = (prob_full * (prob_grad - center)).astype(BF16)
    query_grad = (
        jnp.einsum("hbk,khe->bhe", score_grad, key_rows, preferred_element_type=F32) * score_scale
    )
    key_sum = (
        jnp.einsum("hbk,bhe->khe", score_grad, query_rows, preferred_element_type=F32) * score_scale
    )
    return (query_grad, key_sum, value_sum)


def layer(sizes):
    n_dp, n_mp = sizes

    def per_device(
        tokens,
        cotangent,
        segments,
        lengths,
        scale_levels,
        first_gain,
        first_shift,
        input_weight,
        input_bias,
        output_weight,
        output_bias,
        second_gain,
        second_shift,
        expand_weight,
        expand_bias,
        reduce_weight,
        reduce_bias,
    ):
        me = lax.axis_index("mp")
        group = lax.axis_index("dp")
        own_count, width = tokens.shape
        local_width = input_weight.shape[2]
        head_count = local_width // HD
        item_blocks = [
            lax.dynamic_slice_in_dim(segments, (me ^ j) * own_count, own_count)
            for j in range(n_mp)
        ]
        items = jnp.concatenate(item_blocks)
        positions, valid_rows = position_rows(
            item_blocks[0], lengths[0], scale_levels[0], me * own_count, width
        )
        group_patches = jnp.sum(lengths).astype(F32)
        residual = tokens.astype(F32) + positions
        normed_one, inverse_one = normalize(residual)
        attn_input = (normed_one * first_gain + first_shift).astype(BF16)
        attn_rows = jnp.concatenate(gather_rows(attn_input, n_mp))
        grad_out = cotangent.astype(F32) * valid_rows[:, None]
        grad_all = jnp.concatenate(gather_rows(grad_out.astype(BF16), n_mp))
        reduce_bias_part = jnp.sum(grad_out, 0)

        projected = jnp.einsum("rd,tde->tre", attn_rows, input_weight, preferred_element_type=F32)
        bias_rows = jnp.stack([input_bias[0], jnp.zeros_like(input_bias[0]), input_bias[1]])
        group_rows = n_mp * own_count
        qkv_rows = (
            (projected + bias_rows[:, None, :])
            .astype(BF16)
            .reshape(3, group_rows, head_count, HD)
        )
        query_rows, key_rows, value_rows = (qkv_rows[0], qkv_rows[1], qkv_rows[2])
        attended, log_totals = attend_forward(query_rows, key_rows, value_rows, items)
        heads_out = attended.astype(BF16).reshape(group_rows, local_width)
        attn_sum = scatter_rows(
            row_blocks(jnp.dot(heads_out, output_weight, preferred_element_type=F32), n_mp), n_mp
        )
        hidden_res = residual + attn_sum + output_bias
        normed_two, inverse_two = normalize(hidden_res)
        mlp_input = (normed_two * second_gain + second_shift).astype(BF16)
        mlp_rows = jnp.concatenate(gather_rows(mlp_input, n_mp))
        pre_act = jnp.dot(mlp_rows, expand_weight, preferred_element_type=F32) + expand_bias
        cdf = 0.5 * (1.0 + lax.erf(pre_act * (0.5**0.5)))
        activated = (pre_act * cdf).astype(BF16)
        act_grad = column_contract(grad_all, reduce_weight)
        slope = cdf + pre_act * jnp.exp(-0.5 * pre_act * pre_act) * 0.3989422804014327
        pre_grad = (act_grad * slope).astype(BF16)
        activated, pre_grad = lax.optimization_barrier((activated, pre_grad))
        normed_grad_two = scatter_rows(
            row_blocks(column_contract(pre_grad, expand_weight), n_mp), n_mp
        )
        reduce_grad = dp_sum(row_contract(activated, grad_all), n_dp, group, 0)
        expand_grad = dp_sum(row_contract(mlp_rows, pre_grad), n_dp, group, 0)
        expand_bias_grad = jnp.sum(pre_grad, 0, dtype=F32)
        mlp_sum = scatter_rows(
            row_blocks(jnp.dot(activated, reduce_weight, preferred_element_type=F32), n_mp), n_mp
        )
        block_output = (hidden_res + mlp_sum + reduce_bias).astype(BF16)
        gain_two_part = jnp.sum(normed_grad_two * normed_two, 0)
        shift_two_part = jnp.sum(normed_grad_two, 0)
        residual_grad = grad_out + normalize_back(
            normed_grad_two, normed_two, inverse_two, second_gain
        )
        branch_grad = residual_grad.astype(BF16)
        out_bias_part = jnp.sum(branch_grad, 0, dtype=F32)
        branch_all = jnp.concatenate(gather_rows(branch_grad, n_mp))
        output_grad = dp_sum(row_contract(heads_out, branch_all), n_dp, group, 0)
        head_grads = column_contract(branch_all, output_weight).astype(BF16)
        query_grad, key_grad, value_grad = attend_back(
            query_rows,
            key_rows,
            value_rows,
            head_grads.reshape(group_rows, head_count, HD),
            log_totals,
            items,
        )
        qkv_grad = (
            jnp.stack([query_grad, key_grad, value_grad])
            .astype(BF16)
            .reshape(3, group_rows, local_width)
        )
        qv_grad = jnp.stack(
            [jnp.sum(qkv_grad[0], 0, dtype=F32), jnp.sum(qkv_grad[2], 0, dtype=F32)]
        )
        input_grad = dp_sum(
            jnp.einsum("rd,tre->tde", attn_rows, qkv_grad, preferred_element_type=F32),
            n_dp,
            group,
            1,
        )
        normed_grad_one = scatter_rows(
            row_blocks(
                jnp.einsum("tre,tde->rd", qkv_grad, input_weight, preferred_element_type=F32), n_mp
            ),
            n_mp,
        )
        gain_one_part = jnp.sum(normed_grad_one * normed_one, 0)
        shift_one_part = jnp.sum(normed_grad_one, 0)
        input_gradient = residual_grad + normalize_back(
            normed_grad_one, normed_one, inverse_one, first_gain
        )
        both = (("dp", n_dp), ("mp", n_mp))
        early = butterfly(
            jnp.stack([gain_two_part, shift_two_part, out_bias_part, reduce_bias_part]), both
        )
        local = butterfly(
            jnp.concatenate([expand_bias_grad, jnp.full((128,), group_patches)])[None],
            (("dp", n_dp),),
        )[0]
        expand_bias_total = local[: expand_bias_grad.shape[0]]
        factor = lax.rsqrt(local[expand_bias_grad.shape[0]])
        late = butterfly(jnp.stack([gain_one_part, shift_one_part]), both)
        qv_total = butterfly(qv_grad, (("dp", n_dp),))
        return (
            block_output,
            input_gradient,
            late[0] * factor,
            late[1] * factor,
            input_grad.astype(F32) * factor,
            qv_total * factor,
            output_grad.astype(F32) * factor,
            early[2] * factor,
            early[0] * factor,
            early[1] * factor,
            expand_grad.astype(F32) * factor,
            expand_bias_total * factor,
            reduce_grad.astype(F32) * factor,
            early[3] * factor,
        )

    return per_device


def solution(mesh):
    placed = (
        P(("dp", "mp"), None),
        P(("dp", "mp"), None),
        P("dp"),
        P("dp", None),
        P("dp"),
        P(),
        P(),
        P(None, None, "mp"),
        P(None, "mp"),
        P("mp", None),
        P(),
        P(),
        P(),
        P(None, "mp"),
        P("mp"),
        P("mp", None),
        P(),
    )
    return jax.shard_map(
        layer((mesh.shape["dp"], mesh.shape["mp"])),
        mesh=mesh,
        in_specs=placed,
        out_specs=(
            P(("dp", "mp"), None),
            P(("dp", "mp"), None),
            P(),
            P(),
            P(None, None, "mp"),
            P(None, "mp"),
            P("mp", None),
            P(),
            P(),
            P(),
            P(None, "mp"),
            P("mp"),
            P("mp", None),
            P(),
        ),
        check_vma=False,
    )
```

time: 662 us -> 430 us (0.65)
  waiting for transfers between devices: 401 us -> 223 us
  starting transfers between devices: 1.01 us -> 66.1 us
  blocking collectives: 62.7 us -> 0 us
  matrix products: 90.5 us -> 70.7 us
  local copies, waits for them, and re-layouts: 25.6 us -> 11.6 us
  between operations: 16.7 us -> 4.35 us
    ppermute x0 -> x64, waiting for transfers between devices: none -> 223 us  [swap(): return lax.ppermute(array, axis, [(i, i ^ bit) for i in range(size)])]
    psum x1 -> x0, waiting for transfers between devices: 179 us -> none  [per_device(): lax.psum(input_grad.astype(jnp.bfloat16), 'dp').astype(jnp.float32)]
    reduce_scatter x4 -> x0, waiting for transfers between devices: 144 us -> none  [the longest x1 44.7 us: per_device(): lax.psum_scatter(jnp.dot(heads_out, output_weight, preferred_element_type...]
    all_gather x4 -> x0, waiting for transfers between devices: 77.4 us -> none  [the longest x1 25.2 us: per_device(): attn_rows = lax.all_gather(attn_input, 'mp', axis=0, tiled=True)]
    ppermute x0 -> x64, starting transfers between devices: none -> 66.1 us  [swap(): return lax.ppermute(array, axis, [(i, i ^ bit) for i in range(size)])]
    psum x2 -> x0, blocking collectives: 62.7 us -> none  [the longest x1 39.7 us: per_device(): lax.psum((gain_one_part, shift_one_part, gain_two_part, shift_two_part, o...]
    dot_general x3, matrix products: 22.2 us -> 9.19 us  [column_contract(): lax.dot_general(left_side, right_side, (((1,), (1,)), ((), ())), preferre...]
    another operation x10 -> x5, local copies, waits for them, and re-layouts: 8.65 us -> 1.57 us  [the longest x3 1.4 us: per_device(): jnp.stack([query_grad, key_grad, value_grad]).astype(BF16)]
  transfers between devices with their start and end apart: 9 -> 64, of which waited for: 9 -> 29; matrix products, arithmetic and copies ran while one was open for 7% -> 19% of each run, Pallas kernels for 0% -> 0%
where the time goes in v1:
time: 430 us; the launch traced here: 425 us
  waiting for transfers between devices  223 us (52%)
  matrix products  70.7 us (16%)
  starting transfers between devices  66.1 us (15%)
  other arithmetic  49.4 us (11%)
  local copies, waits for them, and re-layouts  11.6 us (3%)
  between operations  4.35 us (1%)
    ppermute x64, waiting for transfers between devices, swap(): return lax.ppermute(array, axis, [(i, i ^ bit) for i in range(size)])  223 us
    ppermute x64, starting transfers between devices, swap(): return lax.ppermute(array, axis, [(i, i ^ bit) for i in range(size)])  66.1 us
    dot_general x1, matrix products, attend_back(): jnp.einsum('bhe,khe->hbk', head_grads, value_rows, preferred_element_type...  12.2 us
    convert_element_type x1, other arithmetic, attend_back(): score_grad = (prob_full * (prob_grad - center)).astype(BF16)  12.2 us
    dot_general x3, matrix products, column_contract(): lax.dot_general(left_side, right_side, (((1,), (1,)), ((), ())), preferre...  9.19 us
    dot_general x3, matrix products, row_contract(): lax.dot_general(left_side, right_side, (((0,), (0,)), ((), ())), preferre...  8.95 us
  transfers between devices with their start and end apart: 64, of which 29 were waited for; matrix products, arithmetic and copies ran while one was open for 19% of the time, Pallas kernels for 0%

profile of v1, /device:TPU:0, one launch (start us, length us, event | category | flops | bytes accessed | tf_op | source)
XLA Modules:
  0.0 425.2 jit_solution(4950450837247918507)
XLA Ops:
  10.8 3.0 collective-permute-start.1
  13.9 12.1 %collective-permute-done.1 = bf16[256,1024]{1,0:T(8,128)(2,1)} collective-permute-done((bf16[256,1024]{1,0:T(8,128)(2,1)}, bf16[256,1024]{1,0:T(8,128)(2,1)}, u32[]{:S(2)}, u32[]{:S(2)}) %collective-permute-start.1) | collective-permute-done | bytes 524320 | tf_op jit(solution)/shard_map/ppermute | solution.py:69
  28.1 3.9 fusion.12
  32.2 3.8 select_reduce_fusion
  36.0 3.7 fusion
  41.8 5.0 %fusion.18 = bf16[4,64,1024]{2,1,0:T(8,128)(2,1)S(1)} fusion(bf16[1024,4,64]{0,2,1:T(8,128)(2,1)S(1)} %bitcast.76, f32[4,1024,1024]{1,2,0:T(8,128)S(1)} %get-tuple-element.95, f32[4,1024]{1,0:T(4,128)S(1)} %fusion, f32[4,1024]{1,0:T(4,128)S(1)} %get-tuple-element.94, pred[1024,1024]{0,1:T(8,128)(4,1)S(1)} %broadcast_compare_fusion), kind=kOutput, calls=%fused_computation.48 | convolution fusion | flops 558104576 | bytes 18907136 | tf_op jit(solution)/shard_map/hbk,khe->bhe/dot_general | solution.py:134
  51.7 12.2 %collective-permute-done.5 = bf16[256,1024]{1,0:T(8,128)(2,1)S(1)} collective-permute-done((bf16[256,1024]{1,0:T(8,128)(2,1)S(1)}, bf16[256,1024]{1,0:T(8,128)(2,1)S(1)}, u32[]{:S(2)}, u32[]{:S(2)}) %collective-permute-start.5) | collective-permute-done | bytes 524320 | tf_op jit(solution)/shard_map/ppermute | solution.py:69
  68.3 13.1 %collective-permute-done.7 = bf16[256,1024]{1,0:T(8,128)(2,1)} collective-permute-done((bf16[256,1024]{1,0:T(8,128)(2,1)}, bf16[256,1024]{1,0:T(8,128)(2,1)}, u32[]{:S(2)}, u32[]{:S(2)}) %collective-permute-start.7) | collective-permute-done | bytes 524320 | tf_op jit(solution)/shard_map/ppermute | solution.py:69
  82.5 8.4 %collective-permute-done.10 = bf16[256,1024]{1,0:T(8,128)(2,1)} collective-permute-done((bf16[256,1024]{1,0:T(8,128)(2,1)}, bf16[256,1024]{1,0:T(8,128)(2,1)}, u32[]{:S(2)}, u32[]{:S(2)}) %collective-permute-start.10) | collective-permute-done | bytes 524320 | tf_op jit(solution)/shard_map/ppermute | solution.py:69
  91.0 4.9 %multiply_convert_fusion.1 = (bf16[1024,1024]{1,0:T(8,128)(2,1)S(1)}, f32[1024,1024]{1,0:T(8,128)S(1)}) fusion(f32[1024]{0:T(1024)S(1)} %copy-done.38, bf16[1024,1024]{1,0:T(8,128)(2,1)S(1)} %copy-done, bf16[256,1024]{1,0:T(8,128)(2,1)} %collective-permute-done.8, bf16[256,1024]{1,0:T(8,128)(2,1)} %collective-permute-done.7, ...), kind=kOutput, calls=%fused_computation.21 | convolution fusion | flops 2162163712 | bytes 10489856 | tf_op jit(solution)/shard_map/dot_general | solution.py:221
  95.9 6.0 %fusion.11 = bf16[1024,1024]{1,0:T(8,128)(2,1)S(1)} fusion(f32[1024,1024]{1,0:T(8,128)S(1)} %get-tuple-element.99, bf16[1024,1024]{1,0:T(8,128)(2,1)S(1)} %copy-done.35, f32[1024]{0:T(1024)S(1)} %copy-done.38, bf16[256,1024]{1,0:T(8,128)(2,1)S(1)} %collective-permute-done.11, bf16[256,1024]{1,0:T(8,128)(2,1)} %collective-permute-done.10, ...), kind=kOutput, calls=%fused_computation.17 | convolution fusion | flops 2167406592 | bytes 10489856 | tf_op jit(solution)/shard_map/dot_general | solution.py:20
  107.1 3.8 fusion.37
  114.1 22.8 %collective-permute-done.29 = f32[1,1152]{1,0:T(1,128)S(1)} collective-permute-done((f32[1,1152]{1,0:T(1,128)S(1)}, f32[1,1152]{1,0:T(1,128)S(1)}, u32[]{:S(2)}, u32[]{:S(2)}) %collective-permute-start.29) | collective-permute-done | bytes 4640 | tf_op jit(solution)/shard_map/ppermute | solution.py:69
  140.4 3.9 fusion.38
  144.4 2.7 collective-permute-start.31
  153.7 12.7 %collective-permute-done.14 = bf16[256,1024]{1,0:T(8,128)(2,1)S(1)} collective-permute-done((bf16[256,1024]{1,0:T(8,128)(2,1)S(1)}, bf16[256,1024]{1,0:T(8,128)(2,1)S(1)}, u32[]{:S(2)}, u32[]{:S(2)}) %collective-permute-start.14) | collective-permute-done | bytes 524320 | tf_op jit(solution)/shard_map/ppermute | solution.py:69
  169.1 3.2 collective-permute-done.47
  176.4 2.7 collective-permute-start.49
  179.6 5.3 %collective-permute-done.49 = f32[4,1024]{1,0:T(4,128)S(1)} collective-permute-done((f32[4,1024]{1,0:T(4,128)S(1)}, f32[4,1024]{1,0:T(4,128)S(1)}, u32[]{:S(2)}, u32[]{:S(2)}) %collective-permute-start.49) | collective-permute-done | bytes 16416 | tf_op jit(solution)/shard_map/ppermute | solution.py:69
  184.9 3.6 collective-permute-start.53
  193.6 13.1 %collective-permute-done.53 = bf16[256,1024]{1,0:T(8,128)(2,1)S(1)} collective-permute-done((bf16[256,1024]{1,0:T(8,128)(2,1)S(1)}, bf16[256,1024]{1,0:T(8,128)(2,1)S(1)}, u32[]{:S(2)}, u32[]{:S(2)}) %collective-permute-start.53) | collective-permute-done | bytes 524320 | tf_op jit(solution)/shard_map/ppermute | solution.py:69
  207.8 2.9 collective-permute-start.61
  210.7 15.7 %collective-permute-done.54 = bf16[128,1024]{1,0:T(8,128)(2,1)S(1)} collective-permute-done((bf16[128,1024]{1,0:T(8,128)(2,1)S(1)}, bf16[128,1024]{1,0:T(8,128)(2,1)S(1)}, u32[]{:S(2)}, u32[]{:S(2)}) %collective-permute-start.54) | collective-permute-done | bytes 262176 | tf_op jit(solution)/shard_map/ppermute | solution.py:69
  227.4 12.2 %multiply_reduce_fusion = (f32[4,1024]{1,0:T(4,128)S(1)}, f32[4,1024,1024]{1,2,0:T(8,128)}) fusion(f32[4,1024,1024]{1,2,0:T(8,128)} %copy-done.2, f32[4,1024]{1,0:T(4,128)S(1)} %log_add_fusion, pred[1024,1024]{0,1:T(8,128)(4,1)S(1)} %broadcast_compare_fusion, bf16[1024,4,64]{0,2,1:T(8,128)(2,1)S(1)} %bitcast.80, bf16[1024,4,64]{0,2,1:T(8,128)(2,1)S(1)} %bitcast.77), kind=kOutput, calls=%fused_computation.1 | convolution fusion | flops 557838336 | bytes 35684352 | tf_op jit(solution)/shard_map/bhe,khe->hbk/dot_general | solution.py:147
  239.7 8.6 %convert_reduce_fusion.1 = (f32[4,64]{1,0:T(4,128)S(1)}, bf16[4,64,1024]{2,1,0:T(8,128)(2,1)}) fusion(bf16[1024,4,64]{0,2,1:T(8,128)(2,1)S(1)} %bitcast.81, f32[4,1024,1024]{1,2,0:T(8,128)} %copy-done.2, f32[4,1024]{1,0:T(4,128)S(1)} %log_add_fusion, pred[1024,1024]{0,1:T(8,128)(4,1)S(1)} %broadcast_compare_fusion), kind=kOutput, calls=%fused_computation.74 | convolution fusion | flops 554434304 | bytes 18891776 | tf_op jit(solution)/shard_map/hbk,bhe->khe/dot_general | solution.py:146
  248.3 12.2 %multiply_convert_fusion = bf16[4,1024,1024]{1,2,0:T(8,128)(2,1)S(1)} fusion(f32[4,1024,1024]{1,2,0:T(8,128)} %get-tuple-element.105, f32[4,1024,1024]{1,2,0:T(8,128)} %copy-done.2, f32[4,1024]{1,0:T(4,128)S(1)} %get-tuple-element.104, f32[4,1024]{1,0:T(4,128)S(1)} %log_add_fusion, pred[1024,1024]{0,1:T(8,128)(4,1)S(1)} %broadcast_compare_fusion), kind=kLoop, calls=%fused_computation | loop fusion | flops 25165824 | bytes 43024384 | tf_op jit(solution)/shard_map/convert_element_type | solution.py:149
  262.2 2.7 fusion.17
  270.5 3.5 fusion.74
  274.0 3.2 fusion.35
  281.1 2.6 collective-permute-start.62
  283.9 11.9 %collective-permute-done.39 = f32[2,256]{1,0:T(2,128)S(1)} collective-permute-done((f32[2,256]{1,0:T(2,128)S(1)}, f32[2,256]{1,0:T(2,128)S(1)}, u32[]{:S(2)}, u32[]{:S(2)}) %collective-permute-start.39) | collective-permute-done | bytes 2080 | tf_op jit(solution)/shard_map/ppermute | solution.py:69
  297.6 3.2 collective-permute-done.42
  302.8 2.5 collective-permute-done.40
  307.9 2.7 collective-permute-done.43
  310.6 2.4 collective-permute-start.56
  314.6 8.2 %collective-permute-done.44 = bf16[32,1024]{1,0:T(8,128)(2,1)S(1)} collective-permute-done((bf16[32,1024]{1,0:T(8,128)(2,1)S(1)}, bf16[32,1024]{1,0:T(8,128)(2,1)S(1)}, u32[]{:S(2)}, u32[]{:S(2)}) %collective-permute-start.44) | collective-permute-done | bytes 65568 | tf_op jit(solution)/shard_map/ppermute | solution.py:69
  324.4 2.7 collective-permute-start.45
  327.6 2.5 collective-permute-done.45
  332.5 36.9 %collective-permute-done.46 = bf16[128,1024]{1,0:T(8,128)(2,1)S(1)} collective-permute-done((bf16[128,1024]{1,0:T(8,128)(2,1)S(1)}, bf16[128,1024]{1,0:T(8,128)(2,1)S(1)}, u32[]{:S(2)}, u32[]{:S(2)}) %collective-permute-start.46) | collective-permute-done | bytes 262176 | tf_op jit(solution)/shard_map/ppermute | solution.py:69
  375.2 4.5 %collective-permute-done.33 = bf16[3,256,256]{1,2,0:T(8,128)(2,1)S(1)} collective-permute-done((bf16[3,256,256]{1,2,0:T(8,128)(2,1)S(1)}, bf16[3,256,256]{1,2,0:T(8,128)(2,1)S(1)}, u32[]{:S(2)}, u32[]{:S(2)}) %collective-permute-start.33) | collective-permute-done | bytes 393248 | tf_op jit(solution)/shard_map/ppermute | solution.py:69
  382.2 7.1 %collective-permute-done.34 = bf16[3,128,256]{1,2,0:T(8,128)(2,1)S(1)} collective-permute-done((bf16[3,128,256]{1,2,0:T(8,128)(2,1)S(1)}, bf16[3,128,256]{1,2,0:T(8,128)(2,1)S(1)}, u32[]{:S(2)}, u32[]{:S(2)}) %collective-permute-start.34) | collective-permute-done | bytes 196640 | tf_op jit(solution)/shard_map/ppermute | solution.py:69
  389.4 3.0 collective-permute-start.26
  392.4 5.1 %collective-permute-done.35 = bf16[3,128,256]{1,2,0:T(8,128)(2,1)S(1)} collective-permute-done((bf16[3,128,256]{1,2,0:T(8,128)(2,1)S(1)}, bf16[3,128,256]{1,2,0:T(8,128)(2,1)S(1)}, u32[]{:S(2)}, u32[]{:S(2)}) %collective-permute-start.35) | collective-permute-done | bytes 196640 | tf_op jit(solution)/shard_map/ppermute | solution.py:69
  399.5 5.9 %collective-permute-done.36 = bf16[3,256,256]{1,2,0:T(8,128)(2,1)S(1)} collective-permute-done((bf16[3,256,256]{1,2,0:T(8,128)(2,1)S(1)}, bf16[3,256,256]{1,2,0:T(8,128)(2,1)S(1)}, u32[]{:S(2)}, u32[]{:S(2)}) %collective-permute-start.36) | collective-permute-done | bytes 393248 | tf_op jit(solution)/shard_map/ppermute | solution.py:69
  408.5 2.9 convert_multiply_fusion
  411.4 2.9 convert_multiply_fusion.1
  414.3 4.8 %collective-permute-done.37 = bf16[3,512,256]{1,2,0:T(8,128)(2,1)S(1)} collective-permute-done((bf16[3,512,256]{1,2,0:T(8,128)(2,1)S(1)}, bf16[3,512,256]{1,2,0:T(8,128)(2,1)S(1)}, u32[]{:S(2)}, u32[]{:S(2)}) %collective-permute-start.37) | collective-permute-done | bytes 786464 | tf_op jit(solution)/shard_map/ppermute | solution.py:69
  421.3 3.5 copy.50
  (286 shorter events, 94.9 us)
Async XLA Ops:
  10.8 15.2 %collective-permute-start.1 = (bf16[256,1024]{1,0:T(8,128)(2,1)}, bf16[256,1024]{1,0:T(8,128)(2,1)}, u32[]{:S(2)}, u32[]{:S(2)}) collective-permute-start(bf16[256,1024]{1,0:T(8,128)(2,1)} %add_convert_fusion.2), channel_id=1, source_target_pairs={{0,2},{1,3},{2,0},{3,1},{4,6},{5,7},{6,4},{7,5},{8,10},{9,11},{10,... | collective-permute-start | bytes 1572872 | tf_op jit(solution)/shard_map/ppermute | solution.py:69
  13.8 13.1 %collective-permute-start = (bf16[256,1024]{1,0:T(8,128)(2,1)}, bf16[256,1024]{1,0:T(8,128)(2,1)}, u32[]{:S(2)}, u32[]{:S(2)}) collective-permute-start(bf16[256,1024]{1,0:T(8,128)(2,1)} %add_convert_fusion.2), channel_id=1, source_target_pairs={{0,1},{1,0},{2,3},{3,2},{4,5},{5,4},{6,7},{7,6},{8,9},{9,8},{10,11... | collective-permute-start | bytes 1572872 | tf_op jit(solution)/shard_map/ppermute | solution.py:69
  49.9 14.0 %collective-permute-start.5 = (bf16[256,1024]{1,0:T(8,128)(2,1)S(1)}, bf16[256,1024]{1,0:T(8,128)(2,1)S(1)}, u32[]{:S(2)}, u32[]{:S(2)}) collective-permute-start(bf16[256,1024]{1,0:T(8,128)(2,1)S(1)} %fusion.28), channel_id=1, source_target_pairs={{0,2},{1,3},{2,0},{3,1},{4,6},{5,7},{6,4},{7,5},{8,10},{9,11},{10,... | collective-permute-start | bytes 1572872 | tf_op jit(solution)/shard_map/ppermute | solution.py:69
  66.3 15.1 %collective-permute-start.7 = (bf16[256,1024]{1,0:T(8,128)(2,1)}, bf16[256,1024]{1,0:T(8,128)(2,1)}, u32[]{:S(2)}, u32[]{:S(2)}) collective-permute-start(bf16[256,1024]{1,0:T(8,128)(2,1)} %add_convert_fusion.1), channel_id=1, source_target_pairs={{0,2},{1,3},{2,0},{3,1},{4,6},{5,7},{6,4},{7,5},{8,10},{9,11},{10,... | collective-permute-start | bytes 1572872 | tf_op jit(solution)/shard_map/ppermute | solution.py:69
  68.0 22.9 %collective-permute-start.10 = (bf16[256,1024]{1,0:T(8,128)(2,1)}, bf16[256,1024]{1,0:T(8,128)(2,1)}, u32[]{:S(2)}, u32[]{:S(2)}) collective-permute-start(bf16[256,1024]{1,0:T(8,128)(2,1)} %get-tuple-element.91), channel_id=1, source_target_pairs={{0,2},{1,3},{2,0},{3,1},{4,6},{5,7},{6,4},{7,5},{8,10},{9,11},{10,... | collective-permute-start | bytes 1572872 | tf_op jit(solution)/shard_map/ppermute | solution.py:69
  68.3 22.7 %collective-permute-start.6 = (bf16[256,1024]{1,0:T(8,128)(2,1)}, bf16[256,1024]{1,0:T(8,128)(2,1)}, u32[]{:S(2)}, u32[]{:S(2)}) collective-permute-start(bf16[256,1024]{1,0:T(8,128)(2,1)} %add_convert_fusion.1), channel_id=1, source_target_pairs={{0,1},{1,0},{2,3},{3,2},{4,5},{5,4},{6,7},{7,6},{8,9},{9,8},{10,11... | collective-permute-start | bytes 1572872 | tf_op jit(solution)/shard_map/ppermute | solution.py:69
  81.4 9.6 %collective-permute-start.8 = (bf16[256,1024]{1,0:T(8,128)(2,1)}, bf16[256,1024]{1,0:T(8,128)(2,1)}, u32[]{:S(2)}, u32[]{:S(2)}) collective-permute-start(bf16[256,1024]{1,0:T(8,128)(2,1)} %collective-permute-done.7), channel_id=1, source_target_pairs={{0,1},{1,0},{2,3},{3,2},{4,5},{5,4},{6,7},{7,6},{8,9},{9,8},{10,11... | collective-permute-start | bytes 1572872 | tf_op jit(solution)/shard_map/ppermute | solution.py:69
  81.4 14.5 %collective-permute-start.9 = (bf16[256,1024]{1,0:T(8,128)(2,1)}, bf16[256,1024]{1,0:T(8,128)(2,1)}, u32[]{:S(2)}, u32[]{:S(2)}) collective-permute-start(bf16[256,1024]{1,0:T(8,128)(2,1)} %get-tuple-element.91), channel_id=1, source_target_pairs={{0,1},{1,0},{2,3},{3,2},{4,5},{5,4},{6,7},{7,6},{8,9},{9,8},{10,11... | collective-permute-start | bytes 1572872 | tf_op jit(solution)/shard_map/ppermute | solution.py:69
  111.1 57.7 %collective-permute-start.58 = (bf16[512,1024]{1,0:T(8,128)(2,1)S(1)}, bf16[512,1024]{1,0:T(8,128)(2,1)S(1)}, u32[]{:S(2)}, u32[]{:S(2)}) collective-permute-start(bf16[512,1024]{1,0:T(8,128)(2,1)S(1)} %dynamic-slice_convert_fusion), channel_id=1, source_target_pairs={{0,4},{4,0},{8,12},{12,8},{16,20},{20,16},{24,28},{28,24},{1,5},{5... | collective-permute-start | bytes 3145736 | tf_op jit(solution)/shard_map/ppermute | solution.py:69
  113.0 23.9 %collective-permute-start.29 = (f32[1,1152]{1,0:T(1,128)S(1)}, f32[1,1152]{1,0:T(1,128)S(1)}, u32[]{:S(2)}, u32[]{:S(2)}) collective-permute-start(f32[1,1152]{1,0:T(1,128)S(1)} %broadcast_in_dim.40), channel_id=1, source_target_pairs={{0,4},{4,0},{8,12},{12,8},{16,20},{20,16},{24,28},{28,24},{1,5},{5... | collective-permute-start | bytes 13832 | tf_op jit(solution)/shard_map/ppermute | solution.py:69
  113.3 25.4 %collective-permute-start.16 = (bf16[256,1024]{1,0:T(8,128)(2,1)S(1)}, bf16[256,1024]{1,0:T(8,128)(2,1)S(1)}, u32[]{:S(2)}, u32[]{:S(2)}) collective-permute-start(bf16[256,1024]{1,0:T(8,128)(2,1)S(1)} %get-tuple-element.68), channel_id=1, source_target_pairs={{0,1},{1,0},{2,3},{3,2},{4,5},{5,4},{6,7},{7,6},{8,9},{9,8},{10,11... | collective-permute-start | bytes 1572872 | tf_op jit(solution)/shard_map/ppermute | solution.py:69
  113.5 38.2 %collective-permute-start.13 = (bf16[256,1024]{1,0:T(8,128)(2,1)S(1)}, bf16[256,1024]{1,0:T(8,128)(2,1)S(1)}, u32[]{:S(2)}, u32[]{:S(2)}) collective-permute-start(bf16[256,1024]{1,0:T(8,128)(2,1)S(1)} %get-tuple-element.70), channel_id=1, source_target_pairs={{0,1},{1,0},{2,3},{3,2},{4,5},{5,4},{6,7},{7,6},{8,9},{9,8},{10,11... | collective-permute-start | bytes 1572872 | tf_op jit(solution)/shard_map/ppermute | solution.py:69
  114.0 38.0 %collective-permute-start.15 = (bf16[256,1024]{1,0:T(8,128)(2,1)S(1)}, bf16[256,1024]{1,0:T(8,128)(2,1)S(1)}, u32[]{:S(2)}, u32[]{:S(2)}) collective-permute-start(bf16[256,1024]{1,0:T(8,128)(2,1)S(1)} %get-tuple-element.67), channel_id=1, source_target_pairs={{0,1},{1,0},{2,3},{3,2},{4,5},{5,4},{6,7},{7,6},{8,9},{9,8},{10,11... | collective-permute-start | bytes 1572872 | tf_op jit(solution)/shard_map/ppermute | solution.py:69
  138.9 13.7 %collective-permute-start.17 = (bf16[256,1024]{1,0:T(8,128)(2,1)S(1)}, bf16[256,1024]{1,0:T(8,128)(2,1)S(1)}, u32[]{:S(2)}, u32[]{:S(2)}) collective-permute-start(bf16[256,1024]{1,0:T(8,128)(2,1)S(1)} %fusion.21), channel_id=1, source_target_pairs={{0,2},{1,3},{2,0},{3,1},{4,6},{5,7},{6,4},{7,5},{8,10},{9,11},{10,... | collective-permute-start | bytes 1572872 | tf_op jit(solution)/shard_map/ppermute | solution.py:69
  149.0 30.1 %collective-permute-start.52 = (bf16[512,1024]{1,0:T(8,128)(2,1)S(1)}, bf16[512,1024]{1,0:T(8,128)(2,1)S(1)}, u32[]{:S(2)}, u32[]{:S(2)}) collective-permute-start(bf16[512,1024]{1,0:T(8,128)(2,1)S(1)} %dynamic-slice_convert_fusion.1), channel_id=1, source_target_pairs={{0,4},{4,0},{8,12},{12,8},{16,20},{20,16},{24,28},{28,24},{1,5},{5... | collective-permute-start | bytes 3145736 | tf_op jit(solution)/shard_map/ppermute | solution.py:69
  152.0 14.4 %collective-permute-start.14 = (bf16[256,1024]{1,0:T(8,128)(2,1)S(1)}, bf16[256,1024]{1,0:T(8,128)(2,1)S(1)}, u32[]{:S(2)}, u32[]{:S(2)}) collective-permute-start(bf16[256,1024]{1,0:T(8,128)(2,1)S(1)} %fusion.23), channel_id=1, source_target_pairs={{0,2},{1,3},{2,0},{3,1},{4,6},{5,7},{6,4},{7,5},{8,10},{9,11},{10,... | collective-permute-start | bytes 1572872 | tf_op jit(solution)/shard_map/ppermute | solution.py:69
  173.0 19.4 %collective-permute-start.59 = (bf16[256,1024]{1,0:T(8,128)(2,1)S(1)}, bf16[256,1024]{1,0:T(8,128)(2,1)S(1)}, u32[]{:S(2)}, u32[]{:S(2)}) collective-permute-start(bf16[256,1024]{1,0:T(8,128)(2,1)S(1)} %dynamic-slice_convert_fusion.3), channel_id=1, source_target_pairs={{0,8},{4,12},{8,0},{12,4},{16,24},{20,28},{24,16},{28,20},{1,9},{5... | collective-permute-start | bytes 1572872 | tf_op jit(solution)/shard_map/ppermute | solution.py:69
  176.4 8.5 %collective-permute-start.49 = (f32[4,1024]{1,0:T(4,128)S(1)}, f32[4,1024]{1,0:T(4,128)S(1)}, u32[]{:S(2)}, u32[]{:S(2)}) collective-permute-start(f32[4,1024]{1,0:T(4,128)S(1)} %fusion.99), channel_id=1, source_target_pairs={{0,16},{4,20},{8,24},{12,28},{16,0},{20,4},{24,8},{28,12},{1,17},{... | collective-permute-start | bytes 49160 | tf_op jit(solution)/shard_map/ppermute | solution.py:69
  184.9 21.8 %collective-permute-start.53 = (bf16[256,1024]{1,0:T(8,128)(2,1)S(1)}, bf16[256,1024]{1,0:T(8,128)(2,1)S(1)}, u32[]{:S(2)}, u32[]{:S(2)}) collective-permute-start(bf16[256,1024]{1,0:T(8,128)(2,1)S(1)} %dynamic-slice_convert_fusion.4), channel_id=1, source_target_pairs={{0,8},{4,12},{8,0},{12,4},{16,24},{20,28},{24,16},{28,20},{1,9},{5... | collective-permute-start | bytes 1572872 | tf_op jit(solution)/shard_map/ppermute | solution.py:69
  189.7 17.3 %collective-permute-start.19 = (bf16[256,1024]{1,0:T(8,128)(2,1)S(1)}, bf16[256,1024]{1,0:T(8,128)(2,1)S(1)}, u32[]{:S(2)}, u32[]{:S(2)}) collective-permute-start(bf16[256,1024]{1,0:T(8,128)(2,1)S(1)} %get-tuple-element.55), channel_id=1, source_target_pairs={{0,2},{1,3},{2,0},{3,1},{4,6},{5,7},{6,4},{7,5},{8,10},{9,11},{10,... | collective-permute-start | bytes 1572872 | tf_op jit(solution)/shard_map/ppermute | solution.py:69
  191.2 35.3 %collective-permute-start.18 = (bf16[256,1024]{1,0:T(8,128)(2,1)S(1)}, bf16[256,1024]{1,0:T(8,128)(2,1)S(1)}, u32[]{:S(2)}, u32[]{:S(2)}) collective-permute-start(bf16[256,1024]{1,0:T(8,128)(2,1)S(1)} %get-tuple-element.55), channel_id=1, source_target_pairs={{0,1},{1,0},{2,3},{3,2},{4,5},{5,4},{6,7},{7,6},{8,9},{9,8},{10,11... | collective-permute-start | bytes 1572872 | tf_op jit(solution)/shard_map/ppermute | solution.py:69
  192.6 15.1 %collective-permute-start.60 = (bf16[128,1024]{1,0:T(8,128)(2,1)S(1)}, bf16[128,1024]{1,0:T(8,128)(2,1)S(1)}, u32[]{:S(2)}, u32[]{:S(2)}) collective-permute-start(bf16[128,1024]{1,0:T(8,128)(2,1)S(1)} %dynamic-slice_convert_fusion.6), channel_id=1, source_target_pairs={{0,16},{4,20},{8,24},{12,28},{16,0},{20,4},{24,8},{28,12},{1,17},{... | collective-permute-start | bytes 786440 | tf_op jit(solution)/shard_map/ppermute | solution.py:69
  206.9 19.4 %collective-permute-start.54 = (bf16[128,1024]{1,0:T(8,128)(2,1)S(1)}, bf16[128,1024]{1,0:T(8,128)(2,1)S(1)}, u32[]{:S(2)}, u32[]{:S(2)}) collective-permute-start(bf16[128,1024]{1,0:T(8,128)(2,1)S(1)} %dynamic-slice_convert_fusion.7), channel_id=1, source_target_pairs={{0,16},{4,20},{8,24},{12,28},{16,0},{20,4},{24,8},{28,12},{1,17},{... | collective-permute-start | bytes 786440 | tf_op jit(solution)/shard_map/ppermute | solution.py:69
  207.0 19.5 %collective-permute-start.20 = (bf16[256,1024]{1,0:T(8,128)(2,1)S(1)}, bf16[256,1024]{1,0:T(8,128)(2,1)S(1)}, u32[]{:S(2)}, u32[]{:S(2)}) collective-permute-start(bf16[256,1024]{1,0:T(8,128)(2,1)S(1)} %collective-permute-done.19), channel_id=1, source_target_pairs={{0,1},{1,0},{2,3},{3,2},{4,5},{5,4},{6,7},{7,6},{8,9},{9,8},{10,11... | collective-permute-start | bytes 1572872 | tf_op jit(solution)/shard_map/ppermute | solution.py:69
  207.8 70.2 %collective-permute-start.61 = (bf16[128,1024]{1,0:T(8,128)(2,1)S(1)}, bf16[128,1024]{1,0:T(8,128)(2,1)}, u32[]{:S(2)}, u32[]{:S(2)}) collective-permute-start(bf16[128,1024]{1,0:T(8,128)(2,1)S(1)} %add_convert_fusion.3), channel_id=1, source_target_pairs={{0,16},{4,20},{8,24},{12,28},{16,0},{20,4},{24,8},{28,12},{1,17},{... | collective-permute-start | bytes 786440 | tf_op jit(solution)/shard_map/ppermute | solution.py:69
  226.4 52.9 %collective-permute-start.55 = (bf16[128,1024]{1,0:T(8,128)(2,1)S(1)}, bf16[128,1024]{1,0:T(8,128)(2,1)}, u32[]{:S(2)}, u32[]{:S(2)}) collective-permute-start(bf16[128,1024]{1,0:T(8,128)(2,1)S(1)} %add_convert_fusion.4), channel_id=1, source_target_pairs={{0,16},{4,20},{8,24},{12,28},{16,0},{20,4},{24,8},{28,12},{1,17},{... | collective-permute-start | bytes 786440 | tf_op jit(solution)/shard_map/ppermute | solution.py:69
  266.8 16.9 %collective-permute-start.41 = (bf16[128,1024]{1,0:T(8,128)(2,1)}, bf16[128,1024]{1,0:T(8,128)(2,1)S(1)}, u32[]{:S(2)}, u32[]{:S(2)}) collective-permute-start(bf16[128,1024]{1,0:T(8,128)(2,1)} %dynamic-slice_convert_fusion.8), channel_id=1, source_target_pairs={{0,4},{4,0},{8,12},{12,8},{16,20},{20,16},{24,28},{28,24},{1,5},{5... | collective-permute-start | bytes 786440 | tf_op jit(solution)/shard_map/ppermute | solution.py:69
  267.5 13.6 %collective-permute-start.38 = (f32[2,256]{1,0:T(2,128)S(1)}, f32[2,256]{1,0:T(2,128)S(1)}, u32[]{:S(2)}, u32[]{:S(2)}) collective-permute-start(f32[2,256]{1,0:T(2,128)S(1)} %pad_maximum_fusion.15), channel_id=1, source_target_pairs={{0,4},{4,0},{8,12},{12,8},{16,20},{20,16},{24,28},{28,24},{1,5},{5... | collective-permute-start | bytes 6152 | tf_op jit(solution)/shard_map/ppermute | solution.py:69
  277.4 53.0 %collective-permute-start.32 = (bf16[3,512,256]{1,2,0:T(8,128)(2,1)S(1)}, bf16[3,512,256]{1,2,0:T(8,128)(2,1)S(1)}, u32[]{:S(2)}, u32[]{:S(2)}) collective-permute-start(bf16[3,512,256]{1,2,0:T(8,128)(2,1)S(1)} %fusion.36), channel_id=1, source_target_pairs={{0,4},{4,0},{8,12},{12,8},{16,20},{20,16},{24,28},{28,24},{1,5},{5... | collective-permute-start | bytes 2359304 | tf_op jit(solution)/shard_map/ppermute | solution.py:69
  278.0 35.0 %collective-permute-start.22 = (bf16[256,1024]{1,0:T(8,128)(2,1)S(1)}, bf16[256,1024]{1,0:T(8,128)(2,1)S(1)}, u32[]{:S(2)}, u32[]{:S(2)}) collective-permute-start(bf16[256,1024]{1,0:T(8,128)(2,1)S(1)} %get-tuple-element.66), channel_id=1, source_target_pairs={{0,1},{1,0},{2,3},{3,2},{4,5},{5,4},{6,7},{7,6},{8,9},{9,8},{10,11... | collective-permute-start | bytes 1572872 | tf_op jit(solution)/shard_map/ppermute | solution.py:69
  279.3 93.6 %collective-permute-start.21 = (bf16[256,1024]{1,0:T(8,128)(2,1)S(1)}, bf16[256,1024]{1,0:T(8,128)(2,1)S(1)}, u32[]{:S(2)}, u32[]{:S(2)}) collective-permute-start(bf16[256,1024]{1,0:T(8,128)(2,1)S(1)} %get-tuple-element.65), channel_id=1, source_target_pairs={{0,1},{1,0},{2,3},{3,2},{4,5},{5,4},{6,7},{7,6},{8,9},{9,8},{10,11... | collective-permute-start | bytes 1572872 | tf_op jit(solution)/shard_map/ppermute | solution.py:69
  281.1 32.4 %collective-permute-start.62 = (bf16[256,1024]{1,0:T(8,128)(2,1)S(1)}, bf16[256,1024]{1,0:T(8,128)(2,1)S(1)}, u32[]{:S(2)}, u32[]{:S(2)}) collective-permute-start(bf16[256,1024]{1,0:T(8,128)(2,1)S(1)} %maximum_select_fusion.8), channel_id=1, source_target_pairs={{0,8},{4,12},{8,0},{12,4},{16,24},{20,28},{24,16},{28,20},{1,9},{5... | collective-permute-start | bytes 1572872 | tf_op jit(solution)/shard_map/ppermute | solution.py:69
  283.7 12.1 %collective-permute-start.39 = (f32[2,256]{1,0:T(2,128)S(1)}, f32[2,256]{1,0:T(2,128)S(1)}, u32[]{:S(2)}, u32[]{:S(2)}) collective-permute-start(f32[2,256]{1,0:T(2,128)S(1)} %fusion.54), channel_id=1, source_target_pairs={{0,8},{4,12},{8,0},{12,4},{16,24},{20,28},{24,16},{28,20},{1,9},{5... | collective-permute-start | bytes 6152 | tf_op jit(solution)/shard_map/ppermute | solution.py:69
  310.6 13.8 %collective-permute-start.56 = (bf16[256,1024]{1,0:T(8,128)(2,1)S(1)}, bf16[256,1024]{1,0:T(8,128)(2,1)S(1)}, u32[]{:S(2)}, u32[]{:S(2)}) collective-permute-start(bf16[256,1024]{1,0:T(8,128)(2,1)S(1)} %maximum_select_fusion.7), channel_id=1, source_target_pairs={{0,8},{4,12},{8,0},{12,4},{16,24},{20,28},{24,16},{28,20},{1,9},{5... | collective-permute-start | bytes 1572872 | tf_op jit(solution)/shard_map/ppermute | solution.py:69
  313.1 9.7 %collective-permute-start.44 = (bf16[32,1024]{1,0:T(8,128)(2,1)S(1)}, bf16[32,1024]{1,0:T(8,128)(2,1)S(1)}, u32[]{:S(2)}, u32[]{:S(2)}) collective-permute-start(bf16[32,1024]{1,0:T(8,128)(2,1)S(1)} %add_convert_fusion.6), channel_id=1, source_target_pairs={{0,16},{4,20},{8,24},{12,28},{16,0},{20,4},{24,8},{28,12},{1,17},{... | collective-permute-start | bytes 196616 | tf_op jit(solution)/shard_map/ppermute | solution.py:69
  313.5 59.4 %collective-permute-start.23 = (bf16[256,1024]{1,0:T(8,128)(2,1)S(1)}, bf16[256,1024]{1,0:T(8,128)(2,1)S(1)}, u32[]{:S(2)}, u32[]{:S(2)}) collective-permute-start(bf16[256,1024]{1,0:T(8,128)(2,1)S(1)} %fusion.19), channel_id=1, source_target_pairs={{0,2},{1,3},{2,0},{3,1},{4,6},{5,7},{6,4},{7,5},{8,10},{9,11},{10,... | collective-permute-start | bytes 1572872 | tf_op jit(solution)/shard_map/ppermute | solution.py:69
  322.8 85.7 %collective-permute-start.63 = (bf16[512,1024]{1,0:T(8,128)(2,1)S(1)}, bf16[512,1024]{1,0:T(8,128)(2,1)S(1)}, u32[]{:S(2)}, u32[]{:S(2)}) collective-permute-start(bf16[512,1024]{1,0:T(8,128)(2,1)S(1)} %maximum_select_fusion.4), channel_id=1, source_target_pairs={{0,4},{4,0},{8,12},{12,8},{16,20},{20,16},{24,28},{28,24},{1,5},{5... | collective-permute-start | bytes 3145736 | tf_op jit(solution)/shard_map/ppermute | solution.py:69
  330.1 81.3 %collective-permute-start.57 = (bf16[512,1024]{1,0:T(8,128)(2,1)S(1)}, bf16[512,1024]{1,0:T(8,128)(2,1)S(1)}, u32[]{:S(2)}, u32[]{:S(2)}) collective-permute-start(bf16[512,1024]{1,0:T(8,128)(2,1)S(1)} %maximum_select_fusion.3), channel_id=1, source_target_pairs={{0,4},{4,0},{8,12},{12,8},{16,20},{20,16},{24,28},{28,24},{1,5},{5... | collective-permute-start | bytes 3145736 | tf_op jit(solution)/shard_map/ppermute | solution.py:69
  330.4 39.0 %collective-permute-start.46 = (bf16[128,1024]{1,0:T(8,128)(2,1)S(1)}, bf16[128,1024]{1,0:T(8,128)(2,1)S(1)}, u32[]{:S(2)}, u32[]{:S(2)}) collective-permute-start(bf16[128,1024]{1,0:T(8,128)(2,1)S(1)} %maximum_select_fusion.10), channel_id=1, source_target_pairs={{0,4},{4,0},{8,12},{12,8},{16,20},{20,16},{24,28},{28,24},{1,5},{5... | collective-permute-start | bytes 786440 | tf_op jit(solution)/shard_map/ppermute | solution.py:69
  369.4 10.3 %collective-permute-start.33 = (bf16[3,256,256]{1,2,0:T(8,128)(2,1)S(1)}, bf16[3,256,256]{1,2,0:T(8,128)(2,1)S(1)}, u32[]{:S(2)}, u32[]{:S(2)}) collective-permute-start(bf16[3,256,256]{1,2,0:T(8,128)(2,1)S(1)} %dynamic-slice_convert_fusion.5), channel_id=1, source_target_pairs={{0,8},{4,12},{8,0},{12,4},{16,24},{20,28},{24,16},{28,20},{1,9},{5... | collective-permute-start | bytes 1179656 | tf_op jit(solution)/shard_map/ppermute | solution.py:69
  373.6 8.1 %collective-permute-start.24 = (f32[2,1024]{1,0:T(2,128)S(1)}, f32[2,1024]{1,0:T(2,128)S(1)}, u32[]{:S(2)}, u32[]{:S(2)}) collective-permute-start(f32[2,1024]{1,0:T(2,128)S(1)} %pad_maximum_fusion.13), channel_id=1, source_target_pairs={{0,4},{4,0},{8,12},{12,8},{16,20},{20,16},{24,28},{28,24},{1,5},{5... | collective-permute-start | bytes 24584 | tf_op jit(solution)/shard_map/ppermute | solution.py:69
  379.9 9.4 %collective-permute-start.34 = (bf16[3,128,256]{1,2,0:T(8,128)(2,1)S(1)}, bf16[3,128,256]{1,2,0:T(8,128)(2,1)S(1)}, u32[]{:S(2)}, u32[]{:S(2)}) collective-permute-start(bf16[3,128,256]{1,2,0:T(8,128)(2,1)S(1)} %dynamic-slice_convert_fusion.9), channel_id=1, source_target_pairs={{0,16},{4,20},{8,24},{12,28},{16,0},{20,4},{24,8},{28,12},{1,17},{... | collective-permute-start | bytes 589832 | tf_op jit(solution)/shard_map/ppermute | solution.py:69
  381.7 7.7 %collective-permute-start.25 = (f32[2,1024]{1,0:T(2,128)S(1)}, f32[2,1024]{1,0:T(2,128)S(1)}, u32[]{:S(2)}, u32[]{:S(2)}) collective-permute-start(f32[2,1024]{1,0:T(2,128)S(1)} %fusion.55), channel_id=1, source_target_pairs={{0,8},{4,12},{8,0},{12,4},{16,24},{20,28},{24,16},{28,20},{1,9},{5... | collective-permute-start | bytes 24584 | tf_op jit(solution)/shard_map/ppermute | solution.py:69
  389.3 8.1 %collective-permute-start.35 = (bf16[3,128,256]{1,2,0:T(8,128)(2,1)S(1)}, bf16[3,128,256]{1,2,0:T(8,128)(2,1)S(1)}, u32[]{:S(2)}, u32[]{:S(2)}) collective-permute-start(bf16[3,128,256]{1,2,0:T(8,128)(2,1)S(1)} %add_convert_fusion.5), channel_id=1, source_target_pairs={{0,16},{4,20},{8,24},{12,28},{16,0},{20,4},{24,8},{28,12},{1,17},{... | collective-permute-start | bytes 589832 | tf_op jit(solution)/shard_map/ppermute | solution.py:69
  389.4 8.3 %collective-permute-start.26 = (f32[2,1024]{1,0:T(2,128)S(1)}, f32[2,1024]{1,0:T(2,128)S(1)}, u32[]{:S(2)}, u32[]{:S(2)}) collective-permute-start(f32[2,1024]{1,0:T(2,128)S(1)} %fusion.101), channel_id=1, source_target_pairs={{0,16},{4,20},{8,24},{12,28},{16,0},{20,4},{24,8},{28,12},{1,17},{... | collective-permute-start | bytes 24584 | tf_op jit(solution)/shard_map/ppermute | solution.py:69
  397.6 7.8 %collective-permute-start.36 = (bf16[3,256,256]{1,2,0:T(8,128)(2,1)S(1)}, bf16[3,256,256]{1,2,0:T(8,128)(2,1)S(1)}, u32[]{:S(2)}, u32[]{:S(2)}) collective-permute-start(bf16[3,256,256]{1,2,0:T(8,128)(2,1)S(1)} %maximum_select_fusion.9), channel_id=1, source_target_pairs={{0,8},{4,12},{8,0},{12,4},{16,24},{20,28},{24,16},{28,20},{1,9},{5... | collective-permute-start | bytes 1179656 | tf_op jit(solution)/shard_map/ppermute | solution.py:69
  399.0 8.9 %collective-permute-start.28 = (f32[2,1024]{1,0:T(2,128)S(1)}, f32[2,1024]{1,0:T(2,128)S(1)}, u32[]{:S(2)}, u32[]{:S(2)}) collective-permute-start(f32[2,1024]{1,0:T(2,128)S(1)} %add.334), channel_id=1, source_target_pairs={{0,2},{1,3},{2,0},{3,1},{4,6},{5,7},{6,4},{7,5},{8,10},{9,11},{10,... | collective-permute-start | bytes 24584 | tf_op jit(solution)/shard_map/ppermute | solution.py:69
  405.6 13.5 %collective-permute-start.37 = (bf16[3,512,256]{1,2,0:T(8,128)(2,1)S(1)}, bf16[3,512,256]{1,2,0:T(8,128)(2,1)S(1)}, u32[]{:S(2)}, u32[]{:S(2)}) collective-permute-start(bf16[3,512,256]{1,2,0:T(8,128)(2,1)S(1)} %maximum_select_fusion.5), channel_id=1, source_target_pairs={{0,4},{4,0},{8,12},{12,8},{16,20},{20,16},{24,28},{28,24},{1,5},{5... | collective-permute-start | bytes 2359304 | tf_op jit(solution)/shard_map/ppermute | solution.py:69
  (55 other events, 702.8 us)

commit v2 on v1

v2 whole, which is shorter than its diff:
```python
import functools
import jax
import jax.numpy as jnp
from jax import lax
from jax.experimental import pallas as pl
from jax.experimental.pallas import tpu as pltpu
from jax.sharding import PartitionSpec as P

F32 = jnp.float32
BF16 = jnp.bfloat16
PAIR = 128
HD = 64
EXCLUDED = -1e30


def dot_nn(a, b):
    return lax.dot_general(a, b, (((1,), (0,)), ((), ())), preferred_element_type=F32)


def dot_nt(a, b):
    return lax.dot_general(a, b, (((1,), (1,)), ((), ())), preferred_element_type=F32)


def dot_tn(a, b):
    return lax.dot_general(a, b, (((0,), (0,)), ((), ())), preferred_element_type=F32)


def head_lanes(head):
    lane = lax.broadcasted_iota(jnp.int32, (1, PAIR), 1)
    return (lane >= head * HD) & (lane < (head + 1) * HD)


def attend_kernel(halves, q_ref, pick_ref, *refs):
    k_refs, v_refs, bar_refs = (
        refs[:halves],
        refs[halves : 2 * halves],
        refs[2 * halves : 3 * halves],
    )
    out_ref, log_ref = refs[3 * halves :]
    query = q_ref[0]
    scaled = query * jnp.asarray(HD**-0.5, BF16)
    pick = pick_ref[...]
    keys = [jnp.concatenate([k[0], b[...]], 1) for k, b in zip(k_refs, bar_refs)]
    rows = []
    for head in range(2):
        own = jnp.where(head_lanes(head), scaled, jnp.zeros_like(scaled))
        probe = jnp.concatenate([own, pick], 1)
        scores = [dot_nt(k, probe) for k in keys]
        top = functools.reduce(
            jnp.maximum, [jnp.max(s, 0, keepdims=True) for s in scores]
        )
        powers = [jnp.exp(s - top) for s in scores]
        total = functools.reduce(
            jnp.add, [jnp.sum(p, 0, keepdims=True) for p in powers]
        )
        summed = functools.reduce(
            jnp.add, [dot_tn(v[0], p.astype(BF16)) for v, p in zip(v_refs, powers)]
        )
        rows.append((summed / total)[head * HD : (head + 1) * HD])
        log_ref[0, head : head + 1, :] = top + jnp.log(total)
    out_ref[...] = jnp.concatenate(rows, 0).T.astype(BF16)


def attend_forward(query, pick, keys, values, bars, tile=256):
    _, count, width = query.shape
    halves = len(keys)
    pairs = width // PAIR
    tile = min(tile, count)
    grid = (pairs, count // tile)
    key_spec = [pl.BlockSpec((1, k.shape[1], PAIR), lambda p, i: (0, 0, p)) for k in keys]
    bar_spec = [pl.BlockSpec((b.shape[0], PAIR), lambda p, i: (0, 0)) for b in bars]
    total_keys = sum(k.shape[1] for k in keys)
    return pl.pallas_call(
        functools.partial(attend_kernel, halves),
        grid=grid,
        in_specs=[
            pl.BlockSpec((1, tile, PAIR), lambda p, i: (0, i, p)),
            pl.BlockSpec((tile, PAIR), lambda p, i: (i, 0)),
            *key_spec,
            *key_spec,
            *bar_spec,
        ],
        out_specs=[
            pl.BlockSpec((tile, PAIR), lambda p, i: (i, p)),
            pl.BlockSpec((1, 8, tile), lambda p, i: (p, 0, i)),
        ],
        out_shape=[
            jax.ShapeDtypeStruct((count, width), BF16),
            jax.ShapeDtypeStruct((pairs, 8, count), F32),
        ],
        cost_estimate=pl.CostEstimate(
            flops=16 * count * total_keys * width,
            bytes_accessed=6 * total_keys * width,
            transcendentals=count * total_keys * width // HD,
        ),
        name="attend_forward",
    )(query, pick, *keys, *values, *bars)


def attend_back_kernel(halves, first, last, q_ref, pick_ref, grad_ref, out_ref, log_ref, *refs):
    k_refs, v_refs, bar_refs = (
        refs[:halves],
        refs[halves : 2 * halves],
        refs[2 * halves : 3 * halves],
    )
    rest = refs[3 * halves :]
    if not first:
        k_in, v_in = rest[:halves], rest[halves : 2 * halves]
        rest = rest[2 * halves :]
    q_grad_ref = rest[0]
    k_out, v_out = rest[1 : 1 + halves], rest[1 + halves : 1 + 2 * halves]
    if last:
        k_sum, v_sum = (
            rest[1 + 2 * halves : 1 + 3 * halves],
            rest[1 + 3 * halves : 1 + 4 * halves],
        )
    else:
        k_sum, v_sum = k_out, v_out
    step = pl.program_id(1)

    @pl.when(step == 0)
    def _():
        for n in range(halves):
            if first:
                k_sum[n][...] = jnp.zeros_like(k_sum[n])
                v_sum[n][...] = jnp.zeros_like(v_sum[n])
            else:
                k_sum[n][...] = k_in[n][...]
                v_sum[n][...] = v_in[n][...]

    scaled = q_ref[0] * jnp.asarray(HD**-0.5, BF16)
    grad = grad_ref[...]
    pick = pick_ref[...]
    both = (grad.astype(F32) * out_ref[...].astype(F32)).T
    owns = [jnp.where(head_lanes(h), scaled, jnp.zeros_like(scaled)) for h in range(2)]
    grads = [jnp.where(head_lanes(h), grad, jnp.zeros_like(grad)) for h in range(2)]
    probes = [jnp.concatenate([own, pick], 1) for own in owns]
    centers = [jnp.sum(both[h * HD : (h + 1) * HD], 0, keepdims=True) for h in range(2)]
    stacked_q = jnp.concatenate(owns, 0)
    stacked_g = jnp.concatenate(grads, 0)
    q_parts = [0.0, 0.0]
    for n in range(halves):
        keys = k_refs[n][0]
        values = v_refs[n][0]
        wide = jnp.concatenate([keys, bar_refs[n][...]], 1)
        probs = []
        slopes = []
        for h in range(2):
            prob = jnp.exp(dot_nt(wide, probes[h]) - log_ref[0, h : h + 1, :])
            slope = (prob * (dot_nt(values, grads[h]) - centers[h])).astype(BF16)
            probs.append(prob.astype(BF16))
            slopes.append(slope)
            q_parts[h] = q_parts[h] + dot_tn(keys, slope)
        v_sum[n][...] += dot_nn(jnp.concatenate(probs, 1), stacked_g)
        k_sum[n][...] += dot_nn(jnp.concatenate(slopes, 1), stacked_q)
    rows = [q_parts[h][h * HD : (h + 1) * HD] * (HD**-0.5) for h in range(2)]
    q_grad_ref[...] = jnp.concatenate(rows, 0).T.astype(BF16)

    if last:

        @pl.when(step == pl.num_programs(1) - 1)
        def _():
            for n in range(halves):
                k_out[n][...] = k_sum[n][...].astype(BF16)
                v_out[n][...] = v_sum[n][...].astype(BF16)


def attend_back(query, pick, grad, out, logs, keys, values, bars, carried, last, tile=256):
    _, count, width = query.shape
    halves = len(keys)
    pairs = width // PAIR
    tile = min(tile, count)
    first = carried is None
    key_spec = [pl.BlockSpec((1, k.shape[1], PAIR), lambda p, i: (0, 0, p)) for k in keys]
    bar_spec = [pl.BlockSpec((b.shape[0], PAIR), lambda p, i: (0, 0)) for b in bars]
    sum_spec = [pl.BlockSpec((k.shape[1], PAIR), lambda p, i: (0, p)) for k in keys]
    row_spec = pl.BlockSpec((tile, PAIR), lambda p, i: (i, p))
    sum_type = BF16 if last else F32
    sums = [jax.ShapeDtypeStruct((k.shape[1], width), sum_type) for k in keys]
    total_keys = sum(k.shape[1] for k in keys)
    scratch = []
    if last:
        scratch = [pltpu.VMEM((k.shape[1], PAIR), F32) for k in keys] * 2
    extra = [] if first else list(carried[0]) + list(carried[1])
    result = pl.pallas_call(
        functools.partial(attend_back_kernel, halves, first, last),
        grid=(pairs, count // tile),
        in_specs=[
            pl.BlockSpec((1, tile, PAIR), lambda p, i: (0, i, p)),
            pl.BlockSpec((tile, PAIR), lambda p, i: (i, 0)),
            row_spec,
            row_spec,
            pl.BlockSpec((1, 8, tile), lambda p, i: (p, 0, i)),
            *key_spec,
            *key_spec,
            *bar_spec,
            *([] if first else sum_spec * 2),
        ],
        out_specs=[row_spec, *sum_spec, *sum_spec],
        out_shape=[jax.ShapeDtypeStruct((count, width), BF16), *sums, *sums],
        scratch_shapes=scratch,
        cost_estimate=pl.CostEstimate(
            flops=40 * count * total_keys * width,
            bytes_accessed=16 * total_keys * width,
            transcendentals=count * total_keys * width // HD,
        ),
        name="attend_back",
    )(query, pick, grad, out, logs, *keys, *values, *bars, *extra)
    return result[0], result[1 : 1 + halves], result[1 + halves :]


def mlp_kernel(x_ref, grad_ref, up_ref, bias_ref, down_ref, act_ref, slope_ref, back_ref):
    pre = dot_nn(x_ref[...], up_ref[...]) + bias_ref[...]
    upstream = dot_nt(grad_ref[...], down_ref[...])
    cdf = 0.5 + 0.5 * lax.erf(pre * (0.5**0.5))
    act_ref[...] = (pre * cdf).astype(BF16)
    density = jnp.exp(-0.5 * pre * pre) * 0.3989422804014327
    slope = (upstream * (cdf + pre * density)).astype(BF16)
    slope_ref[...] = slope
    back_ref[...] = dot_nt(slope, up_ref[...]).astype(BF16)


def mlp_both(x, grad, up, bias, down, tile=256):
    count, width = x.shape
    hidden = up.shape[1]
    tile = min(tile, count)
    whole = lambda i: (0, 0)
    return pl.pallas_call(
        mlp_kernel,
        grid=(count // tile,),
        in_specs=[
            pl.BlockSpec((tile, width), lambda i: (i, 0)),
            pl.BlockSpec((tile, width), lambda i: (i, 0)),
            pl.BlockSpec((width, hidden), whole, pipeline_mode=pl.Buffered(1)),
            pl.BlockSpec((1, hidden), whole),
            pl.BlockSpec((hidden, width), whole, pipeline_mode=pl.Buffered(1)),
        ],
        out_specs=[
            pl.BlockSpec((tile, hidden), lambda i: (i, 0)),
            pl.BlockSpec((tile, hidden), lambda i: (i, 0)),
            pl.BlockSpec((tile, width), lambda i: (i, 0)),
        ],
        out_shape=[
            jax.ShapeDtypeStruct((count, hidden), BF16),
            jax.ShapeDtypeStruct((count, hidden), BF16),
            jax.ShapeDtypeStruct((count, width), BF16),
        ],
        cost_estimate=pl.CostEstimate(
            flops=6 * count * width * hidden,
            bytes_accessed=4 * width * hidden + 10 * count * width,
            transcendentals=2 * count * hidden,
        ),
        name="mlp_both",
    )(x, grad, up, bias[None], down)


EPSILON = 1e-06


def normalize(values):
    center = values - jnp.mean(values, -1, keepdims=True)
    inverse = lax.rsqrt(jnp.mean(center * center, -1, keepdims=True) + EPSILON)
    return (center * inverse, inverse)


def normalize_back(upstream, normed, inverse, gain):
    scaled = upstream * gain
    return inverse * (
        scaled
        - jnp.mean(scaled, -1, keepdims=True)
        - normed * jnp.mean(scaled * normed, -1, keepdims=True)
    )


def position_rows(own_items, item_lengths, level, first_row, width):
    slot_count = item_lengths.shape[0]
    slot_index = lax.broadcasted_iota(jnp.int32, (1, slot_count), 1)
    start_row = jnp.sum(jnp.where(slot_index < own_items[:, None], item_lengths[None, :], 0), 1)
    row_index = first_row + jnp.arange(own_items.shape[0], dtype=jnp.int32)
    valid_rows = (own_items < slot_count).astype(F32)
    level_ratio = jnp.exp2(level.astype(F32) - 2.0)
    places = (row_index - start_row).astype(F32) * level_ratio
    half_width = width // 2
    frequency = jnp.exp(-jnp.log(10000.0) * jnp.arange(half_width, dtype=F32) / half_width)
    angles = places[:, None] * frequency[None, :]
    return (
        jnp.concatenate([jnp.sin(angles), jnp.cos(angles)], 1) * valid_rows[:, None],
        valid_rows,
    )


def bits_of(size):
    bits = []
    step = 1
    while step < size:
        bits.append(step)
        step *= 2
    return bits


def tie(*arrays):
    return lax.optimization_barrier(arrays)


def swap(array, axis, size, bit):
    return lax.ppermute(array, axis, [(i, i ^ bit) for i in range(size)])


def gather_near(own, count):
    blocks = {0: own}
    for bit in reversed(bits_of(count)[:-1]):
        blocks.update(
            {j | bit: swap(rows, "mp", count, bit) for j, rows in list(blocks.items())}
        )
    return jnp.concatenate([blocks[j] for j in range(count // 2)])


def scatter_near(rows, count):
    size = rows.shape[0] // (count // 2)
    held = {j: rows[j * size : (j + 1) * size] for j in range(count // 2)}
    for bit in bits_of(count)[:-1]:
        arrived = {
            j ^ bit: swap(held[j].astype(BF16), "mp", count, bit) for j in held if j & bit
        }
        held = {j: held[j].astype(F32) + arrived[j].astype(F32) for j in arrived}
    return held[0]


class DpSum:
    def __init__(self, count, index, order):
        self.count, self.index, self.order = count, index, order

    def high(self, bit):
        return (self.index & bit) != 0

    def open(self, left, right):
        half = left.shape[1] // 2
        top = jnp.where(self.high(self.order[0]), half, 0)
        send = dot_tn(lax.dynamic_slice_in_dim(left, half - top, half, 1), right).astype(BF16)
        self.held = dot_tn(lax.dynamic_slice_in_dim(left, top, half, 1), right).astype(BF16)
        return send

    def split(self, bit):
        half = self.held.shape[0] // 2
        top = jnp.where(self.high(bit), half, 0)
        send = lax.dynamic_slice_in_dim(self.held, half - top, half, 0)
        self.held = lax.dynamic_slice_in_dim(self.held, top, half, 0)
        return send

    def add(self, arrived):
        self.held = (self.held.astype(F32) + arrived.astype(F32)).astype(BF16)

    def join(self, bit, arrived):
        self.held = jnp.where(
            self.high(bit),
            jnp.concatenate([arrived, self.held]),
            jnp.concatenate([self.held, arrived]),
        )

    def pass_on(self, array, bit):
        return swap(array, "dp", self.count, bit)

    def halve_rest(self):
        for bit in self.order[1:]:
            self.add(self.pass_on(self.split(bit), bit))

    def double_all(self):
        for bit in reversed(self.order):
            self.join(bit, self.pass_on(self.held, bit))
        return self.held


def butterfly(values, sizes):
    for axis, size in sizes:
        for bit in bits_of(size):
            values = values + swap(values, axis, size, bit)
    return values


def layer(sizes):
    n_dp, n_mp = sizes
    far_bit = n_mp // 2
    dp_bits = bits_of(n_dp)

    def per_device(
        tokens,
        cotangent,
        segments,
        lengths,
        scale_levels,
        first_gain,
        first_shift,
        input_weight,
        input_bias,
        output_weight,
        output_bias,
        second_gain,
        second_shift,
        expand_weight,
        expand_bias,
        reduce_weight,
        reduce_bias,
    ):
        me = lax.axis_index("mp")
        group = lax.axis_index("dp")
        own_count, width = tokens.shape
        local_width = input_weight.shape[2]
        half_count = own_count * n_mp // 2
        item_blocks = [
            lax.dynamic_slice_in_dim(segments, (me ^ j) * own_count, own_count)
            for j in range(n_mp)
        ]
        positions, valid_rows = position_rows(
            item_blocks[0], lengths[0], scale_levels[0], me * own_count, width
        )
        residual = tokens.astype(F32) + positions
        normed_one, inverse_one = normalize(residual)
        attn_input = (normed_one * first_gain + first_shift).astype(BF16)
        grad_low = (cotangent.astype(F32) * valid_rows[:, None]).astype(BF16)

        far_own = swap(attn_input, "mp", n_mp, far_bit)
        attn_near = gather_near(attn_input, n_mp)
        far_own, grad_low = tie(far_own, grad_low)
        attn_far = gather_near(far_own, n_mp)
        grad_far = swap(grad_low, "mp", n_mp, far_bit)

        lanes = lax.broadcasted_iota(jnp.int32, (1, PAIR), 1)
        half_items = [
            jnp.concatenate(item_blocks[: n_mp // 2]),
            jnp.concatenate(item_blocks[n_mp // 2 :]),
        ]
        picks = [(items[:, None] == lanes).astype(BF16) for items in half_items]
        bars = [
            jnp.where(items[:, None] == lanes, 0.0, EXCLUDED).astype(BF16) for items in half_items
        ]
        bias_rows = jnp.stack([input_bias[0], jnp.zeros_like(input_bias[0]), input_bias[1]])

        def project(rows):
            wide = jnp.einsum("rd,tde->tre", rows, input_weight, preferred_element_type=F32)
            return (wide + bias_rows[:, None, :]).astype(BF16)

        qkv = [project(attn_near), project(attn_far)]
        query = [rows[0:1] for rows in qkv]
        keys = [rows[1:2] for rows in qkv]
        values = [rows[2:3] for rows in qkv]

        heads_far, logs_far = attend_forward(query[1], picks[1], keys, values, bars)
        share_far = dot_nn(heads_far, output_weight).astype(BF16)
        share_far, grad_far = tie(share_far, grad_far)
        sum_far = scatter_near(share_far, n_mp).astype(BF16)
        arrived = swap(sum_far, "mp", n_mp, far_bit)
        heads_near, logs_near = attend_forward(query[0], picks[0], keys, values, bars)
        share_near = dot_nn(heads_near, output_weight).astype(BF16)
        sum_near = scatter_near(share_near, n_mp)
        grad_near = gather_near(grad_low, n_mp)
        grad_far = gather_near(grad_far, n_mp)
        hidden_res = residual + (sum_near + arrived.astype(F32)) + output_bias
        normed_two, inverse_two = normalize(hidden_res)
        mlp_input = (normed_two * second_gain + second_shift).astype(BF16)

        far_own = swap(mlp_input, "mp", n_mp, far_bit)
        mlp_near = gather_near(mlp_input, n_mp)
        act_near, slope_near, back_near = mlp_both(
            mlp_near, grad_near, expand_weight, expand_bias, reduce_weight
        )
        mlp_far = gather_near(far_own, n_mp)
        act_far, slope_far, back_far = mlp_both(
            mlp_far, grad_far, expand_weight, expand_bias, reduce_weight
        )
        sum_far = scatter_near(back_far, n_mp).astype(BF16)
        arrived = swap(sum_far, "mp", n_mp, far_bit)
        sum_near = scatter_near(back_near, n_mp)

        activated = jnp.concatenate([act_near, act_far])
        pre_grad = jnp.concatenate([slope_near, slope_far])
        grad_all = jnp.concatenate([grad_near, grad_far])
        mlp_rows = jnp.concatenate([mlp_near, mlp_far])
        reduce_sum = DpSum(n_dp, group, dp_bits)
        expand_sum = DpSum(n_dp, group, dp_bits[1:] + dp_bits[:1])
        reduce_send = reduce_sum.open(activated, grad_all)
        expand_send = expand_sum.open(mlp_rows, pre_grad)
        reduce_in = reduce_sum.pass_on(reduce_send, reduce_sum.order[0])
        expand_in = expand_sum.pass_on(expand_send, expand_sum.order[0])

        normed_grad_two = sum_near + arrived.astype(F32)
        grad_out = grad_low.astype(F32)
        residual_grad = grad_out + normalize_back(
            normed_grad_two, normed_two, inverse_two, second_gain
        )
        branch_grad = residual_grad.astype(BF16)
        far_own = swap(branch_grad, "mp", n_mp, far_bit)
        branch_near = gather_near(branch_grad, n_mp)
        head_near = dot_nt(branch_near, output_weight).astype(BF16)
        query_near, key_part, value_part = attend_back(
            query[0], picks[0], head_near, heads_near, logs_near, keys, values, bars, None, False
        )
        share_far = dot_nn(act_far, reduce_weight).astype(BF16)
        share_near = dot_nn(act_near, reduce_weight).astype(BF16)
        far_own, share_far, reduce_in, expand_in = tie(far_own, share_far, reduce_in, expand_in)
        branch_far = gather_near(far_own, n_mp)
        head_far = dot_nt(branch_far, output_weight).astype(BF16)
        out_far = swap(scatter_near(share_far, n_mp).astype(BF16), "mp", n_mp, far_bit)
        out_near = scatter_near(share_near, n_mp)
        query_far, key_grads, value_grads = attend_back(
            query[1],
            picks[1],
            head_far,
            heads_far,
            logs_far,
            keys,
            values,
            bars,
            (key_part, value_part),
            True,
        )
        reduce_sum.add(reduce_in)
        expand_sum.add(expand_in)

        qkv_near = jnp.concatenate([query_near, key_grads[0], value_grads[0]], 1)
        qkv_far = jnp.concatenate([query_far, key_grads[1], value_grads[1]], 1)
        weight_wide = jnp.concatenate([input_weight[0], input_weight[1], input_weight[2]], 1)
        share_far = dot_nt(qkv_far, weight_wide).astype(BF16)
        share_far, out_far = tie(share_far, out_far)
        sum_far = scatter_near(share_far, n_mp).astype(BF16)
        arrived = swap(sum_far, "mp", n_mp, far_bit)
        sum_near = scatter_near(dot_nt(qkv_near, weight_wide).astype(BF16), n_mp)
        block_output = (hidden_res + (out_near + out_far.astype(F32)) + reduce_bias).astype(BF16)

        qkv_all = jnp.concatenate([qkv_near, qkv_far])
        attn_rows = jnp.concatenate([attn_near, attn_far])
        branch_all = jnp.concatenate([branch_near, branch_far])
        heads_all = jnp.concatenate([heads_near, heads_far])
        output_sum = DpSum(n_dp, group, dp_bits)
        input_sum = DpSum(n_dp, group, dp_bits)
        output_sum.add(output_sum.pass_on(output_sum.open(heads_all, branch_all), dp_bits[0]))
        input_sum.add(input_sum.pass_on(input_sum.open(attn_rows, qkv_all), dp_bits[0]))

        normed_grad_one = sum_near + arrived.astype(F32)
        input_gradient = residual_grad + normalize_back(
            normed_grad_one, normed_one, inverse_one, first_gain
        )
        reduce_sum.halve_rest()
        expand_sum.halve_rest()
        reduce_grad = reduce_sum.double_all()
        expand_grad = expand_sum.double_all()
        output_sum.halve_rest()
        input_sum.halve_rest()
        output_grad = output_sum.double_all()
        input_grad = input_sum.double_all()

        both = (("mp", n_mp), ("dp", n_dp))
        dp_only = (("dp", n_dp),)
        early = butterfly(
            jnp.stack(
                [
                    jnp.sum(normed_grad_two * normed_two, 0),
                    jnp.sum(normed_grad_two, 0),
                    jnp.sum(branch_grad, 0, dtype=F32),
                    jnp.sum(grad_out, 0),
                ]
            ),
            both,
        )
        hidden = expand_bias.shape[0]
        patches = jnp.sum(lengths).astype(F32)
        local = butterfly(
            jnp.concatenate([jnp.sum(pre_grad, 0, dtype=F32), jnp.full((PAIR,), patches)])[None],
            dp_only,
        )[0]
        factor = lax.rsqrt(local[hidden])
        late = butterfly(
            jnp.stack([jnp.sum(normed_grad_one * normed_one, 0), jnp.sum(normed_grad_one, 0)]),
            both,
        )
        wide_sums = jnp.sum(qkv_all, 0, dtype=F32)
        qv_total = butterfly(
            jnp.stack([wide_sums[:local_width], wide_sums[2 * local_width :]]), dp_only
        )
        input_total = input_grad.astype(F32) * factor
        return (
            block_output,
            input_gradient,
            late[0] * factor,
            late[1] * factor,
            jnp.stack(
                [input_total[:, t * local_width : (t + 1) * local_width] for t in range(3)]
            ),
            qv_total * factor,
            output_grad.astype(F32) * factor,
            early[2] * factor,
            early[0] * factor,
            early[1] * factor,
            expand_grad.astype(F32) * factor,
            local[:hidden] * factor,
            reduce_grad.astype(F32) * factor,
            early[3] * factor,
        )

    return per_device


def solution(mesh):
    placed = (
        P(("dp", "mp"), None),
        P(("dp", "mp"), None),
        P("dp"),
        P("dp", None),
        P("dp"),
        P(),
        P(),
        P(None, None, "mp"),
        P(None, "mp"),
        P("mp", None),
        P(),
        P(),
        P(),
        P(None, "mp"),
        P("mp"),
        P("mp", None),
        P(),
    )
    return jax.shard_map(
        layer((mesh.shape["dp"], mesh.shape["mp"])),
        mesh=mesh,
        in_specs=placed,
        out_specs=(
            P(("dp", "mp"), None),
            P(("dp", "mp"), None),
            P(),
            P(),
            P(None, None, "mp"),
            P(None, "mp"),
            P("mp", None),
            P(),
            P(),
            P(),
            P(None, "mp"),
            P("mp"),
            P("mp", None),
            P(),
        ),
        check_vma=False,
    )
```

time: 430 us -> 379 us (0.88)
  waiting for transfers between devices: 223 us -> 169 us
  Pallas kernels: 0 us -> 48.2 us
  matrix products: 70.7 us -> 27.6 us
  starting transfers between devices: 66.1 us -> 52.4 us
  local copies, waits for them, and re-layouts: 11.6 us -> 23 us
    ppermute x64, waiting for transfers between devices: 223 us -> 169 us  [swap(): return lax.ppermute(array, axis, [(i, i ^ bit) for i in range(size)])]
    pallas_call x0 -> x6, Pallas kernels: none -> 48.2 us  [the longest x2 19.8 us: attend_back(): pl.pallas_call(functools.partial(attend_back_kernel, halves, first, last)...]
    dot_general x18, matrix products: 70.7 us -> 27.6 us  [the longest x8 10.6 us: dot_tn(): lax.dot_general(a, b, (((0,), (0,)), ((), ())), preferred_element_type=F32)]
    ppermute x64, starting transfers between devices: 66.1 us -> 52.4 us  [swap(): return lax.ppermute(array, axis, [(i, i ^ bit) for i in range(size)])]
    concatenate x1 -> x7, other arithmetic: 0.01 us -> 11.9 us  [the longest x4 7.88 us: gather_near(): return jnp.concatenate([blocks[j] for j in range(count // 2)])]
    slice x6 -> x12, local copies, waits for them, and re-layouts: 0.91 us -> 6.26 us  [the longest x8 3.87 us: scatter_near(): held = {j: rows[j * size:(j + 1) * size] for j in range(count // 2)}]
    unnamed x79 -> x112, local copies, waits for them, and re-layouts: 7.42 us -> 10.5 us
    convert_element_type x9 -> x19, other arithmetic: 13 us -> 11.8 us  [the longest x10 3.64 us: add(): self.held = (self.held.astype(F32) + arrived.astype(F32)).astype(BF16)]
  transfers between devices with their start and end apart: 64 -> 64, of which waited for: 29 -> 26; matrix products, arithmetic and copies ran while one was open for 19% -> 23% of each run, Pallas kernels for 0% -> 11%
where the time goes in v2:
time: 379 us; the launch traced here: 374 us
  waiting for transfers between devices  169 us (45%)
  starting transfers between devices  52.4 us (14%)
  other arithmetic  49.4 us (13%)
  Pallas kernels  48.2 us (13%)
  matrix products  27.6 us (7%)
  local copies, waits for them, and re-layouts  23 us (6%)
  between operations  4.38 us (1%)
    ppermute x64, waiting for transfers between devices, swap(): return lax.ppermute(array, axis, [(i, i ^ bit) for i in range(size)])  169 us
    ppermute x64, starting transfers between devices, swap(): return lax.ppermute(array, axis, [(i, i ^ bit) for i in range(size)])  52.4 us
    pallas_call x2, Pallas kernels, attend_back(): pl.pallas_call(functools.partial(attend_back_kernel, halves, first, last)...  19.8 us
    pallas_call x2, Pallas kernels, mlp_both(): pl.pallas_call(mlp_kernel, grid=(count // tile,), in_specs=[pl.BlockSpec(...  14.4 us
    pallas_call x2, Pallas kernels, attend_forward(): pl.pallas_call(functools.partial(attend_kernel, halves), grid=grid, in_sp...  14 us
    dot_general x8, matrix products, dot_tn(): lax.dot_general(a, b, (((0,), (0,)), ((), ())), preferred_element_type=F32)  10.6 us
    unnamed x112, local copies, waits for them, and re-layouts  10.5 us
    dot_general x4, matrix products, dot_nn(): lax.dot_general(a, b, (((1,), (0,)), ((), ())), preferred_element_type=F32)  8.18 us
  transfers between devices with their start and end apart: 64, of which 26 were waited for; matrix products, arithmetic and copies ran while one was open for 23% of the time, Pallas kernels for 11%

profile of v2, /device:TPU:0, one launch (start us, length us, event | category | flops | bytes accessed | tf_op | source)
XLA Modules:
  0.0 373.8 jit_solution(17568832106570503896)
XLA Ops:
  2.9 1.9 multiply_sine_fusion
  7.6 2.6 collective-permute-start.1
  12.8 2.6 slice_bitcast_fusion.5
  15.4 7.4 %collective-permute-done.1 = bf16[256,1024]{1,0:T(8,128)(2,1)} collective-permute-done((bf16[256,1024]{1,0:T(8,128)(2,1)S(1)}, bf16[256,1024]{1,0:T(8,128)(2,1)}, u32[]{:S(2)}, u32[]{:S(2)}) %collective-permute-start.1) | collective-permute-done | bytes 524320 | tf_op jit(solution)/shard_map/ppermute | solution.py:306
  26.5 2.2 fusion.1
  29.7 7.1 %attend_forward.3 = (bf16[512,256]{1,0:T(8,128)(2,1)}, f32[2,8,512]{2,1,0:T(8,128)}) custom-call(bf16[1,512,256]{2,1,0:T(8,128)(2,1)} %get-tuple-element.101.q_ref, bf16[512,128]{1,0:T(8,128)(2,1)} %fusion.24.pick_ref, bf16[1,512,256]{2,1,0:T(8,128)(2,1)} %get-tuple-element.99.refs_0_, bf16[1,512,256]{2,1,0:T(8,128)(2,1)} %get-tuple-element.102.refs_1_, ...), custom_call_target="tpu_custom_call" | custom-call | flops 2147483648 | bytes 1572864 | tf_op jit(solution)/shard_map/attend_forward/pallas_call | solution.py:73
  41.7 6.9 %attend_forward.2 = (bf16[512,256]{1,0:T(8,128)(2,1)}, f32[2,8,512]{2,1,0:T(8,128)}) custom-call(bf16[1,512,256]{2,1,0:T(8,128)(2,1)} %get-tuple-element.97.q_ref, bf16[512,128]{1,0:T(8,128)(2,1)} %fusion.25.pick_ref, bf16[1,512,256]{2,1,0:T(8,128)(2,1)} %get-tuple-element.99.refs_0_, bf16[1,512,256]{2,1,0:T(8,128)(2,1)} %get-tuple-element.102.refs_1_, ...), custom_call_target="tpu_custom_call" | custom-call | flops 2147483648 | bytes 1572864 | tf_op jit(solution)/shard_map/attend_forward/pallas_call | solution.py:73
  53.7 2.1 pad_maximum_fusion.7.grad_ref
  55.8 2.5 pad_maximum_fusion.2
  58.3 7.5 %collective-permute-done.6 = bf16[256,1024]{1,0:T(8,128)(2,1)S(1)} collective-permute-done((bf16[256,1024]{1,0:T(8,128)(2,1)S(1)}, bf16[256,1024]{1,0:T(8,128)(2,1)S(1)}, u32[]{:S(2)}, u32[]{:S(2)}) %collective-permute-start.6) | collective-permute-done | bytes 524320 | tf_op jit(solution)/shard_map/ppermute | solution.py:306
  69.8 2.5 pad_maximum_fusion.9.grad_ref
  73.4 9.0 %collective-permute-done.11 = bf16[256,1024]{1,0:T(8,128)(2,1)} collective-permute-done((bf16[256,1024]{1,0:T(8,128)(2,1)S(1)}, bf16[256,1024]{1,0:T(8,128)(2,1)}, u32[]{:S(2)}, u32[]{:S(2)}) %collective-permute-start.11) | collective-permute-done | bytes 524320 | tf_op jit(solution)/shard_map/ppermute | solution.py:306
  82.4 7.1 %mlp_both.2 = (bf16[512,1024]{1,0:T(8,128)(2,1)}, bf16[512,1024]{1,0:T(8,128)(2,1)}, bf16[512,1024]{1,0:T(8,128)(2,1)}) custom-call(bf16[512,1024]{1,0:T(8,128)(2,1)} %pad_maximum_fusion.6.x_ref, bf16[512,1024]{1,0:T(8,128)(2,1)} %pad_maximum_fusion.7.grad_ref, bf16[1024,1024]{1,0:T(8,128)(2,1)} %up_ref.3, f32[1,1024]{1,0:T(1,128)} %bitcast.92, ...), custom_call_target="tpu_custom_call" | custom-call | flops 3221225472 | bytes 9437184 | tf_op jit(solution)/shard_map/mlp_both/pallas_call | solution.py:228
  89.5 4.2 %convolution_convert_fusion.7 = bf16[512,1024]{1,0:T(8,128)(2,1)} fusion(bf16[512,1024]{1,0:T(8,128)(2,1)} %get-tuple-element.49, bf16[1024,1024]{1,0:T(8,128)(2,1)} %down_ref.3), kind=kOutput, calls=%fused_computation.26 | convolution fusion | flops 1074266112 | bytes 4194304 | tf_op jit(solution)/shard_map/dot_general | solution.py:17
  93.6 2.2 pad_maximum_fusion.8.x_ref
  95.9 7.3 %mlp_both.3 = (bf16[512,1024]{1,0:T(8,128)(2,1)}, bf16[512,1024]{1,0:T(8,128)(2,1)}, bf16[512,1024]{1,0:T(8,128)(2,1)}) custom-call(bf16[512,1024]{1,0:T(8,128)(2,1)} %pad_maximum_fusion.8.x_ref, bf16[512,1024]{1,0:T(8,128)(2,1)} %pad_maximum_fusion.9.grad_ref, bf16[1024,1024]{1,0:T(8,128)(2,1)} %up_ref.3, f32[1,1024]{1,0:T(1,128)} %bitcast.93, ...), custom_call_target="tpu_custom_call" | custom-call | flops 3221225472 | bytes 9437184 | tf_op jit(solution)/shard_map/mlp_both/pallas_call | solution.py:228
  114.6 10.0 %collective-permute-done.15 = bf16[256,1024]{1,0:T(8,128)(2,1)S(1)} collective-permute-done((bf16[256,1024]{1,0:T(8,128)(2,1)S(1)}, bf16[256,1024]{1,0:T(8,128)(2,1)S(1)}, u32[]{:S(2)}, u32[]{:S(2)}) %collective-permute-start.15) | collective-permute-done | bytes 524320 | tf_op jit(solution)/shard_map/ppermute | solution.py:306
  131.3 22.7 %collective-permute-done.31 = f32[1,1152]{1,0:T(1,128)S(1)} collective-permute-done((f32[1,1152]{1,0:T(1,128)S(1)}, f32[1,1152]{1,0:T(1,128)S(1)}, u32[]{:S(2)}, u32[]{:S(2)}) %collective-permute-start.31) | collective-permute-done | bytes 4640 | tf_op jit(solution)/shard_map/ppermute | solution.py:306
  158.5 2.7 collective-permute-start.33
  167.6 2.9 collective-permute-done.53
  171.2 2.7 collective-permute-done.16
  180.8 9.4 %attend_back.2 = (bf16[512,256]{1,0:T(8,128)(2,1)}, f32[512,256]{1,0:T(8,128)}, f32[512,256]{1,0:T(8,128)}, f32[512,256]{1,0:T(8,128)}, f32[512,256]{1,0:T(8,128)}) custom-call(bf16[1,512,256]{2,1,0:T(8,128)(2,1)} %get-tuple-element.97.q_ref, bf16[512,128]{1,0:T(8,128)(2,1)} %fusion.25.pick_ref, bf16[512,256]{1,0:T(8,128)(2,1)} %convolution_convert_fusion.14.grad_ref, ...), custom_call_target="tpu_custom_call" | custom-call | flops 5368709120 | bytes 4194304 | tf_op jit(solution)/shard_map/attend_back/pallas_call | solution.py:185
  191.3 2.4 convolution_convert_fusion.15.grad_ref
  193.6 10.3 %attend_back.3 = (bf16[512,256]{1,0:T(8,128)(2,1)}, bf16[512,256]{1,0:T(8,128)(2,1)}, bf16[512,256]{1,0:T(8,128)(2,1)}, bf16[512,256]{1,0:T(8,128)(2,1)}, bf16[512,256]{1,0:T(8,128)(2,1)}) custom-call(bf16[1,512,256]{2,1,0:T(8,128)(2,1)} %get-tuple-element.101.q_ref, bf16[512,128]{1,0:T(8,128)(2,1)} %fusion.24.pick_ref, ...), custom_call_target="tpu_custom_call" | custom-call | flops 5368709120 | bytes 4194304 | tf_op jit(solution)/shard_map/attend_back/pallas_call | solution.py:185
  212.1 2.6 collective-permute-start.60
  227.8 3.0 collective-permute-done.42
  232.5 5.0 %collective-permute-done.43 = bf16[128,1024]{1,0:T(8,128)(2,1)S(1)} collective-permute-done((bf16[128,1024]{1,0:T(8,128)(2,1)S(1)}, bf16[128,1024]{1,0:T(8,128)(2,1)S(1)}, u32[]{:S(2)}, u32[]{:S(2)}) %collective-permute-start.43) | collective-permute-done | bytes 262176 | tf_op jit(solution)/shard_map/ppermute | solution.py:306
  240.4 4.8 %collective-permute-done.44 = bf16[64,1024]{1,0:T(8,128)(2,1)S(1)} collective-permute-done((bf16[64,1024]{1,0:T(8,128)(2,1)S(1)}, bf16[64,1024]{1,0:T(8,128)(2,1)S(1)}, u32[]{:S(2)}, u32[]{:S(2)}) %collective-permute-start.44) | collective-permute-done | bytes 131104 | tf_op jit(solution)/shard_map/ppermute | solution.py:306
  246.5 5.4 %collective-permute-done.45 = bf16[32,1024]{1,0:T(8,128)(2,1)S(1)} collective-permute-done((bf16[32,1024]{1,0:T(8,128)(2,1)S(1)}, bf16[32,1024]{1,0:T(8,128)(2,1)S(1)}, u32[]{:S(2)}, u32[]{:S(2)}) %collective-permute-start.45) | collective-permute-done | bytes 65568 | tf_op jit(solution)/shard_map/ppermute | solution.py:306
  252.0 6.7 %collective-permute-done.22 = bf16[256,1024]{1,0:T(8,128)(2,1)S(1)} collective-permute-done((bf16[256,1024]{1,0:T(8,128)(2,1)S(1)}, bf16[256,1024]{1,0:T(8,128)(2,1)S(1)}, u32[]{:S(2)}, u32[]{:S(2)}) %collective-permute-start.22) | collective-permute-done | bytes 524320 | tf_op jit(solution)/shard_map/ppermute | solution.py:306
  260.6 2.2 add_convert_fusion.8
  262.8 4.8 %collective-permute-done.46 = bf16[32,1024]{1,0:T(8,128)(2,1)S(1)} collective-permute-done((bf16[32,1024]{1,0:T(8,128)(2,1)S(1)}, bf16[32,1024]{1,0:T(8,128)(2,1)S(1)}, u32[]{:S(2)}, u32[]{:S(2)}) %collective-permute-start.46) | collective-permute-done | bytes 65568 | tf_op jit(solution)/shard_map/ppermute | solution.py:306
  267.9 2.1 collective-permute-start.62
  270.1 4.0 %collective-permute-done.47 = bf16[64,1024]{1,0:T(8,128)(2,1)S(1)} collective-permute-done((bf16[64,1024]{1,0:T(8,128)(2,1)S(1)}, bf16[64,1024]{1,0:T(8,128)(2,1)S(1)}, u32[]{:S(2)}, u32[]{:S(2)}) %collective-permute-start.47) | collective-permute-done | bytes 131104 | tf_op jit(solution)/shard_map/ppermute | solution.py:306
  275.4 6.2 %collective-permute-done.48 = bf16[128,1024]{1,0:T(8,128)(2,1)S(1)} collective-permute-done((bf16[128,1024]{1,0:T(8,128)(2,1)S(1)}, bf16[128,1024]{1,0:T(8,128)(2,1)S(1)}, u32[]{:S(2)}, u32[]{:S(2)}) %collective-permute-start.48) | collective-permute-done | bytes 262176 | tf_op jit(solution)/shard_map/ppermute | solution.py:306
  285.5 7.2 %collective-permute-done.62 = bf16[256,1024]{1,0:T(8,128)(2,1)S(1)} collective-permute-done((bf16[256,1024]{1,0:T(8,128)(2,1)S(1)}, bf16[256,1024]{1,0:T(8,128)(2,1)S(1)}, u32[]{:S(2)}, u32[]{:S(2)}) %collective-permute-start.62) | collective-permute-done | bytes 524320 | tf_op jit(solution)/shard_map/ppermute | solution.py:306
  293.9 5.5 %collective-permute-done.57 = bf16[256,1024]{1,0:T(8,128)(2,1)S(1)} collective-permute-done((bf16[256,1024]{1,0:T(8,128)(2,1)S(1)}, bf16[256,1024]{1,0:T(8,128)(2,1)S(1)}, u32[]{:S(2)}, u32[]{:S(2)}) %collective-permute-start.57) | collective-permute-done | bytes 524320 | tf_op jit(solution)/shard_map/ppermute | solution.py:306
  299.9 5.1 %collective-permute-done.35 = bf16[256,768]{1,0:T(8,128)(2,1)S(1)} collective-permute-done((bf16[256,768]{1,0:T(8,128)(2,1)S(1)}, bf16[256,768]{1,0:T(8,128)(2,1)S(1)}, u32[]{:S(2)}, u32[]{:S(2)}) %collective-permute-start.35) | collective-permute-done | bytes 393248 | tf_op jit(solution)/shard_map/ppermute | solution.py:306
  306.0 23.1 %collective-permute-done.36 = bf16[128,768]{1,0:T(8,128)(2,1)S(1)} collective-permute-done((bf16[128,768]{1,0:T(8,128)(2,1)S(1)}, bf16[128,768]{1,0:T(8,128)(2,1)S(1)}, u32[]{:S(2)}, u32[]{:S(2)}) %collective-permute-start.36) | collective-permute-done | bytes 196640 | tf_op jit(solution)/shard_map/ppermute | solution.py:306
  329.1 3.4 collective-permute-start.37
  333.9 7.9 %collective-permute-done.37 = bf16[128,768]{1,0:T(8,128)(2,1)S(1)} collective-permute-done((bf16[128,768]{1,0:T(8,128)(2,1)S(1)}, bf16[128,768]{1,0:T(8,128)(2,1)S(1)}, u32[]{:S(2)}, u32[]{:S(2)}) %collective-permute-start.37) | collective-permute-done | bytes 196640 | tf_op jit(solution)/shard_map/ppermute | solution.py:306
  342.9 2.8 collective-permute-done.28
  345.7 2.0 collective-permute-start.29
  347.7 4.8 %collective-permute-done.29 = f32[2,1024]{1,0:T(2,128)S(1)} collective-permute-done((f32[2,1024]{1,0:T(2,128)S(1)}, f32[2,1024]{1,0:T(2,128)S(1)}, u32[]{:S(2)}, u32[]{:S(2)}) %collective-permute-start.29) | collective-permute-done | bytes 8224 | tf_op jit(solution)/shard_map/ppermute | solution.py:306
  357.8 2.9 convert_multiply_fusion
  360.7 2.9 convert_multiply_fusion.1
  363.6 7.4 %collective-permute-done.39 = bf16[512,768]{1,0:T(8,128)(2,1)S(1)} collective-permute-done((bf16[512,768]{1,0:T(8,128)(2,1)S(1)}, bf16[512,768]{1,0:T(8,128)(2,1)S(1)}, u32[]{:S(2)}, u32[]{:S(2)}) %collective-permute-start.39) | collective-permute-done | bytes 786464 | tf_op jit(solution)/shard_map/ppermute | solution.py:306
  371.7 1.9 pad_maximum_fusion
  (337 shorter events, 107.6 us)
Async XLA Ops:
  7.0 17.5 %collective-permute-start = (bf16[256,1024]{1,0:T(8,128)(2,1)S(1)}, bf16[256,1024]{1,0:T(8,128)(2,1)S(1)}, u32[]{:S(2)}, u32[]{:S(2)}) collective-permute-start(bf16[256,1024]{1,0:T(8,128)(2,1)S(1)} %add_convert_fusion.13), channel_id=1, source_target_pairs={{0,1},{1,0},{2,3},{3,2},{4,5},{5,4},{6,7},{7,6},{8,9},{9,8},{10,11... | collective-permute-start | bytes 1572872 | tf_op jit(solution)/shard_map/ppermute | solution.py:306
  7.6 15.2 %collective-permute-start.1 = (bf16[256,1024]{1,0:T(8,128)(2,1)S(1)}, bf16[256,1024]{1,0:T(8,128)(2,1)}, u32[]{:S(2)}, u32[]{:S(2)}) collective-permute-start(bf16[256,1024]{1,0:T(8,128)(2,1)S(1)} %add_convert_fusion.13), channel_id=1, source_target_pairs={{0,2},{1,3},{2,0},{3,1},{4,6},{5,7},{6,4},{7,5},{8,10},{9,11},{10,... | collective-permute-start | bytes 1572872 | tf_op jit(solution)/shard_map/ppermute | solution.py:306
  22.8 15.4 %collective-permute-start.4 = (bf16[256,1024]{1,0:T(8,128)(2,1)S(1)}, bf16[256,1024]{1,0:T(8,128)(2,1)}, u32[]{:S(2)}, u32[]{:S(2)}) collective-permute-start(bf16[256,1024]{1,0:T(8,128)(2,1)S(1)} %get-tuple-element.47), channel_id=1, source_target_pairs={{0,2},{1,3},{2,0},{3,1},{4,6},{5,7},{6,4},{7,5},{8,10},{9,11},{10,... | collective-permute-start | bytes 1572872 | tf_op jit(solution)/shard_map/ppermute | solution.py:306
  39.0 11.3 %collective-permute-start.5 = (bf16[256,1024]{1,0:T(8,128)(2,1)}, bf16[256,1024]{1,0:T(8,128)(2,1)}, u32[]{:S(2)}, u32[]{:S(2)}) collective-permute-start(bf16[256,1024]{1,0:T(8,128)(2,1)} %slice.133), channel_id=1, source_target_pairs={{0,1},{1,0},{2,3},{3,2},{4,5},{5,4},{6,7},{7,6},{8,9},{9,8},{10,11... | collective-permute-start | bytes 1572872 | tf_op jit(solution)/shard_map/ppermute | solution.py:306
  41.3 11.2 %collective-permute-start.8 = (bf16[256,1024]{1,0:T(8,128)(2,1)S(1)}, bf16[256,1024]{1,0:T(8,128)(2,1)}, u32[]{:S(2)}, u32[]{:S(2)}) collective-permute-start(bf16[256,1024]{1,0:T(8,128)(2,1)S(1)} %get-tuple-element.47), channel_id=1, source_target_pairs={{0,1},{1,0},{2,3},{3,2},{4,5},{5,4},{6,7},{7,6},{8,9},{9,8},{10,11... | collective-permute-start | bytes 1572872 | tf_op jit(solution)/shard_map/ppermute | solution.py:306
  50.0 8.3 %collective-permute-start.3 = (bf16[256,1024]{1,0:T(8,128)(2,1)S(1)}, bf16[256,1024]{1,0:T(8,128)(2,1)S(1)}, u32[]{:S(2)}, u32[]{:S(2)}) collective-permute-start(bf16[256,1024]{1,0:T(8,128)(2,1)S(1)} %slice.168), channel_id=1, source_target_pairs={{0,1},{1,0},{2,3},{3,2},{4,5},{5,4},{6,7},{7,6},{8,9},{9,8},{10,11... | collective-permute-start | bytes 1572872 | tf_op jit(solution)/shard_map/ppermute | solution.py:306
  51.6 14.2 %collective-permute-start.6 = (bf16[256,1024]{1,0:T(8,128)(2,1)S(1)}, bf16[256,1024]{1,0:T(8,128)(2,1)S(1)}, u32[]{:S(2)}, u32[]{:S(2)}) collective-permute-start(bf16[256,1024]{1,0:T(8,128)(2,1)S(1)} %add_convert_fusion.12), channel_id=1, source_target_pairs={{0,2},{1,3},{2,0},{3,1},{4,6},{5,7},{6,4},{7,5},{8,10},{9,11},{10,... | collective-permute-start | bytes 1572872 | tf_op jit(solution)/shard_map/ppermute | solution.py:306
  52.3 16.6 %collective-permute-start.13 = (bf16[256,1024]{1,0:T(8,128)(2,1)}, bf16[256,1024]{1,0:T(8,128)(2,1)S(1)}, u32[]{:S(2)}, u32[]{:S(2)}) collective-permute-start(bf16[256,1024]{1,0:T(8,128)(2,1)} %collective-permute-done.4), channel_id=1, source_target_pairs={{0,1},{1,0},{2,3},{3,2},{4,5},{5,4},{6,7},{7,6},{8,9},{9,8},{10,11... | collective-permute-start | bytes 1572872 | tf_op jit(solution)/shard_map/ppermute | solution.py:306
  68.0 14.4 %collective-permute-start.11 = (bf16[256,1024]{1,0:T(8,128)(2,1)S(1)}, bf16[256,1024]{1,0:T(8,128)(2,1)}, u32[]{:S(2)}, u32[]{:S(2)}) collective-permute-start(bf16[256,1024]{1,0:T(8,128)(2,1)S(1)} %add_convert_fusion.11), channel_id=1, source_target_pairs={{0,2},{1,3},{2,0},{3,1},{4,6},{5,7},{6,4},{7,5},{8,10},{9,11},{10,... | collective-permute-start | bytes 1572872 | tf_op jit(solution)/shard_map/ppermute | solution.py:306
  82.4 11.3 %collective-permute-start.12 = (bf16[256,1024]{1,0:T(8,128)(2,1)}, bf16[256,1024]{1,0:T(8,128)(2,1)}, u32[]{:S(2)}, u32[]{:S(2)}) collective-permute-start(bf16[256,1024]{1,0:T(8,128)(2,1)} %collective-permute-done.11), channel_id=1, source_target_pairs={{0,1},{1,0},{2,3},{3,2},{4,5},{5,4},{6,7},{7,6},{8,9},{9,8},{10,11... | collective-permute-start | bytes 1572872 | tf_op jit(solution)/shard_map/ppermute | solution.py:306
  106.3 8.3 %collective-permute-start.10 = (bf16[256,1024]{1,0:T(8,128)(2,1)S(1)}, bf16[256,1024]{1,0:T(8,128)(2,1)S(1)}, u32[]{:S(2)}, u32[]{:S(2)}) collective-permute-start(bf16[256,1024]{1,0:T(8,128)(2,1)S(1)} %slice.137), channel_id=1, source_target_pairs={{0,1},{1,0},{2,3},{3,2},{4,5},{5,4},{6,7},{7,6},{8,9},{9,8},{10,11... | collective-permute-start | bytes 1572872 | tf_op jit(solution)/shard_map/ppermute | solution.py:306
  110.4 14.2 %collective-permute-start.15 = (bf16[256,1024]{1,0:T(8,128)(2,1)S(1)}, bf16[256,1024]{1,0:T(8,128)(2,1)S(1)}, u32[]{:S(2)}, u32[]{:S(2)}) collective-permute-start(bf16[256,1024]{1,0:T(8,128)(2,1)S(1)} %add_convert_fusion.10), channel_id=1, source_target_pairs={{0,2},{1,3},{2,0},{3,1},{4,6},{5,7},{6,4},{7,5},{8,10},{9,11},{10,... | collective-permute-start | bytes 1572872 | tf_op jit(solution)/shard_map/ppermute | solution.py:306
  112.5 58.7 %collective-permute-start.18 = (bf16[512,1024]{1,0:T(8,128)(2,1)S(1)}, bf16[512,1024]{1,0:T(8,128)(2,1)S(1)}, u32[]{:S(2)}, u32[]{:S(2)}) collective-permute-start(bf16[512,1024]{1,0:T(8,128)(2,1)S(1)} %convolution_convert_fusion.4), channel_id=1, source_target_pairs={{0,8},{4,12},{8,0},{12,4},{16,24},{20,28},{24,16},{28,20},{1,9},{5... | collective-permute-start | bytes 3145736 | tf_op jit(solution)/shard_map/ppermute | solution.py:306
  128.3 42.9 %collective-permute-start.17 = (bf16[512,1024]{1,0:T(8,128)(2,1)S(1)}, bf16[512,1024]{1,0:T(8,128)(2,1)S(1)}, u32[]{:S(2)}, u32[]{:S(2)}) collective-permute-start(bf16[512,1024]{1,0:T(8,128)(2,1)S(1)} %convolution_convert_fusion.5), channel_id=1, source_target_pairs={{0,4},{4,0},{8,12},{12,8},{16,20},{20,16},{24,28},{28,24},{1,5},{5... | collective-permute-start | bytes 3145736 | tf_op jit(solution)/shard_map/ppermute | solution.py:306
  129.9 24.1 %collective-permute-start.31 = (f32[1,1152]{1,0:T(1,128)S(1)}, f32[1,1152]{1,0:T(1,128)S(1)}, u32[]{:S(2)}, u32[]{:S(2)}) collective-permute-start(f32[1,1152]{1,0:T(1,128)S(1)} %broadcast_in_dim.34), channel_id=1, source_target_pairs={{0,4},{4,0},{8,12},{12,8},{16,20},{20,16},{24,28},{28,24},{1,5},{5... | collective-permute-start | bytes 13832 | tf_op jit(solution)/shard_map/ppermute | solution.py:306
  130.4 25.2 %collective-permute-start.50 = (f32[4,1024]{1,0:T(4,128)S(1)}, f32[4,1024]{1,0:T(4,128)S(1)}, u32[]{:S(2)}, u32[]{:S(2)}) collective-permute-start(f32[4,1024]{1,0:T(4,128)S(1)} %fusion.46), channel_id=1, source_target_pairs={{0,2},{1,3},{2,0},{3,1},{4,6},{5,7},{6,4},{7,5},{8,10},{9,11},{10,... | collective-permute-start | bytes 49160 | tf_op jit(solution)/shard_map/ppermute | solution.py:306
  161.2 12.7 %collective-permute-start.16 = (bf16[256,1024]{1,0:T(8,128)(2,1)S(1)}, bf16[256,1024]{1,0:T(8,128)(2,1)}, u32[]{:S(2)}, u32[]{:S(2)}) collective-permute-start(bf16[256,1024]{1,0:T(8,128)(2,1)S(1)} %get-tuple-element.83), channel_id=1, source_target_pairs={{0,2},{1,3},{2,0},{3,1},{4,6},{5,7},{6,4},{7,5},{8,10},{9,11},{10,... | collective-permute-start | bytes 1572872 | tf_op jit(solution)/shard_map/ppermute | solution.py:306
  164.0 96.2 %collective-permute-start.9 = (bf16[256,1024]{1,0:T(8,128)(2,1)}, bf16[256,1024]{1,0:T(8,128)(2,1)}, u32[]{:S(2)}, u32[]{:S(2)}) collective-permute-start(bf16[256,1024]{1,0:T(8,128)(2,1)} %slice.171), channel_id=1, source_target_pairs={{0,1},{1,0},{2,3},{3,2},{4,5},{5,4},{6,7},{7,6},{8,9},{9,8},{10,11... | collective-permute-start | bytes 1572872 | tf_op jit(solution)/shard_map/ppermute | solution.py:306
  170.5 8.6 %collective-permute-start.20 = (bf16[256,1024]{1,0:T(8,128)(2,1)S(1)}, bf16[256,1024]{1,0:T(8,128)(2,1)S(1)}, u32[]{:S(2)}, u32[]{:S(2)}) collective-permute-start(bf16[256,1024]{1,0:T(8,128)(2,1)S(1)} %get-tuple-element.83), channel_id=1, source_target_pairs={{0,1},{1,0},{2,3},{3,2},{4,5},{5,4},{6,7},{7,6},{8,9},{9,8},{10,11... | collective-permute-start | bytes 1572872 | tf_op jit(solution)/shard_map/ppermute | solution.py:306
  175.2 35.3 %collective-permute-start.59 = (bf16[256,1024]{1,0:T(8,128)(2,1)}, bf16[256,1024]{1,0:T(8,128)(2,1)}, u32[]{:S(2)}, u32[]{:S(2)}) collective-permute-start(bf16[256,1024]{1,0:T(8,128)(2,1)} %constant_dynamic-slice_fusion.1), channel_id=1, source_target_pairs={{0,8},{4,12},{8,0},{12,4},{16,24},{20,28},{24,16},{28,20},{1,9},{5... | collective-permute-start | bytes 1572872 | tf_op jit(solution)/shard_map/ppermute | solution.py:306
  177.9 42.0 %collective-permute-start.54 = (bf16[256,1024]{1,0:T(8,128)(2,1)}, bf16[256,1024]{1,0:T(8,128)(2,1)}, u32[]{:S(2)}, u32[]{:S(2)}) collective-permute-start(bf16[256,1024]{1,0:T(8,128)(2,1)} %constant_dynamic-slice_fusion.3), channel_id=1, source_target_pairs={{0,16},{4,20},{8,24},{12,28},{16,0},{20,4},{24,8},{28,12},{1,17},{... | collective-permute-start | bytes 1572872 | tf_op jit(solution)/shard_map/ppermute | solution.py:306
  178.3 13.0 %collective-permute-start.19 = (bf16[256,1024]{1,0:T(8,128)(2,1)}, bf16[256,1024]{1,0:T(8,128)(2,1)}, u32[]{:S(2)}, u32[]{:S(2)}) collective-permute-start(bf16[256,1024]{1,0:T(8,128)(2,1)} %collective-permute-done.16), channel_id=1, source_target_pairs={{0,1},{1,0},{2,3},{3,2},{4,5},{5,4},{6,7},{7,6},{8,9},{9,8},{10,11... | collective-permute-start | bytes 1572872 | tf_op jit(solution)/shard_map/ppermute | solution.py:306
  179.1 47.1 %collective-permute-start.21 = (bf16[256,1024]{1,0:T(8,128)(2,1)}, bf16[256,1024]{1,0:T(8,128)(2,1)}, u32[]{:S(2)}, u32[]{:S(2)}) collective-permute-start(bf16[256,1024]{1,0:T(8,128)(2,1)} %slice.144), channel_id=1, source_target_pairs={{0,1},{1,0},{2,3},{3,2},{4,5},{5,4},{6,7},{7,6},{8,9},{9,8},{10,11... | collective-permute-start | bytes 1572872 | tf_op jit(solution)/shard_map/ppermute | solution.py:306
  212.1 27.1 %collective-permute-start.60 = (bf16[128,1024]{1,0:T(8,128)(2,1)S(1)}, bf16[128,1024]{1,0:T(8,128)(2,1)S(1)}, u32[]{:S(2)}, u32[]{:S(2)}) collective-permute-start(bf16[128,1024]{1,0:T(8,128)(2,1)S(1)} %constant_dynamic-slice_fusion), channel_id=1, source_target_pairs={{0,16},{4,20},{8,24},{12,28},{16,0},{20,4},{24,8},{28,12},{1,17},{... | collective-permute-start | bytes 786440 | tf_op jit(solution)/shard_map/ppermute | solution.py:306
  214.7 6.8 %collective-permute-start.40 = (f32[2,256]{1,0:T(2,128)S(1)}, f32[2,256]{1,0:T(2,128)S(1)}, u32[]{:S(2)}, u32[]{:S(2)}) collective-permute-start(f32[2,256]{1,0:T(2,128)S(1)} %pad_maximum_fusion.19), channel_id=1, source_target_pairs={{0,4},{4,0},{8,12},{12,8},{16,20},{20,16},{24,28},{28,24},{1,5},{5... | collective-permute-start | bytes 6152 | tf_op jit(solution)/shard_map/ppermute | solution.py:306
  222.6 23.4 %collective-permute-start.55 = (bf16[128,1024]{1,0:T(8,128)(2,1)S(1)}, bf16[128,1024]{1,0:T(8,128)(2,1)S(1)}, u32[]{:S(2)}, u32[]{:S(2)}) collective-permute-start(bf16[128,1024]{1,0:T(8,128)(2,1)S(1)} %constant_dynamic-slice_fusion.2), channel_id=1, source_target_pairs={{0,4},{4,0},{8,12},{12,8},{16,20},{20,16},{24,28},{28,24},{1,5},{5... | collective-permute-start | bytes 786440 | tf_op jit(solution)/shard_map/ppermute | solution.py:306
  225.3 12.1 %collective-permute-start.43 = (bf16[128,1024]{1,0:T(8,128)(2,1)S(1)}, bf16[128,1024]{1,0:T(8,128)(2,1)S(1)}, u32[]{:S(2)}, u32[]{:S(2)}) collective-permute-start(bf16[128,1024]{1,0:T(8,128)(2,1)S(1)} %convolution_convert_fusion.12), channel_id=1, source_target_pairs={{0,4},{4,0},{8,12},{12,8},{16,20},{20,16},{24,28},{28,24},{1,5},{5... | collective-permute-start | bytes 786440 | tf_op jit(solution)/shard_map/ppermute | solution.py:306
  230.8 43.3 %collective-permute-start.34 = (bf16[512,768]{1,0:T(8,128)(2,1)S(1)}, bf16[512,768]{1,0:T(8,128)(2,1)S(1)}, u32[]{:S(2)}, u32[]{:S(2)}) collective-permute-start(bf16[512,768]{1,0:T(8,128)(2,1)S(1)} %convolution_convert_fusion.10), channel_id=1, source_target_pairs={{0,4},{4,0},{8,12},{12,8},{16,20},{20,16},{24,28},{28,24},{1,5},{5... | collective-permute-start | bytes 2359304 | tf_op jit(solution)/shard_map/ppermute | solution.py:306
  237.4 67.8 %collective-permute-start.23 = (bf16[256,1024]{1,0:T(8,128)(2,1)S(1)}, bf16[256,1024]{1,0:T(8,128)(2,1)S(1)}, u32[]{:S(2)}, u32[]{:S(2)}) collective-permute-start(bf16[256,1024]{1,0:T(8,128)(2,1)S(1)} %slice.173), channel_id=1, source_target_pairs={{0,1},{1,0},{2,3},{3,2},{4,5},{5,4},{6,7},{7,6},{8,9},{9,8},{10,11... | collective-permute-start | bytes 1572872 | tf_op jit(solution)/shard_map/ppermute | solution.py:306
  245.2 13.5 %collective-permute-start.22 = (bf16[256,1024]{1,0:T(8,128)(2,1)S(1)}, bf16[256,1024]{1,0:T(8,128)(2,1)S(1)}, u32[]{:S(2)}, u32[]{:S(2)}) collective-permute-start(bf16[256,1024]{1,0:T(8,128)(2,1)S(1)} %add_convert_fusion.9), channel_id=1, source_target_pairs={{0,2},{1,3},{2,0},{3,1},{4,6},{5,7},{6,4},{7,5},{8,10},{9,11},{10,... | collective-permute-start | bytes 1572872 | tf_op jit(solution)/shard_map/ppermute | solution.py:306
  252.0 15.7 %collective-permute-start.61 = (bf16[128,1024]{1,0:T(8,128)(2,1)S(1)}, bf16[128,1024]{1,0:T(8,128)(2,1)S(1)}, u32[]{:S(2)}, u32[]{:S(2)}) collective-permute-start(bf16[128,1024]{1,0:T(8,128)(2,1)S(1)} %add_convert_fusion.15), channel_id=1, source_target_pairs={{0,16},{4,20},{8,24},{12,28},{16,0},{20,4},{24,8},{28,12},{1,17},{... | collective-permute-start | bytes 786440 | tf_op jit(solution)/shard_map/ppermute | solution.py:306
  258.6 9.2 %collective-permute-start.56 = (bf16[128,1024]{1,0:T(8,128)(2,1)S(1)}, bf16[128,1024]{1,0:T(8,128)(2,1)S(1)}, u32[]{:S(2)}, u32[]{:S(2)}) collective-permute-start(bf16[128,1024]{1,0:T(8,128)(2,1)S(1)} %add_convert_fusion.16), channel_id=1, source_target_pairs={{0,4},{4,0},{8,12},{12,8},{16,20},{20,16},{24,28},{28,24},{1,5},{5... | collective-permute-start | bytes 786440 | tf_op jit(solution)/shard_map/ppermute | solution.py:306
  260.2 7.4 %collective-permute-start.46 = (bf16[32,1024]{1,0:T(8,128)(2,1)S(1)}, bf16[32,1024]{1,0:T(8,128)(2,1)S(1)}, u32[]{:S(2)}, u32[]{:S(2)}) collective-permute-start(bf16[32,1024]{1,0:T(8,128)(2,1)S(1)} %add_convert_fusion.19), channel_id=1, source_target_pairs={{0,16},{4,20},{8,24},{12,28},{16,0},{20,4},{24,8},{28,12},{1,17},{... | collective-permute-start | bytes 196616 | tf_op jit(solution)/shard_map/ppermute | solution.py:306
  267.6 16.4 %collective-permute-start.24 = (bf16[256,1024]{1,0:T(8,128)(2,1)S(1)}, bf16[256,1024]{1,0:T(8,128)(2,1)S(1)}, u32[]{:S(2)}, u32[]{:S(2)}) collective-permute-start(bf16[256,1024]{1,0:T(8,128)(2,1)S(1)} %slice.148), channel_id=1, source_target_pairs={{0,1},{1,0},{2,3},{3,2},{4,5},{5,4},{6,7},{7,6},{8,9},{9,8},{10,11... | collective-permute-start | bytes 1572872 | tf_op jit(solution)/shard_map/ppermute | solution.py:306
  267.9 24.8 %collective-permute-start.62 = (bf16[256,1024]{1,0:T(8,128)(2,1)S(1)}, bf16[256,1024]{1,0:T(8,128)(2,1)S(1)}, u32[]{:S(2)}, u32[]{:S(2)}) collective-permute-start(bf16[256,1024]{1,0:T(8,128)(2,1)S(1)} %maximum_select_fusion.8), channel_id=1, source_target_pairs={{0,8},{4,12},{8,0},{12,4},{16,24},{20,28},{24,16},{28,20},{1,9},{5... | collective-permute-start | bytes 1572872 | tf_op jit(solution)/shard_map/ppermute | solution.py:306
  274.1 25.3 %collective-permute-start.57 = (bf16[256,1024]{1,0:T(8,128)(2,1)S(1)}, bf16[256,1024]{1,0:T(8,128)(2,1)S(1)}, u32[]{:S(2)}, u32[]{:S(2)}) collective-permute-start(bf16[256,1024]{1,0:T(8,128)(2,1)S(1)} %maximum_select_fusion.7), channel_id=1, source_target_pairs={{0,16},{4,20},{8,24},{12,28},{16,0},{20,4},{24,8},{28,12},{1,17},{... | collective-permute-start | bytes 1572872 | tf_op jit(solution)/shard_map/ppermute | solution.py:306
  274.2 7.4 %collective-permute-start.48 = (bf16[128,1024]{1,0:T(8,128)(2,1)S(1)}, bf16[128,1024]{1,0:T(8,128)(2,1)S(1)}, u32[]{:S(2)}, u32[]{:S(2)}) collective-permute-start(bf16[128,1024]{1,0:T(8,128)(2,1)S(1)} %maximum_select_fusion.10), channel_id=1, source_target_pairs={{0,4},{4,0},{8,12},{12,8},{16,20},{20,16},{24,28},{28,24},{1,5},{5... | collective-permute-start | bytes 786440 | tf_op jit(solution)/shard_map/ppermute | solution.py:306
  281.6 23.4 %collective-permute-start.35 = (bf16[256,768]{1,0:T(8,128)(2,1)S(1)}, bf16[256,768]{1,0:T(8,128)(2,1)S(1)}, u32[]{:S(2)}, u32[]{:S(2)}) collective-permute-start(bf16[256,768]{1,0:T(8,128)(2,1)S(1)} %constant_dynamic-slice_fusion.7), channel_id=1, source_target_pairs={{0,8},{4,12},{8,0},{12,4},{16,24},{20,28},{24,16},{28,20},{1,9},{5... | collective-permute-start | bytes 1179656 | tf_op jit(solution)/shard_map/ppermute | solution.py:306
  284.2 21.0 %collective-permute-start.25 = (bf16[256,1024]{1,0:T(8,128)(2,1)S(1)}, bf16[256,1024]{1,0:T(8,128)(2,1)S(1)}, u32[]{:S(2)}, u32[]{:S(2)}) collective-permute-start(bf16[256,1024]{1,0:T(8,128)(2,1)S(1)} %add_convert_fusion.7), channel_id=1, source_target_pairs={{0,2},{1,3},{2,0},{3,1},{4,6},{5,7},{6,4},{7,5},{8,10},{9,11},{10,... | collective-permute-start | bytes 1572872 | tf_op jit(solution)/shard_map/ppermute | solution.py:306
  293.2 64.6 %collective-permute-start.63 = (bf16[512,1024]{1,0:T(8,128)(2,1)S(1)}, bf16[512,1024]{1,0:T(8,128)(2,1)S(1)}, u32[]{:S(2)}, u32[]{:S(2)}) collective-permute-start(bf16[512,1024]{1,0:T(8,128)(2,1)S(1)} %maximum_select_fusion.4), channel_id=1, source_target_pairs={{0,4},{4,0},{8,12},{12,8},{16,20},{20,16},{24,28},{28,24},{1,5},{5... | collective-permute-start | bytes 3145736 | tf_op jit(solution)/shard_map/ppermute | solution.py:306
  299.9 60.8 %collective-permute-start.58 = (bf16[512,1024]{1,0:T(8,128)(2,1)S(1)}, bf16[512,1024]{1,0:T(8,128)(2,1)S(1)}, u32[]{:S(2)}, u32[]{:S(2)}) collective-permute-start(bf16[512,1024]{1,0:T(8,128)(2,1)S(1)} %maximum_select_fusion.3), channel_id=1, source_target_pairs={{0,8},{4,12},{8,0},{12,4},{16,24},{20,28},{24,16},{28,20},{1,9},{5... | collective-permute-start | bytes 3145736 | tf_op jit(solution)/shard_map/ppermute | solution.py:306
  305.1 23.9 %collective-permute-start.36 = (bf16[128,768]{1,0:T(8,128)(2,1)S(1)}, bf16[128,768]{1,0:T(8,128)(2,1)S(1)}, u32[]{:S(2)}, u32[]{:S(2)}) collective-permute-start(bf16[128,768]{1,0:T(8,128)(2,1)S(1)} %constant_dynamic-slice_fusion.6), channel_id=1, source_target_pairs={{0,16},{4,20},{8,24},{12,28},{16,0},{20,4},{24,8},{28,12},{1,17},{... | collective-permute-start | bytes 589832 | tf_op jit(solution)/shard_map/ppermute | solution.py:306
  305.9 26.7 %collective-permute-start.26 = (f32[2,1024]{1,0:T(2,128)S(1)}, f32[2,1024]{1,0:T(2,128)S(1)}, u32[]{:S(2)}, u32[]{:S(2)}) collective-permute-start(f32[2,1024]{1,0:T(2,128)S(1)} %pad_maximum_fusion.17), channel_id=1, source_target_pairs={{0,1},{1,0},{2,3},{3,2},{4,5},{5,4},{6,7},{7,6},{8,9},{9,8},{10,11... | collective-permute-start | bytes 24584 | tf_op jit(solution)/shard_map/ppermute | solution.py:306
  329.1 12.6 %collective-permute-start.37 = (bf16[128,768]{1,0:T(8,128)(2,1)S(1)}, bf16[128,768]{1,0:T(8,128)(2,1)S(1)}, u32[]{:S(2)}, u32[]{:S(2)}) collective-permute-start(bf16[128,768]{1,0:T(8,128)(2,1)S(1)} %add_convert_fusion.17), channel_id=1, source_target_pairs={{0,16},{4,20},{8,24},{12,28},{16,0},{20,4},{24,8},{28,12},{1,17},{... | collective-permute-start | bytes 589832 | tf_op jit(solution)/shard_map/ppermute | solution.py:306
  332.6 9.3 %collective-permute-start.27 = (f32[2,1024]{1,0:T(2,128)S(1)}, f32[2,1024]{1,0:T(2,128)S(1)}, u32[]{:S(2)}, u32[]{:S(2)}) collective-permute-start(f32[2,1024]{1,0:T(2,128)S(1)} %fusion.45), channel_id=1, source_target_pairs={{0,2},{1,3},{2,0},{3,1},{4,6},{5,7},{6,4},{7,5},{8,10},{9,11},{10,... | collective-permute-start | bytes 24584 | tf_op jit(solution)/shard_map/ppermute | solution.py:306
  341.8 10.7 %collective-permute-start.38 = (bf16[256,768]{1,0:T(8,128)(2,1)S(1)}, bf16[256,768]{1,0:T(8,128)(2,1)S(1)}, u32[]{:S(2)}, u32[]{:S(2)}) collective-permute-start(bf16[256,768]{1,0:T(8,128)(2,1)S(1)} %maximum_select_fusion.9), channel_id=1, source_target_pairs={{0,8},{4,12},{8,0},{12,4},{16,24},{20,28},{24,16},{28,20},{1,9},{5... | collective-permute-start | bytes 1179656 | tf_op jit(solution)/shard_map/ppermute | solution.py:306
  345.7 6.8 %collective-permute-start.29 = (f32[2,1024]{1,0:T(2,128)S(1)}, f32[2,1024]{1,0:T(2,128)S(1)}, u32[]{:S(2)}, u32[]{:S(2)}) collective-permute-start(f32[2,1024]{1,0:T(2,128)S(1)} %add.313), channel_id=1, source_target_pairs={{0,8},{4,12},{8,0},{12,4},{16,24},{20,28},{24,16},{28,20},{1,9},{5... | collective-permute-start | bytes 24584 | tf_op jit(solution)/shard_map/ppermute | solution.py:306
  352.8 18.1 %collective-permute-start.39 = (bf16[512,768]{1,0:T(8,128)(2,1)S(1)}, bf16[512,768]{1,0:T(8,128)(2,1)S(1)}, u32[]{:S(2)}, u32[]{:S(2)}) collective-permute-start(bf16[512,768]{1,0:T(8,128)(2,1)S(1)} %maximum_select_fusion.5), channel_id=1, source_target_pairs={{0,4},{4,0},{8,12},{12,8},{16,20},{20,16},{24,28},{28,24},{1,5},{5... | collective-permute-start | bytes 2359304 | tf_op jit(solution)/shard_map/ppermute | solution.py:306
  (67 other events, 499.8 us)

commit v3 on v2

--- a/solution.py
+++ b/solution.py
@@ -11,6 +11,7 @@
 PAIR = 128
 HD = 64
 EXCLUDED = -1e30
+LIGHT = pl.CostEstimate(flops=1024, bytes_accessed=1024, transcendentals=0)
 
 
 def dot_nn(a, b):
@@ -37,10 +38,9 @@
         refs[2 * halves : 3 * halves],
     )
     out_ref, log_ref = refs[3 * halves :]
-    query = q_ref[0]
-    scaled = query * jnp.asarray(HD**-0.5, BF16)
+    scaled = q_ref[...] * jnp.asarray(HD**-0.5, BF16)
     pick = pick_ref[...]
-    keys = [jnp.concatenate([k[0], b[...]], 1) for k, b in zip(k_refs, bar_refs)]
+    keys = [jnp.concatenate([k[...], b[...]], 1) for k, b in zip(k_refs, bar_refs)]
     rows = []
     for head in range(2):
         own = jnp.where(head_lanes(head), scaled, jnp.zeros_like(scaled))
@@ -54,30 +54,30 @@
             jnp.add, [jnp.sum(p, 0, keepdims=True) for p in powers]
         )
         summed = functools.reduce(
-            jnp.add, [dot_tn(v[0], p.astype(BF16)) for v, p in zip(v_refs, powers)]
+            jnp.add, [dot_tn(v[...], p.astype(BF16)) for v, p in zip(v_refs, powers)]
         )
         rows.append((summed / total)[head * HD : (head + 1) * HD])
         log_ref[0, head : head + 1, :] = top + jnp.log(total)
     out_ref[...] = jnp.concatenate(rows, 0).T.astype(BF16)
 
 
-def attend_forward(query, pick, keys, values, bars, tile=256):
-    _, count, width = query.shape
-    halves = len(keys)
+def attend_forward(own, pick, halves, bars, tile=256):
+    count = own.shape[0]
+    width = own.shape[1] // 3
     pairs = width // PAIR
     tile = min(tile, count)
-    grid = (pairs, count // tile)
-    key_spec = [pl.BlockSpec((1, k.shape[1], PAIR), lambda p, i: (0, 0, p)) for k in keys]
+    key_spec = [pl.BlockSpec((h.shape[0], PAIR), lambda p, i: (0, pairs + p)) for h in halves]
+    value_spec = [pl.BlockSpec((h.shape[0], PAIR), lambda p, i: (0, 2 * pairs + p)) for h in halves]
     bar_spec = [pl.BlockSpec((b.shape[0], PAIR), lambda p, i: (0, 0)) for b in bars]
-    total_keys = sum(k.shape[1] for k in keys)
+    total_keys = sum(h.shape[0] for h in halves)
     return pl.pallas_call(
-        functools.partial(attend_kernel, halves),
-        grid=grid,
+        functools.partial(attend_kernel, len(halves)),
+        grid=(pairs, count // tile),
         in_specs=[
-            pl.BlockSpec((1, tile, PAIR), lambda p, i: (0, i, p)),
+            pl.BlockSpec((tile, PAIR), lambda p, i: (i, p)),
             pl.BlockSpec((tile, PAIR), lambda p, i: (i, 0)),
             *key_spec,
-            *key_spec,
+            *value_spec,
             *bar_spec,
         ],
         out_specs=[
@@ -88,13 +88,10 @@
             jax.ShapeDtypeStruct((count, width), BF16),
             jax.ShapeDtypeStruct((pairs, 8, count), F32),
         ],
-        cost_estimate=pl.CostEstimate(
-            flops=16 * count * total_keys * width,
-            bytes_accessed=6 * total_keys * width,
-            transcendentals=count * total_keys * width // HD,
-        ),
+        cost_estimate=LIGHT,
+        compiler_params=pltpu.CompilerParams(vmem_limit_bytes=24 * 2**20),
         name="attend_forward",
-    )(query, pick, *keys, *values, *bars)
+    )(own, pick, *halves, *halves, *bars)
 
 
 def attend_back_kernel(halves, first, last, q_ref, pick_ref, grad_ref, out_ref, log_ref, *refs):
@@ -128,7 +125,7 @@
                 k_sum[n][...] = k_in[n][...]
                 v_sum[n][...] = v_in[n][...]
 
-    scaled = q_ref[0] * jnp.asarray(HD**-0.5, BF16)
+    scaled = q_ref[...] * jnp.asarray(HD**-0.5, BF16)
     grad = grad_ref[...]
     pick = pick_ref[...]
     both = (grad.astype(F32) * out_ref[...].astype(F32)).T
@@ -140,8 +137,8 @@
     stacked_g = jnp.concatenate(grads, 0)
     q_parts = [0.0, 0.0]
     for n in range(halves):
-        keys = k_refs[n][0]
-        values = v_refs[n][0]
+        keys = k_refs[n][...]
+        values = v_refs[n][...]
         wide = jnp.concatenate([keys, bar_refs[n][...]], 1)
         probs = []
         slopes = []
@@ -165,48 +162,47 @@
                 v_out[n][...] = v_sum[n][...].astype(BF16)
 
 
-def attend_back(query, pick, grad, out, logs, keys, values, bars, carried, last, tile=256):
-    _, count, width = query.shape
-    halves = len(keys)
+def attend_back(own, pick, grad, out, logs, halves, bars, carried, last, tile=256):
+    count = own.shape[0]
+    width = own.shape[1] // 3
     pairs = width // PAIR
     tile = min(tile, count)
     first = carried is None
-    key_spec = [pl.BlockSpec((1, k.shape[1], PAIR), lambda p, i: (0, 0, p)) for k in keys]
+    key_spec = [pl.BlockSpec((h.shape[0], PAIR), lambda p, i: (0, pairs + p)) for h in halves]
+    value_spec = [pl.BlockSpec((h.shape[0], PAIR), lambda p, i: (0, 2 * pairs + p)) for h in halves]
     bar_spec = [pl.BlockSpec((b.shape[0], PAIR), lambda p, i: (0, 0)) for b in bars]
-    sum_spec = [pl.BlockSpec((k.shape[1], PAIR), lambda p, i: (0, p)) for k in keys]
+    sum_spec = [pl.BlockSpec((h.shape[0], PAIR), lambda p, i: (0, p)) for h in halves]
     row_spec = pl.BlockSpec((tile, PAIR), lambda p, i: (i, p))
     sum_type = BF16 if last else F32
-    sums = [jax.ShapeDtypeStruct((k.shape[1], width), sum_type) for k in keys]
-    total_keys = sum(k.shape[1] for k in keys)
+    sums = [jax.ShapeDtypeStruct((h.shape[0], width), sum_type) for h in halves]
+    total_keys = sum(h.shape[0] for h in halves)
     scratch = []
     if last:
-        scratch = [pltpu.VMEM((k.shape[1], PAIR), F32) for k in keys] * 2
+        scratch = [pltpu.VMEM((h.shape[0], PAIR), F32) for h in halves] * 2
     extra = [] if first else list(carried[0]) + list(carried[1])
+    parts = len(halves)
     result = pl.pallas_call(
-        functools.partial(attend_back_kernel, halves, first, last),
+        functools.partial(attend_back_kernel, parts, first, last),
         grid=(pairs, count // tile),
         in_specs=[
-            pl.BlockSpec((1, tile, PAIR), lambda p, i: (0, i, p)),
+            row_spec,
             pl.BlockSpec((tile, PAIR), lambda p, i: (i, 0)),
             row_spec,
             row_spec,
             pl.BlockSpec((1, 8, tile), lambda p, i: (p, 0, i)),
             *key_spec,
-            *key_spec,
+            *value_spec,
             *bar_spec,
             *([] if first else sum_spec * 2),
         ],
         out_specs=[row_spec, *sum_spec, *sum_spec],
         out_shape=[jax.ShapeDtypeStruct((count, width), BF16), *sums, *sums],
         scratch_shapes=scratch,
-        cost_estimate=pl.CostEstimate(
-            flops=40 * count * total_keys * width,
-            bytes_accessed=16 * total_keys * width,
-            transcendentals=count * total_keys * width // HD,
-        ),
+        cost_estimate=LIGHT,
+        compiler_params=pltpu.CompilerParams(vmem_limit_bytes=24 * 2**20),
         name="attend_back",
-    )(query, pick, grad, out, logs, *keys, *values, *bars, *extra)
-    return result[0], result[1 : 1 + halves], result[1 + halves :]
+    )(own, pick, grad, out, logs, *halves, *halves, *bars, *extra)
+    return result[0], result[1 : 1 + parts], result[1 + parts :]
 
 
 def mlp_kernel(x_ref, grad_ref, up_ref, bias_ref, down_ref, act_ref, slope_ref, back_ref):
@@ -245,11 +241,8 @@
             jax.ShapeDtypeStruct((count, hidden), BF16),
             jax.ShapeDtypeStruct((count, width), BF16),
         ],
-        cost_estimate=pl.CostEstimate(
-            flops=6 * count * width * hidden,
-            bytes_accessed=4 * width * hidden + 10 * count * width,
-            transcendentals=2 * count * hidden,
-        ),
+        cost_estimate=LIGHT,
+        compiler_params=pltpu.CompilerParams(vmem_limit_bytes=24 * 2**20),
         name="mlp_both",
     )(x, grad, up, bias[None], down)
 
@@ -328,46 +321,86 @@
 
 class DpSum:
     def __init__(self, count, index, order):
-        self.count, self.index, self.order = count, index, order
+        self.count, self.index = count, index
+        self.order = order
+        self.steps = list(order) + list(reversed(order))
+        self.at = 0
 
     def high(self, bit):
         return (self.index & bit) != 0
 
-    def open(self, left, right):
-        half = left.shape[1] // 2
+    def open(self, pairs):
+        half = pairs[0][0].shape[1] // 2
         top = jnp.where(self.high(self.order[0]), half, 0)
-        send = dot_tn(lax.dynamic_slice_in_dim(left, half - top, half, 1), right).astype(BF16)
-        self.held = dot_tn(lax.dynamic_slice_in_dim(left, top, half, 1), right).astype(BF16)
-        return send
-
-    def split(self, bit):
-        half = self.held.shape[0] // 2
-        top = jnp.where(self.high(bit), half, 0)
-        send = lax.dynamic_slice_in_dim(self.held, half - top, half, 0)
-        self.held = lax.dynamic_slice_in_dim(self.held, top, half, 0)
-        return send
-
-    def add(self, arrived):
-        self.held = (self.held.astype(F32) + arrived.astype(F32)).astype(BF16)
-
-    def join(self, bit, arrived):
-        self.held = jnp.where(
-            self.high(bit),
-            jnp.concatenate([arrived, self.held]),
-            jnp.concatenate([self.held, arrived]),
-        )
-
-    def pass_on(self, array, bit):
-        return swap(array, "dp", self.count, bit)
-
-    def halve_rest(self):
-        for bit in self.order[1:]:
-            self.add(self.pass_on(self.split(bit), bit))
-
-    def double_all(self):
-        for bit in reversed(self.order):
-            self.join(bit, self.pass_on(self.held, bit))
-        return self.held
+
+        def part(start):
+            dots = [
+                dot_tn(lax.dynamic_slice_in_dim(left, start, half, 1), right)
+                for left, right in pairs
+            ]
+            return functools.reduce(jnp.add, dots).astype(BF16)
+
+        self.send = part(half - top)
+        self.held = part(top)
+
+    def launch(self):
+        self.flying = swap(self.send, "dp", self.count, self.steps[self.at])
+
+    def land(self):
+        bit = self.steps[self.at]
+        if self.at < len(self.order):
+            self.held = (self.held.astype(F32) + self.flying.astype(F32)).astype(BF16)
+        else:
+            self.held = jnp.where(
+                self.high(bit),
+                jnp.concatenate([self.flying, self.held]),
+                jnp.concatenate([self.held, self.flying]),
+            )
+        self.at += 1
+        if self.at < len(self.order):
+            half = self.held.shape[0] // 2
+            top = jnp.where(self.high(self.steps[self.at]), half, 0)
+            self.send = lax.dynamic_slice_in_dim(self.held, half - top, half, 0)
+            self.held = lax.dynamic_slice_in_dim(self.held, top, half, 0)
+        else:
+            self.send = self.held
+
+    def busy(self):
+        return self.at < len(self.steps)
+
+
+class SmallSum:
+    def __init__(self, count, order, values):
+        self.count, self.steps, self.at = count, list(order), 0
+        self.send = self.held = values
+
+    def launch(self):
+        self.held = self.send
+        self.flying = swap(self.send, "dp", self.count, self.steps[self.at])
+
+    def land(self):
+        self.send = self.held = self.held + self.flying
+        self.at += 1
+
+    def busy(self):
+        return self.at < len(self.steps)
+
+
+def await_all(chain, sums):
+    tied = tie(*chain, *[s.flying for s in sums])
+    for s, value in zip(sums, tied[len(chain) :]):
+        s.flying = value
+        s.land()
+    return tied[: len(chain)]
+
+
+def start_all(chain, sums):
+    sums = [s for s in sums if s.busy()]
+    tied = tie(*chain, *[s.send for s in sums])
+    for s, value in zip(sums, tied[len(chain) :]):
+        s.send = value
+        s.launch()
+    return tied[: len(chain)]
 
 
 def butterfly(values, sizes):
@@ -420,10 +453,6 @@
 
         far_own = swap(attn_input, "mp", n_mp, far_bit)
         attn_near = gather_near(attn_input, n_mp)
-        far_own, grad_low = tie(far_own, grad_low)
-        attn_far = gather_near(far_own, n_mp)
-        grad_far = swap(grad_low, "mp", n_mp, far_bit)
-
         lanes = lax.broadcasted_iota(jnp.int32, (1, PAIR), 1)
         half_items = [
             jnp.concatenate(item_blocks[: n_mp // 2]),
@@ -433,27 +462,29 @@
         bars = [
             jnp.where(items[:, None] == lanes, 0.0, EXCLUDED).astype(BF16) for items in half_items
         ]
-        bias_rows = jnp.stack([input_bias[0], jnp.zeros_like(input_bias[0]), input_bias[1]])
+        bias_wide = jnp.concatenate([input_bias[0], jnp.zeros_like(input_bias[0]), input_bias[1]])
+        weight_wide = jnp.concatenate([input_weight[0], input_weight[1], input_weight[2]], 1)
 
         def project(rows):
-            wide = jnp.einsum("rd,tde->tre", rows, input_weight, preferred_element_type=F32)
-            return (wide + bias_rows[:, None, :]).astype(BF16)
-
-        qkv = [project(attn_near), project(attn_far)]
-        query = [rows[0:1] for rows in qkv]
-        keys = [rows[1:2] for rows in qkv]
-        values = [rows[2:3] for rows in qkv]
-
-        heads_far, logs_far = attend_forward(query[1], picks[1], keys, values, bars)
+            return (dot_nn(rows, weight_wide) + bias_wide).astype(BF16)
+
+        near = project(attn_near)
+        far_own, near, grad_low = tie(far_own, near, grad_low)
+        attn_far = gather_near(far_own, n_mp)
+        grad_far = swap(grad_low, "mp", n_mp, far_bit)
+        far = project(attn_far)
+
+        heads_far, logs_far = attend_forward(far, picks[1], [near, far], bars)
         share_far = dot_nn(heads_far, output_weight).astype(BF16)
-        share_far, grad_far = tie(share_far, grad_far)
         sum_far = scatter_near(share_far, n_mp).astype(BF16)
+        sum_far, near = tie(sum_far, near)
         arrived = swap(sum_far, "mp", n_mp, far_bit)
-        heads_near, logs_near = attend_forward(query[0], picks[0], keys, values, bars)
+        heads_near, logs_near = attend_forward(near, picks[0], [near, far], bars)
         share_near = dot_nn(heads_near, output_weight).astype(BF16)
         sum_near = scatter_near(share_near, n_mp)
         grad_near = gather_near(grad_low, n_mp)
         grad_far = gather_near(grad_far, n_mp)
+        arrived, grad_near, grad_far = tie(arrived, grad_near, grad_far)
         hidden_res = residual + (sum_near + arrived.astype(F32)) + output_bias
         normed_two, inverse_two = normalize(hidden_res)
         mlp_input = (normed_two * second_gain + second_shift).astype(BF16)
@@ -463,24 +494,28 @@
         act_near, slope_near, back_near = mlp_both(
             mlp_near, grad_near, expand_weight, expand_bias, reduce_weight
         )
+        share_near = dot_nn(act_near, reduce_weight).astype(BF16)
+        sum_near = scatter_near(back_near, n_mp)
+        far_own, sum_near, share_near = tie(far_own, sum_near, share_near)
         mlp_far = gather_near(far_own, n_mp)
         act_far, slope_far, back_far = mlp_both(
             mlp_far, grad_far, expand_weight, expand_bias, reduce_weight
         )
+        swapped = dp_bits[1:2] + dp_bits[:1] + dp_bits[2:]
+        reduce_sum = DpSum(n_dp, group, dp_bits)
+        expand_sum = DpSum(n_dp, group, swapped)
+        output_sum = DpSum(n_dp, group, dp_bits)
+        input_sum = DpSum(n_dp, group, dp_bits)
+        reduce_sum.open([(act_near, grad_near), (act_far, grad_far)])
         sum_far = scatter_near(back_far, n_mp).astype(BF16)
+        sum_far, slope_near, slope_far = start_all((sum_far, slope_near, slope_far), [reduce_sum])
         arrived = swap(sum_far, "mp", n_mp, far_bit)
-        sum_near = scatter_near(back_near, n_mp)
-
-        activated = jnp.concatenate([act_near, act_far])
-        pre_grad = jnp.concatenate([slope_near, slope_far])
-        grad_all = jnp.concatenate([grad_near, grad_far])
-        mlp_rows = jnp.concatenate([mlp_near, mlp_far])
-        reduce_sum = DpSum(n_dp, group, dp_bits)
-        expand_sum = DpSum(n_dp, group, dp_bits[1:] + dp_bits[:1])
-        reduce_send = reduce_sum.open(activated, grad_all)
-        expand_send = expand_sum.open(mlp_rows, pre_grad)
-        reduce_in = reduce_sum.pass_on(reduce_send, reduce_sum.order[0])
-        expand_in = expand_sum.pass_on(expand_send, expand_sum.order[0])
+        expand_sum.open([(mlp_near, slope_near), (mlp_far, slope_far)])
+        (sum_near,) = start_all((sum_near,), [expand_sum])
+        share_far = dot_nn(act_far, reduce_weight).astype(BF16)
+        arrived, share_far, reduce_sum.held, expand_sum.held = tie(
+            arrived, share_far, reduce_sum.held, expand_sum.held
+        )
 
         normed_grad_two = sum_near + arrived.astype(F32)
         grad_out = grad_low.astype(F32)
@@ -490,66 +525,15 @@
         branch_grad = residual_grad.astype(BF16)
         far_own = swap(branch_grad, "mp", n_mp, far_bit)
         branch_near = gather_near(branch_grad, n_mp)
+        out_sum = scatter_near(share_far, n_mp).astype(BF16)
+        branch_near, out_sum = tie(branch_near, out_sum)
+        out_far = swap(out_sum, "mp", n_mp, far_bit)
         head_near = dot_nt(branch_near, output_weight).astype(BF16)
         query_near, key_part, value_part = attend_back(
-            query[0], picks[0], head_near, heads_near, logs_near, keys, values, bars, None, False
-        )
-        share_far = dot_nn(act_far, reduce_weight).astype(BF16)
-        share_near = dot_nn(act_near, reduce_weight).astype(BF16)
-        far_own, share_far, reduce_in, expand_in = tie(far_own, share_far, reduce_in, expand_in)
-        branch_far = gather_near(far_own, n_mp)
-        head_far = dot_nt(branch_far, output_weight).astype(BF16)
-        out_far = swap(scatter_near(share_far, n_mp).astype(BF16), "mp", n_mp, far_bit)
+            near, picks[0], head_near, heads_near, logs_near, [near, far], bars, None, False
+        )
         out_near = scatter_near(share_near, n_mp)
-        query_far, key_grads, value_grads = attend_back(
-            query[1],
-            picks[1],
-            head_far,
-            heads_far,
-            logs_far,
-            keys,
-            values,
-            bars,
-            (key_part, value_part),
-            True,
-        )
-        reduce_sum.add(reduce_in)
-        expand_sum.add(expand_in)
-
-        qkv_near = jnp.concatenate([query_near, key_grads[0], value_grads[0]], 1)
-        qkv_far = jnp.concatenate([query_far, key_grads[1], value_grads[1]], 1)
-        weight_wide = jnp.concatenate([input_weight[0], input_weight[1], input_weight[2]], 1)
-        share_far = dot_nt(qkv_far, weight_wide).astype(BF16)
-        share_far, out_far = tie(share_far, out_far)
-        sum_far = scatter_near(share_far, n_mp).astype(BF16)
-        arrived = swap(sum_far, "mp", n_mp, far_bit)
-        sum_near = scatter_near(dot_nt(qkv_near, weight_wide).astype(BF16), n_mp)
-        block_output = (hidden_res + (out_near + out_far.astype(F32)) + reduce_bias).astype(BF16)
-
-        qkv_all = jnp.concatenate([qkv_near, qkv_far])
-        attn_rows = jnp.concatenate([attn_near, attn_far])
-        branch_all = jnp.concatenate([branch_near, branch_far])
-        heads_all = jnp.concatenate([heads_near, heads_far])
-        output_sum = DpSum(n_dp, group, dp_bits)
-        input_sum = DpSum(n_dp, group, dp_bits)
-        output_sum.add(output_sum.pass_on(output_sum.open(heads_all, branch_all), dp_bits[0]))
-        input_sum.add(input_sum.pass_on(input_sum.open(attn_rows, qkv_all), dp_bits[0]))
-
-        normed_grad_one = sum_near + arrived.astype(F32)
-        input_gradient = residual_grad + normalize_back(
-            normed_grad_one, normed_one, inverse_one, first_gain
-        )
-        reduce_sum.halve_rest()
-        expand_sum.halve_rest()
-        reduce_grad = reduce_sum.double_all()
-        expand_grad = expand_sum.double_all()
-        output_sum.halve_rest()
-        input_sum.halve_rest()
-        output_grad = output_sum.double_all()
-        input_grad = input_sum.double_all()
-
-        both = (("mp", n_mp), ("dp", n_dp))
-        dp_only = (("dp", n_dp),)
+        over_mp = (("mp", n_mp),)
         early = butterfly(
             jnp.stack(
                 [
@@ -559,43 +543,100 @@
                     jnp.sum(grad_out, 0),
                 ]
             ),
-            both,
-        )
-        hidden = expand_bias.shape[0]
-        patches = jnp.sum(lengths).astype(F32)
-        local = butterfly(
-            jnp.concatenate([jnp.sum(pre_grad, 0, dtype=F32), jnp.full((PAIR,), patches)])[None],
-            dp_only,
-        )[0]
-        factor = lax.rsqrt(local[hidden])
+            over_mp,
+        )
+        far_own, query_near = await_all((far_own, query_near), [reduce_sum, expand_sum])
+        branch_far = gather_near(far_own, n_mp)
+        (branch_far,) = start_all((branch_far,), [reduce_sum, expand_sum])
+        output_sum.open([(heads_near, branch_near), (heads_far, branch_far)])
+        head_far = dot_nt(branch_far, output_weight).astype(BF16)
+        head_far, out_near, early = start_all((head_far, out_near, early), [output_sum])
+        query_far, key_grads, value_grads = attend_back(
+            far,
+            picks[1],
+            head_far,
+            heads_far,
+            logs_far,
+            [near, far],
+            bars,
+            (key_part, value_part),
+            True,
+        )
+
+        qkv_near = jnp.concatenate([query_near, key_grads[0], value_grads[0]], 1)
+        qkv_far = jnp.concatenate([query_far, key_grads[1], value_grads[1]], 1)
+        input_sum.open([(attn_near, qkv_near), (attn_far, qkv_far)])
+        share_far = dot_nt(qkv_far, weight_wide).astype(BF16)
+        sum_far = scatter_near(share_far, n_mp).astype(BF16)
+        (sum_far,) = start_all((sum_far,), [input_sum])
+        arrived = swap(sum_far, "mp", n_mp, far_bit)
+        sum_near = scatter_near(dot_nt(qkv_near, weight_wide).astype(BF16), n_mp)
+        sum_near, input_sum.held = await_all(
+            (sum_near, input_sum.held), [reduce_sum, expand_sum]
+        )
+        (sum_near,) = start_all((sum_near,), [reduce_sum, expand_sum])
+        (arrived,) = await_all((arrived,), [output_sum])
+        arrived, sum_near, out_far = start_all((arrived, sum_near, out_far), [output_sum])
+        block_output = (hidden_res + (out_near + out_far.astype(F32)) + reduce_bias).astype(BF16)
+        normed_grad_one = sum_near + arrived.astype(F32)
+        input_gradient = residual_grad + normalize_back(
+            normed_grad_one, normed_one, inverse_one, first_gain
+        )
         late = butterfly(
             jnp.stack([jnp.sum(normed_grad_one * normed_one, 0), jnp.sum(normed_grad_one, 0)]),
-            both,
-        )
-        wide_sums = jnp.sum(qkv_all, 0, dtype=F32)
-        qv_total = butterfly(
-            jnp.stack([wide_sums[:local_width], wide_sums[2 * local_width :]]), dp_only
-        )
-        input_total = input_grad.astype(F32) * factor
+            over_mp,
+        )
+        hidden = expand_bias.shape[0]
+        hidden_sums = jnp.sum(slope_near, 0, dtype=F32) + jnp.sum(slope_far, 0, dtype=F32)
+        wide_sums = jnp.sum(qkv_near, 0, dtype=F32) + jnp.sum(qkv_far, 0, dtype=F32)
+        small = SmallSum(
+            n_dp,
+            dp_bits,
+            jnp.concatenate(
+                [
+                    early.reshape(-1),
+                    late.reshape(-1),
+                    wide_sums[:local_width],
+                    wide_sums[2 * local_width :],
+                    hidden_sums,
+                    jnp.full((PAIR,), jnp.sum(lengths).astype(F32)),
+                ]
+            ),
+        )
+        (block_output,) = start_all((block_output,), [small])
+        sums = [input_sum, small, output_sum, reduce_sum, expand_sum]
+        token = block_output
+        while any(s.busy() for s in sums):
+            for s in sums:
+                if s.busy():
+                    (token,) = await_all((token,), [s])
+                    (token,) = start_all((token,), [s])
+        block_output = token
+
+        total = small.held
+        rows = total[: 6 * width].reshape(6, width)
+        rest = total[6 * width :]
+        factor = lax.rsqrt(rest[2 * local_width + hidden])
+        rows = rows * factor
+        input_total = input_sum.held.astype(F32) * factor
         return (
             block_output,
             input_gradient,
-            late[0] * factor,
-            late[1] * factor,
+            rows[4],
+            rows[5],
             jnp.stack(
                 [input_total[:, t * local_width : (t + 1) * local_width] for t in range(3)]
             ),
-            qv_total * factor,
-            output_grad.astype(F32) * factor,
-            early[2] * factor,
-            early[0] * factor,
-            early[1] * factor,
-            expand_grad.astype(F32) * factor,
-            local[:hidden] * factor,
-            reduce_grad.astype(F32) * factor,
-            early[3] * factor,
-        )
-
+            rest[: 2 * local_width].reshape(2, local_width) * factor,
+            output_sum.held.astype(F32) * factor,
+            rows[2],
+            rows[0],
+            rows[1],
+            expand_sum.held.astype(F32) * factor,
+            rest[2 * local_width : 2 * local_width + hidden] * factor,
+            reduce_sum.held.astype(F32) * factor,
+            rows[3],
+        )
     return per_device
 
 

time: 379 us -> 323 us (0.85)
  other arithmetic: 49.4 us -> 35.3 us
  Pallas kernels: 48.2 us -> 34.9 us
  waiting for transfers between devices: 169 us -> 156 us
  matrix products: 27.6 us -> 19.2 us
  local copies, waits for them, and re-layouts: 23 us -> 18 us
    ppermute x64 -> x55, waiting for transfers between devices: 169 us -> 156 us  [swap(): return lax.ppermute(array, axis, [(i, i ^ bit) for i in range(size)])]
    pallas_call x4, Pallas kernels: 33.8 us -> 27.2 us  [the longest x2 16.4 us: attend_back(): pl.pallas_call(functools.partial(attend_back_kernel, parts, first, last),...]
    pallas_call x2, Pallas kernels: 14.4 us -> 7.78 us  [mlp_both(): pl.pallas_call(mlp_kernel, grid=(count // tile,), in_specs=[pl.BlockSpec(...]
    concatenate x4 -> x5, other arithmetic: 7.88 us -> 1.32 us  [gather_near(): return jnp.concatenate([blocks[j] for j in range(count // 2)])]
    concatenate x3 -> x2, other arithmetic: 4.01 us -> 0.02 us  [the longest x1 0.01 us: per_device(): jnp.concatenate([input_bias[0], jnp.zeros_like(input_bias[0]), input_bias...]
    mul x8 -> x7, other arithmetic: 9.72 us -> 12.2 us  [the longest x1 4.4 us: per_device(): expand_sum.held.astype(F32) * factor]
    ppermute x64 -> x55, starting transfers between devices: 52.4 us -> 50.5 us  [swap(): return lax.ppermute(array, axis, [(i, i ^ bit) for i in range(size)])]
    dot_general x4 -> x6, matrix products: 8.18 us -> 6.35 us  [dot_nn(): lax.dot_general(a, b, (((1,), (0,)), ((), ())), preferred_element_type=F32)]
  transfers between devices with their start and end apart: 64 -> 55, of which waited for: 26 -> 31; matrix products, arithmetic and copies ran while one was open for 23% -> 17% of each run, Pallas kernels for 11% -> 10%
where the time goes in v3:
time: 323 us; the launch traced here: 318 us
  waiting for transfers between devices  156 us (48%)
  starting transfers between devices  50.5 us (16%)
  other arithmetic  35.3 us (11%)
  Pallas kernels  34.9 us (11%)
  matrix products  19.2 us (6%)
  local copies, waits for them, and re-layouts  18 us (6%)
  between operations  4.55 us (1%)
    ppermute x55, waiting for transfers between devices, swap(): return lax.ppermute(array, axis, [(i, i ^ bit) for i in range(size)])  156 us
    ppermute x55, starting transfers between devices, swap(): return lax.ppermute(array, axis, [(i, i ^ bit) for i in range(size)])  50.5 us
    pallas_call x2, Pallas kernels, attend_back(): pl.pallas_call(functools.partial(attend_back_kernel, parts, first, last),...  16.4 us
    unnamed x134, local copies, waits for them, and re-layouts  10.9 us
    pallas_call x2, Pallas kernels, attend_forward(): pl.pallas_call(functools.partial(attend_kernel, len(halves)), grid=(pairs...  10.8 us
    dot_general x16, matrix products, dot_tn(): lax.dot_general(a, b, (((0,), (0,)), ((), ())), preferred_element_type=F32)  9.87 us
    pallas_call x2, Pallas kernels, mlp_both(): pl.pallas_call(mlp_kernel, grid=(count // tile,), in_specs=[pl.BlockSpec(...  7.78 us
  transfers between devices with their start and end apart: 55, of which 31 were waited for; matrix products, arithmetic and copies ran while one was open for 17% of the time, Pallas kernels for 10%

profile of v3, /device:TPU:0, one launch (start us, length us, event | category | flops | bytes accessed | tf_op | source)
XLA Modules:
  0.0 318.3 jit_solution(11363489266721076902)
XLA Ops:
  2.9 1.9 multiply_sine_fusion
  8.3 2.6 collective-permute-start
  13.6 9.8 %collective-permute-done = bf16[256,1024]{1,0:T(8,128)(2,1)} collective-permute-done((bf16[256,1024]{1,0:T(8,128)(2,1)S(1)}, bf16[256,1024]{1,0:T(8,128)(2,1)}, u32[]{:S(2)}, u32[]{:S(2)}) %collective-permute-start) | collective-permute-done | bytes 524320 | tf_op jit(solution)/shard_map/ppermute | solution.py:299
  23.7 1.8 collective-permute-start.7
  28.7 5.5 %attend_forward.2 = (bf16[512,256]{1,0:T(8,128)(2,1)S(1)}, f32[2,8,512]{2,1,0:T(8,128)S(1)}) custom-call(bf16[512,768]{1,0:T(8,128)(2,1)S(1)} %add_convert_fusion.9.q_ref.refs_1_.refs_3_, bf16[512,128]{1,0:T(8,128)(2,1)S(1)} %fusion.27.pick_ref, bf16[512,768]{1,0:T(8,128)(2,1)S(1)} %add_convert_fusion.10.refs_0_.refs_2_.q_ref, ...), custom_call_target="tpu_custom_call" | custom-call | flops 1024 | bytes 1024 | tf_op jit(solution)/shard_map/attend_forward/pallas_call | solution.py:73
  35.6 2.5 collective-permute-done.7
  38.3 1.8 collective-permute-start.5
  40.2 5.3 %attend_forward.3 = (bf16[512,256]{1,0:T(8,128)(2,1)S(1)}, f32[2,8,512]{2,1,0:T(8,128)S(1)}) custom-call(bf16[512,768]{1,0:T(8,128)(2,1)S(1)} %add_convert_fusion.10.refs_0_.refs_2_.q_ref, bf16[512,128]{1,0:T(8,128)(2,1)S(1)} %fusion.26.pick_ref, bf16[512,768]{1,0:T(8,128)(2,1)S(1)} %add_convert_fusion.10.refs_0_.refs_2_.q_ref, ...), custom_call_target="tpu_custom_call" | custom-call | flops 1024 | bytes 1024 | tf_op jit(solution)/shard_map/attend_forward/pallas_call | solution.py:73
  47.8 5.0 %collective-permute-done.5 = bf16[256,1024]{1,0:T(8,128)(2,1)S(1)} collective-permute-done((bf16[256,1024]{1,0:T(8,128)(2,1)S(1)}, bf16[256,1024]{1,0:T(8,128)(2,1)S(1)}, u32[]{:S(2)}, u32[]{:S(2)}) %collective-permute-start.5) | collective-permute-done | bytes 524320 | tf_op jit(solution)/shard_map/ppermute | solution.py:299
  54.7 1.9 collective-permute-done.10
  57.4 3.7 %mlp_both.2 = (bf16[512,1024]{1,0:T(8,128)(2,1)S(1)}, bf16[512,1024]{1,0:T(8,128)(2,1)S(1)}, bf16[512,1024]{1,0:T(8,128)(2,1)S(1)}) custom-call(bf16[512,1024]{1,0:T(8,128)(2,1)S(1)} %pad_maximum_fusion.3.x_ref, bf16[512,1024]{1,0:T(8,128)(2,1)S(1)} %pad_maximum_fusion.5.grad_ref, bf16[1024,1024]{1,0:T(8,128)(2,1)S(1)} %copy-done.4, f32[1,1024]{1,0:T(1,128)S(1)} %bitcast.62, ...), custom_call_target="tpu_custom_call" | custom-call | flops 1024 | bytes 1024 | tf_op jit(solution)/shard_map/mlp_both/pallas_call | solution.py:224
  61.3 1.7 collective-permute-start.9
  63.1 2.2 convolution_convert_fusion.3
  66.5 9.2 %collective-permute-done.9 = bf16[256,1024]{1,0:T(8,128)(2,1)} collective-permute-done((bf16[256,1024]{1,0:T(8,128)(2,1)S(1)}, bf16[256,1024]{1,0:T(8,128)(2,1)}, u32[]{:S(2)}, u32[]{:S(2)}) %collective-permute-start.9) | collective-permute-done | bytes 524320 | tf_op jit(solution)/shard_map/ppermute | solution.py:299
  84.7 4.1 %mlp_both.3 = (bf16[512,1024]{1,0:T(8,128)(2,1)S(1)}, bf16[512,1024]{1,0:T(8,128)(2,1)S(1)}, bf16[512,1024]{1,0:T(8,128)(2,1)S(1)}) custom-call(bf16[512,1024]{1,0:T(8,128)(2,1)S(1)} %constant_dynamic-update-slice_fusion.2.x_ref, bf16[512,1024]{1,0:T(8,128)(2,1)S(1)} %copy-done.1, bf16[1024,1024]{1,0:T(8,128)(2,1)S(1)} %copy-done.5, f32[1,1024]{1,0:T(1,128)S(1)} %bitcast.63, ...), custom_call_target="tpu_custom_call" | custom-call | flops 1024 | bytes 1024 | tf_op jit(solution)/shard_map/mlp_both/pallas_call | solution.py:224
  94.6 1.8 collective-permute-start.14
  99.5 9.5 %collective-permute-done.14 = bf16[256,1024]{1,0:T(8,128)(2,1)S(1)} collective-permute-done((bf16[256,1024]{1,0:T(8,128)(2,1)S(1)}, bf16[256,1024]{1,0:T(8,128)(2,1)S(1)}, u32[]{:S(2)}, u32[]{:S(2)}) %collective-permute-start.14) | collective-permute-done | bytes 524320 | tf_op jit(solution)/shard_map/ppermute | solution.py:299
  111.5 1.8 collective-permute-start.23
  119.6 7.9 %attend_back.2 = (bf16[512,256]{1,0:T(8,128)(2,1)S(1)}, f32[512,256]{1,0:T(8,128)S(1)}, f32[512,256]{1,0:T(8,128)S(1)}, f32[512,256]{1,0:T(8,128)S(1)}, f32[512,256]{1,0:T(8,128)S(1)}) custom-call(bf16[512,768]{1,0:T(8,128)(2,1)S(1)} %add_convert_fusion.10.refs_0_.refs_2_.q_ref, bf16[512,128]{1,0:T(8,128)(2,1)S(1)} %copy-done.13, ...), custom_call_target="tpu_custom_call" | custom-call | flops 1024 | bytes 1024 | tf_op jit(solution)/shard_map/attend_back/pallas_call | solution.py:184
  128.2 3.2 %collective-permute-done.15 = bf16[256,1024]{1,0:T(8,128)(2,1)S(1)} collective-permute-done((bf16[256,1024]{1,0:T(8,128)(2,1)S(1)}, bf16[256,1024]{1,0:T(8,128)(2,1)S(1)}, u32[]{:S(2)}, u32[]{:S(2)}) %collective-permute-start.15) | collective-permute-done | bytes 524320 | tf_op jit(solution)/shard_map/ppermute | solution.py:299
  131.4 7.1 %collective-permute-done.19 = bf16[512,1024]{1,0:T(8,128)(2,1)S(1)} collective-permute-done((bf16[512,1024]{1,0:T(8,128)(2,1)S(1)}, bf16[512,1024]{1,0:T(8,128)(2,1)S(1)}, u32[]{:S(2)}, u32[]{:S(2)}) %collective-permute-start.19) | collective-permute-done | bytes 1048608 | tf_op jit(solution)/shard_map/ppermute | solution.py:299
  142.6 8.4 %attend_back.3 = (bf16[512,256]{1,0:T(8,128)(2,1)S(1)}, bf16[512,256]{1,0:T(8,128)(2,1)S(1)}, bf16[512,256]{1,0:T(8,128)(2,1)S(1)}, bf16[512,256]{1,0:T(8,128)(2,1)S(1)}, bf16[512,256]{1,0:T(8,128)(2,1)S(1)}) custom-call(bf16[512,768]{1,0:T(8,128)(2,1)S(1)} %add_convert_fusion.9.q_ref.refs_1_.refs_3_, bf16[512,128]{1,0:T(8,128)(2,1)S(1)} %fusion.27.pick_ref, ...), custom_call_target="tpu_custom_call" | custom-call | flops 1024 | bytes 1024 | tf_op jit(solution)/shard_map/attend_back/pallas_call | solution.py:184
  160.7 10.7 %collective-permute-done.28 = bf16[256,1024]{1,0:T(8,128)(2,1)S(1)} collective-permute-done((bf16[256,1024]{1,0:T(8,128)(2,1)S(1)}, bf16[256,1024]{1,0:T(8,128)(2,1)S(1)}, u32[]{:S(2)}, u32[]{:S(2)}) %collective-permute-start.28) | collective-permute-done | bytes 524320 | tf_op jit(solution)/shard_map/ppermute | solution.py:299
  171.4 2.8 collective-permute-done.29
  176.3 2.6 collective-permute-start.36
  182.5 3.1 collective-permute-done.32
  186.4 7.6 %collective-permute-done.33 = bf16[512,768]{1,0:T(8,128)(2,1)S(1)} collective-permute-done((bf16[512,768]{1,0:T(8,128)(2,1)S(1)}, bf16[512,768]{1,0:T(8,128)(2,1)S(1)}, u32[]{:S(2)}, u32[]{:S(2)}) %collective-permute-start.33) | collective-permute-done | bytes 786464 | tf_op jit(solution)/shard_map/ppermute | solution.py:299
  196.7 4.8 %collective-permute-done.37 = bf16[128,1024]{1,0:T(8,128)(2,1)S(1)} collective-permute-done((bf16[128,1024]{1,0:T(8,128)(2,1)S(1)}, bf16[128,1024]{1,0:T(8,128)(2,1)S(1)}, u32[]{:S(2)}, u32[]{:S(2)}) %collective-permute-start.37) | collective-permute-done | bytes 262176 | tf_op jit(solution)/shard_map/ppermute | solution.py:299
  201.6 3.1 collective-permute-start.40
  204.7 2.9 collective-permute-start.42
  207.6 4.1 %collective-permute-done.38 = bf16[256,768]{1,0:T(8,128)(2,1)S(1)} collective-permute-done((bf16[256,768]{1,0:T(8,128)(2,1)S(1)}, bf16[256,768]{1,0:T(8,128)(2,1)S(1)}, u32[]{:S(2)}, u32[]{:S(2)}) %collective-permute-start.38) | collective-permute-done | bytes 393248 | tf_op jit(solution)/shard_map/ppermute | solution.py:299
  212.3 7.8 %collective-permute-done.40 = bf16[32,1024]{1,0:T(8,128)(2,1)S(1)} collective-permute-done((bf16[32,1024]{1,0:T(8,128)(2,1)S(1)}, bf16[32,1024]{1,0:T(8,128)(2,1)S(1)}, u32[]{:S(2)}, u32[]{:S(2)}) %collective-permute-start.40) | collective-permute-done | bytes 65568 | tf_op jit(solution)/shard_map/ppermute | solution.py:299
  220.1 5.6 %collective-permute-done.41 = bf16[128,1024]{1,0:T(8,128)(2,1)S(1)} collective-permute-done((bf16[128,1024]{1,0:T(8,128)(2,1)S(1)}, bf16[128,1024]{1,0:T(8,128)(2,1)S(1)}, u32[]{:S(2)}, u32[]{:S(2)}) %collective-permute-start.41) | collective-permute-done | bytes 262176 | tf_op jit(solution)/shard_map/ppermute | solution.py:299
  225.9 4.9 %collective-permute-done.42 = bf16[128,1024]{1,0:T(8,128)(2,1)S(1)} collective-permute-done((bf16[128,1024]{1,0:T(8,128)(2,1)S(1)}, bf16[128,1024]{1,0:T(8,128)(2,1)S(1)}, u32[]{:S(2)}, u32[]{:S(2)}) %collective-permute-start.42) | collective-permute-done | bytes 262176 | tf_op jit(solution)/shard_map/ppermute | solution.py:299
  231.0 2.7 collective-permute-start.46
  234.4 2.6 collective-permute-start.45
  237.0 5.1 %collective-permute-done.43 = bf16[128,768]{1,0:T(8,128)(2,1)S(1)} collective-permute-done((bf16[128,768]{1,0:T(8,128)(2,1)S(1)}, bf16[128,768]{1,0:T(8,128)(2,1)S(1)}, u32[]{:S(2)}, u32[]{:S(2)}) %collective-permute-start.43) | collective-permute-done | bytes 196640 | tf_op jit(solution)/shard_map/ppermute | solution.py:299
  242.2 5.7 %collective-permute-done.44 = f32[7808]{0:T(1024)S(1)} collective-permute-done((f32[7808]{0:T(1024)S(1)}, f32[7808]{0:T(1024)S(1)}, u32[]{:S(2)}, u32[]{:S(2)}) %collective-permute-start.44) | collective-permute-done | bytes 31264 | tf_op jit(solution)/shard_map/ppermute | solution.py:299
  248.6 2.7 collective-permute-done.46
  255.7 1.9 collective-permute-start.48
  258.2 20.0 %collective-permute-done.48 = bf16[128,768]{1,0:T(8,128)(2,1)S(1)} collective-permute-done((bf16[128,768]{1,0:T(8,128)(2,1)S(1)}, bf16[128,768]{1,0:T(8,128)(2,1)S(1)}, u32[]{:S(2)}, u32[]{:S(2)}) %collective-permute-start.48) | collective-permute-done | bytes 196640 | tf_op jit(solution)/shard_map/ppermute | solution.py:299
  278.3 3.0 collective-permute-start.52
  283.4 8.4 %collective-permute-done.49 = bf16[64,1024]{1,0:T(8,128)(2,1)} collective-permute-done((bf16[64,1024]{1,0:T(8,128)(2,1)S(1)}, bf16[64,1024]{1,0:T(8,128)(2,1)}, u32[]{:S(2)}, u32[]{:S(2)}) %collective-permute-start.49) | collective-permute-done | bytes 131104 | tf_op jit(solution)/shard_map/ppermute | solution.py:299
  296.6 5.5 %collective-permute-done.53 = bf16[128,1024]{1,0:T(8,128)(2,1)S(1)} collective-permute-done((bf16[128,1024]{1,0:T(8,128)(2,1)S(1)}, bf16[128,1024]{1,0:T(8,128)(2,1)S(1)}, u32[]{:S(2)}, u32[]{:S(2)}) %collective-permute-start.53) | collective-permute-done | bytes 262176 | tf_op jit(solution)/shard_map/ppermute | solution.py:299
  303.2 4.4 %convert_multiply_fusion = f32[1024,1024]{1,0:T(8,128)} fusion(bf16[512,1024]{1,0:T(8,128)(2,1)S(1)} %maximum_select_fusion.3, bf16[512,1024]{1,0:T(8,128)(2,1)} %collective-permute-done.50, f32[]{:T(128)} %bitcast.14, pred[]{:T(512)S(6)} %ne.7), kind=kLoop, calls=%fused_computation | loop fusion | flops 11534336 | bytes 6291461 | tf_op jit(solution)/shard_map/mul | solution.py:637
  307.6 4.4 %convert_multiply_fusion.1 = f32[1024,1024]{1,0:T(8,128)} fusion(bf16[512,1024]{1,0:T(8,128)(2,1)S(1)} %maximum_select_fusion.4, bf16[512,1024]{1,0:T(8,128)(2,1)} %collective-permute-done.51, f32[]{:T(128)} %bitcast.14, pred[]{:T(512)S(6)} %ne.6), kind=kLoop, calls=%fused_computation.1 | loop fusion | flops 11534336 | bytes 6291461 | tf_op jit(solution)/shard_map/mul | solution.py:635
  312.0 3.6 %collective-permute-done.54 = bf16[512,768]{1,0:T(8,128)(2,1)S(1)} collective-permute-done((bf16[512,768]{1,0:T(8,128)(2,1)S(1)}, bf16[512,768]{1,0:T(8,128)(2,1)S(1)}, u32[]{:S(2)}, u32[]{:S(2)}) %collective-permute-start.54) | collective-permute-done | bytes 786464 | tf_op jit(solution)/shard_map/ppermute | solution.py:299
  316.3 1.9 pad_maximum_fusion
  (342 shorter events, 83.2 us)
Async XLA Ops:
  7.7 4.9 %collective-permute-start.1 = (bf16[256,1024]{1,0:T(8,128)(2,1)S(1)}, bf16[256,1024]{1,0:T(8,128)(2,1)S(1)}, u32[]{:S(2)}, u32[]{:S(2)}) collective-permute-start(bf16[256,1024]{1,0:T(8,128)(2,1)S(1)} %add_convert_fusion.19), channel_id=1, source_target_pairs={{0,1},{1,0},{2,3},{3,2},{4,5},{5,4},{6,7},{7,6},{8,9},{9,8},{10,11... | collective-permute-start | bytes 1572872 | tf_op jit(solution)/shard_map/ppermute | solution.py:299
  8.3 15.2 %collective-permute-start = (bf16[256,1024]{1,0:T(8,128)(2,1)S(1)}, bf16[256,1024]{1,0:T(8,128)(2,1)}, u32[]{:S(2)}, u32[]{:S(2)}) collective-permute-start(bf16[256,1024]{1,0:T(8,128)(2,1)S(1)} %add_convert_fusion.19), channel_id=1, source_target_pairs={{0,2},{1,3},{2,0},{3,1},{4,6},{5,7},{6,4},{7,5},{8,10},{9,11},{10,... | collective-permute-start | bytes 1572872 | tf_op jit(solution)/shard_map/ppermute | solution.py:299
  23.7 14.4 %collective-permute-start.7 = (bf16[256,1024]{1,0:T(8,128)(2,1)S(1)}, bf16[256,1024]{1,0:T(8,128)(2,1)S(1)}, u32[]{:S(2)}, u32[]{:S(2)}) collective-permute-start(bf16[256,1024]{1,0:T(8,128)(2,1)S(1)} %get-tuple-element.169), channel_id=1, source_target_pairs={{0,2},{1,3},{2,0},{3,1},{4,6},{5,7},{6,4},{7,5},{8,10},{9,11},{10,... | collective-permute-start | bytes 1572872 | tf_op jit(solution)/shard_map/ppermute | solution.py:299
  35.2 11.1 %collective-permute-start.6 = (bf16[256,1024]{1,0:T(8,128)(2,1)S(1)}, bf16[256,1024]{1,0:T(8,128)(2,1)S(1)}, u32[]{:S(2)}, u32[]{:S(2)}) collective-permute-start(bf16[256,1024]{1,0:T(8,128)(2,1)S(1)} %get-tuple-element.169), channel_id=1, source_target_pairs={{0,1},{1,0},{2,3},{3,2},{4,5},{5,4},{6,7},{7,6},{8,9},{9,8},{10,11... | collective-permute-start | bytes 1572872 | tf_op jit(solution)/shard_map/ppermute | solution.py:299
  38.1 8.6 %collective-permute-start.8 = (bf16[256,1024]{1,0:T(8,128)(2,1)S(1)}, bf16[256,1024]{1,0:T(8,128)(2,1)S(1)}, u32[]{:S(2)}, u32[]{:S(2)}) collective-permute-start(bf16[256,1024]{1,0:T(8,128)(2,1)S(1)} %collective-permute-done.7), channel_id=1, source_target_pairs={{0,1},{1,0},{2,3},{3,2},{4,5},{5,4},{6,7},{7,6},{8,9},{9,8},{10,11... | collective-permute-start | bytes 1572872 | tf_op jit(solution)/shard_map/ppermute | solution.py:299
  38.3 14.4 %collective-permute-start.5 = (bf16[256,1024]{1,0:T(8,128)(2,1)S(1)}, bf16[256,1024]{1,0:T(8,128)(2,1)S(1)}, u32[]{:S(2)}, u32[]{:S(2)}) collective-permute-start(bf16[256,1024]{1,0:T(8,128)(2,1)S(1)} %add_convert_fusion.18), channel_id=1, source_target_pairs={{0,2},{1,3},{2,0},{3,1},{4,6},{5,7},{6,4},{7,5},{8,10},{9,11},{10,... | collective-permute-start | bytes 1572872 | tf_op jit(solution)/shard_map/ppermute | solution.py:299
  46.0 6.7 %collective-permute-start.4 = (bf16[256,1024]{1,0:T(8,128)(2,1)S(1)}, bf16[256,1024]{1,0:T(8,128)(2,1)S(1)}, u32[]{:S(2)}, u32[]{:S(2)}) collective-permute-start(bf16[256,1024]{1,0:T(8,128)(2,1)S(1)} %slice.157), channel_id=1, source_target_pairs={{0,1},{1,0},{2,3},{3,2},{4,5},{5,4},{6,7},{7,6},{8,9},{9,8},{10,11... | collective-permute-start | bytes 1572872 | tf_op jit(solution)/shard_map/ppermute | solution.py:299
  61.1 4.2 %collective-permute-start.11 = (bf16[256,1024]{1,0:T(8,128)(2,1)S(1)}, bf16[256,1024]{1,0:T(8,128)(2,1)S(1)}, u32[]{:S(2)}, u32[]{:S(2)}) collective-permute-start(bf16[256,1024]{1,0:T(8,128)(2,1)S(1)} %slice.128), channel_id=1, source_target_pairs={{0,1},{1,0},{2,3},{3,2},{4,5},{5,4},{6,7},{7,6},{8,9},{9,8},{10,11... | collective-permute-start | bytes 1572872 | tf_op jit(solution)/shard_map/ppermute | solution.py:299
  61.3 14.3 %collective-permute-start.9 = (bf16[256,1024]{1,0:T(8,128)(2,1)S(1)}, bf16[256,1024]{1,0:T(8,128)(2,1)}, u32[]{:S(2)}, u32[]{:S(2)}) collective-permute-start(bf16[256,1024]{1,0:T(8,128)(2,1)S(1)} %add_convert_fusion.17), channel_id=1, source_target_pairs={{0,2},{1,3},{2,0},{3,1},{4,6},{5,7},{6,4},{7,5},{8,10},{9,11},{10,... | collective-permute-start | bytes 1572872 | tf_op jit(solution)/shard_map/ppermute | solution.py:299
  75.6 4.8 %collective-permute-start.12 = (bf16[256,1024]{1,0:T(8,128)(2,1)}, bf16[256,1024]{1,0:T(8,128)(2,1)}, u32[]{:S(2)}, u32[]{:S(2)}) collective-permute-start(bf16[256,1024]{1,0:T(8,128)(2,1)} %collective-permute-done.9), channel_id=1, source_target_pairs={{0,1},{1,0},{2,3},{3,2},{4,5},{5,4},{6,7},{7,6},{8,9},{9,8},{10,11... | collective-permute-start | bytes 1572872 | tf_op jit(solution)/shard_map/ppermute | solution.py:299
  78.8 13.7 %collective-permute-start.21 = (bf16[256,1024]{1,0:T(8,128)(2,1)S(1)}, bf16[256,1024]{1,0:T(8,128)(2,1)S(1)}, u32[]{:S(2)}, u32[]{:S(2)}) collective-permute-start(bf16[256,1024]{1,0:T(8,128)(2,1)S(1)} %slice.134), channel_id=1, source_target_pairs={{0,1},{1,0},{2,3},{3,2},{4,5},{5,4},{6,7},{7,6},{8,9},{9,8},{10,11... | collective-permute-start | bytes 1572872 | tf_op jit(solution)/shard_map/ppermute | solution.py:299
  90.9 3.5 %collective-permute-start.13 = (bf16[256,1024]{1,0:T(8,128)(2,1)S(1)}, bf16[256,1024]{1,0:T(8,128)(2,1)S(1)}, u32[]{:S(2)}, u32[]{:S(2)}) collective-permute-start(bf16[256,1024]{1,0:T(8,128)(2,1)S(1)} %slice.130), channel_id=1, source_target_pairs={{0,1},{1,0},{2,3},{3,2},{4,5},{5,4},{6,7},{7,6},{8,9},{9,8},{10,11... | collective-permute-start | bytes 1572872 | tf_op jit(solution)/shard_map/ppermute | solution.py:299
  94.6 14.4 %collective-permute-start.14 = (bf16[256,1024]{1,0:T(8,128)(2,1)S(1)}, bf16[256,1024]{1,0:T(8,128)(2,1)S(1)}, u32[]{:S(2)}, u32[]{:S(2)}) collective-permute-start(bf16[256,1024]{1,0:T(8,128)(2,1)S(1)} %add_convert_fusion.16), channel_id=1, source_target_pairs={{0,2},{1,3},{2,0},{3,1},{4,6},{5,7},{6,4},{7,5},{8,10},{9,11},{10,... | collective-permute-start | bytes 1572872 | tf_op jit(solution)/shard_map/ppermute | solution.py:299
  110.5 6.8 %collective-permute-start.17 = (bf16[256,1024]{1,0:T(8,128)(2,1)S(1)}, bf16[256,1024]{1,0:T(8,128)(2,1)S(1)}, u32[]{:S(2)}, u32[]{:S(2)}) collective-permute-start(bf16[256,1024]{1,0:T(8,128)(2,1)S(1)} %slice.132), channel_id=1, source_target_pairs={{0,1},{1,0},{2,3},{3,2},{4,5},{5,4},{6,7},{7,6},{8,9},{9,8},{10,11... | collective-permute-start | bytes 1572872 | tf_op jit(solution)/shard_map/ppermute | solution.py:299
  111.1 6.1 %collective-permute-start.16 = (bf16[256,1024]{1,0:T(8,128)(2,1)S(1)}, bf16[256,1024]{1,0:T(8,128)(2,1)S(1)}, u32[]{:S(2)}, u32[]{:S(2)}) collective-permute-start(bf16[256,1024]{1,0:T(8,128)(2,1)S(1)} %get-tuple-element.321), channel_id=1, source_target_pairs={{0,1},{1,0},{2,3},{3,2},{4,5},{5,4},{6,7},{7,6},{8,9},{9,8},{10,11... | collective-permute-start | bytes 1572872 | tf_op jit(solution)/shard_map/ppermute | solution.py:299
  111.5 5.1 %collective-permute-start.23 = (f32[4,1024]{1,0:T(4,128)S(1)}, f32[4,1024]{1,0:T(4,128)S(1)}, u32[]{:S(2)}, u32[]{:S(2)}) collective-permute-start(f32[4,1024]{1,0:T(4,128)S(1)} %fusion.58), channel_id=1, source_target_pairs={{0,2},{1,3},{2,0},{3,1},{4,6},{5,7},{6,4},{7,5},{8,10},{9,11},{10,... | collective-permute-start | bytes 49160 | tf_op jit(solution)/shard_map/ppermute | solution.py:299
  113.5 25.0 %collective-permute-start.19 = (bf16[512,1024]{1,0:T(8,128)(2,1)S(1)}, bf16[512,1024]{1,0:T(8,128)(2,1)S(1)}, u32[]{:S(2)}, u32[]{:S(2)}) collective-permute-start(bf16[512,1024]{1,0:T(8,128)(2,1)S(1)} %add_convert_fusion.4), channel_id=1, source_target_pairs={{0,8},{4,12},{8,0},{12,4},{16,24},{20,28},{24,16},{28,20},{1,9},{5... | collective-permute-start | bytes 3145736 | tf_op jit(solution)/shard_map/ppermute | solution.py:299
  115.1 24.7 %collective-permute-start.18 = (bf16[512,1024]{1,0:T(8,128)(2,1)S(1)}, bf16[512,1024]{1,0:T(8,128)(2,1)S(1)}, u32[]{:S(2)}, u32[]{:S(2)}) collective-permute-start(bf16[512,1024]{1,0:T(8,128)(2,1)S(1)} %add_convert_fusion.5), channel_id=1, source_target_pairs={{0,4},{4,0},{8,12},{12,8},{16,20},{20,16},{24,28},{28,24},{1,5},{5... | collective-permute-start | bytes 3145736 | tf_op jit(solution)/shard_map/ppermute | solution.py:299
  116.6 14.8 %collective-permute-start.15 = (bf16[256,1024]{1,0:T(8,128)(2,1)S(1)}, bf16[256,1024]{1,0:T(8,128)(2,1)S(1)}, u32[]{:S(2)}, u32[]{:S(2)}) collective-permute-start(bf16[256,1024]{1,0:T(8,128)(2,1)S(1)} %get-tuple-element.321), channel_id=1, source_target_pairs={{0,2},{1,3},{2,0},{3,1},{4,6},{5,7},{6,4},{7,5},{8,10},{9,11},{10,... | collective-permute-start | bytes 1572872 | tf_op jit(solution)/shard_map/ppermute | solution.py:299
  117.5 62.1 %collective-permute-start.30 = (bf16[256,1024]{1,0:T(8,128)(2,1)S(1)}, bf16[256,1024]{1,0:T(8,128)(2,1)S(1)}, u32[]{:S(2)}, u32[]{:S(2)}) collective-permute-start(bf16[256,1024]{1,0:T(8,128)(2,1)S(1)} %add_convert_fusion.15), channel_id=1, source_target_pairs={{0,2},{1,3},{2,0},{3,1},{4,6},{5,7},{6,4},{7,5},{8,10},{9,11},{10,... | collective-permute-start | bytes 1572872 | tf_op jit(solution)/shard_map/ppermute | solution.py:299
  154.1 5.0 %collective-permute-start.24 = (bf16[256,1024]{1,0:T(8,128)(2,1)S(1)}, bf16[256,1024]{1,0:T(8,128)(2,1)S(1)}, u32[]{:S(2)}, u32[]{:S(2)}) collective-permute-start(bf16[256,1024]{1,0:T(8,128)(2,1)S(1)} %slice.159), channel_id=1, source_target_pairs={{0,1},{1,0},{2,3},{3,2},{4,5},{5,4},{6,7},{7,6},{8,9},{9,8},{10,11... | collective-permute-start | bytes 1572872 | tf_op jit(solution)/shard_map/ppermute | solution.py:299
  154.3 24.5 %collective-permute-start.26 = (bf16[128,1024]{1,0:T(8,128)(2,1)S(1)}, bf16[128,1024]{1,0:T(8,128)(2,1)S(1)}, u32[]{:S(2)}, u32[]{:S(2)}) collective-permute-start(bf16[128,1024]{1,0:T(8,128)(2,1)S(1)} %fusion), channel_id=1, source_target_pairs={{0,4},{4,0},{8,12},{12,8},{16,20},{20,16},{24,28},{28,24},{1,5},{5... | collective-permute-start | bytes 786440 | tf_op jit(solution)/shard_map/ppermute | solution.py:299
  157.1 14.2 %collective-permute-start.28 = (bf16[256,1024]{1,0:T(8,128)(2,1)S(1)}, bf16[256,1024]{1,0:T(8,128)(2,1)S(1)}, u32[]{:S(2)}, u32[]{:S(2)}) collective-permute-start(bf16[256,1024]{1,0:T(8,128)(2,1)S(1)} %constant_dynamic-slice_fusion.7), channel_id=1, source_target_pairs={{0,8},{4,12},{8,0},{12,4},{16,24},{20,28},{24,16},{28,20},{1,9},{5... | collective-permute-start | bytes 1572872 | tf_op jit(solution)/shard_map/ppermute | solution.py:299
  159.2 15.0 %collective-permute-start.29 = (bf16[256,1024]{1,0:T(8,128)(2,1)S(1)}, bf16[256,1024]{1,0:T(8,128)(2,1)S(1)}, u32[]{:S(2)}, u32[]{:S(2)}) collective-permute-start(bf16[256,1024]{1,0:T(8,128)(2,1)S(1)} %constant_dynamic-slice_fusion.6), channel_id=1, source_target_pairs={{0,4},{4,0},{8,12},{12,8},{16,20},{20,16},{24,28},{28,24},{1,5},{5... | collective-permute-start | bytes 1572872 | tf_op jit(solution)/shard_map/ppermute | solution.py:299
  160.0 19.2 %collective-permute-start.25 = (bf16[256,1024]{1,0:T(8,128)(2,1)S(1)}, bf16[256,1024]{1,0:T(8,128)(2,1)S(1)}, u32[]{:S(2)}, u32[]{:S(2)}) collective-permute-start(bf16[256,1024]{1,0:T(8,128)(2,1)S(1)} %add_convert_fusion.14), channel_id=1, source_target_pairs={{0,2},{1,3},{2,0},{3,1},{4,6},{5,7},{6,4},{7,5},{8,10},{9,11},{10,... | collective-permute-start | bytes 1572872 | tf_op jit(solution)/shard_map/ppermute | solution.py:299
  174.7 19.4 %collective-permute-start.33 = (bf16[512,768]{1,0:T(8,128)(2,1)S(1)}, bf16[512,768]{1,0:T(8,128)(2,1)S(1)}, u32[]{:S(2)}, u32[]{:S(2)}) collective-permute-start(bf16[512,768]{1,0:T(8,128)(2,1)S(1)} %add_convert_fusion.8), channel_id=1, source_target_pairs={{0,4},{4,0},{8,12},{12,8},{16,20},{20,16},{24,28},{28,24},{1,5},{5... | collective-permute-start | bytes 2359304 | tf_op jit(solution)/shard_map/ppermute | solution.py:299
  176.3 19.6 %collective-permute-start.36 = (bf16[128,1024]{1,0:T(8,128)(2,1)S(1)}, bf16[128,1024]{1,0:T(8,128)(2,1)S(1)}, u32[]{:S(2)}, u32[]{:S(2)}) collective-permute-start(bf16[128,1024]{1,0:T(8,128)(2,1)S(1)} %constant_dynamic-slice_fusion.5), channel_id=1, source_target_pairs={{0,16},{4,20},{8,24},{12,28},{16,0},{20,4},{24,8},{28,12},{1,17},{... | collective-permute-start | bytes 786440 | tf_op jit(solution)/shard_map/ppermute | solution.py:299
  178.8 22.6 %collective-permute-start.37 = (bf16[128,1024]{1,0:T(8,128)(2,1)S(1)}, bf16[128,1024]{1,0:T(8,128)(2,1)S(1)}, u32[]{:S(2)}, u32[]{:S(2)}) collective-permute-start(bf16[128,1024]{1,0:T(8,128)(2,1)S(1)} %constant_dynamic-slice_fusion.4), channel_id=1, source_target_pairs={{0,16},{4,20},{8,24},{12,28},{16,0},{20,4},{24,8},{28,12},{1,17},{... | collective-permute-start | bytes 786440 | tf_op jit(solution)/shard_map/ppermute | solution.py:299
  180.3 14.1 %collective-permute-start.35 = (bf16[64,1024]{1,0:T(8,128)(2,1)S(1)}, bf16[64,1024]{1,0:T(8,128)(2,1)S(1)}, u32[]{:S(2)}, u32[]{:S(2)}) collective-permute-start(bf16[64,1024]{1,0:T(8,128)(2,1)S(1)} %constant_dynamic-slice_fusion.3), channel_id=1, source_target_pairs={{0,8},{4,12},{8,0},{12,4},{16,24},{20,28},{24,16},{28,20},{1,9},{5... | collective-permute-start | bytes 393224 | tf_op jit(solution)/shard_map/ppermute | solution.py:299
  181.9 3.7 %collective-permute-start.32 = (f32[2,1024]{1,0:T(2,128)S(1)}, f32[2,1024]{1,0:T(2,128)S(1)}, u32[]{:S(2)}, u32[]{:S(2)}) collective-permute-start(f32[2,1024]{1,0:T(2,128)S(1)} %fusion.57), channel_id=1, source_target_pairs={{0,2},{1,3},{2,0},{3,1},{4,6},{5,7},{6,4},{7,5},{8,10},{9,11},{10,... | collective-permute-start | bytes 24584 | tf_op jit(solution)/shard_map/ppermute | solution.py:299
  185.7 8.7 %collective-permute-start.34 = (f32[7808]{0:T(1024)S(1)}, f32[7808]{0:T(1024)S(1)}, u32[]{:S(2)}, u32[]{:S(2)}) collective-permute-start(f32[7808]{0:T(1024)S(1)} %constant_dynamic-update-slice_fusion.11), channel_id=1, source_target_pairs={{0,4},{4,0},{8,12},{12,8},{16,20},{20,16},{24,28},{28,24},{1,5},{5... | collective-permute-start | bytes 93704 | tf_op jit(solution)/shard_map/ppermute | solution.py:299
  195.8 15.9 %collective-permute-start.38 = (bf16[256,768]{1,0:T(8,128)(2,1)S(1)}, bf16[256,768]{1,0:T(8,128)(2,1)S(1)}, u32[]{:S(2)}, u32[]{:S(2)}) collective-permute-start(bf16[256,768]{1,0:T(8,128)(2,1)S(1)} %constant_dynamic-slice_fusion.2), channel_id=1, source_target_pairs={{0,8},{4,12},{8,0},{12,4},{16,24},{20,28},{24,16},{28,20},{1,9},{5... | collective-permute-start | bytes 1179656 | tf_op jit(solution)/shard_map/ppermute | solution.py:299
  201.5 10.8 %collective-permute-start.39 = (f32[7808]{0:T(1024)S(1)}, f32[7808]{0:T(1024)S(1)}, u32[]{:S(2)}, u32[]{:S(2)}) collective-permute-start(f32[7808]{0:T(1024)S(1)} %add.342), channel_id=1, source_target_pairs={{0,8},{4,12},{8,0},{12,4},{16,24},{20,28},{24,16},{28,20},{1,9},{5... | collective-permute-start | bytes 93704 | tf_op jit(solution)/shard_map/ppermute | solution.py:299
  201.6 18.5 %collective-permute-start.40 = (bf16[32,1024]{1,0:T(8,128)(2,1)S(1)}, bf16[32,1024]{1,0:T(8,128)(2,1)S(1)}, u32[]{:S(2)}, u32[]{:S(2)}) collective-permute-start(bf16[32,1024]{1,0:T(8,128)(2,1)S(1)} %constant_dynamic-slice_fusion.1), channel_id=1, source_target_pairs={{0,16},{4,20},{8,24},{12,28},{16,0},{20,4},{24,8},{28,12},{1,17},{... | collective-permute-start | bytes 196616 | tf_op jit(solution)/shard_map/ppermute | solution.py:299
  204.7 21.0 %collective-permute-start.41 = (bf16[128,1024]{1,0:T(8,128)(2,1)S(1)}, bf16[128,1024]{1,0:T(8,128)(2,1)S(1)}, u32[]{:S(2)}, u32[]{:S(2)}) collective-permute-start(bf16[128,1024]{1,0:T(8,128)(2,1)S(1)} %add_convert_fusion.22), channel_id=1, source_target_pairs={{0,16},{4,20},{8,24},{12,28},{16,0},{20,4},{24,8},{28,12},{1,17},{... | collective-permute-start | bytes 786440 | tf_op jit(solution)/shard_map/ppermute | solution.py:299
  204.7 26.1 %collective-permute-start.42 = (bf16[128,1024]{1,0:T(8,128)(2,1)S(1)}, bf16[128,1024]{1,0:T(8,128)(2,1)S(1)}, u32[]{:S(2)}, u32[]{:S(2)}) collective-permute-start(bf16[128,1024]{1,0:T(8,128)(2,1)S(1)} %add_convert_fusion.21), channel_id=1, source_target_pairs={{0,16},{4,20},{8,24},{12,28},{16,0},{20,4},{24,8},{28,12},{1,17},{... | collective-permute-start | bytes 786440 | tf_op jit(solution)/shard_map/ppermute | solution.py:299
  231.0 11.1 %collective-permute-start.43 = (bf16[128,768]{1,0:T(8,128)(2,1)S(1)}, bf16[128,768]{1,0:T(8,128)(2,1)S(1)}, u32[]{:S(2)}, u32[]{:S(2)}) collective-permute-start(bf16[128,768]{1,0:T(8,128)(2,1)S(1)} %constant_dynamic-slice_fusion), channel_id=1, source_target_pairs={{0,16},{4,20},{8,24},{12,28},{16,0},{20,4},{24,8},{28,12},{1,17},{... | collective-permute-start | bytes 589832 | tf_op jit(solution)/shard_map/ppermute | solution.py:299
  231.0 20.3 %collective-permute-start.46 = (bf16[256,1024]{1,0:T(8,128)(2,1)S(1)}, bf16[256,1024]{1,0:T(8,128)(2,1)S(1)}, u32[]{:S(2)}, u32[]{:S(2)}) collective-permute-start(bf16[256,1024]{1,0:T(8,128)(2,1)S(1)} %maximum_select_fusion.6), channel_id=1, source_target_pairs={{0,8},{4,12},{8,0},{12,4},{16,24},{20,28},{24,16},{28,20},{1,9},{5... | collective-permute-start | bytes 1572872 | tf_op jit(solution)/shard_map/ppermute | solution.py:299
  233.7 18.1 %collective-permute-start.47 = (bf16[256,1024]{1,0:T(8,128)(2,1)S(1)}, bf16[256,1024]{1,0:T(8,128)(2,1)S(1)}, u32[]{:S(2)}, u32[]{:S(2)}) collective-permute-start(bf16[256,1024]{1,0:T(8,128)(2,1)S(1)} %maximum_select_fusion.7), channel_id=1, source_target_pairs={{0,4},{4,0},{8,12},{12,8},{16,20},{20,16},{24,28},{28,24},{1,5},{5... | collective-permute-start | bytes 1572872 | tf_op jit(solution)/shard_map/ppermute | solution.py:299
  234.1 13.8 %collective-permute-start.44 = (f32[7808]{0:T(1024)S(1)}, f32[7808]{0:T(1024)S(1)}, u32[]{:S(2)}, u32[]{:S(2)}) collective-permute-start(f32[7808]{0:T(1024)S(1)} %add.348), channel_id=1, source_target_pairs={{0,16},{4,20},{8,24},{12,28},{16,0},{20,4},{24,8},{28,12},{1,17},{... | collective-permute-start | bytes 93704 | tf_op jit(solution)/shard_map/ppermute | solution.py:299
  234.4 14.2 %collective-permute-start.45 = (bf16[32,1024]{1,0:T(8,128)(2,1)S(1)}, bf16[32,1024]{1,0:T(8,128)(2,1)S(1)}, u32[]{:S(2)}, u32[]{:S(2)}) collective-permute-start(bf16[32,1024]{1,0:T(8,128)(2,1)S(1)} %add_convert_fusion.26), channel_id=1, source_target_pairs={{0,16},{4,20},{8,24},{12,28},{16,0},{20,4},{24,8},{28,12},{1,17},{... | collective-permute-start | bytes 196616 | tf_op jit(solution)/shard_map/ppermute | solution.py:299
  252.3 42.3 %collective-permute-start.50 = (bf16[512,1024]{1,0:T(8,128)(2,1)S(1)}, bf16[512,1024]{1,0:T(8,128)(2,1)}, u32[]{:S(2)}, u32[]{:S(2)}) collective-permute-start(bf16[512,1024]{1,0:T(8,128)(2,1)S(1)} %maximum_select_fusion.3), channel_id=1, source_target_pairs={{0,4},{4,0},{8,12},{12,8},{16,20},{20,16},{24,28},{28,24},{1,5},{5... | collective-permute-start | bytes 3145736 | tf_op jit(solution)/shard_map/ppermute | solution.py:299
  252.7 41.9 %collective-permute-start.51 = (bf16[512,1024]{1,0:T(8,128)(2,1)S(1)}, bf16[512,1024]{1,0:T(8,128)(2,1)}, u32[]{:S(2)}, u32[]{:S(2)}) collective-permute-start(bf16[512,1024]{1,0:T(8,128)(2,1)S(1)} %maximum_select_fusion.4), channel_id=1, source_target_pairs={{0,8},{4,12},{8,0},{12,4},{16,24},{20,28},{24,16},{28,20},{1,9},{5... | collective-permute-start | bytes 3145736 | tf_op jit(solution)/shard_map/ppermute | solution.py:299
  255.7 22.6 %collective-permute-start.48 = (bf16[128,768]{1,0:T(8,128)(2,1)S(1)}, bf16[128,768]{1,0:T(8,128)(2,1)S(1)}, u32[]{:S(2)}, u32[]{:S(2)}) collective-permute-start(bf16[128,768]{1,0:T(8,128)(2,1)S(1)} %add_convert_fusion.24), channel_id=1, source_target_pairs={{0,16},{4,20},{8,24},{12,28},{16,0},{20,4},{24,8},{28,12},{1,17},{... | collective-permute-start | bytes 589832 | tf_op jit(solution)/shard_map/ppermute | solution.py:299
  278.3 16.2 %collective-permute-start.52 = (bf16[256,768]{1,0:T(8,128)(2,1)S(1)}, bf16[256,768]{1,0:T(8,128)(2,1)S(1)}, u32[]{:S(2)}, u32[]{:S(2)}) collective-permute-start(bf16[256,768]{1,0:T(8,128)(2,1)S(1)} %maximum_select_fusion.9), channel_id=1, source_target_pairs={{0,8},{4,12},{8,0},{12,4},{16,24},{20,28},{24,16},{28,20},{1,9},{5... | collective-permute-start | bytes 1179656 | tf_op jit(solution)/shard_map/ppermute | solution.py:299
  281.3 10.5 %collective-permute-start.49 = (bf16[64,1024]{1,0:T(8,128)(2,1)S(1)}, bf16[64,1024]{1,0:T(8,128)(2,1)}, u32[]{:S(2)}, u32[]{:S(2)}) collective-permute-start(bf16[64,1024]{1,0:T(8,128)(2,1)S(1)} %maximum_select_fusion.11), channel_id=1, source_target_pairs={{0,8},{4,12},{8,0},{12,4},{16,24},{20,28},{24,16},{28,20},{1,9},{5... | collective-permute-start | bytes 393224 | tf_op jit(solution)/shard_map/ppermute | solution.py:299
  292.8 9.2 %collective-permute-start.53 = (bf16[128,1024]{1,0:T(8,128)(2,1)S(1)}, bf16[128,1024]{1,0:T(8,128)(2,1)S(1)}, u32[]{:S(2)}, u32[]{:S(2)}) collective-permute-start(bf16[128,1024]{1,0:T(8,128)(2,1)S(1)} %maximum_select_fusion.10), channel_id=1, source_target_pairs={{0,4},{4,0},{8,12},{12,8},{16,20},{20,16},{24,28},{28,24},{1,5},{5... | collective-permute-start | bytes 786440 | tf_op jit(solution)/shard_map/ppermute | solution.py:299
  294.9 20.7 %collective-permute-start.54 = (bf16[512,768]{1,0:T(8,128)(2,1)S(1)}, bf16[512,768]{1,0:T(8,128)(2,1)S(1)}, u32[]{:S(2)}, u32[]{:S(2)}) collective-permute-start(bf16[512,768]{1,0:T(8,128)(2,1)S(1)} %maximum_select_fusion.5), channel_id=1, source_target_pairs={{0,4},{4,0},{8,12},{12,8},{16,20},{20,16},{24,28},{28,24},{1,5},{5... | collective-permute-start | bytes 2359304 | tf_op jit(solution)/shard_map/ppermute | solution.py:299
  (69 other events, 374.5 us)

commit v4 on v3

--- a/solution.py
+++ b/solution.py
@@ -308,15 +308,20 @@
     return jnp.concatenate([blocks[j] for j in range(count // 2)])
 
 
-def scatter_near(rows, count):
-    size = rows.shape[0] // (count // 2)
-    held = {j: rows[j * size : (j + 1) * size] for j in range(count // 2)}
-    for bit in bits_of(count)[:-1]:
+def scatter_near(pieces, count):
+    held = dict(enumerate(pieces))
+    bits = bits_of(count)[:-1]
+    for bit in bits:
         arrived = {
             j ^ bit: swap(held[j].astype(BF16), "mp", count, bit) for j in held if j & bit
         }
+        if bit == bits[-1]:
+            return held[0], arrived[0]
         held = {j: held[j].astype(F32) + arrived[j].astype(F32) for j in arrived}
-    return held[0]
+
+
+def add_up(pair):
+    return pair[0].astype(F32) + pair[1].astype(F32)
 
 
 class DpSum:
@@ -329,19 +334,19 @@
     def high(self, bit):
         return (self.index & bit) != 0
 
+    def half(self, pairs, other):
+        size = pairs[0][0].shape[1] // 2
+        top = jnp.where(self.high(self.order[0]) != other, size, 0)
+        dots = [
+            dot_tn(lax.dynamic_slice_in_dim(left, top, size, 1), right) for left, right in pairs
+        ]
+        return functools.reduce(jnp.add, dots).astype(BF16)
+
     def open(self, pairs):
-        half = pairs[0][0].shape[1] // 2
-        top = jnp.where(self.high(self.order[0]), half, 0)
-
-        def part(start):
-            dots = [
-                dot_tn(lax.dynamic_slice_in_dim(left, start, half, 1), right)
-                for left, right in pairs
-            ]
-            return functools.reduce(jnp.add, dots).astype(BF16)
-
-        self.send = part(half - top)
-        self.held = part(top)
+        self.send = self.half(pairs, True)
+
+    def keep(self, pairs):
+        self.held = self.half(pairs, False)
 
     def launch(self):
         self.flying = swap(self.send, "dp", self.count, self.steps[self.at])
@@ -475,17 +480,21 @@
         far = project(attn_far)
 
         heads_far, logs_far = attend_forward(far, picks[1], [near, far], bars)
-        share_far = dot_nn(heads_far, output_weight).astype(BF16)
-        sum_far = scatter_near(share_far, n_mp).astype(BF16)
+        near_count = n_mp // 2
+
+        def cut(rows):
+            rows = rows.astype(BF16)
+            return [rows[j * own_count : (j + 1) * own_count] for j in range(near_count)]
+
+        sum_far = add_up(scatter_near(cut(dot_nn(heads_far, output_weight)), n_mp)).astype(BF16)
         sum_far, near = tie(sum_far, near)
         arrived = swap(sum_far, "mp", n_mp, far_bit)
         heads_near, logs_near = attend_forward(near, picks[0], [near, far], bars)
-        share_near = dot_nn(heads_near, output_weight).astype(BF16)
-        sum_near = scatter_near(share_near, n_mp)
+        sum_near = scatter_near(cut(dot_nn(heads_near, output_weight)), n_mp)
         grad_near = gather_near(grad_low, n_mp)
         grad_far = gather_near(grad_far, n_mp)
         arrived, grad_near, grad_far = tie(arrived, grad_near, grad_far)
-        hidden_res = residual + (sum_near + arrived.astype(F32)) + output_bias
+        hidden_res = residual + (add_up(sum_near) + arrived.astype(F32)) + output_bias
         normed_two, inverse_two = normalize(hidden_res)
         mlp_input = (normed_two * second_gain + second_shift).astype(BF16)
 
@@ -494,30 +503,38 @@
         act_near, slope_near, back_near = mlp_both(
             mlp_near, grad_near, expand_weight, expand_bias, reduce_weight
         )
-        share_near = dot_nn(act_near, reduce_weight).astype(BF16)
-        sum_near = scatter_near(back_near, n_mp)
-        far_own, sum_near, share_near = tie(far_own, sum_near, share_near)
+        far_own, act_near, slope_near, back_near = tie(far_own, act_near, slope_near, back_near)
         mlp_far = gather_near(far_own, n_mp)
+        sum_near = scatter_near(cut(back_near), n_mp)
         act_far, slope_far, back_far = mlp_both(
             mlp_far, grad_far, expand_weight, expand_bias, reduce_weight
         )
+        act_far, slope_far, back_far, *sum_near = tie(act_far, slope_far, back_far, *sum_near)
         swapped = dp_bits[1:2] + dp_bits[:1] + dp_bits[2:]
         reduce_sum = DpSum(n_dp, group, dp_bits)
         expand_sum = DpSum(n_dp, group, swapped)
         output_sum = DpSum(n_dp, group, dp_bits)
         input_sum = DpSum(n_dp, group, dp_bits)
+        sum_far = add_up(scatter_near(cut(back_far), n_mp)).astype(BF16)
         reduce_sum.open([(act_near, grad_near), (act_far, grad_far)])
-        sum_far = scatter_near(back_far, n_mp).astype(BF16)
-        sum_far, slope_near, slope_far = start_all((sum_far, slope_near, slope_far), [reduce_sum])
+        sum_far, slope_near, slope_far, act_far = start_all(
+            (sum_far, slope_near, slope_far, act_far), [reduce_sum]
+        )
         arrived = swap(sum_far, "mp", n_mp, far_bit)
         expand_sum.open([(mlp_near, slope_near), (mlp_far, slope_far)])
-        (sum_near,) = start_all((sum_near,), [expand_sum])
-        share_far = dot_nn(act_far, reduce_weight).astype(BF16)
-        arrived, share_far, reduce_sum.held, expand_sum.held = tie(
-            arrived, share_far, reduce_sum.held, expand_sum.held
-        )
-
-        normed_grad_two = sum_near + arrived.astype(F32)
+        sum_near[0], act_near, act_far, slope_near, slope_far = start_all(
+            (sum_near[0], act_near, act_far, slope_near, slope_far), [expand_sum]
+        )
+        reduce_sum.keep([(act_near, grad_near), (act_far, grad_far)])
+        expand_sum.keep([(mlp_near, slope_near), (mlp_far, slope_far)])
+        out_far = scatter_near(cut(dot_nn(act_far, reduce_weight)), n_mp)
+        out_near = scatter_near(cut(dot_nn(act_near, reduce_weight)), n_mp)
+        held = [reduce_sum.held, expand_sum.held]
+        arrived, *held = tie(arrived, *held, *out_far, *out_near)
+        reduce_sum.held, expand_sum.held = held[:2]
+        out_far, out_near = held[2:4], held[4:]
+
+        normed_grad_two = add_up(sum_near) + arrived.astype(F32)
         grad_out = grad_low.astype(F32)
         residual_grad = grad_out + normalize_back(
             normed_grad_two, normed_two, inverse_two, second_gain
@@ -525,32 +542,20 @@
         branch_grad = residual_grad.astype(BF16)
         far_own = swap(branch_grad, "mp", n_mp, far_bit)
         branch_near = gather_near(branch_grad, n_mp)
-        out_sum = scatter_near(share_far, n_mp).astype(BF16)
-        branch_near, out_sum = tie(branch_near, out_sum)
-        out_far = swap(out_sum, "mp", n_mp, far_bit)
         head_near = dot_nt(branch_near, output_weight).astype(BF16)
         query_near, key_part, value_part = attend_back(
             near, picks[0], head_near, heads_near, logs_near, [near, far], bars, None, False
         )
-        out_near = scatter_near(share_near, n_mp)
-        over_mp = (("mp", n_mp),)
-        early = butterfly(
-            jnp.stack(
-                [
-                    jnp.sum(normed_grad_two * normed_two, 0),
-                    jnp.sum(normed_grad_two, 0),
-                    jnp.sum(branch_grad, 0, dtype=F32),
-                    jnp.sum(grad_out, 0),
-                ]
-            ),
-            over_mp,
-        )
-        far_own, query_near = await_all((far_own, query_near), [reduce_sum, expand_sum])
+        far_own, query_near, normed_grad_two, branch_grad, *out_far = await_all(
+            (far_own, query_near, normed_grad_two, branch_grad, *out_far),
+            [reduce_sum, expand_sum],
+        )
         branch_far = gather_near(far_own, n_mp)
         (branch_far,) = start_all((branch_far,), [reduce_sum, expand_sum])
-        output_sum.open([(heads_near, branch_near), (heads_far, branch_far)])
+        branch_pairs = [(heads_near, branch_near), (heads_far, branch_far)]
+        output_sum.open(branch_pairs)
         head_far = dot_nt(branch_far, output_weight).astype(BF16)
-        head_far, out_near, early = start_all((head_far, out_near, early), [output_sum])
+        (head_far,) = start_all((head_far,), [output_sum])
         query_far, key_grads, value_grads = attend_back(
             far,
             picks[1],
@@ -562,29 +567,40 @@
             (key_part, value_part),
             True,
         )
-
+        query_far, query_near, branch_far, normed_grad_two, branch_grad, *out_far = await_all(
+            (query_far, query_near, branch_far, normed_grad_two, branch_grad, *out_far),
+            [reduce_sum, expand_sum],
+        )
+        qkv_far = jnp.concatenate([query_far, key_grads[1], value_grads[1]], 1)
+        sum_far = scatter_near(cut(dot_nt(qkv_far, weight_wide)), n_mp)
         qkv_near = jnp.concatenate([query_near, key_grads[0], value_grads[0]], 1)
-        qkv_far = jnp.concatenate([query_far, key_grads[1], value_grads[1]], 1)
-        input_sum.open([(attn_near, qkv_near), (attn_far, qkv_far)])
-        share_far = dot_nt(qkv_far, weight_wide).astype(BF16)
-        sum_far = scatter_near(share_far, n_mp).astype(BF16)
-        (sum_far,) = start_all((sum_far,), [input_sum])
+        (qkv_near,) = start_all((qkv_near,), [reduce_sum, expand_sum])
+        pairs = [(attn_near, qkv_near), (attn_far, qkv_far)]
+        input_sum.open(pairs)
+        sum_far, qkv_near = start_all((add_up(sum_far).astype(BF16), qkv_near), [input_sum])
         arrived = swap(sum_far, "mp", n_mp, far_bit)
-        sum_near = scatter_near(dot_nt(qkv_near, weight_wide).astype(BF16), n_mp)
-        sum_near, input_sum.held = await_all(
-            (sum_near, input_sum.held), [reduce_sum, expand_sum]
-        )
-        (sum_near,) = start_all((sum_near,), [reduce_sum, expand_sum])
-        (arrived,) = await_all((arrived,), [output_sum])
-        arrived, sum_near, out_far = start_all((arrived, sum_near, out_far), [output_sum])
-        block_output = (hidden_res + (out_near + out_far.astype(F32)) + reduce_bias).astype(BF16)
-        normed_grad_one = sum_near + arrived.astype(F32)
+        sum_near = scatter_near(cut(dot_nt(qkv_near, weight_wide)), n_mp)
+        input_sum.keep(pairs)
+        output_sum.keep([(heads_near, branch_near), (heads_far, branch_far)])
+        arrived, input_sum.held, output_sum.held, *sum_near = tie(
+            arrived, input_sum.held, output_sum.held, *sum_near
+        )
+        normed_grad_one = add_up(sum_near) + arrived.astype(F32)
         input_gradient = residual_grad + normalize_back(
             normed_grad_one, normed_one, inverse_one, first_gain
         )
-        late = butterfly(
-            jnp.stack([jnp.sum(normed_grad_one * normed_one, 0), jnp.sum(normed_grad_one, 0)]),
-            over_mp,
+        both = butterfly(
+            jnp.stack(
+                [
+                    jnp.sum(normed_grad_two * normed_two, 0),
+                    jnp.sum(normed_grad_two, 0),
+                    jnp.sum(branch_grad, 0, dtype=F32),
+                    jnp.sum(grad_out, 0),
+                    jnp.sum(normed_grad_one * normed_one, 0),
+                    jnp.sum(normed_grad_one, 0),
+                ]
+            ),
+            (("mp", n_mp),),
         )
         hidden = expand_bias.shape[0]
         hidden_sums = jnp.sum(slope_near, 0, dtype=F32) + jnp.sum(slope_far, 0, dtype=F32)
@@ -594,8 +610,7 @@
             dp_bits,
             jnp.concatenate(
                 [
-                    early.reshape(-1),
-                    late.reshape(-1),
+                    both.reshape(-1),
                     wide_sums[:local_width],
                     wide_sums[2 * local_width :],
                     hidden_sums,
@@ -603,15 +618,23 @@
                 ]
             ),
         )
-        (block_output,) = start_all((block_output,), [small])
-        sums = [input_sum, small, output_sum, reduce_sum, expand_sum]
-        token = block_output
+        sums = [reduce_sum, expand_sum, output_sum, input_sum]
+        token, small.send = await_all((input_gradient, small.send), sums)
+        token, *out_far = start_all((token, *out_far), sums)
+        token, out_far = tie(token, add_up(out_far).astype(BF16))
+        out_far = swap(out_far, "mp", n_mp, far_bit)
+        (token,) = await_all((token,), sums)
+        sums.append(small)
+        (token,) = start_all((token,), sums)
+        token, out_far = await_all((token, out_far), sums)
+        block_output = (
+            hidden_res + (add_up(out_near) + out_far.astype(F32)) + reduce_bias
+        ).astype(BF16)
         while any(s.busy() for s in sums):
-            for s in sums:
-                if s.busy():
-                    (token,) = await_all((token,), [s])
-                    (token,) = start_all((token,), [s])
-        block_output = token
+            sums = [s for s in sums if s.busy()]
+            (token,) = start_all((token,), sums)
+            (token,) = await_all((token,), sums)
+        input_gradient = token
 
         total = small.held
         rows = total[: 6 * width].reshape(6, width)

time: 323 us -> 312 us (0.966)
  waiting for transfers between devices: 156 us -> 118 us
  other arithmetic: 35.3 us -> 50.5 us
  matrix products: 19.2 us -> 28.3 us
    ppermute x55 -> x53, waiting for transfers between devices: 156 us -> 118 us  [swap(): return lax.ppermute(array, axis, [(i, i ^ bit) for i in range(size)])]
    convert_element_type x11 -> x12, other arithmetic: 1.78 us -> 10.9 us  [land(): self.held = (self.held.astype(F32) + self.flying.astype(F32)).astype(BF16)]
    dot_general x16, matrix products: 9.87 us -> 18.8 us  [dot_tn(): lax.dot_general(a, b, (((0,), (0,)), ((), ())), preferred_element_type=F32)]
    convert_element_type x5 -> x6, other arithmetic: 1.83 us -> 5.18 us  [the longest x1 2.23 us: per_device(): branch_grad = residual_grad.astype(BF16)]
    ppermute x55 -> x53, starting transfers between devices: 50.5 us -> 49.6 us  [swap(): return lax.ppermute(array, axis, [(i, i ^ bit) for i in range(size)])]
    unnamed x134 -> x177, local copies, waits for them, and re-layouts: 10.9 us -> 10.8 us
  transfers between devices with their start and end apart: 55 -> 53, of which waited for: 31 -> 20; matrix products, arithmetic and copies ran while one was open for 17% -> 22% of each run, Pallas kernels for 10% -> 11%
where the time goes in v4:
time: 312 us; the launch traced here: 307 us
  waiting for transfers between devices  118 us (38%)
  other arithmetic  50.5 us (16%)
  starting transfers between devices  49.6 us (16%)
  Pallas kernels  34.9 us (11%)
  matrix products  28.3 us (9%)
  local copies, waits for them, and re-layouts  21 us (7%)
  between operations  4.78 us (2%)
    ppermute x53, waiting for transfers between devices, swap(): return lax.ppermute(array, axis, [(i, i ^ bit) for i in range(size)])  118 us
    ppermute x53, starting transfers between devices, swap(): return lax.ppermute(array, axis, [(i, i ^ bit) for i in range(size)])  49.6 us
    dot_general x16, matrix products, dot_tn(): lax.dot_general(a, b, (((0,), (0,)), ((), ())), preferred_element_type=F32)  18.8 us
    pallas_call x2, Pallas kernels, attend_back(): pl.pallas_call(functools.partial(attend_back_kernel, parts, first, last),...  16.3 us
    convert_element_type x12, other arithmetic, land(): self.held = (self.held.astype(F32) + self.flying.astype(F32)).astype(BF16)  10.9 us
    pallas_call x2, Pallas kernels, attend_forward(): pl.pallas_call(functools.partial(attend_kernel, len(halves)), grid=(pairs...  10.8 us
    unnamed x177, local copies, waits for them, and re-layouts  10.8 us
    pallas_call x2, Pallas kernels, mlp_both(): pl.pallas_call(mlp_kernel, grid=(count // tile,), in_specs=[pl.BlockSpec(...  7.78 us
  transfers between devices with their start and end apart: 53, of which 20 were waited for; matrix products, arithmetic and copies ran while one was open for 22% of the time, Pallas kernels for 11%

profile of v4, /device:TPU:0, one launch (start us, length us, event | category | flops | bytes accessed | tf_op | source)
XLA Modules:
  0.0 307.1 jit_solution(4808410892719602705)
XLA Ops:
  2.9 1.9 multiply_sine_fusion
  8.8 2.6 collective-permute-start
  14.2 9.7 %collective-permute-done = bf16[256,1024]{1,0:T(8,128)(2,1)S(1)} collective-permute-done((bf16[256,1024]{1,0:T(8,128)(2,1)S(1)}, bf16[256,1024]{1,0:T(8,128)(2,1)S(1)}, u32[]{:S(2)}, u32[]{:S(2)}) %collective-permute-start) | collective-permute-done | bytes 524320 | tf_op jit(solution)/shard_map/ppermute | solution.py:299
  24.2 1.8 collective-permute-start.7
  28.1 5.5 %attend_forward.2 = (bf16[512,256]{1,0:T(8,128)(2,1)S(1)}, f32[2,8,512]{2,1,0:T(8,128)S(1)}) custom-call(bf16[512,768]{1,0:T(8,128)(2,1)S(1)} %add_convert_fusion.9.q_ref.refs_1_.refs_3_, bf16[512,128]{1,0:T(8,128)(2,1)S(1)} %fusion.26.pick_ref, bf16[512,768]{1,0:T(8,128)(2,1)S(1)} %add_convert_fusion.10.refs_0_.refs_2_.q_ref, ...), custom_call_target="tpu_custom_call" | custom-call | flops 1024 | bytes 1024 | tf_op jit(solution)/shard_map/attend_forward/pallas_call | solution.py:73
  35.0 3.6 %collective-permute-done.7 = bf16[256,1024]{1,0:T(8,128)(2,1)S(1)} collective-permute-done((bf16[256,1024]{1,0:T(8,128)(2,1)S(1)}, bf16[256,1024]{1,0:T(8,128)(2,1)S(1)}, u32[]{:S(2)}, u32[]{:S(2)}) %collective-permute-start.7) | collective-permute-done | bytes 524320 | tf_op jit(solution)/shard_map/ppermute | solution.py:299
  38.8 1.8 collective-permute-start.5
  40.6 5.3 %attend_forward.3 = (bf16[512,256]{1,0:T(8,128)(2,1)S(1)}, f32[2,8,512]{2,1,0:T(8,128)S(1)}) custom-call(bf16[512,768]{1,0:T(8,128)(2,1)S(1)} %add_convert_fusion.10.refs_0_.refs_2_.q_ref, bf16[512,128]{1,0:T(8,128)(2,1)S(1)} %fusion.25.pick_ref, bf16[512,768]{1,0:T(8,128)(2,1)S(1)} %add_convert_fusion.10.refs_0_.refs_2_.q_ref, ...), custom_call_target="tpu_custom_call" | custom-call | flops 1024 | bytes 1024 | tf_op jit(solution)/shard_map/attend_forward/pallas_call | solution.py:73
  48.3 5.0 %collective-permute-done.5 = bf16[256,1024]{1,0:T(8,128)(2,1)S(1)} collective-permute-done((bf16[256,1024]{1,0:T(8,128)(2,1)S(1)}, bf16[256,1024]{1,0:T(8,128)(2,1)S(1)}, u32[]{:S(2)}, u32[]{:S(2)}) %collective-permute-start.5) | collective-permute-done | bytes 524320 | tf_op jit(solution)/shard_map/ppermute | solution.py:299
  54.3 1.8 collective-permute-start.9
  57.0 3.7 %mlp_both.2 = (bf16[512,1024]{1,0:T(8,128)(2,1)S(1)}, bf16[512,1024]{1,0:T(8,128)(2,1)S(1)}, bf16[512,1024]{1,0:T(8,128)(2,1)S(1)}) custom-call(bf16[512,1024]{1,0:T(8,128)(2,1)S(1)} %pad_maximum_fusion.3.x_ref, bf16[512,1024]{1,0:T(8,128)(2,1)S(1)} %pad_maximum_fusion.5.grad_ref, bf16[1024,1024]{1,0:T(8,128)(2,1)S(1)} %copy-done.6, f32[1,1024]{1,0:T(1,128)S(1)} %bitcast.52, ...), custom_call_target="tpu_custom_call" | custom-call | flops 1024 | bytes 1024 | tf_op jit(solution)/shard_map/mlp_both/pallas_call | solution.py:224
  62.6 6.1 %collective-permute-done.9 = bf16[256,1024]{1,0:T(8,128)(2,1)} collective-permute-done((bf16[256,1024]{1,0:T(8,128)(2,1)S(1)}, bf16[256,1024]{1,0:T(8,128)(2,1)}, u32[]{:S(2)}, u32[]{:S(2)}) %collective-permute-start.9) | collective-permute-done | bytes 524320 | tf_op jit(solution)/shard_map/ppermute | solution.py:299
  75.7 4.1 %mlp_both.3 = (bf16[512,1024]{1,0:T(8,128)(2,1)S(1)}, bf16[512,1024]{1,0:T(8,128)(2,1)S(1)}, bf16[512,1024]{1,0:T(8,128)(2,1)S(1)}) custom-call(bf16[512,1024]{1,0:T(8,128)(2,1)S(1)} %constant_dynamic-update-slice_fusion.2.x_ref, bf16[512,1024]{1,0:T(8,128)(2,1)S(1)} %copy-done.1, bf16[1024,1024]{1,0:T(8,128)(2,1)S(1)} %copy-done.7, f32[1,1024]{1,0:T(1,128)S(1)} %bitcast.53, ...), custom_call_target="tpu_custom_call" | custom-call | flops 1024 | bytes 1024 | tf_op jit(solution)/shard_map/mlp_both/pallas_call | solution.py:224
  81.5 1.8 add_convert_fusion.5
  83.5 1.8 collective-permute-start.14
  93.5 1.8 add_convert_fusion.3
  98.9 1.8 add_convert_fusion.2
  100.8 2.0 multiply_reduce_fusion.7
  102.8 2.2 fusion.59
  107.6 2.2 convert_reduce_fusion
  111.5 7.9 %attend_back.2 = (bf16[512,256]{1,0:T(8,128)(2,1)S(1)}, f32[512,256]{1,0:T(8,128)S(1)}, f32[512,256]{1,0:T(8,128)S(1)}, f32[512,256]{1,0:T(8,128)S(1)}, f32[512,256]{1,0:T(8,128)S(1)}) custom-call(bf16[512,768]{1,0:T(8,128)(2,1)S(1)} %add_convert_fusion.10.refs_0_.refs_2_.q_ref, bf16[512,128]{1,0:T(8,128)(2,1)S(1)} %copy-done.15, ...), custom_call_target="tpu_custom_call" | custom-call | flops 1024 | bytes 1024 | tf_op jit(solution)/shard_map/attend_back/pallas_call | solution.py:184
  119.7 2.3 collective-permute-done.20
  129.2 2.2 fusion
  133.4 8.4 %attend_back.3 = (bf16[512,256]{1,0:T(8,128)(2,1)S(1)}, bf16[512,256]{1,0:T(8,128)(2,1)S(1)}, bf16[512,256]{1,0:T(8,128)(2,1)S(1)}, bf16[512,256]{1,0:T(8,128)(2,1)S(1)}, bf16[512,256]{1,0:T(8,128)(2,1)S(1)}) custom-call(bf16[512,768]{1,0:T(8,128)(2,1)S(1)} %add_convert_fusion.9.q_ref.refs_1_.refs_3_, bf16[512,128]{1,0:T(8,128)(2,1)S(1)} %fusion.26.pick_ref, ...), custom_call_target="tpu_custom_call" | custom-call | flops 1024 | bytes 1024 | tf_op jit(solution)/shard_map/attend_back/pallas_call | solution.py:184
  147.7 2.7 collective-permute-start.29
  160.2 9.8 %collective-permute-done.25 = bf16[256,1024]{1,0:T(8,128)(2,1)S(1)} collective-permute-done((bf16[256,1024]{1,0:T(8,128)(2,1)S(1)}, bf16[256,1024]{1,0:T(8,128)(2,1)S(1)}, u32[]{:S(2)}, u32[]{:S(2)}) %collective-permute-start.25) | collective-permute-done | bytes 524320 | tf_op jit(solution)/shard_map/ppermute | solution.py:299
  172.9 3.0 multiply_add_fusion
  176.4 2.8 collective-permute-done.32
  179.2 1.8 add_convert_fusion.22
  181.0 1.8 add_convert_fusion.23
  188.1 2.6 collective-permute-start.33
  193.8 16.2 %collective-permute-done.35 = bf16[64,1024]{1,0:T(8,128)(2,1)S(1)} collective-permute-done((bf16[64,1024]{1,0:T(8,128)(2,1)S(1)}, bf16[64,1024]{1,0:T(8,128)(2,1)S(1)}, u32[]{:S(2)}, u32[]{:S(2)}) %collective-permute-start.35) | collective-permute-done | bytes 131104 | tf_op jit(solution)/shard_map/ppermute | solution.py:299
  210.0 2.7 collective-permute-done.34
  215.1 2.8 collective-permute-start.41
  219.4 7.4 %collective-permute-done.42 = f32[7808]{0:T(1024)S(1)} collective-permute-done((f32[7808]{0:T(1024)S(1)}, f32[7808]{0:T(1024)S(1)}, u32[]{:S(2)}, u32[]{:S(2)}) %collective-permute-start.42) | collective-permute-done | bytes 31264 | tf_op jit(solution)/shard_map/ppermute | solution.py:299
  228.0 4.5 %collective-permute-done.40 = bf16[32,1024]{1,0:T(8,128)(2,1)S(1)} collective-permute-done((bf16[32,1024]{1,0:T(8,128)(2,1)S(1)}, bf16[32,1024]{1,0:T(8,128)(2,1)S(1)}, u32[]{:S(2)}, u32[]{:S(2)}) %collective-permute-start.40) | collective-permute-done | bytes 65568 | tf_op jit(solution)/shard_map/ppermute | solution.py:299
  234.5 1.9 collective-permute-start.46
  237.5 2.0 collective-permute-start.47
  239.5 23.0 %collective-permute-done.47 = f32[7808]{0:T(1024)S(1)} collective-permute-done((f32[7808]{0:T(1024)S(1)}, f32[7808]{0:T(1024)S(1)}, u32[]{:S(2)}, u32[]{:S(2)}) %collective-permute-start.47) | collective-permute-done | bytes 31264 | tf_op jit(solution)/shard_map/ppermute | solution.py:299
  263.5 2.1 collective-permute-start.50
  267.0 5.1 %collective-permute-done.50 = f32[7808]{0:T(1024)S(1)} collective-permute-done((f32[7808]{0:T(1024)S(1)}, f32[7808]{0:T(1024)S(1)}, u32[]{:S(2)}, u32[]{:S(2)}) %collective-permute-start.50) | collective-permute-done | bytes 31264 | tf_op jit(solution)/shard_map/ppermute | solution.py:299
  272.1 3.6 %collective-permute-done.48 = bf16[64,1024]{1,0:T(8,128)(2,1)S(1)} collective-permute-done((bf16[64,1024]{1,0:T(8,128)(2,1)S(1)}, bf16[64,1024]{1,0:T(8,128)(2,1)S(1)}, u32[]{:S(2)}, u32[]{:S(2)}) %collective-permute-start.48) | collective-permute-done | bytes 131104 | tf_op jit(solution)/shard_map/ppermute | solution.py:299
  277.9 2.3 collective-permute-start.52
  280.8 3.1 convert_multiply_fusion.1
  284.5 4.4 %convert_multiply_fusion = f32[1024,1024]{1,0:T(8,128)} fusion(bf16[512,1024]{1,0:T(8,128)(2,1)S(1)} %maximum_select_fusion.3, bf16[512,1024]{1,0:T(8,128)(2,1)} %copy-done.54, f32[]{:T(128)} %bitcast.14, pred[]{:T(512)S(6)} %ne.10), kind=kLoop, calls=%fused_computation | loop fusion | flops 11534336 | bytes 6291461 | tf_op jit(solution)/shard_map/mul | solution.py:660
  288.9 13.3 %collective-permute-done.51 = bf16[128,1024]{1,0:T(8,128)(2,1)} collective-permute-done((bf16[128,1024]{1,0:T(8,128)(2,1)S(1)}, bf16[128,1024]{1,0:T(8,128)(2,1)}, u32[]{:S(2)}, u32[]{:S(2)}) %collective-permute-start.51) | collective-permute-done | bytes 262176 | tf_op jit(solution)/shard_map/ppermute | solution.py:299
  302.1 2.2 convert_multiply_fusion.3
  305.0 1.9 pad_maximum_fusion
  (377 shorter events, 92.5 us)
Async XLA Ops:
  8.3 4.9 %collective-permute-start.1 = (bf16[256,1024]{1,0:T(8,128)(2,1)S(1)}, bf16[256,1024]{1,0:T(8,128)(2,1)S(1)}, u32[]{:S(2)}, u32[]{:S(2)}) collective-permute-start(bf16[256,1024]{1,0:T(8,128)(2,1)S(1)} %add_convert_fusion.19), channel_id=1, source_target_pairs={{0,1},{1,0},{2,3},{3,2},{4,5},{5,4},{6,7},{7,6},{8,9},{9,8},{10,11... | collective-permute-start | bytes 1572872 | tf_op jit(solution)/shard_map/ppermute | solution.py:299
  8.8 15.1 %collective-permute-start = (bf16[256,1024]{1,0:T(8,128)(2,1)S(1)}, bf16[256,1024]{1,0:T(8,128)(2,1)S(1)}, u32[]{:S(2)}, u32[]{:S(2)}) collective-permute-start(bf16[256,1024]{1,0:T(8,128)(2,1)S(1)} %add_convert_fusion.19), channel_id=1, source_target_pairs={{0,2},{1,3},{2,0},{3,1},{4,6},{5,7},{6,4},{7,5},{8,10},{9,11},{10,... | collective-permute-start | bytes 1572872 | tf_op jit(solution)/shard_map/ppermute | solution.py:299
  24.2 14.4 %collective-permute-start.7 = (bf16[256,1024]{1,0:T(8,128)(2,1)S(1)}, bf16[256,1024]{1,0:T(8,128)(2,1)S(1)}, u32[]{:S(2)}, u32[]{:S(2)}) collective-permute-start(bf16[256,1024]{1,0:T(8,128)(2,1)S(1)} %get-tuple-element.167), channel_id=1, source_target_pairs={{0,2},{1,3},{2,0},{3,1},{4,6},{5,7},{6,4},{7,5},{8,10},{9,11},{10,... | collective-permute-start | bytes 1572872 | tf_op jit(solution)/shard_map/ppermute | solution.py:299
  34.1 4.5 %collective-permute-start.3 = (bf16[256,1024]{1,0:T(8,128)(2,1)S(1)}, bf16[256,1024]{1,0:T(8,128)(2,1)S(1)}, u32[]{:S(2)}, u32[]{:S(2)}) collective-permute-start(bf16[256,1024]{1,0:T(8,128)(2,1)S(1)} %slice.155), channel_id=1, source_target_pairs={{0,1},{1,0},{2,3},{3,2},{4,5},{5,4},{6,7},{7,6},{8,9},{9,8},{10,11... | collective-permute-start | bytes 1572872 | tf_op jit(solution)/shard_map/ppermute | solution.py:299
  34.6 12.2 %collective-permute-start.6 = (bf16[256,1024]{1,0:T(8,128)(2,1)S(1)}, bf16[256,1024]{1,0:T(8,128)(2,1)S(1)}, u32[]{:S(2)}, u32[]{:S(2)}) collective-permute-start(bf16[256,1024]{1,0:T(8,128)(2,1)S(1)} %get-tuple-element.167), channel_id=1, source_target_pairs={{0,1},{1,0},{2,3},{3,2},{4,5},{5,4},{6,7},{7,6},{8,9},{9,8},{10,11... | collective-permute-start | bytes 1572872 | tf_op jit(solution)/shard_map/ppermute | solution.py:299
  38.6 8.6 %collective-permute-start.8 = (bf16[256,1024]{1,0:T(8,128)(2,1)S(1)}, bf16[256,1024]{1,0:T(8,128)(2,1)S(1)}, u32[]{:S(2)}, u32[]{:S(2)}) collective-permute-start(bf16[256,1024]{1,0:T(8,128)(2,1)S(1)} %collective-permute-done.7), channel_id=1, source_target_pairs={{0,1},{1,0},{2,3},{3,2},{4,5},{5,4},{6,7},{7,6},{8,9},{9,8},{10,11... | collective-permute-start | bytes 1572872 | tf_op jit(solution)/shard_map/ppermute | solution.py:299
  38.8 14.4 %collective-permute-start.5 = (bf16[256,1024]{1,0:T(8,128)(2,1)S(1)}, bf16[256,1024]{1,0:T(8,128)(2,1)S(1)}, u32[]{:S(2)}, u32[]{:S(2)}) collective-permute-start(bf16[256,1024]{1,0:T(8,128)(2,1)S(1)} %add_convert_fusion.18), channel_id=1, source_target_pairs={{0,2},{1,3},{2,0},{3,1},{4,6},{5,7},{6,4},{7,5},{8,10},{9,11},{10,... | collective-permute-start | bytes 1572872 | tf_op jit(solution)/shard_map/ppermute | solution.py:299
  46.5 6.7 %collective-permute-start.4 = (bf16[256,1024]{1,0:T(8,128)(2,1)S(1)}, bf16[256,1024]{1,0:T(8,128)(2,1)S(1)}, u32[]{:S(2)}, u32[]{:S(2)}) collective-permute-start(bf16[256,1024]{1,0:T(8,128)(2,1)S(1)} %slice.157), channel_id=1, source_target_pairs={{0,1},{1,0},{2,3},{3,2},{4,5},{5,4},{6,7},{7,6},{8,9},{9,8},{10,11... | collective-permute-start | bytes 1572872 | tf_op jit(solution)/shard_map/ppermute | solution.py:299
  54.3 14.4 %collective-permute-start.9 = (bf16[256,1024]{1,0:T(8,128)(2,1)S(1)}, bf16[256,1024]{1,0:T(8,128)(2,1)}, u32[]{:S(2)}, u32[]{:S(2)}) collective-permute-start(bf16[256,1024]{1,0:T(8,128)(2,1)S(1)} %add_convert_fusion.17), channel_id=1, source_target_pairs={{0,2},{1,3},{2,0},{3,1},{4,6},{5,7},{6,4},{7,5},{8,10},{9,11},{10,... | collective-permute-start | bytes 1572872 | tf_op jit(solution)/shard_map/ppermute | solution.py:299
  69.8 10.1 %collective-permute-start.12 = (bf16[256,1024]{1,0:T(8,128)(2,1)}, bf16[256,1024]{1,0:T(8,128)(2,1)}, u32[]{:S(2)}, u32[]{:S(2)}) collective-permute-start(bf16[256,1024]{1,0:T(8,128)(2,1)} %get-tuple-element.337), channel_id=1, source_target_pairs={{0,1},{1,0},{2,3},{3,2},{4,5},{5,4},{6,7},{7,6},{8,9},{9,8},{10,11... | collective-permute-start | bytes 1572872 | tf_op jit(solution)/shard_map/ppermute | solution.py:299
  83.5 17.2 %collective-permute-start.14 = (bf16[256,1024]{1,0:T(8,128)(2,1)S(1)}, bf16[256,1024]{1,0:T(8,128)(2,1)S(1)}, u32[]{:S(2)}, u32[]{:S(2)}) collective-permute-start(bf16[256,1024]{1,0:T(8,128)(2,1)S(1)} %add_convert_fusion.16), channel_id=1, source_target_pairs={{0,2},{1,3},{2,0},{3,1},{4,6},{5,7},{6,4},{7,5},{8,10},{9,11},{10,... | collective-permute-start | bytes 1572872 | tf_op jit(solution)/shard_map/ppermute | solution.py:299
  85.3 34.4 %collective-permute-start.19 = (bf16[512,1024]{1,0:T(8,128)(2,1)}, bf16[512,1024]{1,0:T(8,128)(2,1)}, u32[]{:S(2)}, u32[]{:S(2)}) collective-permute-start(bf16[512,1024]{1,0:T(8,128)(2,1)} %add_convert_fusion.5), channel_id=1, source_target_pairs={{0,4},{4,0},{8,12},{12,8},{16,20},{20,16},{24,28},{28,24},{1,5},{5... | collective-permute-start | bytes 3145736 | tf_op jit(solution)/shard_map/ppermute | solution.py:299
  91.5 9.2 %collective-permute-start.16 = (bf16[256,1024]{1,0:T(8,128)(2,1)S(1)}, bf16[256,1024]{1,0:T(8,128)(2,1)S(1)}, u32[]{:S(2)}, u32[]{:S(2)}) collective-permute-start(bf16[256,1024]{1,0:T(8,128)(2,1)S(1)} %get-tuple-element.333), channel_id=1, source_target_pairs={{0,1},{1,0},{2,3},{3,2},{4,5},{5,4},{6,7},{7,6},{8,9},{9,8},{10,11... | collective-permute-start | bytes 1572872 | tf_op jit(solution)/shard_map/ppermute | solution.py:299
  96.1 4.6 %collective-permute-start.15 = (bf16[256,1024]{1,0:T(8,128)(2,1)S(1)}, bf16[256,1024]{1,0:T(8,128)(2,1)S(1)}, u32[]{:S(2)}, u32[]{:S(2)}) collective-permute-start(bf16[256,1024]{1,0:T(8,128)(2,1)S(1)} %get-tuple-element.335), channel_id=1, source_target_pairs={{0,1},{1,0},{2,3},{3,2},{4,5},{5,4},{6,7},{7,6},{8,9},{9,8},{10,11... | collective-permute-start | bytes 1572872 | tf_op jit(solution)/shard_map/ppermute | solution.py:299
  96.6 25.4 %collective-permute-start.20 = (bf16[512,1024]{1,0:T(8,128)(2,1)}, bf16[512,1024]{1,0:T(8,128)(2,1)}, u32[]{:S(2)}, u32[]{:S(2)}) collective-permute-start(bf16[512,1024]{1,0:T(8,128)(2,1)} %add_convert_fusion.4), channel_id=1, source_target_pairs={{0,8},{4,12},{8,0},{12,4},{16,24},{20,28},{24,16},{28,20},{1,9},{5... | collective-permute-start | bytes 3145736 | tf_op jit(solution)/shard_map/ppermute | solution.py:299
  105.0 4.8 %collective-permute-start.18 = (bf16[256,1024]{1,0:T(8,128)(2,1)}, bf16[256,1024]{1,0:T(8,128)(2,1)}, u32[]{:S(2)}, u32[]{:S(2)}) collective-permute-start(bf16[256,1024]{1,0:T(8,128)(2,1)} %get-tuple-element.240), channel_id=1, source_target_pairs={{0,1},{1,0},{2,3},{3,2},{4,5},{5,4},{6,7},{7,6},{8,9},{9,8},{10,11... | collective-permute-start | bytes 1572872 | tf_op jit(solution)/shard_map/ppermute | solution.py:299
  105.0 14.6 %collective-permute-start.17 = (bf16[256,1024]{1,0:T(8,128)(2,1)}, bf16[256,1024]{1,0:T(8,128)(2,1)}, u32[]{:S(2)}, u32[]{:S(2)}) collective-permute-start(bf16[256,1024]{1,0:T(8,128)(2,1)} %get-tuple-element.240), channel_id=1, source_target_pairs={{0,2},{1,3},{2,0},{3,1},{4,6},{5,7},{6,4},{7,5},{8,10},{9,11},{10,... | collective-permute-start | bytes 1572872 | tf_op jit(solution)/shard_map/ppermute | solution.py:299
  122.0 3.5 %collective-permute-start.21 = (bf16[256,1024]{1,0:T(8,128)(2,1)}, bf16[256,1024]{1,0:T(8,128)(2,1)S(1)}, u32[]{:S(2)}, u32[]{:S(2)}) collective-permute-start(bf16[256,1024]{1,0:T(8,128)(2,1)} %collective-permute-done.17), channel_id=1, source_target_pairs={{0,1},{1,0},{2,3},{3,2},{4,5},{5,4},{6,7},{7,6},{8,9},{9,8},{10,11... | collective-permute-start | bytes 1572872 | tf_op jit(solution)/shard_map/ppermute | solution.py:299
  126.6 15.2 %collective-permute-start.22 = (bf16[256,1024]{1,0:T(8,128)(2,1)S(1)}, bf16[256,1024]{1,0:T(8,128)(2,1)S(1)}, u32[]{:S(2)}, u32[]{:S(2)}) collective-permute-start(bf16[256,1024]{1,0:T(8,128)(2,1)S(1)} %constant_dynamic-slice_fusion.7), channel_id=1, source_target_pairs={{0,8},{4,12},{8,0},{12,4},{16,24},{20,28},{24,16},{28,20},{1,9},{5... | collective-permute-start | bytes 1572872 | tf_op jit(solution)/shard_map/ppermute | solution.py:299
  128.2 14.8 %collective-permute-start.23 = (bf16[256,1024]{1,0:T(8,128)(2,1)S(1)}, bf16[256,1024]{1,0:T(8,128)(2,1)S(1)}, u32[]{:S(2)}, u32[]{:S(2)}) collective-permute-start(bf16[256,1024]{1,0:T(8,128)(2,1)S(1)} %constant_dynamic-slice_fusion.6), channel_id=1, source_target_pairs={{0,4},{4,0},{8,12},{12,8},{16,20},{20,16},{24,28},{28,24},{1,5},{5... | collective-permute-start | bytes 1572872 | tf_op jit(solution)/shard_map/ppermute | solution.py:299
  131.9 44.5 %collective-permute-start.31 = (bf16[128,1024]{1,0:T(8,128)(2,1)}, bf16[128,1024]{1,0:T(8,128)(2,1)}, u32[]{:S(2)}, u32[]{:S(2)}) collective-permute-start(bf16[128,1024]{1,0:T(8,128)(2,1)} %fusion), channel_id=1, source_target_pairs={{0,4},{4,0},{8,12},{12,8},{16,20},{20,16},{24,28},{28,24},{1,5},{5... | collective-permute-start | bytes 786440 | tf_op jit(solution)/shard_map/ppermute | solution.py:299
  147.7 28.7 %collective-permute-start.29 = (bf16[128,1024]{1,0:T(8,128)(2,1)}, bf16[128,1024]{1,0:T(8,128)(2,1)}, u32[]{:S(2)}, u32[]{:S(2)}) collective-permute-start(bf16[128,1024]{1,0:T(8,128)(2,1)} %constant_dynamic-slice_fusion.5), channel_id=1, source_target_pairs={{0,16},{4,20},{8,24},{12,28},{16,0},{20,4},{24,8},{28,12},{1,17},{... | collective-permute-start | bytes 786440 | tf_op jit(solution)/shard_map/ppermute | solution.py:299
  150.4 26.0 %collective-permute-start.30 = (bf16[128,1024]{1,0:T(8,128)(2,1)}, bf16[128,1024]{1,0:T(8,128)(2,1)}, u32[]{:S(2)}, u32[]{:S(2)}) collective-permute-start(bf16[128,1024]{1,0:T(8,128)(2,1)} %constant_dynamic-slice_fusion.4), channel_id=1, source_target_pairs={{0,16},{4,20},{8,24},{12,28},{16,0},{20,4},{24,8},{28,12},{1,17},{... | collective-permute-start | bytes 786440 | tf_op jit(solution)/shard_map/ppermute | solution.py:299
  150.8 3.5 %collective-permute-start.24 = (bf16[256,1024]{1,0:T(8,128)(2,1)S(1)}, bf16[256,1024]{1,0:T(8,128)(2,1)S(1)}, u32[]{:S(2)}, u32[]{:S(2)}) collective-permute-start(bf16[256,1024]{1,0:T(8,128)(2,1)S(1)} %slice.163), channel_id=1, source_target_pairs={{0,1},{1,0},{2,3},{3,2},{4,5},{5,4},{6,7},{7,6},{8,9},{9,8},{10,11... | collective-permute-start | bytes 1572872 | tf_op jit(solution)/shard_map/ppermute | solution.py:299
  155.6 4.0 %collective-permute-start.26 = (bf16[256,1024]{1,0:T(8,128)(2,1)S(1)}, bf16[256,1024]{1,0:T(8,128)(2,1)S(1)}, u32[]{:S(2)}, u32[]{:S(2)}) collective-permute-start(bf16[256,1024]{1,0:T(8,128)(2,1)S(1)} %get-tuple-element.331), channel_id=1, source_target_pairs={{0,1},{1,0},{2,3},{3,2},{4,5},{5,4},{6,7},{7,6},{8,9},{9,8},{10,11... | collective-permute-start | bytes 1572872 | tf_op jit(solution)/shard_map/ppermute | solution.py:299
  156.1 13.9 %collective-permute-start.25 = (bf16[256,1024]{1,0:T(8,128)(2,1)S(1)}, bf16[256,1024]{1,0:T(8,128)(2,1)S(1)}, u32[]{:S(2)}, u32[]{:S(2)}) collective-permute-start(bf16[256,1024]{1,0:T(8,128)(2,1)S(1)} %add_convert_fusion.15), channel_id=1, source_target_pairs={{0,2},{1,3},{2,0},{3,1},{4,6},{5,7},{6,4},{7,5},{8,10},{9,11},{10,... | collective-permute-start | bytes 1572872 | tf_op jit(solution)/shard_map/ppermute | solution.py:299
  159.6 19.6 %collective-permute-start.32 = (bf16[512,768]{1,0:T(8,128)(2,1)}, bf16[512,768]{1,0:T(8,128)(2,1)}, u32[]{:S(2)}, u32[]{:S(2)}) collective-permute-start(bf16[512,768]{1,0:T(8,128)(2,1)} %add_convert_fusion.8), channel_id=1, source_target_pairs={{0,4},{4,0},{8,12},{12,8},{16,20},{20,16},{24,28},{28,24},{1,5},{5... | collective-permute-start | bytes 2359304 | tf_op jit(solution)/shard_map/ppermute | solution.py:299
  172.4 3.9 %collective-permute-start.28 = (f32[6,1024]{1,0:T(8,128)S(1)}, f32[6,1024]{1,0:T(8,128)S(1)}, u32[]{:S(2)}, u32[]{:S(2)}) collective-permute-start(f32[6,1024]{1,0:T(8,128)S(1)} %add.311), channel_id=1, source_target_pairs={{0,2},{1,3},{2,0},{3,1},{4,6},{5,7},{6,4},{7,5},{8,10},{9,11},{10,... | collective-permute-start | bytes 73736 | tf_op jit(solution)/shard_map/ppermute | solution.py:299
  186.0 26.7 %collective-permute-start.36 = (bf16[256,768]{1,0:T(8,128)(2,1)}, bf16[256,768]{1,0:T(8,128)(2,1)}, u32[]{:S(2)}, u32[]{:S(2)}) collective-permute-start(bf16[256,768]{1,0:T(8,128)(2,1)} %constant_dynamic-slice_fusion.2), channel_id=1, source_target_pairs={{0,8},{4,12},{8,0},{12,4},{16,24},{20,28},{24,16},{28,20},{1,9},{5... | collective-permute-start | bytes 1179656 | tf_op jit(solution)/shard_map/ppermute | solution.py:299
  186.5 23.5 %collective-permute-start.35 = (bf16[64,1024]{1,0:T(8,128)(2,1)S(1)}, bf16[64,1024]{1,0:T(8,128)(2,1)S(1)}, u32[]{:S(2)}, u32[]{:S(2)}) collective-permute-start(bf16[64,1024]{1,0:T(8,128)(2,1)S(1)} %constant_dynamic-slice_fusion.3), channel_id=1, source_target_pairs={{0,8},{4,12},{8,0},{12,4},{16,24},{20,28},{24,16},{28,20},{1,9},{5... | collective-permute-start | bytes 393224 | tf_op jit(solution)/shard_map/ppermute | solution.py:299
  188.1 21.9 %collective-permute-start.33 = (bf16[128,1024]{1,0:T(8,128)(2,1)}, bf16[128,1024]{1,0:T(8,128)(2,1)S(1)}, u32[]{:S(2)}, u32[]{:S(2)}) collective-permute-start(bf16[128,1024]{1,0:T(8,128)(2,1)} %add_convert_fusion.23), channel_id=1, source_target_pairs={{0,16},{4,20},{8,24},{12,28},{16,0},{20,4},{24,8},{28,12},{1,17},{... | collective-permute-start | bytes 786440 | tf_op jit(solution)/shard_map/ppermute | solution.py:299
  190.7 22.0 %collective-permute-start.34 = (bf16[128,1024]{1,0:T(8,128)(2,1)}, bf16[128,1024]{1,0:T(8,128)(2,1)S(1)}, u32[]{:S(2)}, u32[]{:S(2)}) collective-permute-start(bf16[128,1024]{1,0:T(8,128)(2,1)} %add_convert_fusion.22), channel_id=1, source_target_pairs={{0,16},{4,20},{8,24},{12,28},{16,0},{20,4},{24,8},{28,12},{1,17},{... | collective-permute-start | bytes 786440 | tf_op jit(solution)/shard_map/ppermute | solution.py:299
  192.2 40.2 %collective-permute-start.37 = (bf16[256,1024]{1,0:T(8,128)(2,1)S(1)}, bf16[256,1024]{1,0:T(8,128)(2,1)S(1)}, u32[]{:S(2)}, u32[]{:S(2)}) collective-permute-start(bf16[256,1024]{1,0:T(8,128)(2,1)S(1)} %add_convert_fusion.12), channel_id=1, source_target_pairs={{0,2},{1,3},{2,0},{3,1},{4,6},{5,7},{6,4},{7,5},{8,10},{9,11},{10,... | collective-permute-start | bytes 1572872 | tf_op jit(solution)/shard_map/ppermute | solution.py:299
  214.2 18.3 %collective-permute-start.38 = (bf16[256,1024]{1,0:T(8,128)(2,1)S(1)}, bf16[256,1024]{1,0:T(8,128)(2,1)S(1)}, u32[]{:S(2)}, u32[]{:S(2)}) collective-permute-start(bf16[256,1024]{1,0:T(8,128)(2,1)S(1)} %maximum_select_fusion.6), channel_id=1, source_target_pairs={{0,8},{4,12},{8,0},{12,4},{16,24},{20,28},{24,16},{28,20},{1,9},{5... | collective-permute-start | bytes 1572872 | tf_op jit(solution)/shard_map/ppermute | solution.py:299
  214.5 18.0 %collective-permute-start.39 = (bf16[256,1024]{1,0:T(8,128)(2,1)S(1)}, bf16[256,1024]{1,0:T(8,128)(2,1)S(1)}, u32[]{:S(2)}, u32[]{:S(2)}) collective-permute-start(bf16[256,1024]{1,0:T(8,128)(2,1)S(1)} %maximum_select_fusion.7), channel_id=1, source_target_pairs={{0,4},{4,0},{8,12},{12,8},{16,20},{20,16},{24,28},{28,24},{1,5},{5... | collective-permute-start | bytes 1572872 | tf_op jit(solution)/shard_map/ppermute | solution.py:299
  215.1 17.3 %collective-permute-start.41 = (bf16[128,768]{1,0:T(8,128)(2,1)S(1)}, bf16[128,768]{1,0:T(8,128)(2,1)S(1)}, u32[]{:S(2)}, u32[]{:S(2)}) collective-permute-start(bf16[128,768]{1,0:T(8,128)(2,1)S(1)} %constant_dynamic-slice_fusion), channel_id=1, source_target_pairs={{0,16},{4,20},{8,24},{12,28},{16,0},{20,4},{24,8},{28,12},{1,17},{... | collective-permute-start | bytes 589832 | tf_op jit(solution)/shard_map/ppermute | solution.py:299
  217.9 8.9 %collective-permute-start.42 = (f32[7808]{0:T(1024)S(1)}, f32[7808]{0:T(1024)S(1)}, u32[]{:S(2)}, u32[]{:S(2)}) collective-permute-start(f32[7808]{0:T(1024)S(1)} %copy-done.67), channel_id=1, source_target_pairs={{0,4},{4,0},{8,12},{12,8},{16,20},{20,16},{24,28},{28,24},{1,5},{5... | collective-permute-start | bytes 93704 | tf_op jit(solution)/shard_map/ppermute | solution.py:299
  226.8 5.7 %collective-permute-start.40 = (bf16[32,1024]{1,0:T(8,128)(2,1)S(1)}, bf16[32,1024]{1,0:T(8,128)(2,1)S(1)}, u32[]{:S(2)}, u32[]{:S(2)}) collective-permute-start(bf16[32,1024]{1,0:T(8,128)(2,1)S(1)} %constant_dynamic-slice_fusion.1), channel_id=1, source_target_pairs={{0,16},{4,20},{8,24},{12,28},{16,0},{20,4},{24,8},{28,12},{1,17},{... | collective-permute-start | bytes 196616 | tf_op jit(solution)/shard_map/ppermute | solution.py:299
  233.6 28.9 %collective-permute-start.43 = (bf16[512,1024]{1,0:T(8,128)(2,1)S(1)}, bf16[512,1024]{1,0:T(8,128)(2,1)S(1)}, u32[]{:S(2)}, u32[]{:S(2)}) collective-permute-start(bf16[512,1024]{1,0:T(8,128)(2,1)S(1)} %maximum_select_fusion.3), channel_id=1, source_target_pairs={{0,4},{4,0},{8,12},{12,8},{16,20},{20,16},{24,28},{28,24},{1,5},{5... | collective-permute-start | bytes 3145736 | tf_op jit(solution)/shard_map/ppermute | solution.py:299
  234.5 28.0 %collective-permute-start.44 = (bf16[512,1024]{1,0:T(8,128)(2,1)S(1)}, bf16[512,1024]{1,0:T(8,128)(2,1)S(1)}, u32[]{:S(2)}, u32[]{:S(2)}) collective-permute-start(bf16[512,1024]{1,0:T(8,128)(2,1)S(1)} %maximum_select_fusion.4), channel_id=1, source_target_pairs={{0,8},{4,12},{8,0},{12,4},{16,24},{20,28},{24,16},{28,20},{1,9},{5... | collective-permute-start | bytes 3145736 | tf_op jit(solution)/shard_map/ppermute | solution.py:299
  234.5 27.9 %collective-permute-start.46 = (bf16[128,768]{1,0:T(8,128)(2,1)S(1)}, bf16[128,768]{1,0:T(8,128)(2,1)S(1)}, u32[]{:S(2)}, u32[]{:S(2)}) collective-permute-start(bf16[128,768]{1,0:T(8,128)(2,1)S(1)} %add_convert_fusion.24), channel_id=1, source_target_pairs={{0,16},{4,20},{8,24},{12,28},{16,0},{20,4},{24,8},{28,12},{1,17},{... | collective-permute-start | bytes 589832 | tf_op jit(solution)/shard_map/ppermute | solution.py:299
  236.5 26.0 %collective-permute-start.45 = (bf16[32,1024]{1,0:T(8,128)(2,1)S(1)}, bf16[32,1024]{1,0:T(8,128)(2,1)S(1)}, u32[]{:S(2)}, u32[]{:S(2)}) collective-permute-start(bf16[32,1024]{1,0:T(8,128)(2,1)S(1)} %add_convert_fusion.26), channel_id=1, source_target_pairs={{0,16},{4,20},{8,24},{12,28},{16,0},{20,4},{24,8},{28,12},{1,17},{... | collective-permute-start | bytes 196616 | tf_op jit(solution)/shard_map/ppermute | solution.py:299
  237.5 25.0 %collective-permute-start.47 = (f32[7808]{0:T(1024)S(1)}, f32[7808]{0:T(1024)S(1)}, u32[]{:S(2)}, u32[]{:S(2)}) collective-permute-start(f32[7808]{0:T(1024)S(1)} %add.330), channel_id=1, source_target_pairs={{0,8},{4,12},{8,0},{12,4},{16,24},{20,28},{24,16},{28,20},{1,9},{5... | collective-permute-start | bytes 93704 | tf_op jit(solution)/shard_map/ppermute | solution.py:299
  262.6 13.1 %collective-permute-start.49 = (bf16[256,768]{1,0:T(8,128)(2,1)S(1)}, bf16[256,768]{1,0:T(8,128)(2,1)S(1)}, u32[]{:S(2)}, u32[]{:S(2)}) collective-permute-start(bf16[256,768]{1,0:T(8,128)(2,1)S(1)} %maximum_select_fusion.9), channel_id=1, source_target_pairs={{0,8},{4,12},{8,0},{12,4},{16,24},{20,28},{24,16},{28,20},{1,9},{5... | collective-permute-start | bytes 1179656 | tf_op jit(solution)/shard_map/ppermute | solution.py:299
  263.5 8.6 %collective-permute-start.50 = (f32[7808]{0:T(1024)S(1)}, f32[7808]{0:T(1024)S(1)}, u32[]{:S(2)}, u32[]{:S(2)}) collective-permute-start(f32[7808]{0:T(1024)S(1)} %add.331), channel_id=1, source_target_pairs={{0,16},{4,20},{8,24},{12,28},{16,0},{20,4},{24,8},{28,12},{1,17},{... | collective-permute-start | bytes 93704 | tf_op jit(solution)/shard_map/ppermute | solution.py:299
  265.6 10.1 %collective-permute-start.48 = (bf16[64,1024]{1,0:T(8,128)(2,1)S(1)}, bf16[64,1024]{1,0:T(8,128)(2,1)S(1)}, u32[]{:S(2)}, u32[]{:S(2)}) collective-permute-start(bf16[64,1024]{1,0:T(8,128)(2,1)S(1)} %maximum_select_fusion.11), channel_id=1, source_target_pairs={{0,8},{4,12},{8,0},{12,4},{16,24},{20,28},{24,16},{28,20},{1,9},{5... | collective-permute-start | bytes 393224 | tf_op jit(solution)/shard_map/ppermute | solution.py:299
  277.9 24.2 %collective-permute-start.52 = (bf16[512,768]{1,0:T(8,128)(2,1)S(1)}, bf16[512,768]{1,0:T(8,128)(2,1)S(1)}, u32[]{:S(2)}, u32[]{:S(2)}) collective-permute-start(bf16[512,768]{1,0:T(8,128)(2,1)S(1)} %maximum_select_fusion.5), channel_id=1, source_target_pairs={{0,4},{4,0},{8,12},{12,8},{16,20},{20,16},{24,28},{28,24},{1,5},{5... | collective-permute-start | bytes 2359304 | tf_op jit(solution)/shard_map/ppermute | solution.py:299
  280.8 21.3 %collective-permute-start.51 = (bf16[128,1024]{1,0:T(8,128)(2,1)S(1)}, bf16[128,1024]{1,0:T(8,128)(2,1)}, u32[]{:S(2)}, u32[]{:S(2)}) collective-permute-start(bf16[128,1024]{1,0:T(8,128)(2,1)S(1)} %maximum_select_fusion.10), channel_id=1, source_target_pairs={{0,4},{4,0},{8,12},{12,8},{16,20},{20,16},{24,28},{28,24},{1,5},{5... | collective-permute-start | bytes 786440 | tf_op jit(solution)/shard_map/ppermute | solution.py:299
  (90 other events, 603.9 us)

commit v5 on v4

--- a/solution.py
+++ b/solution.py
@@ -205,18 +205,21 @@
     return result[0], result[1 : 1 + parts], result[1 + parts :]
 
 
-def mlp_kernel(x_ref, grad_ref, up_ref, bias_ref, down_ref, act_ref, slope_ref, back_ref):
+def mlp_kernel(x_ref, grad_ref, up_ref, bias_ref, down_ref, act_ref, slope_ref, back_ref, *share_ref):
     pre = dot_nn(x_ref[...], up_ref[...]) + bias_ref[...]
     upstream = dot_nt(grad_ref[...], down_ref[...])
     cdf = 0.5 + 0.5 * lax.erf(pre * (0.5**0.5))
-    act_ref[...] = (pre * cdf).astype(BF16)
+    act = (pre * cdf).astype(BF16)
+    act_ref[...] = act
+    if share_ref:
+        share_ref[0][...] = dot_nn(act, down_ref[...]).astype(BF16)
     density = jnp.exp(-0.5 * pre * pre) * 0.3989422804014327
     slope = (upstream * (cdf + pre * density)).astype(BF16)
     slope_ref[...] = slope
     back_ref[...] = dot_nt(slope, up_ref[...]).astype(BF16)
 
 
-def mlp_both(x, grad, up, bias, down, tile=256):
+def mlp_both(x, grad, up, bias, down, share, tile=256):
     count, width = x.shape
     hidden = up.shape[1]
     tile = min(tile, count)
@@ -234,12 +237,12 @@
         out_specs=[
             pl.BlockSpec((tile, hidden), lambda i: (i, 0)),
             pl.BlockSpec((tile, hidden), lambda i: (i, 0)),
-            pl.BlockSpec((tile, width), lambda i: (i, 0)),
+            *[pl.BlockSpec((tile, width), lambda i: (i, 0))] * (1 + share),
         ],
         out_shape=[
             jax.ShapeDtypeStruct((count, hidden), BF16),
             jax.ShapeDtypeStruct((count, hidden), BF16),
-            jax.ShapeDtypeStruct((count, width), BF16),
+            *[jax.ShapeDtypeStruct((count, width), BF16)] * (1 + share),
         ],
         cost_estimate=LIGHT,
         compiler_params=pltpu.CompilerParams(vmem_limit_bytes=24 * 2**20),
@@ -363,10 +366,11 @@
             )
         self.at += 1
         if self.at < len(self.order):
-            half = self.held.shape[0] // 2
-            top = jnp.where(self.high(self.steps[self.at]), half, 0)
-            self.send = lax.dynamic_slice_in_dim(self.held, half - top, half, 0)
-            self.held = lax.dynamic_slice_in_dim(self.held, top, half, 0)
+            rows, width = self.held.shape
+            halves = self.held.reshape(2, rows // 2, width)
+            place = self.high(self.steps[self.at]).astype(jnp.int32)
+            self.send = lax.dynamic_index_in_dim(halves, 1 - place, 0, False)
+            self.held = lax.dynamic_index_in_dim(halves, place, 0, False)
         else:
             self.send = self.held
 
@@ -500,14 +504,16 @@
 
         far_own = swap(mlp_input, "mp", n_mp, far_bit)
         mlp_near = gather_near(mlp_input, n_mp)
-        act_near, slope_near, back_near = mlp_both(
-            mlp_near, grad_near, expand_weight, expand_bias, reduce_weight
-        )
-        far_own, act_near, slope_near, back_near = tie(far_own, act_near, slope_near, back_near)
+        act_near, slope_near, back_near, share_near = mlp_both(
+            mlp_near, grad_near, expand_weight, expand_bias, reduce_weight, True
+        )
+        far_own, act_near, slope_near, back_near, share_near = tie(
+            far_own, act_near, slope_near, back_near, share_near
+        )
         mlp_far = gather_near(far_own, n_mp)
         sum_near = scatter_near(cut(back_near), n_mp)
-        act_far, slope_far, back_far = mlp_both(
-            mlp_far, grad_far, expand_weight, expand_bias, reduce_weight
+        act_far, slope_far, back_far, share_far = mlp_both(
+            mlp_far, grad_far, expand_weight, expand_bias, reduce_weight, True
         )
         act_far, slope_far, back_far, *sum_near = tie(act_far, slope_far, back_far, *sum_near)
         swapped = dp_bits[1:2] + dp_bits[:1] + dp_bits[2:]
@@ -527,8 +533,8 @@
         )
         reduce_sum.keep([(act_near, grad_near), (act_far, grad_far)])
         expand_sum.keep([(mlp_near, slope_near), (mlp_far, slope_far)])
-        out_far = scatter_near(cut(dot_nn(act_far, reduce_weight)), n_mp)
-        out_near = scatter_near(cut(dot_nn(act_near, reduce_weight)), n_mp)
+        out_far = scatter_near(cut(share_far), n_mp)
+        out_near = scatter_near(cut(share_near), n_mp)
         held = [reduce_sum.held, expand_sum.held]
         arrived, *held = tie(arrived, *held, *out_far, *out_near)
         reduce_sum.held, expand_sum.held = held[:2]
@@ -567,10 +573,11 @@
             (key_part, value_part),
             True,
         )
-        query_far, query_near, branch_far, normed_grad_two, branch_grad, *out_far = await_all(
-            (query_far, query_near, branch_far, normed_grad_two, branch_grad, *out_far),
-            [reduce_sum, expand_sum],
-        )
+        tied = (query_near, branch_far, normed_grad_two, branch_grad, grad_low)
+        tied = (query_far, *tied, slope_near, slope_far, *out_far)
+        tied = await_all(tied, [reduce_sum, expand_sum])
+        query_far, query_near, branch_far, normed_grad_two, branch_grad, grad_low = tied[:6]
+        slope_near, slope_far, *out_far = tied[6:]
         qkv_far = jnp.concatenate([query_far, key_grads[1], value_grads[1]], 1)
         sum_far = scatter_near(cut(dot_nt(qkv_far, weight_wide)), n_mp)
         qkv_near = jnp.concatenate([query_near, key_grads[0], value_grads[0]], 1)
@@ -595,7 +602,7 @@
                     jnp.sum(normed_grad_two * normed_two, 0),
                     jnp.sum(normed_grad_two, 0),
                     jnp.sum(branch_grad, 0, dtype=F32),
-                    jnp.sum(grad_out, 0),
+                    jnp.sum(grad_low, 0, dtype=F32),
                     jnp.sum(normed_grad_one * normed_one, 0),
                     jnp.sum(normed_grad_one, 0),
                 ]
@@ -618,22 +625,37 @@
                 ]
             ),
         )
-        sums = [reduce_sum, expand_sum, output_sum, input_sum]
+        sums = [reduce_sum, expand_sum, input_sum, output_sum]
         token, small.send = await_all((input_gradient, small.send), sums)
-        token, *out_far = start_all((token, *out_far), sums)
+        token, *out_far = start_all((token, *out_far), sums[:2])
+        token, *out_far = start_all((token, *out_far), sums[2:])
         token, out_far = tie(token, add_up(out_far).astype(BF16))
         out_far = swap(out_far, "mp", n_mp, far_bit)
-        (token,) = await_all((token,), sums)
-        sums.append(small)
-        (token,) = start_all((token,), sums)
-        token, out_far = await_all((token, out_far), sums)
-        block_output = (
-            hidden_res + (add_up(out_near) + out_far.astype(F32)) + reduce_bias
-        ).astype(BF16)
-        while any(s.busy() for s in sums):
-            sums = [s for s in sums if s.busy()]
-            (token,) = start_all((token,), sums)
-            (token,) = await_all((token,), sums)
+        quick = [input_sum, output_sum, small]
+        slow = [reduce_sum, expand_sum]
+        waiting = {"f": quick, "s": slow, "r": slow, "e": [], "R": slow[:1], "E": slow[1:]}
+        sending = {"f": quick, "s": slow, "r": slow[:1], "e": slow[1:], "R": [], "E": []}
+        flying = list(sums)
+        totals = {}
+        turns = "fsfsffsf" if len(dp_bits) == 3 else "fs" * 2 * len(dp_bits)
+        for n, turn in enumerate(turns):
+            if n == 4:
+                block_output = (
+                    hidden_res + (add_up(out_near) + out_far.astype(F32)) + reduce_bias
+                ).astype(BF16)
+                token, block_output = tie(token, block_output)
+            landing = [s for s in waiting[turn] if s in flying]
+            token, out_far = await_all((token, out_far), landing)
+            flying = [s for s in flying if s not in landing]
+            leaving = [s for s in sending[turn] if s.busy() and s not in flying]
+            token, out_far = start_all((token, out_far), leaving)
+            flying += leaving
+            for s in slow:
+                if not (s.busy() or small.busy() or s in totals):
+                    factor = lax.rsqrt(small.held[-1])
+                    token, totals[s] = tie(token, s.held.astype(F32) * factor)
+        if any(s.busy() for s in sums) or flying:
+            raise ValueError("unfinished sums")
         input_gradient = token
 
         total = small.held
@@ -655,9 +677,9 @@
             rows[2],
             rows[0],
             rows[1],
-            expand_sum.held.astype(F32) * factor,
+            totals[expand_sum],
             rest[2 * local_width : 2 * local_width + hidden] * factor,
-            reduce_sum.held.astype(F32) * factor,
+            totals[reduce_sum],
             rows[3],
         )
     return per_device

time: 312 us -> 294 us (0.942)
  waiting for transfers between devices: 118 us -> 97.4 us
  starting transfers between devices: 49.6 us -> 56.6 us
  other arithmetic: 50.5 us -> 44.6 us
    ppermute x53, waiting for transfers between devices: 118 us -> 97.4 us  [swap(): return lax.ppermute(array, axis, [(i, i ^ bit) for i in range(size)])]
    ppermute x53, starting transfers between devices: 49.6 us -> 56.6 us  [swap(): return lax.ppermute(array, axis, [(i, i ^ bit) for i in range(size)])]
    unnamed x177 -> x175, local copies, waits for them, and re-layouts: 10.8 us -> 11.7 us
  transfers between devices with their start and end apart: 53 -> 53, of which waited for: 20 -> 21; matrix products, arithmetic and copies ran while one was open for 22% -> 23% of each run, Pallas kernels for 11% -> 13%
where the time goes in v5:
time: 294 us; the launch traced here: 289 us
  waiting for transfers between devices  97.4 us (33%)
  starting transfers between devices  56.6 us (19%)
  other arithmetic  44.6 us (15%)
  Pallas kernels  37.1 us (13%)
  matrix products  25.2 us (9%)
  local copies, waits for them, and re-layouts  22.6 us (8%)
  between operations  5.34 us (2%)
    ppermute x53, waiting for transfers between devices, swap(): return lax.ppermute(array, axis, [(i, i ^ bit) for i in range(size)])  97.4 us
    ppermute x53, starting transfers between devices, swap(): return lax.ppermute(array, axis, [(i, i ^ bit) for i in range(size)])  56.6 us
    dot_general x16, matrix products, dot_tn(): lax.dot_general(a, b, (((0,), (0,)), ((), ())), preferred_element_type=F32)  18.3 us
    pallas_call x2, Pallas kernels, attend_back(): pl.pallas_call(functools.partial(attend_back_kernel, parts, first, last),...  16.5 us
    unnamed x175, local copies, waits for them, and re-layouts  11.7 us
    pallas_call x2, Pallas kernels, attend_forward(): pl.pallas_call(functools.partial(attend_kernel, len(halves)), grid=(pairs...  10.8 us
    pallas_call x2, Pallas kernels, mlp_both(): pl.pallas_call(mlp_kernel, grid=(count // tile,), in_specs=[pl.BlockSpec(...  9.78 us
    mul x2, other arithmetic, per_device(): token, totals[s] = tie(token, s.held.astype(F32) * factor)  9.6 us
  transfers between devices with their start and end apart: 53, of which 21 were waited for; matrix products, arithmetic and copies ran while one was open for 23% of the time, Pallas kernels for 13%

profile of v5, /device:TPU:0, one launch (start us, length us, event | category | flops | bytes accessed | tf_op | source)
XLA Modules:
  0.0 288.9 jit_solution(4310603597688162497)
XLA Ops:
  2.9 1.9 multiply_sine_fusion
  8.8 2.6 collective-permute-start
  14.2 9.7 %collective-permute-done = bf16[256,1024]{1,0:T(8,128)(2,1)S(1)} collective-permute-done((bf16[256,1024]{1,0:T(8,128)(2,1)S(1)}, bf16[256,1024]{1,0:T(8,128)(2,1)S(1)}, u32[]{:S(2)}, u32[]{:S(2)}) %collective-permute-start) | collective-permute-done | bytes 524320 | tf_op jit(solution)/shard_map/ppermute | solution.py:302
  24.2 1.8 collective-permute-start.7
  28.1 5.5 %attend_forward.2 = (bf16[512,256]{1,0:T(8,128)(2,1)S(1)}, f32[2,8,512]{2,1,0:T(8,128)S(1)}) custom-call(bf16[512,768]{1,0:T(8,128)(2,1)S(1)} %add_convert_fusion.9.q_ref.refs_1_.refs_3_, bf16[512,128]{1,0:T(8,128)(2,1)S(1)} %fusion.33.pick_ref, bf16[512,768]{1,0:T(8,128)(2,1)S(1)} %add_convert_fusion.10.refs_0_.refs_2_.q_ref, ...), custom_call_target="tpu_custom_call" | custom-call | flops 1024 | bytes 1024 | tf_op jit(solution)/shard_map/attend_forward/pallas_call | solution.py:73
  35.0 3.6 %collective-permute-done.7 = bf16[256,1024]{1,0:T(8,128)(2,1)S(1)} collective-permute-done((bf16[256,1024]{1,0:T(8,128)(2,1)S(1)}, bf16[256,1024]{1,0:T(8,128)(2,1)S(1)}, u32[]{:S(2)}, u32[]{:S(2)}) %collective-permute-start.7) | collective-permute-done | bytes 524320 | tf_op jit(solution)/shard_map/ppermute | solution.py:302
  38.8 1.8 collective-permute-start.5
  40.6 5.3 %attend_forward.3 = (bf16[512,256]{1,0:T(8,128)(2,1)S(1)}, f32[2,8,512]{2,1,0:T(8,128)S(1)}) custom-call(bf16[512,768]{1,0:T(8,128)(2,1)S(1)} %add_convert_fusion.10.refs_0_.refs_2_.q_ref, bf16[512,128]{1,0:T(8,128)(2,1)S(1)} %fusion.32.pick_ref, bf16[512,768]{1,0:T(8,128)(2,1)S(1)} %add_convert_fusion.10.refs_0_.refs_2_.q_ref, ...), custom_call_target="tpu_custom_call" | custom-call | flops 1024 | bytes 1024 | tf_op jit(solution)/shard_map/attend_forward/pallas_call | solution.py:73
  48.3 4.9 %collective-permute-done.5 = bf16[256,1024]{1,0:T(8,128)(2,1)S(1)} collective-permute-done((bf16[256,1024]{1,0:T(8,128)(2,1)S(1)}, bf16[256,1024]{1,0:T(8,128)(2,1)S(1)}, u32[]{:S(2)}, u32[]{:S(2)}) %collective-permute-start.5) | collective-permute-done | bytes 524320 | tf_op jit(solution)/shard_map/ppermute | solution.py:302
  54.8 1.8 collective-permute-start.9
  57.5 4.8 %mlp_both.2 = (bf16[512,1024]{1,0:T(8,128)(2,1)S(1)}, bf16[512,1024]{1,0:T(8,128)(2,1)S(1)}, bf16[512,1024]{1,0:T(8,128)(2,1)S(1)}, bf16[512,1024]{1,0:T(8,128)(2,1)S(1)}) custom-call(bf16[512,1024]{1,0:T(8,128)(2,1)S(1)} %pad_maximum_fusion.3.x_ref, bf16[512,1024]{1,0:T(8,128)(2,1)S(1)} %pad_maximum_fusion.5.grad_ref, bf16[1024,1024]{1,0:T(8,128)(2,1)S(1)} %copy-done.8, ...), custom_call_target="tpu_custom_call" | custom-call | flops 1024 | bytes 1024 | tf_op jit(solution)/shard_map/mlp_both/pallas_call | solution.py:227
  65.2 4.0 %collective-permute-done.9 = bf16[256,1024]{1,0:T(8,128)(2,1)} collective-permute-done((bf16[256,1024]{1,0:T(8,128)(2,1)S(1)}, bf16[256,1024]{1,0:T(8,128)(2,1)}, u32[]{:S(2)}, u32[]{:S(2)}) %collective-permute-start.9) | collective-permute-done | bytes 524320 | tf_op jit(solution)/shard_map/ppermute | solution.py:302
  70.8 2.2 fusion.72
  76.8 5.0 %mlp_both.3 = (bf16[512,1024]{1,0:T(8,128)(2,1)S(1)}, bf16[512,1024]{1,0:T(8,128)(2,1)S(1)}, bf16[512,1024]{1,0:T(8,128)(2,1)S(1)}, bf16[512,1024]{1,0:T(8,128)(2,1)S(1)}) custom-call(bf16[512,1024]{1,0:T(8,128)(2,1)S(1)} %constant_dynamic-update-slice_fusion.2.x_ref, bf16[512,1024]{1,0:T(8,128)(2,1)S(1)} %copy-done.2, bf16[1024,1024]{1,0:T(8,128)(2,1)S(1)} %copy-done.9, ...), custom_call_target="tpu_custom_call" | custom-call | flops 1024 | bytes 1024 | tf_op jit(solution)/shard_map/mlp_both/pallas_call | solution.py:227
  84.5 1.8 add_convert_fusion.5
  88.0 1.8 add_convert_fusion.4
  89.8 1.7 collective-permute-start.14
  95.4 1.7 add_convert_fusion.3
  97.9 1.8 add_convert_fusion.2
  99.7 4.2 %collective-permute-done.14 = bf16[256,1024]{1,0:T(8,128)(2,1)S(1)} collective-permute-done((bf16[256,1024]{1,0:T(8,128)(2,1)S(1)}, bf16[256,1024]{1,0:T(8,128)(2,1)S(1)}, u32[]{:S(2)}, u32[]{:S(2)}) %collective-permute-start.14) | collective-permute-done | bytes 524320 | tf_op jit(solution)/shard_map/ppermute | solution.py:302
  107.0 1.8 collective-permute-start.17
  111.6 7.9 %attend_back.2 = (bf16[512,256]{1,0:T(8,128)(2,1)S(1)}, f32[512,256]{1,0:T(8,128)S(1)}, f32[512,256]{1,0:T(8,128)S(1)}, f32[512,256]{1,0:T(8,128)S(1)}, f32[512,256]{1,0:T(8,128)S(1)}) custom-call(bf16[512,768]{1,0:T(8,128)(2,1)S(1)} %add_convert_fusion.10.refs_0_.refs_2_.q_ref, bf16[512,128]{1,0:T(8,128)(2,1)S(1)} %copy-done.17, ...), custom_call_target="tpu_custom_call" | custom-call | flops 1024 | bytes 1024 | tf_op jit(solution)/shard_map/attend_back/pallas_call | solution.py:184
  119.5 1.8 collective-permute-done.17
  121.5 1.7 add_convert_fusion
  123.3 1.6 add_convert_fusion.1
  126.1 1.9 collective-permute-start.22
  129.8 2.1 fusion
  133.0 8.6 %attend_back.3 = (bf16[512,256]{1,0:T(8,128)(2,1)S(1)}, bf16[512,256]{1,0:T(8,128)(2,1)S(1)}, bf16[512,256]{1,0:T(8,128)(2,1)S(1)}, bf16[512,256]{1,0:T(8,128)(2,1)S(1)}, bf16[512,256]{1,0:T(8,128)(2,1)S(1)}) custom-call(bf16[512,768]{1,0:T(8,128)(2,1)S(1)} %add_convert_fusion.9.q_ref.refs_1_.refs_3_, bf16[512,128]{1,0:T(8,128)(2,1)S(1)} %fusion.33.pick_ref, ...), custom_call_target="tpu_custom_call" | custom-call | flops 1024 | bytes 1024 | tf_op jit(solution)/shard_map/attend_back/pallas_call | solution.py:184
  148.2 2.7 collective-permute-start.29
  151.5 2.2 fusion.1
  161.3 10.2 %collective-permute-done.25 = bf16[256,1024]{1,0:T(8,128)(2,1)S(1)} collective-permute-done((bf16[256,1024]{1,0:T(8,128)(2,1)S(1)}, bf16[256,1024]{1,0:T(8,128)(2,1)S(1)}, u32[]{:S(2)}, u32[]{:S(2)}) %collective-permute-start.25) | collective-permute-done | bytes 524320 | tf_op jit(solution)/shard_map/ppermute | solution.py:302
  175.2 3.0 %multiply_add_fusion = f32[256,1024]{1,0:T(8,128)} fusion(f32[256,1024]{1,0:T(8,128)} %get-tuple-element.371, f32[256,1024]{1,0:T(8,128)S(1)} %copy-done.31, f32[256]{0:T(256)S(1)} %broadcast_multiply_fusion, f32[256]{0:T(256)S(1)} %broadcast_multiply_fusion.1, f32[1024]{0:T(1024)S(1)} %copy-done.70, f32[256]{0:T(256)S(1)} %copy-done.76, ...), kind=kLoop, calls=%fused_computation.65 | loop fusion | flops 3407872 | bytes 4726784 | tf_op jit(solution)/shard_map/add | solution.py:596
  187.5 2.6 collective-permute-start.36
  190.4 18.8 %collective-permute-done.35 = bf16[64,1024]{1,0:T(8,128)(2,1)S(1)} collective-permute-done((bf16[64,1024]{1,0:T(8,128)(2,1)S(1)}, bf16[64,1024]{1,0:T(8,128)(2,1)S(1)}, u32[]{:S(2)}, u32[]{:S(2)}) %collective-permute-start.35) | collective-permute-done | bytes 131104 | tf_op jit(solution)/shard_map/ppermute | solution.py:302
  209.4 2.8 collective-permute-done.37
  212.3 3.0 %collective-permute-start.39 = (bf16[32,1024]{1,0:T(8,128)(2,1)S(1)}, bf16[32,1024]{1,0:T(8,128)(2,1)S(1)}, u32[]{:S(2)}, u32[]{:S(2)}) collective-permute-start(bf16[32,1024]{1,0:T(8,128)(2,1)S(1)} %dynamic-slice_bitcast_fusion.7), channel_id=1, source_target_pairs={{0,16},{4,20},{8,24},{12,28},{16,0},{20,4},{24,8},{28,12},{1,17},{... | collective-permute-start | bytes 196616 | tf_op jit(solution)/shard_map/ppermute | solution.py:302
  215.5 4.1 %collective-permute-start.41 = (bf16[256,1024]{1,0:T(8,128)(2,1)S(1)}, bf16[256,1024]{1,0:T(8,128)(2,1)S(1)}, u32[]{:S(2)}, u32[]{:S(2)}) collective-permute-start(bf16[256,1024]{1,0:T(8,128)(2,1)S(1)} %maximum_select_fusion.6), channel_id=1, source_target_pairs={{0,8},{4,12},{8,0},{12,4},{16,24},{20,28},{24,16},{28,20},{1,9},{5... | collective-permute-start | bytes 1572872 | tf_op jit(solution)/shard_map/ppermute | solution.py:302
  221.6 7.5 %collective-permute-done.40 = f32[7808]{0:T(1024)S(1)} collective-permute-done((f32[7808]{0:T(1024)S(1)}, f32[7808]{0:T(1024)S(1)}, u32[]{:S(2)}, u32[]{:S(2)}) %collective-permute-start.40) | collective-permute-done | bytes 31264 | tf_op jit(solution)/shard_map/ppermute | solution.py:302
  229.2 3.0 %collective-permute-start.43 = (bf16[128,768]{1,0:T(8,128)(2,1)S(1)}, bf16[128,768]{1,0:T(8,128)(2,1)S(1)}, u32[]{:S(2)}, u32[]{:S(2)}) collective-permute-start(bf16[128,768]{1,0:T(8,128)(2,1)S(1)} %fusion.30), channel_id=1, source_target_pairs={{0,16},{4,20},{8,24},{12,28},{16,0},{20,4},{24,8},{28,12},{1,17},{... | collective-permute-start | bytes 589832 | tf_op jit(solution)/shard_map/ppermute | solution.py:302
  235.6 4.0 %collective-permute-done.45 = f32[7808]{0:T(1024)S(1)} collective-permute-done((f32[7808]{0:T(1024)S(1)}, f32[7808]{0:T(1024)S(1)}, u32[]{:S(2)}, u32[]{:S(2)}) %collective-permute-start.45) | collective-permute-done | bytes 31264 | tf_op jit(solution)/shard_map/ppermute | solution.py:302
  239.7 2.5 collective-permute-start.46
  242.4 2.1 collective-permute-start.48
  247.0 8.3 %collective-permute-done.48 = f32[7808]{0:T(1024)S(1)} collective-permute-done((f32[7808]{0:T(1024)S(1)}, f32[7808]{0:T(1024)S(1)}, u32[]{:S(2)}, u32[]{:S(2)}) %collective-permute-start.48) | collective-permute-done | bytes 31264 | tf_op jit(solution)/shard_map/ppermute | solution.py:302
  261.9 9.0 %collective-permute-done.49 = bf16[512,1024]{1,0:T(8,128)(2,1)} collective-permute-done((bf16[512,1024]{1,0:T(8,128)(2,1)}, bf16[512,1024]{1,0:T(8,128)(2,1)}, u32[]{:S(2)}, u32[]{:S(2)}) %collective-permute-start.49) | collective-permute-done | bytes 1048608 | tf_op jit(solution)/shard_map/ppermute | solution.py:302
  271.4 5.2 %convert_multiply_fusion.1 = f32[1024,1024]{1,0:T(8,128)} fusion(bf16[512,1024]{1,0:T(8,128)(2,1)} %maximum_select_fusion.3, bf16[512,1024]{1,0:T(8,128)(2,1)} %collective-permute-done.49, f32[]{:T(128)} %bitcast.38, pred[]{:T(512)S(6)} %ne.10), kind=kLoop, calls=%fused_computation.1 | loop fusion | flops 11534336 | bytes 6291461 | tf_op jit(solution)/shard_map/mul | solution.py:656
  276.7 4.4 %convert_multiply_fusion = f32[1024,1024]{1,0:T(8,128)} fusion(bf16[512,1024]{1,0:T(8,128)(2,1)S(1)} %maximum_select_fusion.4, bf16[512,1024]{1,0:T(8,128)(2,1)} %collective-permute-done.50, f32[]{:T(128)} %bitcast.38, pred[]{:T(512)S(6)} %ne.12), kind=kLoop, calls=%fused_computation | loop fusion | flops 11534336 | bytes 6291461 | tf_op jit(solution)/shard_map/mul | solution.py:656
  281.0 3.9 %collective-permute-done.52 = bf16[128,1024]{1,0:T(8,128)(2,1)S(1)} collective-permute-done((bf16[128,1024]{1,0:T(8,128)(2,1)S(1)}, bf16[128,1024]{1,0:T(8,128)(2,1)S(1)}, u32[]{:S(2)}, u32[]{:S(2)}) %collective-permute-start.52) | collective-permute-done | bytes 262176 | tf_op jit(solution)/shard_map/ppermute | solution.py:302
  286.8 1.9 pad_maximum_fusion
  (373 shorter events, 87.1 us)
Async XLA Ops:
  8.3 4.9 %collective-permute-start.1 = (bf16[256,1024]{1,0:T(8,128)(2,1)S(1)}, bf16[256,1024]{1,0:T(8,128)(2,1)S(1)}, u32[]{:S(2)}, u32[]{:S(2)}) collective-permute-start(bf16[256,1024]{1,0:T(8,128)(2,1)S(1)} %add_convert_fusion.17), channel_id=1, source_target_pairs={{0,1},{1,0},{2,3},{3,2},{4,5},{5,4},{6,7},{7,6},{8,9},{9,8},{10,11... | collective-permute-start | bytes 1572872 | tf_op jit(solution)/shard_map/ppermute | solution.py:302
  8.8 15.1 %collective-permute-start = (bf16[256,1024]{1,0:T(8,128)(2,1)S(1)}, bf16[256,1024]{1,0:T(8,128)(2,1)S(1)}, u32[]{:S(2)}, u32[]{:S(2)}) collective-permute-start(bf16[256,1024]{1,0:T(8,128)(2,1)S(1)} %add_convert_fusion.17), channel_id=1, source_target_pairs={{0,2},{1,3},{2,0},{3,1},{4,6},{5,7},{6,4},{7,5},{8,10},{9,11},{10,... | collective-permute-start | bytes 1572872 | tf_op jit(solution)/shard_map/ppermute | solution.py:302
  24.2 14.4 %collective-permute-start.7 = (bf16[256,1024]{1,0:T(8,128)(2,1)S(1)}, bf16[256,1024]{1,0:T(8,128)(2,1)S(1)}, u32[]{:S(2)}, u32[]{:S(2)}) collective-permute-start(bf16[256,1024]{1,0:T(8,128)(2,1)S(1)} %get-tuple-element.269), channel_id=1, source_target_pairs={{0,2},{1,3},{2,0},{3,1},{4,6},{5,7},{6,4},{7,5},{8,10},{9,11},{10,... | collective-permute-start | bytes 1572872 | tf_op jit(solution)/shard_map/ppermute | solution.py:302
  34.2 4.4 %collective-permute-start.3 = (bf16[256,1024]{1,0:T(8,128)(2,1)S(1)}, bf16[256,1024]{1,0:T(8,128)(2,1)S(1)}, u32[]{:S(2)}, u32[]{:S(2)}) collective-permute-start(bf16[256,1024]{1,0:T(8,128)(2,1)S(1)} %slice.160), channel_id=1, source_target_pairs={{0,1},{1,0},{2,3},{3,2},{4,5},{5,4},{6,7},{7,6},{8,9},{9,8},{10,11... | collective-permute-start | bytes 1572872 | tf_op jit(solution)/shard_map/ppermute | solution.py:302
  34.6 12.2 %collective-permute-start.6 = (bf16[256,1024]{1,0:T(8,128)(2,1)S(1)}, bf16[256,1024]{1,0:T(8,128)(2,1)S(1)}, u32[]{:S(2)}, u32[]{:S(2)}) collective-permute-start(bf16[256,1024]{1,0:T(8,128)(2,1)S(1)} %get-tuple-element.269), channel_id=1, source_target_pairs={{0,1},{1,0},{2,3},{3,2},{4,5},{5,4},{6,7},{7,6},{8,9},{9,8},{10,11... | collective-permute-start | bytes 1572872 | tf_op jit(solution)/shard_map/ppermute | solution.py:302
  38.6 8.6 %collective-permute-start.8 = (bf16[256,1024]{1,0:T(8,128)(2,1)S(1)}, bf16[256,1024]{1,0:T(8,128)(2,1)S(1)}, u32[]{:S(2)}, u32[]{:S(2)}) collective-permute-start(bf16[256,1024]{1,0:T(8,128)(2,1)S(1)} %collective-permute-done.7), channel_id=1, source_target_pairs={{0,1},{1,0},{2,3},{3,2},{4,5},{5,4},{6,7},{7,6},{8,9},{9,8},{10,11... | collective-permute-start | bytes 1572872 | tf_op jit(solution)/shard_map/ppermute | solution.py:302
  38.8 14.4 %collective-permute-start.5 = (bf16[256,1024]{1,0:T(8,128)(2,1)S(1)}, bf16[256,1024]{1,0:T(8,128)(2,1)S(1)}, u32[]{:S(2)}, u32[]{:S(2)}) collective-permute-start(bf16[256,1024]{1,0:T(8,128)(2,1)S(1)} %add_convert_fusion.16), channel_id=1, source_target_pairs={{0,2},{1,3},{2,0},{3,1},{4,6},{5,7},{6,4},{7,5},{8,10},{9,11},{10,... | collective-permute-start | bytes 1572872 | tf_op jit(solution)/shard_map/ppermute | solution.py:302
  46.5 6.7 %collective-permute-start.4 = (bf16[256,1024]{1,0:T(8,128)(2,1)S(1)}, bf16[256,1024]{1,0:T(8,128)(2,1)S(1)}, u32[]{:S(2)}, u32[]{:S(2)}) collective-permute-start(bf16[256,1024]{1,0:T(8,128)(2,1)S(1)} %slice.162), channel_id=1, source_target_pairs={{0,1},{1,0},{2,3},{3,2},{4,5},{5,4},{6,7},{7,6},{8,9},{9,8},{10,11... | collective-permute-start | bytes 1572872 | tf_op jit(solution)/shard_map/ppermute | solution.py:302
  54.8 14.4 %collective-permute-start.9 = (bf16[256,1024]{1,0:T(8,128)(2,1)S(1)}, bf16[256,1024]{1,0:T(8,128)(2,1)}, u32[]{:S(2)}, u32[]{:S(2)}) collective-permute-start(bf16[256,1024]{1,0:T(8,128)(2,1)S(1)} %add_convert_fusion.15), channel_id=1, source_target_pairs={{0,2},{1,3},{2,0},{3,1},{4,6},{5,7},{6,4},{7,5},{8,10},{9,11},{10,... | collective-permute-start | bytes 1572872 | tf_op jit(solution)/shard_map/ppermute | solution.py:302
  69.3 4.9 %collective-permute-start.11 = (bf16[256,1024]{1,0:T(8,128)(2,1)}, bf16[256,1024]{1,0:T(8,128)(2,1)}, u32[]{:S(2)}, u32[]{:S(2)}) collective-permute-start(bf16[256,1024]{1,0:T(8,128)(2,1)} %collective-permute-done.9), channel_id=1, source_target_pairs={{0,1},{1,0},{2,3},{3,2},{4,5},{5,4},{6,7},{7,6},{8,9},{9,8},{10,11... | collective-permute-start | bytes 1572872 | tf_op jit(solution)/shard_map/ppermute | solution.py:302
  70.3 11.5 %collective-permute-start.12 = (bf16[256,1024]{1,0:T(8,128)(2,1)}, bf16[256,1024]{1,0:T(8,128)(2,1)}, u32[]{:S(2)}, u32[]{:S(2)}) collective-permute-start(bf16[256,1024]{1,0:T(8,128)(2,1)} %get-tuple-element.391), channel_id=1, source_target_pairs={{0,1},{1,0},{2,3},{3,2},{4,5},{5,4},{6,7},{7,6},{8,9},{9,8},{10,11... | collective-permute-start | bytes 1572872 | tf_op jit(solution)/shard_map/ppermute | solution.py:302
  73.0 26.6 %collective-permute-start.16 = (bf16[256,1024]{1,0:T(8,128)(2,1)S(1)}, bf16[256,1024]{1,0:T(8,128)(2,1)S(1)}, u32[]{:S(2)}, u32[]{:S(2)}) collective-permute-start(bf16[256,1024]{1,0:T(8,128)(2,1)S(1)} %get-tuple-element.387), channel_id=1, source_target_pairs={{0,1},{1,0},{2,3},{3,2},{4,5},{5,4},{6,7},{7,6},{8,9},{9,8},{10,11... | collective-permute-start | bytes 1572872 | tf_op jit(solution)/shard_map/ppermute | solution.py:302
  81.9 4.4 %collective-permute-start.13 = (bf16[256,1024]{1,0:T(8,128)(2,1)S(1)}, bf16[256,1024]{1,0:T(8,128)(2,1)S(1)}, u32[]{:S(2)}, u32[]{:S(2)}) collective-permute-start(bf16[256,1024]{1,0:T(8,128)(2,1)S(1)} %slice.134), channel_id=1, source_target_pairs={{0,1},{1,0},{2,3},{3,2},{4,5},{5,4},{6,7},{7,6},{8,9},{9,8},{10,11... | collective-permute-start | bytes 1572872 | tf_op jit(solution)/shard_map/ppermute | solution.py:302
  83.3 16.3 %collective-permute-start.15 = (bf16[256,1024]{1,0:T(8,128)(2,1)S(1)}, bf16[256,1024]{1,0:T(8,128)(2,1)S(1)}, u32[]{:S(2)}, u32[]{:S(2)}) collective-permute-start(bf16[256,1024]{1,0:T(8,128)(2,1)S(1)} %get-tuple-element.389), channel_id=1, source_target_pairs={{0,1},{1,0},{2,3},{3,2},{4,5},{5,4},{6,7},{7,6},{8,9},{9,8},{10,11... | collective-permute-start | bytes 1572872 | tf_op jit(solution)/shard_map/ppermute | solution.py:302
  89.8 14.0 %collective-permute-start.14 = (bf16[256,1024]{1,0:T(8,128)(2,1)S(1)}, bf16[256,1024]{1,0:T(8,128)(2,1)S(1)}, u32[]{:S(2)}, u32[]{:S(2)}) collective-permute-start(bf16[256,1024]{1,0:T(8,128)(2,1)S(1)} %add_convert_fusion.14), channel_id=1, source_target_pairs={{0,2},{1,3},{2,0},{3,1},{4,6},{5,7},{6,4},{7,5},{8,10},{9,11},{10,... | collective-permute-start | bytes 1572872 | tf_op jit(solution)/shard_map/ppermute | solution.py:302
  91.6 29.8 %collective-permute-start.20 = (bf16[512,1024]{1,0:T(8,128)(2,1)}, bf16[512,1024]{1,0:T(8,128)(2,1)}, u32[]{:S(2)}, u32[]{:S(2)}) collective-permute-start(bf16[512,1024]{1,0:T(8,128)(2,1)} %add_convert_fusion.4), channel_id=1, source_target_pairs={{0,8},{4,12},{8,0},{12,4},{16,24},{20,28},{24,16},{28,20},{1,9},{5... | collective-permute-start | bytes 3145736 | tf_op jit(solution)/shard_map/ppermute | solution.py:302
  93.2 28.2 %collective-permute-start.19 = (bf16[512,1024]{1,0:T(8,128)(2,1)}, bf16[512,1024]{1,0:T(8,128)(2,1)}, u32[]{:S(2)}, u32[]{:S(2)}) collective-permute-start(bf16[512,1024]{1,0:T(8,128)(2,1)} %add_convert_fusion.5), channel_id=1, source_target_pairs={{0,4},{4,0},{8,12},{12,8},{16,20},{20,16},{24,28},{28,24},{1,5},{5... | collective-permute-start | bytes 3145736 | tf_op jit(solution)/shard_map/ppermute | solution.py:302
  107.0 14.4 %collective-permute-start.17 = (bf16[256,1024]{1,0:T(8,128)(2,1)S(1)}, bf16[256,1024]{1,0:T(8,128)(2,1)}, u32[]{:S(2)}, u32[]{:S(2)}) collective-permute-start(bf16[256,1024]{1,0:T(8,128)(2,1)S(1)} %get-tuple-element.268), channel_id=1, source_target_pairs={{0,2},{1,3},{2,0},{3,1},{4,6},{5,7},{6,4},{7,5},{8,10},{9,11},{10,... | collective-permute-start | bytes 1572872 | tf_op jit(solution)/shard_map/ppermute | solution.py:302
  121.4 3.5 %collective-permute-start.21 = (bf16[256,1024]{1,0:T(8,128)(2,1)}, bf16[256,1024]{1,0:T(8,128)(2,1)S(1)}, u32[]{:S(2)}, u32[]{:S(2)}) collective-permute-start(bf16[256,1024]{1,0:T(8,128)(2,1)} %collective-permute-done.17), channel_id=1, source_target_pairs={{0,1},{1,0},{2,3},{3,2},{4,5},{5,4},{6,7},{7,6},{8,9},{9,8},{10,11... | collective-permute-start | bytes 1572872 | tf_op jit(solution)/shard_map/ppermute | solution.py:302
  126.1 15.5 %collective-permute-start.22 = (bf16[256,1024]{1,0:T(8,128)(2,1)S(1)}, bf16[256,1024]{1,0:T(8,128)(2,1)S(1)}, u32[]{:S(2)}, u32[]{:S(2)}) collective-permute-start(bf16[256,1024]{1,0:T(8,128)(2,1)S(1)} %dynamic-slice_bitcast_fusion.1), channel_id=1, source_target_pairs={{0,8},{4,12},{8,0},{12,4},{16,24},{20,28},{24,16},{28,20},{1,9},{5... | collective-permute-start | bytes 1572872 | tf_op jit(solution)/shard_map/ppermute | solution.py:302
  128.0 14.8 %collective-permute-start.23 = (bf16[256,1024]{1,0:T(8,128)(2,1)S(1)}, bf16[256,1024]{1,0:T(8,128)(2,1)S(1)}, u32[]{:S(2)}, u32[]{:S(2)}) collective-permute-start(bf16[256,1024]{1,0:T(8,128)(2,1)S(1)} %dynamic-slice_bitcast_fusion), channel_id=1, source_target_pairs={{0,4},{4,0},{8,12},{12,8},{16,20},{20,16},{24,28},{28,24},{1,5},{5... | collective-permute-start | bytes 1572872 | tf_op jit(solution)/shard_map/ppermute | solution.py:302
  132.4 45.9 %collective-permute-start.32 = (bf16[128,1024]{1,0:T(8,128)(2,1)}, bf16[128,1024]{1,0:T(8,128)(2,1)}, u32[]{:S(2)}, u32[]{:S(2)}) collective-permute-start(bf16[128,1024]{1,0:T(8,128)(2,1)} %fusion), channel_id=1, source_target_pairs={{0,4},{4,0},{8,12},{12,8},{16,20},{20,16},{24,28},{28,24},{1,5},{5... | collective-permute-start | bytes 786440 | tf_op jit(solution)/shard_map/ppermute | solution.py:302
  148.1 7.7 %collective-permute-start.24 = (bf16[256,1024]{1,0:T(8,128)(2,1)S(1)}, bf16[256,1024]{1,0:T(8,128)(2,1)S(1)}, u32[]{:S(2)}, u32[]{:S(2)}) collective-permute-start(bf16[256,1024]{1,0:T(8,128)(2,1)S(1)} %slice.164), channel_id=1, source_target_pairs={{0,1},{1,0},{2,3},{3,2},{4,5},{5,4},{6,7},{7,6},{8,9},{9,8},{10,11... | collective-permute-start | bytes 1572872 | tf_op jit(solution)/shard_map/ppermute | solution.py:302
  148.2 30.2 %collective-permute-start.29 = (bf16[128,1024]{1,0:T(8,128)(2,1)}, bf16[128,1024]{1,0:T(8,128)(2,1)}, u32[]{:S(2)}, u32[]{:S(2)}) collective-permute-start(bf16[128,1024]{1,0:T(8,128)(2,1)} %dynamic-slice_bitcast_fusion.4), channel_id=1, source_target_pairs={{0,16},{4,20},{8,24},{12,28},{16,0},{20,4},{24,8},{28,12},{1,17},{... | collective-permute-start | bytes 786440 | tf_op jit(solution)/shard_map/ppermute | solution.py:302
  150.8 27.5 %collective-permute-start.30 = (bf16[128,1024]{1,0:T(8,128)(2,1)}, bf16[128,1024]{1,0:T(8,128)(2,1)}, u32[]{:S(2)}, u32[]{:S(2)}) collective-permute-start(bf16[128,1024]{1,0:T(8,128)(2,1)} %dynamic-slice_bitcast_fusion.3), channel_id=1, source_target_pairs={{0,16},{4,20},{8,24},{12,28},{16,0},{20,4},{24,8},{28,12},{1,17},{... | collective-permute-start | bytes 786440 | tf_op jit(solution)/shard_map/ppermute | solution.py:302
  157.1 14.3 %collective-permute-start.25 = (bf16[256,1024]{1,0:T(8,128)(2,1)S(1)}, bf16[256,1024]{1,0:T(8,128)(2,1)S(1)}, u32[]{:S(2)}, u32[]{:S(2)}) collective-permute-start(bf16[256,1024]{1,0:T(8,128)(2,1)S(1)} %add_convert_fusion.13), channel_id=1, source_target_pairs={{0,2},{1,3},{2,0},{3,1},{4,6},{5,7},{6,4},{7,5},{8,10},{9,11},{10,... | collective-permute-start | bytes 1572872 | tf_op jit(solution)/shard_map/ppermute | solution.py:302
  159.7 20.0 %collective-permute-start.31 = (bf16[512,768]{1,0:T(8,128)(2,1)}, bf16[512,768]{1,0:T(8,128)(2,1)}, u32[]{:S(2)}, u32[]{:S(2)}) collective-permute-start(bf16[512,768]{1,0:T(8,128)(2,1)} %add_convert_fusion.8), channel_id=1, source_target_pairs={{0,4},{4,0},{8,12},{12,8},{16,20},{20,16},{24,28},{28,24},{1,5},{5... | collective-permute-start | bytes 2359304 | tf_op jit(solution)/shard_map/ppermute | solution.py:302
  173.8 4.5 %collective-permute-start.28 = (f32[6,1024]{1,0:T(8,128)S(1)}, f32[6,1024]{1,0:T(8,128)S(1)}, u32[]{:S(2)}, u32[]{:S(2)}) collective-permute-start(f32[6,1024]{1,0:T(8,128)S(1)} %add.318), channel_id=1, source_target_pairs={{0,2},{1,3},{2,0},{3,1},{4,6},{5,7},{6,4},{7,5},{8,10},{9,11},{10,... | collective-permute-start | bytes 73736 | tf_op jit(solution)/shard_map/ppermute | solution.py:302
  184.6 24.6 %collective-permute-start.33 = (bf16[256,1024]{1,0:T(8,128)(2,1)S(1)}, bf16[256,1024]{1,0:T(8,128)(2,1)S(1)}, u32[]{:S(2)}, u32[]{:S(2)}) collective-permute-start(bf16[256,1024]{1,0:T(8,128)(2,1)S(1)} %add_convert_fusion.12), channel_id=1, source_target_pairs={{0,2},{1,3},{2,0},{3,1},{4,6},{5,7},{6,4},{7,5},{8,10},{9,11},{10,... | collective-permute-start | bytes 1572872 | tf_op jit(solution)/shard_map/ppermute | solution.py:302
  185.4 23.8 %collective-permute-start.34 = (bf16[256,768]{1,0:T(8,128)(2,1)S(1)}, bf16[256,768]{1,0:T(8,128)(2,1)S(1)}, u32[]{:S(2)}, u32[]{:S(2)}) collective-permute-start(bf16[256,768]{1,0:T(8,128)(2,1)S(1)} %dynamic-slice_bitcast_fusion.2), channel_id=1, source_target_pairs={{0,8},{4,12},{8,0},{12,4},{16,24},{20,28},{24,16},{28,20},{1,9},{5... | collective-permute-start | bytes 1179656 | tf_op jit(solution)/shard_map/ppermute | solution.py:302
  185.9 23.3 %collective-permute-start.35 = (bf16[64,1024]{1,0:T(8,128)(2,1)S(1)}, bf16[64,1024]{1,0:T(8,128)(2,1)S(1)}, u32[]{:S(2)}, u32[]{:S(2)}) collective-permute-start(bf16[64,1024]{1,0:T(8,128)(2,1)S(1)} %dynamic-slice_bitcast_fusion.6), channel_id=1, source_target_pairs={{0,8},{4,12},{8,0},{12,4},{16,24},{20,28},{24,16},{28,20},{1,9},{5... | collective-permute-start | bytes 393224 | tf_op jit(solution)/shard_map/ppermute | solution.py:302
  187.5 22.0 %collective-permute-start.36 = (bf16[128,1024]{1,0:T(8,128)(2,1)S(1)}, bf16[128,1024]{1,0:T(8,128)(2,1)S(1)}, u32[]{:S(2)}, u32[]{:S(2)}) collective-permute-start(bf16[128,1024]{1,0:T(8,128)(2,1)S(1)} %fusion.15), channel_id=1, source_target_pairs={{0,16},{4,20},{8,24},{12,28},{16,0},{20,4},{24,8},{28,12},{1,17},{... | collective-permute-start | bytes 786440 | tf_op jit(solution)/shard_map/ppermute | solution.py:302
  190.0 22.2 %collective-permute-start.37 = (bf16[128,1024]{1,0:T(8,128)(2,1)S(1)}, bf16[128,1024]{1,0:T(8,128)(2,1)S(1)}, u32[]{:S(2)}, u32[]{:S(2)}) collective-permute-start(bf16[128,1024]{1,0:T(8,128)(2,1)S(1)} %fusion.14), channel_id=1, source_target_pairs={{0,16},{4,20},{8,24},{12,28},{16,0},{20,4},{24,8},{28,12},{1,17},{... | collective-permute-start | bytes 786440 | tf_op jit(solution)/shard_map/ppermute | solution.py:302
  212.2 16.9 %collective-permute-start.38 = (bf16[128,768]{1,0:T(8,128)(2,1)S(1)}, bf16[128,768]{1,0:T(8,128)(2,1)S(1)}, u32[]{:S(2)}, u32[]{:S(2)}) collective-permute-start(bf16[128,768]{1,0:T(8,128)(2,1)S(1)} %dynamic-slice_bitcast_fusion.5), channel_id=1, source_target_pairs={{0,16},{4,20},{8,24},{12,28},{16,0},{20,4},{24,8},{28,12},{1,17},{... | collective-permute-start | bytes 589832 | tf_op jit(solution)/shard_map/ppermute | solution.py:302
  212.3 16.8 %collective-permute-start.39 = (bf16[32,1024]{1,0:T(8,128)(2,1)S(1)}, bf16[32,1024]{1,0:T(8,128)(2,1)S(1)}, u32[]{:S(2)}, u32[]{:S(2)}) collective-permute-start(bf16[32,1024]{1,0:T(8,128)(2,1)S(1)} %dynamic-slice_bitcast_fusion.7), channel_id=1, source_target_pairs={{0,16},{4,20},{8,24},{12,28},{16,0},{20,4},{24,8},{28,12},{1,17},{... | collective-permute-start | bytes 196616 | tf_op jit(solution)/shard_map/ppermute | solution.py:302
  215.5 17.1 %collective-permute-start.41 = (bf16[256,1024]{1,0:T(8,128)(2,1)S(1)}, bf16[256,1024]{1,0:T(8,128)(2,1)S(1)}, u32[]{:S(2)}, u32[]{:S(2)}) collective-permute-start(bf16[256,1024]{1,0:T(8,128)(2,1)S(1)} %maximum_select_fusion.6), channel_id=1, source_target_pairs={{0,8},{4,12},{8,0},{12,4},{16,24},{20,28},{24,16},{28,20},{1,9},{5... | collective-permute-start | bytes 1572872 | tf_op jit(solution)/shard_map/ppermute | solution.py:302
  219.6 13.0 %collective-permute-start.42 = (bf16[256,1024]{1,0:T(8,128)(2,1)S(1)}, bf16[256,1024]{1,0:T(8,128)(2,1)S(1)}, u32[]{:S(2)}, u32[]{:S(2)}) collective-permute-start(bf16[256,1024]{1,0:T(8,128)(2,1)S(1)} %maximum_select_fusion.7), channel_id=1, source_target_pairs={{0,4},{4,0},{8,12},{12,8},{16,20},{20,16},{24,28},{28,24},{1,5},{5... | collective-permute-start | bytes 1572872 | tf_op jit(solution)/shard_map/ppermute | solution.py:302
  221.0 8.1 %collective-permute-start.40 = (f32[7808]{0:T(1024)S(1)}, f32[7808]{0:T(1024)S(1)}, u32[]{:S(2)}, u32[]{:S(2)}) collective-permute-start(f32[7808]{0:T(1024)S(1)} %constant_dynamic-update-slice_fusion.8), channel_id=1, source_target_pairs={{0,4},{4,0},{8,12},{12,8},{16,20},{20,16},{24,28},{28,24},{1,5},{5... | collective-permute-start | bytes 93704 | tf_op jit(solution)/shard_map/ppermute | solution.py:302
  229.2 10.4 %collective-permute-start.43 = (bf16[128,768]{1,0:T(8,128)(2,1)S(1)}, bf16[128,768]{1,0:T(8,128)(2,1)S(1)}, u32[]{:S(2)}, u32[]{:S(2)}) collective-permute-start(bf16[128,768]{1,0:T(8,128)(2,1)S(1)} %fusion.30), channel_id=1, source_target_pairs={{0,16},{4,20},{8,24},{12,28},{16,0},{20,4},{24,8},{28,12},{1,17},{... | collective-permute-start | bytes 589832 | tf_op jit(solution)/shard_map/ppermute | solution.py:302
  232.2 7.4 %collective-permute-start.44 = (bf16[32,1024]{1,0:T(8,128)(2,1)S(1)}, bf16[32,1024]{1,0:T(8,128)(2,1)S(1)}, u32[]{:S(2)}, u32[]{:S(2)}) collective-permute-start(bf16[32,1024]{1,0:T(8,128)(2,1)S(1)} %fusion.34), channel_id=1, source_target_pairs={{0,16},{4,20},{8,24},{12,28},{16,0},{20,4},{24,8},{28,12},{1,17},{... | collective-permute-start | bytes 196616 | tf_op jit(solution)/shard_map/ppermute | solution.py:302
  232.3 7.3 %collective-permute-start.45 = (f32[7808]{0:T(1024)S(1)}, f32[7808]{0:T(1024)S(1)}, u32[]{:S(2)}, u32[]{:S(2)}) collective-permute-start(f32[7808]{0:T(1024)S(1)} %add.332), channel_id=1, source_target_pairs={{0,8},{4,12},{8,0},{12,4},{16,24},{20,28},{24,16},{28,20},{1,9},{5... | collective-permute-start | bytes 93704 | tf_op jit(solution)/shard_map/ppermute | solution.py:302
  239.7 15.7 %collective-permute-start.46 = (bf16[256,768]{1,0:T(8,128)(2,1)S(1)}, bf16[256,768]{1,0:T(8,128)(2,1)S(1)}, u32[]{:S(2)}, u32[]{:S(2)}) collective-permute-start(bf16[256,768]{1,0:T(8,128)(2,1)S(1)} %maximum_select_fusion.9), channel_id=1, source_target_pairs={{0,8},{4,12},{8,0},{12,4},{16,24},{20,28},{24,16},{28,20},{1,9},{5... | collective-permute-start | bytes 1179656 | tf_op jit(solution)/shard_map/ppermute | solution.py:302
  242.3 13.1 %collective-permute-start.47 = (bf16[64,1024]{1,0:T(8,128)(2,1)S(1)}, bf16[64,1024]{1,0:T(8,128)(2,1)S(1)}, u32[]{:S(2)}, u32[]{:S(2)}) collective-permute-start(bf16[64,1024]{1,0:T(8,128)(2,1)S(1)} %maximum_select_fusion.11), channel_id=1, source_target_pairs={{0,8},{4,12},{8,0},{12,4},{16,24},{20,28},{24,16},{28,20},{1,9},{5... | collective-permute-start | bytes 393224 | tf_op jit(solution)/shard_map/ppermute | solution.py:302
  242.4 12.9 %collective-permute-start.48 = (f32[7808]{0:T(1024)S(1)}, f32[7808]{0:T(1024)S(1)}, u32[]{:S(2)}, u32[]{:S(2)}) collective-permute-start(f32[7808]{0:T(1024)S(1)} %add.338), channel_id=1, source_target_pairs={{0,16},{4,20},{8,24},{12,28},{16,0},{20,4},{24,8},{28,12},{1,17},{... | collective-permute-start | bytes 93704 | tf_op jit(solution)/shard_map/ppermute | solution.py:302
  244.5 26.3 %collective-permute-start.49 = (bf16[512,1024]{1,0:T(8,128)(2,1)}, bf16[512,1024]{1,0:T(8,128)(2,1)}, u32[]{:S(2)}, u32[]{:S(2)}) collective-permute-start(bf16[512,1024]{1,0:T(8,128)(2,1)} %maximum_select_fusion.3), channel_id=1, source_target_pairs={{0,4},{4,0},{8,12},{12,8},{16,20},{20,16},{24,28},{28,24},{1,5},{5... | collective-permute-start | bytes 3145736 | tf_op jit(solution)/shard_map/ppermute | solution.py:302
  246.0 25.5 %collective-permute-start.50 = (bf16[512,1024]{1,0:T(8,128)(2,1)S(1)}, bf16[512,1024]{1,0:T(8,128)(2,1)}, u32[]{:S(2)}, u32[]{:S(2)}) collective-permute-start(bf16[512,1024]{1,0:T(8,128)(2,1)S(1)} %maximum_select_fusion.4), channel_id=1, source_target_pairs={{0,8},{4,12},{8,0},{12,4},{16,24},{20,28},{24,16},{28,20},{1,9},{5... | collective-permute-start | bytes 3145736 | tf_op jit(solution)/shard_map/ppermute | solution.py:302
  257.2 27.7 %collective-permute-start.51 = (bf16[512,768]{1,0:T(8,128)(2,1)S(1)}, bf16[512,768]{1,0:T(8,128)(2,1)S(1)}, u32[]{:S(2)}, u32[]{:S(2)}) collective-permute-start(bf16[512,768]{1,0:T(8,128)(2,1)S(1)} %maximum_select_fusion.5), channel_id=1, source_target_pairs={{0,4},{4,0},{8,12},{12,8},{16,20},{20,16},{24,28},{28,24},{1,5},{5... | collective-permute-start | bytes 2359304 | tf_op jit(solution)/shard_map/ppermute | solution.py:302
  260.1 24.9 %collective-permute-start.52 = (bf16[128,1024]{1,0:T(8,128)(2,1)S(1)}, bf16[128,1024]{1,0:T(8,128)(2,1)S(1)}, u32[]{:S(2)}, u32[]{:S(2)}) collective-permute-start(bf16[128,1024]{1,0:T(8,128)(2,1)S(1)} %maximum_select_fusion.10), channel_id=1, source_target_pairs={{0,4},{4,0},{8,12},{12,8},{16,20},{20,16},{24,28},{28,24},{1,5},{5... | collective-permute-start | bytes 786440 | tf_op jit(solution)/shard_map/ppermute | solution.py:302
  (89 other events, 465.8 us)

commit v6 on v5

--- a/solution.py
+++ b/solution.py
@@ -205,27 +205,37 @@
     return result[0], result[1 : 1 + parts], result[1 + parts :]
 
 
-def mlp_kernel(x_ref, grad_ref, up_ref, bias_ref, down_ref, act_ref, slope_ref, back_ref, *share_ref):
+def mlp_kernel(per, x_ref, grad_ref, up_ref, bias_ref, down_ref, act_ref, slope_ref, *piece_refs):
     pre = dot_nn(x_ref[...], up_ref[...]) + bias_ref[...]
     upstream = dot_nt(grad_ref[...], down_ref[...])
     cdf = 0.5 + 0.5 * lax.erf(pre * (0.5**0.5))
     act = (pre * cdf).astype(BF16)
     act_ref[...] = act
-    if share_ref:
-        share_ref[0][...] = dot_nn(act, down_ref[...]).astype(BF16)
+    share = dot_nn(act, down_ref[...]).astype(BF16)
     density = jnp.exp(-0.5 * pre * pre) * 0.3989422804014327
     slope = (upstream * (cdf + pre * density)).astype(BF16)
     slope_ref[...] = slope
-    back_ref[...] = dot_nt(slope, up_ref[...]).astype(BF16)
-
-
-def mlp_both(x, grad, up, bias, down, share, tile=256):
+    back = dot_nt(slope, up_ref[...]).astype(BF16)
+    step = pl.program_id(0)
+    tile = x_ref.shape[0]
+    pieces = len(piece_refs) // 2
+    for j in range(pieces):
+
+        @pl.when(step // per == j)
+        def _():
+            rows = pl.ds(pl.multiple_of((step % per) * tile, tile), tile)
+            piece_refs[j][rows, :] = back
+            piece_refs[pieces + j][rows, :] = share
+
+
+def mlp_both(x, grad, up, bias, down, pieces, tile=256):
     count, width = x.shape
     hidden = up.shape[1]
-    tile = min(tile, count)
+    size = count // pieces
+    tile = min(tile, size)
     whole = lambda i: (0, 0)
     return pl.pallas_call(
-        mlp_kernel,
+        functools.partial(mlp_kernel, size // tile),
         grid=(count // tile,),
         in_specs=[
             pl.BlockSpec((tile, width), lambda i: (i, 0)),
@@ -237,12 +247,12 @@
         out_specs=[
             pl.BlockSpec((tile, hidden), lambda i: (i, 0)),
             pl.BlockSpec((tile, hidden), lambda i: (i, 0)),
-            *[pl.BlockSpec((tile, width), lambda i: (i, 0))] * (1 + share),
+            *[pl.BlockSpec((size, width), whole)] * (2 * pieces),
         ],
         out_shape=[
             jax.ShapeDtypeStruct((count, hidden), BF16),
             jax.ShapeDtypeStruct((count, hidden), BF16),
-            *[jax.ShapeDtypeStruct((count, width), BF16)] * (1 + share),
+            *[jax.ShapeDtypeStruct((size, width), BF16)] * (2 * pieces),
         ],
         cost_estimate=LIGHT,
         compiler_params=pltpu.CompilerParams(vmem_limit_bytes=24 * 2**20),
@@ -504,24 +514,25 @@
 
         far_own = swap(mlp_input, "mp", n_mp, far_bit)
         mlp_near = gather_near(mlp_input, n_mp)
-        act_near, slope_near, back_near, share_near = mlp_both(
-            mlp_near, grad_near, expand_weight, expand_bias, reduce_weight, True
-        )
-        far_own, act_near, slope_near, back_near, share_near = tie(
-            far_own, act_near, slope_near, back_near, share_near
+        act_near, slope_near, *pieces_near = mlp_both(
+            mlp_near, grad_near, expand_weight, expand_bias, reduce_weight, near_count
+        )
+        far_own, act_near, slope_near, *pieces_near = tie(
+            far_own, act_near, slope_near, *pieces_near
         )
         mlp_far = gather_near(far_own, n_mp)
-        sum_near = scatter_near(cut(back_near), n_mp)
-        act_far, slope_far, back_far, share_far = mlp_both(
-            mlp_far, grad_far, expand_weight, expand_bias, reduce_weight, True
-        )
-        act_far, slope_far, back_far, *sum_near = tie(act_far, slope_far, back_far, *sum_near)
+        sum_near = scatter_near(pieces_near[:near_count], n_mp)
+        act_far, slope_far, *pieces_far = mlp_both(
+            mlp_far, grad_far, expand_weight, expand_bias, reduce_weight, near_count
+        )
+        act_far, slope_far, *tied = tie(act_far, slope_far, *sum_near, *pieces_far)
+        sum_near, pieces_far = tied[:2], tied[2:]
         swapped = dp_bits[1:2] + dp_bits[:1] + dp_bits[2:]
         reduce_sum = DpSum(n_dp, group, dp_bits)
         expand_sum = DpSum(n_dp, group, swapped)
         output_sum = DpSum(n_dp, group, dp_bits)
         input_sum = DpSum(n_dp, group, dp_bits)
-        sum_far = add_up(scatter_near(cut(back_far), n_mp)).astype(BF16)
+        sum_far = add_up(scatter_near(pieces_far[:near_count], n_mp)).astype(BF16)
         reduce_sum.open([(act_near, grad_near), (act_far, grad_far)])
         sum_far, slope_near, slope_far, act_far = start_all(
             (sum_far, slope_near, slope_far, act_far), [reduce_sum]
@@ -533,8 +544,8 @@
         )
         reduce_sum.keep([(act_near, grad_near), (act_far, grad_far)])
         expand_sum.keep([(mlp_near, slope_near), (mlp_far, slope_far)])
-        out_far = scatter_near(cut(share_far), n_mp)
-        out_near = scatter_near(cut(share_near), n_mp)
+        out_far = scatter_near(pieces_far[near_count:], n_mp)
+        out_near = scatter_near(pieces_near[near_count:], n_mp)
         held = [reduce_sum.held, expand_sum.held]
         arrived, *held = tie(arrived, *held, *out_far, *out_near)
         reduce_sum.held, expand_sum.held = held[:2]

time: 294 us -> 292 us (level)
    slice x8 -> x4, local copies, waits for them, and re-layouts: 4.34 us -> 0.18 us  [cut(): return [rows[j * own_count:(j + 1) * own_count] for j in range(near_count)]]
    unnamed x175 -> x181, local copies, waits for them, and re-layouts: 11.7 us -> 14.4 us
  transfers between devices with their start and end apart: 53 -> 53, of which waited for: 21 -> 22; matrix products, arithmetic and copies ran while one was open for 23% -> 22% of each run, Pallas kernels for 13% -> 13%
where the time goes in v6:
time: 292 us; the launch traced here: 287 us
  waiting for transfers between devices  95.6 us (33%)
  starting transfers between devices  56.4 us (19%)
  other arithmetic  44.5 us (15%)
  Pallas kernels  38.3 us (13%)
  matrix products  25.3 us (9%)
  local copies, waits for them, and re-layouts  21.1 us (7%)
  between operations  5.32 us (2%)
    ppermute x53, waiting for transfers between devices, swap(): return lax.ppermute(array, axis, [(i, i ^ bit) for i in range(size)])  95.6 us
    ppermute x53, starting transfers between devices, swap(): return lax.ppermute(array, axis, [(i, i ^ bit) for i in range(size)])  56.4 us
    dot_general x16, matrix products, dot_tn(): lax.dot_general(a, b, (((0,), (0,)), ((), ())), preferred_element_type=F32)  18.4 us
    pallas_call x2, Pallas kernels, attend_back(): pl.pallas_call(functools.partial(attend_back_kernel, parts, first, last),...  16.5 us
    unnamed x181, local copies, waits for them, and re-layouts  14.4 us
    pallas_call x2, Pallas kernels, mlp_both(): pl.pallas_call(functools.partial(mlp_kernel, size // tile), grid=(count /...  10.9 us
    pallas_call x2, Pallas kernels, attend_forward(): pl.pallas_call(functools.partial(attend_kernel, len(halves)), grid=(pairs...  10.8 us
    mul x2, other arithmetic, per_device(): token, totals[s] = tie(token, s.held.astype(F32) * factor)  9.6 us
  transfers between devices with their start and end apart: 53, of which 22 were waited for; matrix products, arithmetic and copies ran while one was open for 22% of the time, Pallas kernels for 13%

profile of v6, /device:TPU:0, one launch (start us, length us, event | category | flops | bytes accessed | tf_op | source)
XLA Modules:
  0.0 286.6 jit_solution(15533526193294759768)
XLA Ops:
  2.9 1.9 multiply_sine_fusion
  4.9 1.6 fusion.69
  8.8 2.6 collective-permute-start
  14.2 9.7 %collective-permute-done = bf16[256,1024]{1,0:T(8,128)(2,1)S(1)} collective-permute-done((bf16[256,1024]{1,0:T(8,128)(2,1)S(1)}, bf16[256,1024]{1,0:T(8,128)(2,1)S(1)}, u32[]{:S(2)}, u32[]{:S(2)}) %collective-permute-start) | collective-permute-done | bytes 524320 | tf_op jit(solution)/shard_map/ppermute | solution.py:312
  24.2 1.8 collective-permute-start.7
  28.1 5.5 %attend_forward.2 = (bf16[512,256]{1,0:T(8,128)(2,1)S(1)}, f32[2,8,512]{2,1,0:T(8,128)S(1)}) custom-call(bf16[512,768]{1,0:T(8,128)(2,1)S(1)} %add_convert_fusion.9.q_ref.refs_1_.refs_3_, bf16[512,128]{1,0:T(8,128)(2,1)S(1)} %fusion.33.pick_ref, bf16[512,768]{1,0:T(8,128)(2,1)S(1)} %add_convert_fusion.10.refs_0_.refs_2_.q_ref, ...), custom_call_target="tpu_custom_call" | custom-call | flops 1024 | bytes 1024 | tf_op jit(solution)/shard_map/attend_forward/pallas_call | solution.py:73
  35.0 3.6 %collective-permute-done.7 = bf16[256,1024]{1,0:T(8,128)(2,1)S(1)} collective-permute-done((bf16[256,1024]{1,0:T(8,128)(2,1)S(1)}, bf16[256,1024]{1,0:T(8,128)(2,1)S(1)}, u32[]{:S(2)}, u32[]{:S(2)}) %collective-permute-start.7) | collective-permute-done | bytes 524320 | tf_op jit(solution)/shard_map/ppermute | solution.py:312
  38.8 1.8 collective-permute-start.5
  40.6 5.3 %attend_forward.3 = (bf16[512,256]{1,0:T(8,128)(2,1)S(1)}, f32[2,8,512]{2,1,0:T(8,128)S(1)}) custom-call(bf16[512,768]{1,0:T(8,128)(2,1)S(1)} %add_convert_fusion.10.refs_0_.refs_2_.q_ref, bf16[512,128]{1,0:T(8,128)(2,1)S(1)} %fusion.32.pick_ref, bf16[512,768]{1,0:T(8,128)(2,1)S(1)} %add_convert_fusion.10.refs_0_.refs_2_.q_ref, ...), custom_call_target="tpu_custom_call" | custom-call | flops 1024 | bytes 1024 | tf_op jit(solution)/shard_map/attend_forward/pallas_call | solution.py:73
  48.3 5.0 %collective-permute-done.5 = bf16[256,1024]{1,0:T(8,128)(2,1)S(1)} collective-permute-done((bf16[256,1024]{1,0:T(8,128)(2,1)S(1)}, bf16[256,1024]{1,0:T(8,128)(2,1)S(1)}, u32[]{:S(2)}, u32[]{:S(2)}) %collective-permute-start.5) | collective-permute-done | bytes 524320 | tf_op jit(solution)/shard_map/ppermute | solution.py:312
  54.3 1.8 collective-permute-start.9
  57.0 5.8 %mlp_both.2 = (bf16[512,1024]{1,0:T(8,128)(2,1)S(1)}, bf16[512,1024]{1,0:T(8,128)(2,1)S(1)}, bf16[256,1024]{1,0:T(8,128)(2,1)S(1)}, bf16[256,1024]{1,0:T(8,128)(...) custom-call(bf16[512,1024]{1,0:T(8,128)(2,1)S(1)} %pad_maximum_fusion.3.x_ref, ...), custom_call_target="tpu_custom_call" | custom-call | flops 1024 | bytes 1024 | tf_op jit(solution)/shard_map/mlp_both/pallas_call | solution.py:237
  67.1 1.6 collective-permute-done.9
  75.2 5.2 %mlp_both.3 = (bf16[512,1024]{1,0:T(8,128)(2,1)S(1)}, bf16[512,1024]{1,0:T(8,128)(2,1)S(1)}, bf16[256,1024]{1,0:T(8,128)(2,1)S(1)}, bf16[256,1024]{1,0:T(8,128)(...) custom-call(bf16[512,1024]{1,0:T(8,128)(2,1)S(1)} %constant_dynamic-update-slice_fusion.2.x_ref, ...), custom_call_target="tpu_custom_call" | custom-call | flops 1024 | bytes 1024 | tf_op jit(solution)/shard_map/mlp_both/pallas_call | solution.py:237
  82.2 1.8 add_convert_fusion.5
  85.7 1.8 add_convert_fusion.4
  87.5 1.7 collective-permute-start.14
  93.1 1.7 add_convert_fusion.3
  95.6 1.8 add_convert_fusion.2
  97.4 4.1 %collective-permute-done.14 = bf16[256,1024]{1,0:T(8,128)(2,1)S(1)} collective-permute-done((bf16[256,1024]{1,0:T(8,128)(2,1)S(1)}, bf16[256,1024]{1,0:T(8,128)(2,1)S(1)}, u32[]{:S(2)}, u32[]{:S(2)}) %collective-permute-start.14) | collective-permute-done | bytes 524320 | tf_op jit(solution)/shard_map/ppermute | solution.py:312
  104.7 1.8 collective-permute-start.17
  109.3 7.9 %attend_back.2 = (bf16[512,256]{1,0:T(8,128)(2,1)S(1)}, f32[512,256]{1,0:T(8,128)S(1)}, f32[512,256]{1,0:T(8,128)S(1)}, f32[512,256]{1,0:T(8,128)S(1)}, f32[512,256]{1,0:T(8,128)S(1)}) custom-call(bf16[512,768]{1,0:T(8,128)(2,1)S(1)} %add_convert_fusion.10.refs_0_.refs_2_.q_ref, bf16[512,128]{1,0:T(8,128)(2,1)S(1)} %copy-done.17, ...), custom_call_target="tpu_custom_call" | custom-call | flops 1024 | bytes 1024 | tf_op jit(solution)/shard_map/attend_back/pallas_call | solution.py:184
  117.2 1.8 collective-permute-done.17
  119.2 1.7 add_convert_fusion
  120.9 1.6 add_convert_fusion.1
  123.8 1.9 collective-permute-start.22
  127.5 2.1 fusion
  130.7 8.6 %attend_back.3 = (bf16[512,256]{1,0:T(8,128)(2,1)S(1)}, bf16[512,256]{1,0:T(8,128)(2,1)S(1)}, bf16[512,256]{1,0:T(8,128)(2,1)S(1)}, bf16[512,256]{1,0:T(8,128)(2,1)S(1)}, bf16[512,256]{1,0:T(8,128)(2,1)S(1)}) custom-call(bf16[512,768]{1,0:T(8,128)(2,1)S(1)} %add_convert_fusion.9.q_ref.refs_1_.refs_3_, bf16[512,128]{1,0:T(8,128)(2,1)S(1)} %fusion.33.pick_ref, ...), custom_call_target="tpu_custom_call" | custom-call | flops 1024 | bytes 1024 | tf_op jit(solution)/shard_map/attend_back/pallas_call | solution.py:184
  145.9 2.7 collective-permute-start.29
  149.2 2.2 fusion.1
  159.0 10.2 %collective-permute-done.25 = bf16[256,1024]{1,0:T(8,128)(2,1)S(1)} collective-permute-done((bf16[256,1024]{1,0:T(8,128)(2,1)S(1)}, bf16[256,1024]{1,0:T(8,128)(2,1)S(1)}, u32[]{:S(2)}, u32[]{:S(2)}) %collective-permute-start.25) | collective-permute-done | bytes 524320 | tf_op jit(solution)/shard_map/ppermute | solution.py:312
  173.0 3.0 %multiply_add_fusion = f32[256,1024]{1,0:T(8,128)} fusion(f32[256,1024]{1,0:T(8,128)} %get-tuple-element.389, f32[256,1024]{1,0:T(8,128)S(1)} %copy-done.37, f32[256]{0:T(256)S(1)} %broadcast_multiply_fusion, f32[256]{0:T(256)S(1)} %broadcast_multiply_fusion.1, f32[1024]{0:T(1024)S(1)} %copy-done.73, f32[256]{0:T(256)S(1)} %copy-done.79, ...), kind=kLoop, calls=%fused_computation.65 | loop fusion | flops 3407872 | bytes 4726784 | tf_op jit(solution)/shard_map/add | solution.py:607
  185.2 2.6 collective-permute-start.36
  188.1 18.8 %collective-permute-done.35 = bf16[64,1024]{1,0:T(8,128)(2,1)S(1)} collective-permute-done((bf16[64,1024]{1,0:T(8,128)(2,1)S(1)}, bf16[64,1024]{1,0:T(8,128)(2,1)S(1)}, u32[]{:S(2)}, u32[]{:S(2)}) %collective-permute-start.35) | collective-permute-done | bytes 131104 | tf_op jit(solution)/shard_map/ppermute | solution.py:312
  207.1 2.8 collective-permute-done.37
  210.0 3.0 %collective-permute-start.39 = (bf16[32,1024]{1,0:T(8,128)(2,1)S(1)}, bf16[32,1024]{1,0:T(8,128)(2,1)S(1)}, u32[]{:S(2)}, u32[]{:S(2)}) collective-permute-start(bf16[32,1024]{1,0:T(8,128)(2,1)S(1)} %dynamic-slice_bitcast_fusion.7), channel_id=1, source_target_pairs={{0,16},{4,20},{8,24},{12,28},{16,0},{20,4},{24,8},{28,12},{1,17},{... | collective-permute-start | bytes 196616 | tf_op jit(solution)/shard_map/ppermute | solution.py:312
  213.2 4.1 %collective-permute-start.41 = (bf16[256,1024]{1,0:T(8,128)(2,1)S(1)}, bf16[256,1024]{1,0:T(8,128)(2,1)S(1)}, u32[]{:S(2)}, u32[]{:S(2)}) collective-permute-start(bf16[256,1024]{1,0:T(8,128)(2,1)S(1)} %maximum_select_fusion.6), channel_id=1, source_target_pairs={{0,8},{4,12},{8,0},{12,4},{16,24},{20,28},{24,16},{28,20},{1,9},{5... | collective-permute-start | bytes 1572872 | tf_op jit(solution)/shard_map/ppermute | solution.py:312
  219.3 7.5 %collective-permute-done.40 = f32[7808]{0:T(1024)S(1)} collective-permute-done((f32[7808]{0:T(1024)S(1)}, f32[7808]{0:T(1024)S(1)}, u32[]{:S(2)}, u32[]{:S(2)}) %collective-permute-start.40) | collective-permute-done | bytes 31264 | tf_op jit(solution)/shard_map/ppermute | solution.py:312
  226.9 3.0 %collective-permute-start.43 = (bf16[128,768]{1,0:T(8,128)(2,1)S(1)}, bf16[128,768]{1,0:T(8,128)(2,1)S(1)}, u32[]{:S(2)}, u32[]{:S(2)}) collective-permute-start(bf16[128,768]{1,0:T(8,128)(2,1)S(1)} %fusion.30), channel_id=1, source_target_pairs={{0,16},{4,20},{8,24},{12,28},{16,0},{20,4},{24,8},{28,12},{1,17},{... | collective-permute-start | bytes 589832 | tf_op jit(solution)/shard_map/ppermute | solution.py:312
  233.3 3.9 %collective-permute-done.45 = f32[7808]{0:T(1024)S(1)} collective-permute-done((f32[7808]{0:T(1024)S(1)}, f32[7808]{0:T(1024)S(1)}, u32[]{:S(2)}, u32[]{:S(2)}) %collective-permute-start.45) | collective-permute-done | bytes 31264 | tf_op jit(solution)/shard_map/ppermute | solution.py:312
  237.4 2.5 collective-permute-start.46
  240.0 2.1 collective-permute-start.48
  244.7 8.3 %collective-permute-done.48 = f32[7808]{0:T(1024)S(1)} collective-permute-done((f32[7808]{0:T(1024)S(1)}, f32[7808]{0:T(1024)S(1)}, u32[]{:S(2)}, u32[]{:S(2)}) %collective-permute-start.48) | collective-permute-done | bytes 31264 | tf_op jit(solution)/shard_map/ppermute | solution.py:312
  259.6 9.0 %collective-permute-done.49 = bf16[512,1024]{1,0:T(8,128)(2,1)} collective-permute-done((bf16[512,1024]{1,0:T(8,128)(2,1)}, bf16[512,1024]{1,0:T(8,128)(2,1)}, u32[]{:S(2)}, u32[]{:S(2)}) %collective-permute-start.49) | collective-permute-done | bytes 1048608 | tf_op jit(solution)/shard_map/ppermute | solution.py:312
  269.1 5.2 %convert_multiply_fusion.1 = f32[1024,1024]{1,0:T(8,128)} fusion(bf16[512,1024]{1,0:T(8,128)(2,1)} %maximum_select_fusion.3, bf16[512,1024]{1,0:T(8,128)(2,1)} %collective-permute-done.49, f32[]{:T(128)} %bitcast.38, pred[]{:T(512)S(6)} %ne.10), kind=kLoop, calls=%fused_computation.1 | loop fusion | flops 11534336 | bytes 6291461 | tf_op jit(solution)/shard_map/mul | solution.py:667
  274.4 4.4 %convert_multiply_fusion = f32[1024,1024]{1,0:T(8,128)} fusion(bf16[512,1024]{1,0:T(8,128)(2,1)S(1)} %maximum_select_fusion.4, bf16[512,1024]{1,0:T(8,128)(2,1)} %collective-permute-done.50, f32[]{:T(128)} %bitcast.38, pred[]{:T(512)S(6)} %ne.12), kind=kLoop, calls=%fused_computation | loop fusion | flops 11534336 | bytes 6291461 | tf_op jit(solution)/shard_map/mul | solution.py:667
  278.7 3.9 %collective-permute-done.52 = bf16[128,1024]{1,0:T(8,128)(2,1)S(1)} collective-permute-done((bf16[128,1024]{1,0:T(8,128)(2,1)S(1)}, bf16[128,1024]{1,0:T(8,128)(2,1)S(1)}, u32[]{:S(2)}, u32[]{:S(2)}) %collective-permute-start.52) | collective-permute-done | bytes 262176 | tf_op jit(solution)/shard_map/ppermute | solution.py:312
  284.5 1.9 pad_maximum_fusion
  (375 shorter events, 86.7 us)
Async XLA Ops:
  8.3 4.9 %collective-permute-start.1 = (bf16[256,1024]{1,0:T(8,128)(2,1)S(1)}, bf16[256,1024]{1,0:T(8,128)(2,1)S(1)}, u32[]{:S(2)}, u32[]{:S(2)}) collective-permute-start(bf16[256,1024]{1,0:T(8,128)(2,1)S(1)} %add_convert_fusion.17), channel_id=1, source_target_pairs={{0,1},{1,0},{2,3},{3,2},{4,5},{5,4},{6,7},{7,6},{8,9},{9,8},{10,11... | collective-permute-start | bytes 1572872 | tf_op jit(solution)/shard_map/ppermute | solution.py:312
  8.8 15.1 %collective-permute-start = (bf16[256,1024]{1,0:T(8,128)(2,1)S(1)}, bf16[256,1024]{1,0:T(8,128)(2,1)S(1)}, u32[]{:S(2)}, u32[]{:S(2)}) collective-permute-start(bf16[256,1024]{1,0:T(8,128)(2,1)S(1)} %add_convert_fusion.17), channel_id=1, source_target_pairs={{0,2},{1,3},{2,0},{3,1},{4,6},{5,7},{6,4},{7,5},{8,10},{9,11},{10,... | collective-permute-start | bytes 1572872 | tf_op jit(solution)/shard_map/ppermute | solution.py:312
  24.2 14.4 %collective-permute-start.7 = (bf16[256,1024]{1,0:T(8,128)(2,1)S(1)}, bf16[256,1024]{1,0:T(8,128)(2,1)S(1)}, u32[]{:S(2)}, u32[]{:S(2)}) collective-permute-start(bf16[256,1024]{1,0:T(8,128)(2,1)S(1)} %get-tuple-element.287), channel_id=1, source_target_pairs={{0,2},{1,3},{2,0},{3,1},{4,6},{5,7},{6,4},{7,5},{8,10},{9,11},{10,... | collective-permute-start | bytes 1572872 | tf_op jit(solution)/shard_map/ppermute | solution.py:312
  34.2 4.4 %collective-permute-start.3 = (bf16[256,1024]{1,0:T(8,128)(2,1)S(1)}, bf16[256,1024]{1,0:T(8,128)(2,1)S(1)}, u32[]{:S(2)}, u32[]{:S(2)}) collective-permute-start(bf16[256,1024]{1,0:T(8,128)(2,1)S(1)} %slice.128), channel_id=1, source_target_pairs={{0,1},{1,0},{2,3},{3,2},{4,5},{5,4},{6,7},{7,6},{8,9},{9,8},{10,11... | collective-permute-start | bytes 1572872 | tf_op jit(solution)/shard_map/ppermute | solution.py:312
  34.6 12.2 %collective-permute-start.6 = (bf16[256,1024]{1,0:T(8,128)(2,1)S(1)}, bf16[256,1024]{1,0:T(8,128)(2,1)S(1)}, u32[]{:S(2)}, u32[]{:S(2)}) collective-permute-start(bf16[256,1024]{1,0:T(8,128)(2,1)S(1)} %get-tuple-element.287), channel_id=1, source_target_pairs={{0,1},{1,0},{2,3},{3,2},{4,5},{5,4},{6,7},{7,6},{8,9},{9,8},{10,11... | collective-permute-start | bytes 1572872 | tf_op jit(solution)/shard_map/ppermute | solution.py:312
  38.6 8.6 %collective-permute-start.8 = (bf16[256,1024]{1,0:T(8,128)(2,1)S(1)}, bf16[256,1024]{1,0:T(8,128)(2,1)S(1)}, u32[]{:S(2)}, u32[]{:S(2)}) collective-permute-start(bf16[256,1024]{1,0:T(8,128)(2,1)S(1)} %collective-permute-done.7), channel_id=1, source_target_pairs={{0,1},{1,0},{2,3},{3,2},{4,5},{5,4},{6,7},{7,6},{8,9},{9,8},{10,11... | collective-permute-start | bytes 1572872 | tf_op jit(solution)/shard_map/ppermute | solution.py:312
  38.8 14.4 %collective-permute-start.5 = (bf16[256,1024]{1,0:T(8,128)(2,1)S(1)}, bf16[256,1024]{1,0:T(8,128)(2,1)S(1)}, u32[]{:S(2)}, u32[]{:S(2)}) collective-permute-start(bf16[256,1024]{1,0:T(8,128)(2,1)S(1)} %add_convert_fusion.16), channel_id=1, source_target_pairs={{0,2},{1,3},{2,0},{3,1},{4,6},{5,7},{6,4},{7,5},{8,10},{9,11},{10,... | collective-permute-start | bytes 1572872 | tf_op jit(solution)/shard_map/ppermute | solution.py:312
  46.5 6.7 %collective-permute-start.4 = (bf16[256,1024]{1,0:T(8,128)(2,1)S(1)}, bf16[256,1024]{1,0:T(8,128)(2,1)S(1)}, u32[]{:S(2)}, u32[]{:S(2)}) collective-permute-start(bf16[256,1024]{1,0:T(8,128)(2,1)S(1)} %slice.130), channel_id=1, source_target_pairs={{0,1},{1,0},{2,3},{3,2},{4,5},{5,4},{6,7},{7,6},{8,9},{9,8},{10,11... | collective-permute-start | bytes 1572872 | tf_op jit(solution)/shard_map/ppermute | solution.py:312
  54.3 14.4 %collective-permute-start.9 = (bf16[256,1024]{1,0:T(8,128)(2,1)S(1)}, bf16[256,1024]{1,0:T(8,128)(2,1)}, u32[]{:S(2)}, u32[]{:S(2)}) collective-permute-start(bf16[256,1024]{1,0:T(8,128)(2,1)S(1)} %add_convert_fusion.15), channel_id=1, source_target_pairs={{0,2},{1,3},{2,0},{3,1},{4,6},{5,7},{6,4},{7,5},{8,10},{9,11},{10,... | collective-permute-start | bytes 1572872 | tf_op jit(solution)/shard_map/ppermute | solution.py:312
  68.7 11.7 %collective-permute-start.12 = (bf16[256,1024]{1,0:T(8,128)(2,1)}, bf16[256,1024]{1,0:T(8,128)(2,1)}, u32[]{:S(2)}, u32[]{:S(2)}) collective-permute-start(bf16[256,1024]{1,0:T(8,128)(2,1)} %get-tuple-element.217), channel_id=1, source_target_pairs={{0,1},{1,0},{2,3},{3,2},{4,5},{5,4},{6,7},{7,6},{8,9},{9,8},{10,11... | collective-permute-start | bytes 1572872 | tf_op jit(solution)/shard_map/ppermute | solution.py:312
  69.2 28.1 %collective-permute-start.16 = (bf16[256,1024]{1,0:T(8,128)(2,1)}, bf16[256,1024]{1,0:T(8,128)(2,1)S(1)}, u32[]{:S(2)}, u32[]{:S(2)}) collective-permute-start(bf16[256,1024]{1,0:T(8,128)(2,1)} %copy-done.31), channel_id=1, source_target_pairs={{0,1},{1,0},{2,3},{3,2},{4,5},{5,4},{6,7},{7,6},{8,9},{9,8},{10,11... | collective-permute-start | bytes 1572872 | tf_op jit(solution)/shard_map/ppermute | solution.py:312
  80.5 3.5 %collective-permute-start.13 = (bf16[256,1024]{1,0:T(8,128)(2,1)S(1)}, bf16[256,1024]{1,0:T(8,128)(2,1)S(1)}, u32[]{:S(2)}, u32[]{:S(2)}) collective-permute-start(bf16[256,1024]{1,0:T(8,128)(2,1)S(1)} %get-tuple-element.225), channel_id=1, source_target_pairs={{0,1},{1,0},{2,3},{3,2},{4,5},{5,4},{6,7},{7,6},{8,9},{9,8},{10,11... | collective-permute-start | bytes 1572872 | tf_op jit(solution)/shard_map/ppermute | solution.py:312
  80.7 16.7 %collective-permute-start.15 = (bf16[256,1024]{1,0:T(8,128)(2,1)S(1)}, bf16[256,1024]{1,0:T(8,128)(2,1)S(1)}, u32[]{:S(2)}, u32[]{:S(2)}) collective-permute-start(bf16[256,1024]{1,0:T(8,128)(2,1)S(1)} %get-tuple-element.240), channel_id=1, source_target_pairs={{0,1},{1,0},{2,3},{3,2},{4,5},{5,4},{6,7},{7,6},{8,9},{9,8},{10,11... | collective-permute-start | bytes 1572872 | tf_op jit(solution)/shard_map/ppermute | solution.py:312
  87.5 14.0 %collective-permute-start.14 = (bf16[256,1024]{1,0:T(8,128)(2,1)S(1)}, bf16[256,1024]{1,0:T(8,128)(2,1)S(1)}, u32[]{:S(2)}, u32[]{:S(2)}) collective-permute-start(bf16[256,1024]{1,0:T(8,128)(2,1)S(1)} %add_convert_fusion.14), channel_id=1, source_target_pairs={{0,2},{1,3},{2,0},{3,1},{4,6},{5,7},{6,4},{7,5},{8,10},{9,11},{10,... | collective-permute-start | bytes 1572872 | tf_op jit(solution)/shard_map/ppermute | solution.py:312
  89.3 29.8 %collective-permute-start.20 = (bf16[512,1024]{1,0:T(8,128)(2,1)}, bf16[512,1024]{1,0:T(8,128)(2,1)}, u32[]{:S(2)}, u32[]{:S(2)}) collective-permute-start(bf16[512,1024]{1,0:T(8,128)(2,1)} %add_convert_fusion.4), channel_id=1, source_target_pairs={{0,8},{4,12},{8,0},{12,4},{16,24},{20,28},{24,16},{28,20},{1,9},{5... | collective-permute-start | bytes 3145736 | tf_op jit(solution)/shard_map/ppermute | solution.py:312
  90.9 28.2 %collective-permute-start.19 = (bf16[512,1024]{1,0:T(8,128)(2,1)}, bf16[512,1024]{1,0:T(8,128)(2,1)}, u32[]{:S(2)}, u32[]{:S(2)}) collective-permute-start(bf16[512,1024]{1,0:T(8,128)(2,1)} %add_convert_fusion.5), channel_id=1, source_target_pairs={{0,4},{4,0},{8,12},{12,8},{16,20},{20,16},{24,28},{28,24},{1,5},{5... | collective-permute-start | bytes 3145736 | tf_op jit(solution)/shard_map/ppermute | solution.py:312
  104.6 3.2 %collective-permute-start.18 = (bf16[256,1024]{1,0:T(8,128)(2,1)S(1)}, bf16[256,1024]{1,0:T(8,128)(2,1)}, u32[]{:S(2)}, u32[]{:S(2)}) collective-permute-start(bf16[256,1024]{1,0:T(8,128)(2,1)S(1)} %get-tuple-element.286), channel_id=1, source_target_pairs={{0,1},{1,0},{2,3},{3,2},{4,5},{5,4},{6,7},{7,6},{8,9},{9,8},{10,11... | collective-permute-start | bytes 1572872 | tf_op jit(solution)/shard_map/ppermute | solution.py:312
  104.7 14.4 %collective-permute-start.17 = (bf16[256,1024]{1,0:T(8,128)(2,1)S(1)}, bf16[256,1024]{1,0:T(8,128)(2,1)}, u32[]{:S(2)}, u32[]{:S(2)}) collective-permute-start(bf16[256,1024]{1,0:T(8,128)(2,1)S(1)} %get-tuple-element.286), channel_id=1, source_target_pairs={{0,2},{1,3},{2,0},{3,1},{4,6},{5,7},{6,4},{7,5},{8,10},{9,11},{10,... | collective-permute-start | bytes 1572872 | tf_op jit(solution)/shard_map/ppermute | solution.py:312
  119.1 3.5 %collective-permute-start.21 = (bf16[256,1024]{1,0:T(8,128)(2,1)}, bf16[256,1024]{1,0:T(8,128)(2,1)S(1)}, u32[]{:S(2)}, u32[]{:S(2)}) collective-permute-start(bf16[256,1024]{1,0:T(8,128)(2,1)} %collective-permute-done.17), channel_id=1, source_target_pairs={{0,1},{1,0},{2,3},{3,2},{4,5},{5,4},{6,7},{7,6},{8,9},{9,8},{10,11... | collective-permute-start | bytes 1572872 | tf_op jit(solution)/shard_map/ppermute | solution.py:312
  123.8 15.5 %collective-permute-start.22 = (bf16[256,1024]{1,0:T(8,128)(2,1)S(1)}, bf16[256,1024]{1,0:T(8,128)(2,1)S(1)}, u32[]{:S(2)}, u32[]{:S(2)}) collective-permute-start(bf16[256,1024]{1,0:T(8,128)(2,1)S(1)} %dynamic-slice_bitcast_fusion.1), channel_id=1, source_target_pairs={{0,8},{4,12},{8,0},{12,4},{16,24},{20,28},{24,16},{28,20},{1,9},{5... | collective-permute-start | bytes 1572872 | tf_op jit(solution)/shard_map/ppermute | solution.py:312
  125.7 14.8 %collective-permute-start.23 = (bf16[256,1024]{1,0:T(8,128)(2,1)S(1)}, bf16[256,1024]{1,0:T(8,128)(2,1)S(1)}, u32[]{:S(2)}, u32[]{:S(2)}) collective-permute-start(bf16[256,1024]{1,0:T(8,128)(2,1)S(1)} %dynamic-slice_bitcast_fusion), channel_id=1, source_target_pairs={{0,4},{4,0},{8,12},{12,8},{16,20},{20,16},{24,28},{28,24},{1,5},{5... | collective-permute-start | bytes 1572872 | tf_op jit(solution)/shard_map/ppermute | solution.py:312
  130.1 46.0 %collective-permute-start.32 = (bf16[128,1024]{1,0:T(8,128)(2,1)}, bf16[128,1024]{1,0:T(8,128)(2,1)}, u32[]{:S(2)}, u32[]{:S(2)}) collective-permute-start(bf16[128,1024]{1,0:T(8,128)(2,1)} %fusion), channel_id=1, source_target_pairs={{0,4},{4,0},{8,12},{12,8},{16,20},{20,16},{24,28},{28,24},{1,5},{5... | collective-permute-start | bytes 786440 | tf_op jit(solution)/shard_map/ppermute | solution.py:312
  145.8 7.7 %collective-permute-start.24 = (bf16[256,1024]{1,0:T(8,128)(2,1)S(1)}, bf16[256,1024]{1,0:T(8,128)(2,1)S(1)}, u32[]{:S(2)}, u32[]{:S(2)}) collective-permute-start(bf16[256,1024]{1,0:T(8,128)(2,1)S(1)} %slice.132), channel_id=1, source_target_pairs={{0,1},{1,0},{2,3},{3,2},{4,5},{5,4},{6,7},{7,6},{8,9},{9,8},{10,11... | collective-permute-start | bytes 1572872 | tf_op jit(solution)/shard_map/ppermute | solution.py:312
  145.9 30.2 %collective-permute-start.29 = (bf16[128,1024]{1,0:T(8,128)(2,1)}, bf16[128,1024]{1,0:T(8,128)(2,1)}, u32[]{:S(2)}, u32[]{:S(2)}) collective-permute-start(bf16[128,1024]{1,0:T(8,128)(2,1)} %dynamic-slice_bitcast_fusion.4), channel_id=1, source_target_pairs={{0,16},{4,20},{8,24},{12,28},{16,0},{20,4},{24,8},{28,12},{1,17},{... | collective-permute-start | bytes 786440 | tf_op jit(solution)/shard_map/ppermute | solution.py:312
  148.5 27.5 %collective-permute-start.30 = (bf16[128,1024]{1,0:T(8,128)(2,1)}, bf16[128,1024]{1,0:T(8,128)(2,1)}, u32[]{:S(2)}, u32[]{:S(2)}) collective-permute-start(bf16[128,1024]{1,0:T(8,128)(2,1)} %dynamic-slice_bitcast_fusion.3), channel_id=1, source_target_pairs={{0,16},{4,20},{8,24},{12,28},{16,0},{20,4},{24,8},{28,12},{1,17},{... | collective-permute-start | bytes 786440 | tf_op jit(solution)/shard_map/ppermute | solution.py:312
  154.9 14.3 %collective-permute-start.25 = (bf16[256,1024]{1,0:T(8,128)(2,1)S(1)}, bf16[256,1024]{1,0:T(8,128)(2,1)S(1)}, u32[]{:S(2)}, u32[]{:S(2)}) collective-permute-start(bf16[256,1024]{1,0:T(8,128)(2,1)S(1)} %add_convert_fusion.13), channel_id=1, source_target_pairs={{0,2},{1,3},{2,0},{3,1},{4,6},{5,7},{6,4},{7,5},{8,10},{9,11},{10,... | collective-permute-start | bytes 1572872 | tf_op jit(solution)/shard_map/ppermute | solution.py:312
  157.4 20.0 %collective-permute-start.31 = (bf16[512,768]{1,0:T(8,128)(2,1)}, bf16[512,768]{1,0:T(8,128)(2,1)}, u32[]{:S(2)}, u32[]{:S(2)}) collective-permute-start(bf16[512,768]{1,0:T(8,128)(2,1)} %add_convert_fusion.8), channel_id=1, source_target_pairs={{0,4},{4,0},{8,12},{12,8},{16,20},{20,16},{24,28},{28,24},{1,5},{5... | collective-permute-start | bytes 2359304 | tf_op jit(solution)/shard_map/ppermute | solution.py:312
  171.5 4.5 %collective-permute-start.28 = (f32[6,1024]{1,0:T(8,128)S(1)}, f32[6,1024]{1,0:T(8,128)S(1)}, u32[]{:S(2)}, u32[]{:S(2)}) collective-permute-start(f32[6,1024]{1,0:T(8,128)S(1)} %add.318), channel_id=1, source_target_pairs={{0,2},{1,3},{2,0},{3,1},{4,6},{5,7},{6,4},{7,5},{8,10},{9,11},{10,... | collective-permute-start | bytes 73736 | tf_op jit(solution)/shard_map/ppermute | solution.py:312
  182.4 24.6 %collective-permute-start.33 = (bf16[256,1024]{1,0:T(8,128)(2,1)S(1)}, bf16[256,1024]{1,0:T(8,128)(2,1)S(1)}, u32[]{:S(2)}, u32[]{:S(2)}) collective-permute-start(bf16[256,1024]{1,0:T(8,128)(2,1)S(1)} %add_convert_fusion.12), channel_id=1, source_target_pairs={{0,2},{1,3},{2,0},{3,1},{4,6},{5,7},{6,4},{7,5},{8,10},{9,11},{10,... | collective-permute-start | bytes 1572872 | tf_op jit(solution)/shard_map/ppermute | solution.py:312
  183.1 23.8 %collective-permute-start.34 = (bf16[256,768]{1,0:T(8,128)(2,1)S(1)}, bf16[256,768]{1,0:T(8,128)(2,1)S(1)}, u32[]{:S(2)}, u32[]{:S(2)}) collective-permute-start(bf16[256,768]{1,0:T(8,128)(2,1)S(1)} %dynamic-slice_bitcast_fusion.2), channel_id=1, source_target_pairs={{0,8},{4,12},{8,0},{12,4},{16,24},{20,28},{24,16},{28,20},{1,9},{5... | collective-permute-start | bytes 1179656 | tf_op jit(solution)/shard_map/ppermute | solution.py:312
  183.6 23.3 %collective-permute-start.35 = (bf16[64,1024]{1,0:T(8,128)(2,1)S(1)}, bf16[64,1024]{1,0:T(8,128)(2,1)S(1)}, u32[]{:S(2)}, u32[]{:S(2)}) collective-permute-start(bf16[64,1024]{1,0:T(8,128)(2,1)S(1)} %dynamic-slice_bitcast_fusion.6), channel_id=1, source_target_pairs={{0,8},{4,12},{8,0},{12,4},{16,24},{20,28},{24,16},{28,20},{1,9},{5... | collective-permute-start | bytes 393224 | tf_op jit(solution)/shard_map/ppermute | solution.py:312
  185.2 22.0 %collective-permute-start.36 = (bf16[128,1024]{1,0:T(8,128)(2,1)S(1)}, bf16[128,1024]{1,0:T(8,128)(2,1)S(1)}, u32[]{:S(2)}, u32[]{:S(2)}) collective-permute-start(bf16[128,1024]{1,0:T(8,128)(2,1)S(1)} %fusion.15), channel_id=1, source_target_pairs={{0,16},{4,20},{8,24},{12,28},{16,0},{20,4},{24,8},{28,12},{1,17},{... | collective-permute-start | bytes 786440 | tf_op jit(solution)/shard_map/ppermute | solution.py:312
  187.8 22.1 %collective-permute-start.37 = (bf16[128,1024]{1,0:T(8,128)(2,1)S(1)}, bf16[128,1024]{1,0:T(8,128)(2,1)S(1)}, u32[]{:S(2)}, u32[]{:S(2)}) collective-permute-start(bf16[128,1024]{1,0:T(8,128)(2,1)S(1)} %fusion.14), channel_id=1, source_target_pairs={{0,16},{4,20},{8,24},{12,28},{16,0},{20,4},{24,8},{28,12},{1,17},{... | collective-permute-start | bytes 786440 | tf_op jit(solution)/shard_map/ppermute | solution.py:312
  209.9 16.9 %collective-permute-start.38 = (bf16[128,768]{1,0:T(8,128)(2,1)S(1)}, bf16[128,768]{1,0:T(8,128)(2,1)S(1)}, u32[]{:S(2)}, u32[]{:S(2)}) collective-permute-start(bf16[128,768]{1,0:T(8,128)(2,1)S(1)} %dynamic-slice_bitcast_fusion.5), channel_id=1, source_target_pairs={{0,16},{4,20},{8,24},{12,28},{16,0},{20,4},{24,8},{28,12},{1,17},{... | collective-permute-start | bytes 589832 | tf_op jit(solution)/shard_map/ppermute | solution.py:312
  210.0 16.7 %collective-permute-start.39 = (bf16[32,1024]{1,0:T(8,128)(2,1)S(1)}, bf16[32,1024]{1,0:T(8,128)(2,1)S(1)}, u32[]{:S(2)}, u32[]{:S(2)}) collective-permute-start(bf16[32,1024]{1,0:T(8,128)(2,1)S(1)} %dynamic-slice_bitcast_fusion.7), channel_id=1, source_target_pairs={{0,16},{4,20},{8,24},{12,28},{16,0},{20,4},{24,8},{28,12},{1,17},{... | collective-permute-start | bytes 196616 | tf_op jit(solution)/shard_map/ppermute | solution.py:312
  213.2 17.1 %collective-permute-start.41 = (bf16[256,1024]{1,0:T(8,128)(2,1)S(1)}, bf16[256,1024]{1,0:T(8,128)(2,1)S(1)}, u32[]{:S(2)}, u32[]{:S(2)}) collective-permute-start(bf16[256,1024]{1,0:T(8,128)(2,1)S(1)} %maximum_select_fusion.6), channel_id=1, source_target_pairs={{0,8},{4,12},{8,0},{12,4},{16,24},{20,28},{24,16},{28,20},{1,9},{5... | collective-permute-start | bytes 1572872 | tf_op jit(solution)/shard_map/ppermute | solution.py:312
  217.2 13.0 %collective-permute-start.42 = (bf16[256,1024]{1,0:T(8,128)(2,1)S(1)}, bf16[256,1024]{1,0:T(8,128)(2,1)S(1)}, u32[]{:S(2)}, u32[]{:S(2)}) collective-permute-start(bf16[256,1024]{1,0:T(8,128)(2,1)S(1)} %maximum_select_fusion.7), channel_id=1, source_target_pairs={{0,4},{4,0},{8,12},{12,8},{16,20},{20,16},{24,28},{28,24},{1,5},{5... | collective-permute-start | bytes 1572872 | tf_op jit(solution)/shard_map/ppermute | solution.py:312
  218.7 8.0 %collective-permute-start.40 = (f32[7808]{0:T(1024)S(1)}, f32[7808]{0:T(1024)S(1)}, u32[]{:S(2)}, u32[]{:S(2)}) collective-permute-start(f32[7808]{0:T(1024)S(1)} %constant_dynamic-update-slice_fusion.8), channel_id=1, source_target_pairs={{0,4},{4,0},{8,12},{12,8},{16,20},{20,16},{24,28},{28,24},{1,5},{5... | collective-permute-start | bytes 93704 | tf_op jit(solution)/shard_map/ppermute | solution.py:312
  226.9 10.4 %collective-permute-start.43 = (bf16[128,768]{1,0:T(8,128)(2,1)S(1)}, bf16[128,768]{1,0:T(8,128)(2,1)S(1)}, u32[]{:S(2)}, u32[]{:S(2)}) collective-permute-start(bf16[128,768]{1,0:T(8,128)(2,1)S(1)} %fusion.30), channel_id=1, source_target_pairs={{0,16},{4,20},{8,24},{12,28},{16,0},{20,4},{24,8},{28,12},{1,17},{... | collective-permute-start | bytes 589832 | tf_op jit(solution)/shard_map/ppermute | solution.py:312
  229.9 7.4 %collective-permute-start.44 = (bf16[32,1024]{1,0:T(8,128)(2,1)S(1)}, bf16[32,1024]{1,0:T(8,128)(2,1)S(1)}, u32[]{:S(2)}, u32[]{:S(2)}) collective-permute-start(bf16[32,1024]{1,0:T(8,128)(2,1)S(1)} %fusion.34), channel_id=1, source_target_pairs={{0,16},{4,20},{8,24},{12,28},{16,0},{20,4},{24,8},{28,12},{1,17},{... | collective-permute-start | bytes 196616 | tf_op jit(solution)/shard_map/ppermute | solution.py:312
  230.0 7.3 %collective-permute-start.45 = (f32[7808]{0:T(1024)S(1)}, f32[7808]{0:T(1024)S(1)}, u32[]{:S(2)}, u32[]{:S(2)}) collective-permute-start(f32[7808]{0:T(1024)S(1)} %add.332), channel_id=1, source_target_pairs={{0,8},{4,12},{8,0},{12,4},{16,24},{20,28},{24,16},{28,20},{1,9},{5... | collective-permute-start | bytes 93704 | tf_op jit(solution)/shard_map/ppermute | solution.py:312
  237.4 15.7 %collective-permute-start.46 = (bf16[256,768]{1,0:T(8,128)(2,1)S(1)}, bf16[256,768]{1,0:T(8,128)(2,1)S(1)}, u32[]{:S(2)}, u32[]{:S(2)}) collective-permute-start(bf16[256,768]{1,0:T(8,128)(2,1)S(1)} %maximum_select_fusion.9), channel_id=1, source_target_pairs={{0,8},{4,12},{8,0},{12,4},{16,24},{20,28},{24,16},{28,20},{1,9},{5... | collective-permute-start | bytes 1179656 | tf_op jit(solution)/shard_map/ppermute | solution.py:312
  240.0 13.1 %collective-permute-start.47 = (bf16[64,1024]{1,0:T(8,128)(2,1)S(1)}, bf16[64,1024]{1,0:T(8,128)(2,1)S(1)}, u32[]{:S(2)}, u32[]{:S(2)}) collective-permute-start(bf16[64,1024]{1,0:T(8,128)(2,1)S(1)} %maximum_select_fusion.11), channel_id=1, source_target_pairs={{0,8},{4,12},{8,0},{12,4},{16,24},{20,28},{24,16},{28,20},{1,9},{5... | collective-permute-start | bytes 393224 | tf_op jit(solution)/shard_map/ppermute | solution.py:312
  240.0 12.9 %collective-permute-start.48 = (f32[7808]{0:T(1024)S(1)}, f32[7808]{0:T(1024)S(1)}, u32[]{:S(2)}, u32[]{:S(2)}) collective-permute-start(f32[7808]{0:T(1024)S(1)} %add.338), channel_id=1, source_target_pairs={{0,16},{4,20},{8,24},{12,28},{16,0},{20,4},{24,8},{28,12},{1,17},{... | collective-permute-start | bytes 93704 | tf_op jit(solution)/shard_map/ppermute | solution.py:312
  242.2 26.3 %collective-permute-start.49 = (bf16[512,1024]{1,0:T(8,128)(2,1)}, bf16[512,1024]{1,0:T(8,128)(2,1)}, u32[]{:S(2)}, u32[]{:S(2)}) collective-permute-start(bf16[512,1024]{1,0:T(8,128)(2,1)} %maximum_select_fusion.3), channel_id=1, source_target_pairs={{0,4},{4,0},{8,12},{12,8},{16,20},{20,16},{24,28},{28,24},{1,5},{5... | collective-permute-start | bytes 3145736 | tf_op jit(solution)/shard_map/ppermute | solution.py:312
  243.7 25.4 %collective-permute-start.50 = (bf16[512,1024]{1,0:T(8,128)(2,1)S(1)}, bf16[512,1024]{1,0:T(8,128)(2,1)}, u32[]{:S(2)}, u32[]{:S(2)}) collective-permute-start(bf16[512,1024]{1,0:T(8,128)(2,1)S(1)} %maximum_select_fusion.4), channel_id=1, source_target_pairs={{0,8},{4,12},{8,0},{12,4},{16,24},{20,28},{24,16},{28,20},{1,9},{5... | collective-permute-start | bytes 3145736 | tf_op jit(solution)/shard_map/ppermute | solution.py:312
  254.9 27.7 %collective-permute-start.51 = (bf16[512,768]{1,0:T(8,128)(2,1)S(1)}, bf16[512,768]{1,0:T(8,128)(2,1)S(1)}, u32[]{:S(2)}, u32[]{:S(2)}) collective-permute-start(bf16[512,768]{1,0:T(8,128)(2,1)S(1)} %maximum_select_fusion.5), channel_id=1, source_target_pairs={{0,4},{4,0},{8,12},{12,8},{16,20},{20,16},{24,28},{28,24},{1,5},{5... | collective-permute-start | bytes 2359304 | tf_op jit(solution)/shard_map/ppermute | solution.py:312
  257.8 24.9 %collective-permute-start.52 = (bf16[128,1024]{1,0:T(8,128)(2,1)S(1)}, bf16[128,1024]{1,0:T(8,128)(2,1)S(1)}, u32[]{:S(2)}, u32[]{:S(2)}) collective-permute-start(bf16[128,1024]{1,0:T(8,128)(2,1)S(1)} %maximum_select_fusion.10), channel_id=1, source_target_pairs={{0,4},{4,0},{8,12},{12,8},{16,20},{20,16},{24,28},{28,24},{1,5},{5... | collective-permute-start | bytes 786440 | tf_op jit(solution)/shard_map/ppermute | solution.py:312
  (92 other events, 462.1 us)

commit v7 on v6

--- a/solution.py
+++ b/solution.py
@@ -61,7 +61,7 @@
     out_ref[...] = jnp.concatenate(rows, 0).T.astype(BF16)
 
 
-def attend_forward(own, pick, halves, bars, tile=256):
+def attend_forward(own, pick, halves, bars, tile=512):
     count = own.shape[0]
     width = own.shape[1] // 3
     pairs = width // PAIR
@@ -347,19 +347,16 @@
     def high(self, bit):
         return (self.index & bit) != 0
 
-    def half(self, pairs, other):
-        size = pairs[0][0].shape[1] // 2
-        top = jnp.where(self.high(self.order[0]) != other, size, 0)
-        dots = [
-            dot_tn(lax.dynamic_slice_in_dim(left, top, size, 1), right) for left, right in pairs
-        ]
-        return functools.reduce(jnp.add, dots).astype(BF16)
-
     def open(self, pairs):
-        self.send = self.half(pairs, True)
+        total = functools.reduce(jnp.add, [dot_tn(left, right) for left, right in pairs])
+        rows, width = total.shape
+        halves = total.astype(BF16).reshape(2, rows // 2, width)
+        place = self.high(self.order[0]).astype(jnp.int32)
+        self.send = lax.dynamic_index_in_dim(halves, 1 - place, 0, False)
+        self.held = lax.dynamic_index_in_dim(halves, place, 0, False)
 
     def keep(self, pairs):
-        self.held = self.half(pairs, False)
+        pass
 
     def launch(self):
         self.flying = swap(self.send, "dp", self.count, self.steps[self.at])
@@ -637,10 +634,10 @@
             ),
         )
         sums = [reduce_sum, expand_sum, input_sum, output_sum]
-        token, small.send = await_all((input_gradient, small.send), sums)
+        (token,) = await_all((input_gradient,), sums)
         token, *out_far = start_all((token, *out_far), sums[:2])
         token, *out_far = start_all((token, *out_far), sums[2:])
-        token, out_far = tie(token, add_up(out_far).astype(BF16))
+        token, out_far, small.send = tie(token, add_up(out_far).astype(BF16), small.send)
         out_far = swap(out_far, "mp", n_mp, far_bit)
         quick = [input_sum, output_sum, small]
         slow = [reduce_sum, expand_sum]

time: 292 us -> 292 us (level)
  matrix products: 25.3 us -> 16.7 us
  waiting for transfers between devices: 95.6 us -> 100 us
  local copies, waits for them, and re-layouts: 21.1 us -> 25.2 us
  other arithmetic: 44.5 us -> 48.3 us
    dot_general x16 -> x8, matrix products: 18.4 us -> 9.6 us  [dot_tn(): lax.dot_general(a, b, (((0,), (0,)), ((), ())), preferred_element_type=F32)]
    squeeze x0 -> x4, local copies, waits for them, and re-layouts: none -> 5.18 us  [the longest x3 3.65 us: open(): self.held = lax.dynamic_index_in_dim(halves, place, 0, False)]
    ppermute x53, waiting for transfers between devices: 95.6 us -> 100 us  [swap(): return lax.ppermute(array, axis, [(i, i ^ bit) for i in range(size)])]
    unnamed x181 -> x195, local copies, waits for them, and re-layouts: 14.4 us -> 13.4 us
  transfers between devices with their start and end apart: 53 -> 53, of which waited for: 22 -> 24; matrix products, arithmetic and copies ran while one was open for 22% -> 21% of each run, Pallas kernels for 13% -> 13%
where the time goes in v7:
time: 292 us; the launch traced here: 287 us
  waiting for transfers between devices  100 us (34%)
  starting transfers between devices  54.5 us (19%)
  other arithmetic  48.3 us (17%)
  Pallas kernels  36.7 us (13%)
  local copies, waits for them, and re-layouts  25.2 us (9%)
  matrix products  16.7 us (6%)
  between operations  5.47 us (2%)
    ppermute x53, waiting for transfers between devices, swap(): return lax.ppermute(array, axis, [(i, i ^ bit) for i in range(size)])  100 us
    ppermute x53, starting transfers between devices, swap(): return lax.ppermute(array, axis, [(i, i ^ bit) for i in range(size)])  54.5 us
    pallas_call x2, Pallas kernels, attend_back(): pl.pallas_call(functools.partial(attend_back_kernel, parts, first, last),...  16.4 us
    unnamed x195, local copies, waits for them, and re-layouts  13.4 us
    pallas_call x2, Pallas kernels, mlp_both(): pl.pallas_call(functools.partial(mlp_kernel, size // tile), grid=(count /...  11.4 us
    dot_general x8, matrix products, dot_tn(): lax.dot_general(a, b, (((0,), (0,)), ((), ())), preferred_element_type=F32)  9.6 us
    mul x2, other arithmetic, per_device(): token, totals[s] = tie(token, s.held.astype(F32) * factor)  9.56 us
    pallas_call x2, Pallas kernels, attend_forward(): pl.pallas_call(functools.partial(attend_kernel, len(halves)), grid=(pairs...  8.97 us
  transfers between devices with their start and end apart: 53, of which 24 were waited for; matrix products, arithmetic and copies ran while one was open for 21% of the time, Pallas kernels for 13%

profile of v7, /device:TPU:0, one launch (start us, length us, event | category | flops | bytes accessed | tf_op | source)
XLA Modules:
  0.0 287.1 jit_solution(3809894853672819326)
XLA Ops:
  3.0 1.9 multiply_sine_fusion
  4.9 1.6 fusion.20
  8.0 3.0 %collective-permute-start = (bf16[256,1024]{1,0:T(8,128)(2,1)S(1)}, bf16[256,1024]{1,0:T(8,128)(2,1)S(1)}, u32[]{:S(2)}, u32[]{:S(2)}) collective-permute-start(bf16[256,1024]{1,0:T(8,128)(2,1)S(1)} %add_convert_fusion.14), channel_id=1, source_target_pairs={{0,2},{1,3},{2,0},{3,1},{4,6},{5,7},{6,4},{7,5},{8,10},{9,11},{10,... | collective-permute-start | bytes 1572872 | tf_op jit(solution)/shard_map/ppermute | solution.py:312
  13.9 9.0 %collective-permute-done = bf16[256,1024]{1,0:T(8,128)(2,1)S(1)} collective-permute-done((bf16[256,1024]{1,0:T(8,128)(2,1)S(1)}, bf16[256,1024]{1,0:T(8,128)(2,1)S(1)}, u32[]{:S(2)}, u32[]{:S(2)}) %collective-permute-start) | collective-permute-done | bytes 524320 | tf_op jit(solution)/shard_map/ppermute | solution.py:312
  23.2 1.8 collective-permute-start.7
  27.1 4.6 %attend_forward.2 = (bf16[512,256]{1,0:T(8,128)(2,1)S(1)}, f32[2,8,512]{2,1,0:T(8,128)S(1)}) custom-call(bf16[512,768]{1,0:T(8,128)(2,1)S(1)} %add_convert_fusion.6.q_ref.refs_1_.refs_3_, bf16[512,128]{1,0:T(8,128)(2,1)S(1)} %fusion.10.pick_ref, bf16[512,768]{1,0:T(8,128)(2,1)S(1)} %add_convert_fusion.7.refs_0_.refs_2_.q_ref, ...), custom_call_target="tpu_custom_call" | custom-call | flops 1024 | bytes 1024 | tf_op jit(solution)/shard_map/attend_forward/pallas_call | solution.py:73
  33.0 4.5 %collective-permute-done.7 = bf16[256,1024]{1,0:T(8,128)(2,1)S(1)} collective-permute-done((bf16[256,1024]{1,0:T(8,128)(2,1)S(1)}, bf16[256,1024]{1,0:T(8,128)(2,1)S(1)}, u32[]{:S(2)}, u32[]{:S(2)}) %collective-permute-start.7) | collective-permute-done | bytes 524320 | tf_op jit(solution)/shard_map/ppermute | solution.py:312
  37.8 1.8 collective-permute-start.5
  39.6 4.4 %attend_forward.3 = (bf16[512,256]{1,0:T(8,128)(2,1)S(1)}, f32[2,8,512]{2,1,0:T(8,128)S(1)}) custom-call(bf16[512,768]{1,0:T(8,128)(2,1)S(1)} %add_convert_fusion.7.refs_0_.refs_2_.q_ref, bf16[512,128]{1,0:T(8,128)(2,1)S(1)} %fusion.9.pick_ref, bf16[512,768]{1,0:T(8,128)(2,1)S(1)} %add_convert_fusion.7.refs_0_.refs_2_.q_ref, ...), custom_call_target="tpu_custom_call" | custom-call | flops 1024 | bytes 1024 | tf_op jit(solution)/shard_map/attend_forward/pallas_call | solution.py:73
  46.3 5.9 %collective-permute-done.5 = bf16[256,1024]{1,0:T(8,128)(2,1)S(1)} collective-permute-done((bf16[256,1024]{1,0:T(8,128)(2,1)S(1)}, bf16[256,1024]{1,0:T(8,128)(2,1)S(1)}, u32[]{:S(2)}, u32[]{:S(2)}) %collective-permute-start.5) | collective-permute-done | bytes 524320 | tf_op jit(solution)/shard_map/ppermute | solution.py:312
  53.3 1.8 collective-permute-start.9
  56.0 5.8 %mlp_both.2 = (bf16[512,1024]{1,0:T(8,128)(2,1)S(1)}, bf16[512,1024]{1,0:T(8,128)(2,1)S(1)}, bf16[256,1024]{1,0:T(8,128)(2,1)S(1)}, bf16[256,1024]{1,0:T(8,128)(...) custom-call(bf16[512,1024]{1,0:T(8,128)(2,1)S(1)} %pad_maximum_fusion.5.x_ref, ...), custom_call_target="tpu_custom_call" | custom-call | flops 1024 | bytes 1024 | tf_op jit(solution)/shard_map/mlp_both/pallas_call | solution.py:237
  71.1 1.6 copy-done.4
  72.6 1.6 copy-done.6
  74.2 5.6 %mlp_both.3 = (bf16[512,1024]{1,0:T(8,128)(2,1)S(1)}, bf16[512,1024]{1,0:T(8,128)(2,1)S(1)}, bf16[256,1024]{1,0:T(8,128)(2,1)S(1)}, bf16[256,1024]{1,0:T(8,128)(...) custom-call(bf16[512,1024]{1,0:T(8,128)(2,1)S(1)} %constant_dynamic-update-slice_fusion.2.x_ref, ...), custom_call_target="tpu_custom_call" | custom-call | flops 1024 | bytes 1024 | tf_op jit(solution)/shard_map/mlp_both/pallas_call | solution.py:237
  85.0 1.8 collective-permute-start.14
  94.3 4.8 %collective-permute-done.14 = bf16[256,1024]{1,0:T(8,128)(2,1)S(1)} collective-permute-done((bf16[256,1024]{1,0:T(8,128)(2,1)S(1)}, bf16[256,1024]{1,0:T(8,128)(2,1)S(1)}, u32[]{:S(2)}, u32[]{:S(2)}) %collective-permute-start.14) | collective-permute-done | bytes 524320 | tf_op jit(solution)/shard_map/ppermute | solution.py:312
  99.1 1.6 multiply_reduce_fusion.7
  100.7 1.6 fusion.18
  102.4 1.8 collective-permute-start.17
  106.2 1.7 convolution_convert_fusion.5.grad_ref
  108.0 7.9 %attend_back.2 = (bf16[512,256]{1,0:T(8,128)(2,1)S(1)}, f32[512,256]{1,0:T(8,128)S(1)}, f32[512,256]{1,0:T(8,128)S(1)}, f32[512,256]{1,0:T(8,128)S(1)}, f32[512,256]{1,0:T(8,128)S(1)}) custom-call(bf16[512,768]{1,0:T(8,128)(2,1)S(1)} %add_convert_fusion.7.refs_0_.refs_2_.q_ref, bf16[512,128]{1,0:T(8,128)(2,1)S(1)} %copy-done.14, ...), custom_call_target="tpu_custom_call" | custom-call | flops 1024 | bytes 1024 | tf_op jit(solution)/shard_map/attend_back/pallas_call | solution.py:184
  117.6 1.7 add_convert_fusion.4
  119.4 1.6 add_convert_fusion.3
  122.7 1.6 collective-permute-start.22
  125.6 1.7 fusion
  129.5 8.4 %attend_back.3 = (bf16[512,256]{1,0:T(8,128)(2,1)S(1)}, bf16[512,256]{1,0:T(8,128)(2,1)S(1)}, bf16[512,256]{1,0:T(8,128)(2,1)S(1)}, bf16[512,256]{1,0:T(8,128)(2,1)S(1)}, bf16[512,256]{1,0:T(8,128)(2,1)S(1)}) custom-call(bf16[512,768]{1,0:T(8,128)(2,1)S(1)} %add_convert_fusion.6.q_ref.refs_1_.refs_3_, bf16[512,128]{1,0:T(8,128)(2,1)S(1)} %fusion.10.pick_ref, ...), custom_call_target="tpu_custom_call" | custom-call | flops 1024 | bytes 1024 | tf_op jit(solution)/shard_map/attend_back/pallas_call | solution.py:184
  143.8 2.6 collective-permute-start.27
  152.7 2.3 convert_reduce_fusion.4
  156.2 7.0 %collective-permute-done.25 = bf16[256,1024]{1,0:T(8,128)(2,1)S(1)} collective-permute-done((bf16[256,1024]{1,0:T(8,128)(2,1)S(1)}, bf16[256,1024]{1,0:T(8,128)(2,1)S(1)}, u32[]{:S(2)}, u32[]{:S(2)}) %collective-permute-start.25) | collective-permute-done | bytes 524320 | tf_op jit(solution)/shard_map/ppermute | solution.py:312
  168.3 3.2 %multiply_add_fusion = f32[256,1024]{1,0:T(8,128)} fusion(f32[256,1024]{1,0:T(8,128)} %get-tuple-element.381, f32[256,1024]{1,0:T(8,128)S(1)} %copy-done.37, f32[256]{0:T(256)S(1)} %broadcast_multiply_fusion, f32[256]{0:T(256)S(1)} %broadcast_multiply_fusion.1, f32[1024]{0:T(1024)S(1)} %copy-done.75, f32[256]{0:T(256)S(1)} %copy-done.83, ...), kind=kLoop, calls=%fused_computation.52 | loop fusion | flops 3407872 | bytes 4726784 | tf_op jit(solution)/shard_map/add | solution.py:604
  171.7 10.4 %collective-permute-done.29 = bf16[512,768]{1,0:T(8,128)(2,1)} collective-permute-done((bf16[512,768]{1,0:T(8,128)(2,1)}, bf16[512,768]{1,0:T(8,128)(2,1)}, u32[]{:S(2)}, u32[]{:S(2)}) %collective-permute-start.29) | collective-permute-done | bytes 786464 | tf_op jit(solution)/shard_map/ppermute | solution.py:312
  188.7 1.7 collective-permute-start.35
  190.3 2.5 collective-permute-start.36
  193.3 17.7 %collective-permute-done.35 = bf16[64,1024]{1,0:T(8,128)(2,1)S(1)} collective-permute-done((bf16[64,1024]{1,0:T(8,128)(2,1)S(1)}, bf16[64,1024]{1,0:T(8,128)(2,1)S(1)}, u32[]{:S(2)}, u32[]{:S(2)}) %collective-permute-start.35) | collective-permute-done | bytes 131104 | tf_op jit(solution)/shard_map/ppermute | solution.py:312
  211.2 6.1 %collective-permute-done.37 = bf16[128,1024]{1,0:T(8,128)(2,1)S(1)} collective-permute-done((bf16[128,1024]{1,0:T(8,128)(2,1)S(1)}, bf16[128,1024]{1,0:T(8,128)(2,1)S(1)}, u32[]{:S(2)}, u32[]{:S(2)}) %collective-permute-start.37) | collective-permute-done | bytes 262176 | tf_op jit(solution)/shard_map/ppermute | solution.py:312
  217.4 3.0 %collective-permute-start.39 = (bf16[32,1024]{1,0:T(8,128)(2,1)S(1)}, bf16[32,1024]{1,0:T(8,128)(2,1)S(1)}, u32[]{:S(2)}, u32[]{:S(2)}) collective-permute-start(bf16[32,1024]{1,0:T(8,128)(2,1)S(1)} %dynamic-slice_bitcast_fusion.15), channel_id=1, source_target_pairs={{0,16},{4,20},{8,24},{12,28},{16,0},{20,4},{24,8},{28,12},{1,17},{... | collective-permute-start | bytes 196616 | tf_op jit(solution)/shard_map/ppermute | solution.py:312
  220.5 1.9 collective-permute-start.41
  224.4 7.5 %collective-permute-done.40 = f32[7808]{0:T(1024)S(1)} collective-permute-done((f32[7808]{0:T(1024)S(1)}, f32[7808]{0:T(1024)S(1)}, u32[]{:S(2)}, u32[]{:S(2)}) %collective-permute-start.40) | collective-permute-done | bytes 31264 | tf_op jit(solution)/shard_map/ppermute | solution.py:312
  232.0 3.0 %collective-permute-start.43 = (bf16[128,768]{1,0:T(8,128)(2,1)S(1)}, bf16[128,768]{1,0:T(8,128)(2,1)S(1)}, u32[]{:S(2)}, u32[]{:S(2)}) collective-permute-start(bf16[128,768]{1,0:T(8,128)(2,1)S(1)} %fusion.7), channel_id=1, source_target_pairs={{0,16},{4,20},{8,24},{12,28},{16,0},{20,4},{24,8},{28,12},{1,17},{... | collective-permute-start | bytes 589832 | tf_op jit(solution)/shard_map/ppermute | solution.py:312
  239.0 3.4 %collective-permute-done.45 = f32[7808]{0:T(1024)S(1)} collective-permute-done((f32[7808]{0:T(1024)S(1)}, f32[7808]{0:T(1024)S(1)}, u32[]{:S(2)}, u32[]{:S(2)}) %collective-permute-start.45) | collective-permute-done | bytes 31264 | tf_op jit(solution)/shard_map/ppermute | solution.py:312
  242.7 2.4 collective-permute-start.46
  245.2 2.1 collective-permute-start.48
  249.7 8.4 %collective-permute-done.48 = f32[7808]{0:T(1024)S(1)} collective-permute-done((f32[7808]{0:T(1024)S(1)}, f32[7808]{0:T(1024)S(1)}, u32[]{:S(2)}, u32[]{:S(2)}) %collective-permute-start.48) | collective-permute-done | bytes 31264 | tf_op jit(solution)/shard_map/ppermute | solution.py:312
  264.8 7.2 %collective-permute-done.49 = bf16[512,1024]{1,0:T(8,128)(2,1)} collective-permute-done((bf16[512,1024]{1,0:T(8,128)(2,1)}, bf16[512,1024]{1,0:T(8,128)(2,1)}, u32[]{:S(2)}, u32[]{:S(2)}) %collective-permute-start.49) | collective-permute-done | bytes 1048608 | tf_op jit(solution)/shard_map/ppermute | solution.py:312
  273.4 5.2 %convert_multiply_fusion.1 = f32[1024,1024]{1,0:T(8,128)} fusion(bf16[512,1024]{1,0:T(8,128)(2,1)} %maximum_select_fusion.3, bf16[512,1024]{1,0:T(8,128)(2,1)} %collective-permute-done.49, f32[]{:T(128)} %bitcast.50, pred[]{:T(512)S(6)} %ne.6), kind=kLoop, calls=%fused_computation.1 | loop fusion | flops 11534336 | bytes 6291461 | tf_op jit(solution)/shard_map/mul | solution.py:664
  278.6 4.4 %convert_multiply_fusion = f32[1024,1024]{1,0:T(8,128)} fusion(bf16[512,1024]{1,0:T(8,128)(2,1)S(1)} %maximum_select_fusion.4, bf16[512,1024]{1,0:T(8,128)(2,1)} %collective-permute-done.50, f32[]{:T(128)} %bitcast.50, pred[]{:T(512)S(6)} %ne.7), kind=kLoop, calls=%fused_computation | loop fusion | flops 11534336 | bytes 6291461 | tf_op jit(solution)/shard_map/mul | solution.py:664
  285.0 1.9 pad_maximum_fusion
  (385 shorter events, 86.7 us)
Async XLA Ops:
  8.0 14.9 %collective-permute-start = (bf16[256,1024]{1,0:T(8,128)(2,1)S(1)}, bf16[256,1024]{1,0:T(8,128)(2,1)S(1)}, u32[]{:S(2)}, u32[]{:S(2)}) collective-permute-start(bf16[256,1024]{1,0:T(8,128)(2,1)S(1)} %add_convert_fusion.14), channel_id=1, source_target_pairs={{0,2},{1,3},{2,0},{3,1},{4,6},{5,7},{6,4},{7,5},{8,10},{9,11},{10,... | collective-permute-start | bytes 1572872 | tf_op jit(solution)/shard_map/ppermute | solution.py:312
  23.2 14.4 %collective-permute-start.7 = (bf16[256,1024]{1,0:T(8,128)(2,1)S(1)}, bf16[256,1024]{1,0:T(8,128)(2,1)S(1)}, u32[]{:S(2)}, u32[]{:S(2)}) collective-permute-start(bf16[256,1024]{1,0:T(8,128)(2,1)S(1)} %get-tuple-element.298), channel_id=1, source_target_pairs={{0,2},{1,3},{2,0},{3,1},{4,6},{5,7},{6,4},{7,5},{8,10},{9,11},{10,... | collective-permute-start | bytes 1572872 | tf_op jit(solution)/shard_map/ppermute | solution.py:312
  32.3 5.3 %collective-permute-start.3 = (bf16[256,1024]{1,0:T(8,128)(2,1)S(1)}, bf16[256,1024]{1,0:T(8,128)(2,1)S(1)}, u32[]{:S(2)}, u32[]{:S(2)}) collective-permute-start(bf16[256,1024]{1,0:T(8,128)(2,1)S(1)} %slice.128), channel_id=1, source_target_pairs={{0,1},{1,0},{2,3},{3,2},{4,5},{5,4},{6,7},{7,6},{8,9},{9,8},{10,11... | collective-permute-start | bytes 1572872 | tf_op jit(solution)/shard_map/ppermute | solution.py:312
  32.7 12.2 %collective-permute-start.6 = (bf16[256,1024]{1,0:T(8,128)(2,1)S(1)}, bf16[256,1024]{1,0:T(8,128)(2,1)S(1)}, u32[]{:S(2)}, u32[]{:S(2)}) collective-permute-start(bf16[256,1024]{1,0:T(8,128)(2,1)S(1)} %get-tuple-element.298), channel_id=1, source_target_pairs={{0,1},{1,0},{2,3},{3,2},{4,5},{5,4},{6,7},{7,6},{8,9},{9,8},{10,11... | collective-permute-start | bytes 1572872 | tf_op jit(solution)/shard_map/ppermute | solution.py:312
  37.6 7.7 %collective-permute-start.8 = (bf16[256,1024]{1,0:T(8,128)(2,1)S(1)}, bf16[256,1024]{1,0:T(8,128)(2,1)S(1)}, u32[]{:S(2)}, u32[]{:S(2)}) collective-permute-start(bf16[256,1024]{1,0:T(8,128)(2,1)S(1)} %collective-permute-done.7), channel_id=1, source_target_pairs={{0,1},{1,0},{2,3},{3,2},{4,5},{5,4},{6,7},{7,6},{8,9},{9,8},{10,11... | collective-permute-start | bytes 1572872 | tf_op jit(solution)/shard_map/ppermute | solution.py:312
  37.8 14.4 %collective-permute-start.5 = (bf16[256,1024]{1,0:T(8,128)(2,1)S(1)}, bf16[256,1024]{1,0:T(8,128)(2,1)S(1)}, u32[]{:S(2)}, u32[]{:S(2)}) collective-permute-start(bf16[256,1024]{1,0:T(8,128)(2,1)S(1)} %add_convert_fusion.13), channel_id=1, source_target_pairs={{0,2},{1,3},{2,0},{3,1},{4,6},{5,7},{6,4},{7,5},{8,10},{9,11},{10,... | collective-permute-start | bytes 1572872 | tf_op jit(solution)/shard_map/ppermute | solution.py:312
  44.6 7.7 %collective-permute-start.4 = (bf16[256,1024]{1,0:T(8,128)(2,1)S(1)}, bf16[256,1024]{1,0:T(8,128)(2,1)S(1)}, u32[]{:S(2)}, u32[]{:S(2)}) collective-permute-start(bf16[256,1024]{1,0:T(8,128)(2,1)S(1)} %slice.130), channel_id=1, source_target_pairs={{0,1},{1,0},{2,3},{3,2},{4,5},{5,4},{6,7},{7,6},{8,9},{9,8},{10,11... | collective-permute-start | bytes 1572872 | tf_op jit(solution)/shard_map/ppermute | solution.py:312
  53.3 14.4 %collective-permute-start.9 = (bf16[256,1024]{1,0:T(8,128)(2,1)S(1)}, bf16[256,1024]{1,0:T(8,128)(2,1)}, u32[]{:S(2)}, u32[]{:S(2)}) collective-permute-start(bf16[256,1024]{1,0:T(8,128)(2,1)S(1)} %add_convert_fusion.12), channel_id=1, source_target_pairs={{0,2},{1,3},{2,0},{3,1},{4,6},{5,7},{6,4},{7,5},{8,10},{9,11},{10,... | collective-permute-start | bytes 1572872 | tf_op jit(solution)/shard_map/ppermute | solution.py:312
  67.7 12.2 %collective-permute-start.12 = (bf16[256,1024]{1,0:T(8,128)(2,1)}, bf16[256,1024]{1,0:T(8,128)(2,1)}, u32[]{:S(2)}, u32[]{:S(2)}) collective-permute-start(bf16[256,1024]{1,0:T(8,128)(2,1)} %get-tuple-element.213), channel_id=1, source_target_pairs={{0,1},{1,0},{2,3},{3,2},{4,5},{5,4},{6,7},{7,6},{8,9},{9,8},{10,11... | collective-permute-start | bytes 1572872 | tf_op jit(solution)/shard_map/ppermute | solution.py:312
  68.2 26.0 %collective-permute-start.16 = (bf16[256,1024]{1,0:T(8,128)(2,1)}, bf16[256,1024]{1,0:T(8,128)(2,1)S(1)}, u32[]{:S(2)}, u32[]{:S(2)}) collective-permute-start(bf16[256,1024]{1,0:T(8,128)(2,1)} %copy-done.30), channel_id=1, source_target_pairs={{0,1},{1,0},{2,3},{3,2},{4,5},{5,4},{6,7},{7,6},{8,9},{9,8},{10,11... | collective-permute-start | bytes 1572872 | tf_op jit(solution)/shard_map/ppermute | solution.py:312
  79.9 4.9 %collective-permute-start.13 = (bf16[256,1024]{1,0:T(8,128)(2,1)S(1)}, bf16[256,1024]{1,0:T(8,128)(2,1)S(1)}, u32[]{:S(2)}, u32[]{:S(2)}) collective-permute-start(bf16[256,1024]{1,0:T(8,128)(2,1)S(1)} %get-tuple-element.221), channel_id=1, source_target_pairs={{0,1},{1,0},{2,3},{3,2},{4,5},{5,4},{6,7},{7,6},{8,9},{9,8},{10,11... | collective-permute-start | bytes 1572872 | tf_op jit(solution)/shard_map/ppermute | solution.py:312
  81.4 12.8 %collective-permute-start.15 = (bf16[256,1024]{1,0:T(8,128)(2,1)S(1)}, bf16[256,1024]{1,0:T(8,128)(2,1)S(1)}, u32[]{:S(2)}, u32[]{:S(2)}) collective-permute-start(bf16[256,1024]{1,0:T(8,128)(2,1)S(1)} %get-tuple-element.231), channel_id=1, source_target_pairs={{0,1},{1,0},{2,3},{3,2},{4,5},{5,4},{6,7},{7,6},{8,9},{9,8},{10,11... | collective-permute-start | bytes 1572872 | tf_op jit(solution)/shard_map/ppermute | solution.py:312
  85.0 14.0 %collective-permute-start.14 = (bf16[256,1024]{1,0:T(8,128)(2,1)S(1)}, bf16[256,1024]{1,0:T(8,128)(2,1)S(1)}, u32[]{:S(2)}, u32[]{:S(2)}) collective-permute-start(bf16[256,1024]{1,0:T(8,128)(2,1)S(1)} %add_convert_fusion.11), channel_id=1, source_target_pairs={{0,2},{1,3},{2,0},{3,1},{4,6},{5,7},{6,4},{7,5},{8,10},{9,11},{10,... | collective-permute-start | bytes 1572872 | tf_op jit(solution)/shard_map/ppermute | solution.py:312
  91.2 25.9 %collective-permute-start.19 = (bf16[512,1024]{1,0:T(8,128)(2,1)}, bf16[512,1024]{1,0:T(8,128)(2,1)}, u32[]{:S(2)}, u32[]{:S(2)}) collective-permute-start(bf16[512,1024]{1,0:T(8,128)(2,1)} %get-tuple-element.239), channel_id=1, source_target_pairs={{0,4},{4,0},{8,12},{12,8},{16,20},{20,16},{24,28},{28,24},{1,5},{5... | collective-permute-start | bytes 3145736 | tf_op jit(solution)/shard_map/ppermute | solution.py:312
  92.7 25.0 %collective-permute-start.20 = (bf16[512,1024]{1,0:T(8,128)(2,1)}, bf16[512,1024]{1,0:T(8,128)(2,1)}, u32[]{:S(2)}, u32[]{:S(2)}) collective-permute-start(bf16[512,1024]{1,0:T(8,128)(2,1)} %get-tuple-element.240), channel_id=1, source_target_pairs={{0,8},{4,12},{8,0},{12,4},{16,24},{20,28},{24,16},{28,20},{1,9},{5... | collective-permute-start | bytes 3145736 | tf_op jit(solution)/shard_map/ppermute | solution.py:312
  102.3 3.9 %collective-permute-start.18 = (bf16[256,1024]{1,0:T(8,128)(2,1)}, bf16[256,1024]{1,0:T(8,128)(2,1)}, u32[]{:S(2)}, u32[]{:S(2)}) collective-permute-start(bf16[256,1024]{1,0:T(8,128)(2,1)} %get-tuple-element.297), channel_id=1, source_target_pairs={{0,1},{1,0},{2,3},{3,2},{4,5},{5,4},{6,7},{7,6},{8,9},{9,8},{10,11... | collective-permute-start | bytes 1572872 | tf_op jit(solution)/shard_map/ppermute | solution.py:312
  102.4 14.6 %collective-permute-start.17 = (bf16[256,1024]{1,0:T(8,128)(2,1)}, bf16[256,1024]{1,0:T(8,128)(2,1)}, u32[]{:S(2)}, u32[]{:S(2)}) collective-permute-start(bf16[256,1024]{1,0:T(8,128)(2,1)} %get-tuple-element.297), channel_id=1, source_target_pairs={{0,2},{1,3},{2,0},{3,1},{4,6},{5,7},{6,4},{7,5},{8,10},{9,11},{10,... | collective-permute-start | bytes 1572872 | tf_op jit(solution)/shard_map/ppermute | solution.py:312
  117.6 3.5 %collective-permute-start.21 = (bf16[256,1024]{1,0:T(8,128)(2,1)}, bf16[256,1024]{1,0:T(8,128)(2,1)S(1)}, u32[]{:S(2)}, u32[]{:S(2)}) collective-permute-start(bf16[256,1024]{1,0:T(8,128)(2,1)} %collective-permute-done.17), channel_id=1, source_target_pairs={{0,1},{1,0},{2,3},{3,2},{4,5},{5,4},{6,7},{7,6},{8,9},{9,8},{10,11... | collective-permute-start | bytes 1572872 | tf_op jit(solution)/shard_map/ppermute | solution.py:312
  122.7 15.2 %collective-permute-start.22 = (bf16[256,1024]{1,0:T(8,128)(2,1)S(1)}, bf16[256,1024]{1,0:T(8,128)(2,1)S(1)}, u32[]{:S(2)}, u32[]{:S(2)}) collective-permute-start(bf16[256,1024]{1,0:T(8,128)(2,1)S(1)} %dynamic-slice_bitcast_fusion.7), channel_id=1, source_target_pairs={{0,8},{4,12},{8,0},{12,4},{16,24},{20,28},{24,16},{28,20},{1,9},{5... | collective-permute-start | bytes 1572872 | tf_op jit(solution)/shard_map/ppermute | solution.py:312
  124.4 14.8 %collective-permute-start.23 = (bf16[256,1024]{1,0:T(8,128)(2,1)S(1)}, bf16[256,1024]{1,0:T(8,128)(2,1)S(1)}, u32[]{:S(2)}, u32[]{:S(2)}) collective-permute-start(bf16[256,1024]{1,0:T(8,128)(2,1)S(1)} %dynamic-slice_bitcast_fusion.6), channel_id=1, source_target_pairs={{0,4},{4,0},{8,12},{12,8},{16,20},{20,16},{24,28},{28,24},{1,5},{5... | collective-permute-start | bytes 1572872 | tf_op jit(solution)/shard_map/ppermute | solution.py:312
  128.6 43.0 %collective-permute-start.30 = (bf16[128,1024]{1,0:T(8,128)(2,1)}, bf16[128,1024]{1,0:T(8,128)(2,1)}, u32[]{:S(2)}, u32[]{:S(2)}) collective-permute-start(bf16[128,1024]{1,0:T(8,128)(2,1)} %get-tuple-element.280), channel_id=1, source_target_pairs={{0,4},{4,0},{8,12},{12,8},{16,20},{20,16},{24,28},{28,24},{1,5},{5... | collective-permute-start | bytes 786440 | tf_op jit(solution)/shard_map/ppermute | solution.py:312
  141.7 7.4 %collective-permute-start.24 = (bf16[256,1024]{1,0:T(8,128)(2,1)S(1)}, bf16[256,1024]{1,0:T(8,128)(2,1)S(1)}, u32[]{:S(2)}, u32[]{:S(2)}) collective-permute-start(bf16[256,1024]{1,0:T(8,128)(2,1)S(1)} %slice.132), channel_id=1, source_target_pairs={{0,1},{1,0},{2,3},{3,2},{4,5},{5,4},{6,7},{7,6},{8,9},{9,8},{10,11... | collective-permute-start | bytes 1572872 | tf_op jit(solution)/shard_map/ppermute | solution.py:312
  143.8 27.9 %collective-permute-start.27 = (bf16[128,1024]{1,0:T(8,128)(2,1)}, bf16[128,1024]{1,0:T(8,128)(2,1)}, u32[]{:S(2)}, u32[]{:S(2)}) collective-permute-start(bf16[128,1024]{1,0:T(8,128)(2,1)} %dynamic-slice_bitcast_fusion.11), channel_id=1, source_target_pairs={{0,16},{4,20},{8,24},{12,28},{16,0},{20,4},{24,8},{28,12},{1,17},{... | collective-permute-start | bytes 786440 | tf_op jit(solution)/shard_map/ppermute | solution.py:312
  146.4 25.3 %collective-permute-start.28 = (bf16[128,1024]{1,0:T(8,128)(2,1)}, bf16[128,1024]{1,0:T(8,128)(2,1)}, u32[]{:S(2)}, u32[]{:S(2)}) collective-permute-start(bf16[128,1024]{1,0:T(8,128)(2,1)} %dynamic-slice_bitcast_fusion.10), channel_id=1, source_target_pairs={{0,16},{4,20},{8,24},{12,28},{16,0},{20,4},{24,8},{28,12},{1,17},{... | collective-permute-start | bytes 786440 | tf_op jit(solution)/shard_map/ppermute | solution.py:312
  149.3 13.8 %collective-permute-start.25 = (bf16[256,1024]{1,0:T(8,128)(2,1)S(1)}, bf16[256,1024]{1,0:T(8,128)(2,1)S(1)}, u32[]{:S(2)}, u32[]{:S(2)}) collective-permute-start(bf16[256,1024]{1,0:T(8,128)(2,1)S(1)} %add_convert_fusion.10), channel_id=1, source_target_pairs={{0,2},{1,3},{2,0},{3,1},{4,6},{5,7},{6,4},{7,5},{8,10},{9,11},{10,... | collective-permute-start | bytes 1572872 | tf_op jit(solution)/shard_map/ppermute | solution.py:312
  151.8 12.6 %collective-permute-start.26 = (bf16[256,1024]{1,0:T(8,128)(2,1)S(1)}, bf16[256,1024]{1,0:T(8,128)(2,1)S(1)}, u32[]{:S(2)}, u32[]{:S(2)}) collective-permute-start(bf16[256,1024]{1,0:T(8,128)(2,1)S(1)} %get-tuple-element.401), channel_id=1, source_target_pairs={{0,1},{1,0},{2,3},{3,2},{4,5},{5,4},{6,7},{7,6},{8,9},{9,8},{10,11... | collective-permute-start | bytes 1572872 | tf_op jit(solution)/shard_map/ppermute | solution.py:312
  163.1 18.9 %collective-permute-start.29 = (bf16[512,768]{1,0:T(8,128)(2,1)}, bf16[512,768]{1,0:T(8,128)(2,1)}, u32[]{:S(2)}, u32[]{:S(2)}) collective-permute-start(bf16[512,768]{1,0:T(8,128)(2,1)} %get-tuple-element.279), channel_id=1, source_target_pairs={{0,4},{4,0},{8,12},{12,8},{16,20},{20,16},{24,28},{28,24},{1,5},{5... | collective-permute-start | bytes 2359304 | tf_op jit(solution)/shard_map/ppermute | solution.py:312
  166.8 4.8 %collective-permute-start.32 = (f32[6,1024]{1,0:T(8,128)S(1)}, f32[6,1024]{1,0:T(8,128)S(1)}, u32[]{:S(2)}, u32[]{:S(2)}) collective-permute-start(f32[6,1024]{1,0:T(8,128)S(1)} %add.302), channel_id=1, source_target_pairs={{0,2},{1,3},{2,0},{3,1},{4,6},{5,7},{6,4},{7,5},{8,10},{9,11},{10,... | collective-permute-start | bytes 73736 | tf_op jit(solution)/shard_map/ppermute | solution.py:312
  187.0 23.9 %collective-permute-start.33 = (bf16[256,1024]{1,0:T(8,128)(2,1)S(1)}, bf16[256,1024]{1,0:T(8,128)(2,1)S(1)}, u32[]{:S(2)}, u32[]{:S(2)}) collective-permute-start(bf16[256,1024]{1,0:T(8,128)(2,1)S(1)} %add_convert_fusion.9), channel_id=1, source_target_pairs={{0,2},{1,3},{2,0},{3,1},{4,6},{5,7},{6,4},{7,5},{8,10},{9,11},{10,... | collective-permute-start | bytes 1572872 | tf_op jit(solution)/shard_map/ppermute | solution.py:312
  188.3 22.6 %collective-permute-start.34 = (bf16[256,768]{1,0:T(8,128)(2,1)S(1)}, bf16[256,768]{1,0:T(8,128)(2,1)S(1)}, u32[]{:S(2)}, u32[]{:S(2)}) collective-permute-start(bf16[256,768]{1,0:T(8,128)(2,1)S(1)} %dynamic-slice_bitcast_fusion.8), channel_id=1, source_target_pairs={{0,8},{4,12},{8,0},{12,4},{16,24},{20,28},{24,16},{28,20},{1,9},{5... | collective-permute-start | bytes 1179656 | tf_op jit(solution)/shard_map/ppermute | solution.py:312
  188.7 22.3 %collective-permute-start.35 = (bf16[64,1024]{1,0:T(8,128)(2,1)S(1)}, bf16[64,1024]{1,0:T(8,128)(2,1)S(1)}, u32[]{:S(2)}, u32[]{:S(2)}) collective-permute-start(bf16[64,1024]{1,0:T(8,128)(2,1)S(1)} %dynamic-slice_bitcast_fusion.14), channel_id=1, source_target_pairs={{0,8},{4,12},{8,0},{12,4},{16,24},{20,28},{24,16},{28,20},{1,9},{5... | collective-permute-start | bytes 393224 | tf_op jit(solution)/shard_map/ppermute | solution.py:312
  190.3 20.8 %collective-permute-start.36 = (bf16[128,1024]{1,0:T(8,128)(2,1)S(1)}, bf16[128,1024]{1,0:T(8,128)(2,1)S(1)}, u32[]{:S(2)}, u32[]{:S(2)}) collective-permute-start(bf16[128,1024]{1,0:T(8,128)(2,1)S(1)} %fusion.6), channel_id=1, source_target_pairs={{0,16},{4,20},{8,24},{12,28},{16,0},{20,4},{24,8},{28,12},{1,17},{... | collective-permute-start | bytes 786440 | tf_op jit(solution)/shard_map/ppermute | solution.py:312
  192.8 24.4 %collective-permute-start.37 = (bf16[128,1024]{1,0:T(8,128)(2,1)S(1)}, bf16[128,1024]{1,0:T(8,128)(2,1)S(1)}, u32[]{:S(2)}, u32[]{:S(2)}) collective-permute-start(bf16[128,1024]{1,0:T(8,128)(2,1)S(1)} %fusion.5), channel_id=1, source_target_pairs={{0,16},{4,20},{8,24},{12,28},{16,0},{20,4},{24,8},{28,12},{1,17},{... | collective-permute-start | bytes 786440 | tf_op jit(solution)/shard_map/ppermute | solution.py:312
  217.2 14.7 %collective-permute-start.38 = (bf16[128,768]{1,0:T(8,128)(2,1)S(1)}, bf16[128,768]{1,0:T(8,128)(2,1)S(1)}, u32[]{:S(2)}, u32[]{:S(2)}) collective-permute-start(bf16[128,768]{1,0:T(8,128)(2,1)S(1)} %dynamic-slice_bitcast_fusion.13), channel_id=1, source_target_pairs={{0,16},{4,20},{8,24},{12,28},{16,0},{20,4},{24,8},{28,12},{1,17},{... | collective-permute-start | bytes 589832 | tf_op jit(solution)/shard_map/ppermute | solution.py:312
  217.4 14.5 %collective-permute-start.39 = (bf16[32,1024]{1,0:T(8,128)(2,1)S(1)}, bf16[32,1024]{1,0:T(8,128)(2,1)S(1)}, u32[]{:S(2)}, u32[]{:S(2)}) collective-permute-start(bf16[32,1024]{1,0:T(8,128)(2,1)S(1)} %dynamic-slice_bitcast_fusion.15), channel_id=1, source_target_pairs={{0,16},{4,20},{8,24},{12,28},{16,0},{20,4},{24,8},{28,12},{1,17},{... | collective-permute-start | bytes 196616 | tf_op jit(solution)/shard_map/ppermute | solution.py:312
  220.5 15.4 %collective-permute-start.41 = (bf16[256,1024]{1,0:T(8,128)(2,1)S(1)}, bf16[256,1024]{1,0:T(8,128)(2,1)S(1)}, u32[]{:S(2)}, u32[]{:S(2)}) collective-permute-start(bf16[256,1024]{1,0:T(8,128)(2,1)S(1)} %maximum_select_fusion.6), channel_id=1, source_target_pairs={{0,8},{4,12},{8,0},{12,4},{16,24},{20,28},{24,16},{28,20},{1,9},{5... | collective-permute-start | bytes 1572872 | tf_op jit(solution)/shard_map/ppermute | solution.py:312
  222.4 13.5 %collective-permute-start.42 = (bf16[256,1024]{1,0:T(8,128)(2,1)S(1)}, bf16[256,1024]{1,0:T(8,128)(2,1)S(1)}, u32[]{:S(2)}, u32[]{:S(2)}) collective-permute-start(bf16[256,1024]{1,0:T(8,128)(2,1)S(1)} %maximum_select_fusion.7), channel_id=1, source_target_pairs={{0,4},{4,0},{8,12},{12,8},{16,20},{20,16},{24,28},{28,24},{1,5},{5... | collective-permute-start | bytes 1572872 | tf_op jit(solution)/shard_map/ppermute | solution.py:312
  223.9 8.0 %collective-permute-start.40 = (f32[7808]{0:T(1024)S(1)}, f32[7808]{0:T(1024)S(1)}, u32[]{:S(2)}, u32[]{:S(2)}) collective-permute-start(f32[7808]{0:T(1024)S(1)} %constant_dynamic-update-slice_fusion.8), channel_id=1, source_target_pairs={{0,4},{4,0},{8,12},{12,8},{16,20},{20,16},{24,28},{28,24},{1,5},{5... | collective-permute-start | bytes 93704 | tf_op jit(solution)/shard_map/ppermute | solution.py:312
  232.0 10.5 %collective-permute-start.43 = (bf16[128,768]{1,0:T(8,128)(2,1)S(1)}, bf16[128,768]{1,0:T(8,128)(2,1)S(1)}, u32[]{:S(2)}, u32[]{:S(2)}) collective-permute-start(bf16[128,768]{1,0:T(8,128)(2,1)S(1)} %fusion.7), channel_id=1, source_target_pairs={{0,16},{4,20},{8,24},{12,28},{16,0},{20,4},{24,8},{28,12},{1,17},{... | collective-permute-start | bytes 589832 | tf_op jit(solution)/shard_map/ppermute | solution.py:312
  235.0 7.5 %collective-permute-start.44 = (bf16[32,1024]{1,0:T(8,128)(2,1)S(1)}, bf16[32,1024]{1,0:T(8,128)(2,1)S(1)}, u32[]{:S(2)}, u32[]{:S(2)}) collective-permute-start(bf16[32,1024]{1,0:T(8,128)(2,1)S(1)} %fusion.11), channel_id=1, source_target_pairs={{0,16},{4,20},{8,24},{12,28},{16,0},{20,4},{24,8},{28,12},{1,17},{... | collective-permute-start | bytes 196616 | tf_op jit(solution)/shard_map/ppermute | solution.py:312
  235.1 7.3 %collective-permute-start.45 = (f32[7808]{0:T(1024)S(1)}, f32[7808]{0:T(1024)S(1)}, u32[]{:S(2)}, u32[]{:S(2)}) collective-permute-start(f32[7808]{0:T(1024)S(1)} %add.310), channel_id=1, source_target_pairs={{0,8},{4,12},{8,0},{12,4},{16,24},{20,28},{24,16},{28,20},{1,9},{5... | collective-permute-start | bytes 93704 | tf_op jit(solution)/shard_map/ppermute | solution.py:312
  242.7 15.6 %collective-permute-start.46 = (bf16[256,768]{1,0:T(8,128)(2,1)S(1)}, bf16[256,768]{1,0:T(8,128)(2,1)S(1)}, u32[]{:S(2)}, u32[]{:S(2)}) collective-permute-start(bf16[256,768]{1,0:T(8,128)(2,1)S(1)} %maximum_select_fusion.9), channel_id=1, source_target_pairs={{0,8},{4,12},{8,0},{12,4},{16,24},{20,28},{24,16},{28,20},{1,9},{5... | collective-permute-start | bytes 1179656 | tf_op jit(solution)/shard_map/ppermute | solution.py:312
  245.1 13.1 %collective-permute-start.47 = (bf16[64,1024]{1,0:T(8,128)(2,1)S(1)}, bf16[64,1024]{1,0:T(8,128)(2,1)S(1)}, u32[]{:S(2)}, u32[]{:S(2)}) collective-permute-start(bf16[64,1024]{1,0:T(8,128)(2,1)S(1)} %maximum_select_fusion.11), channel_id=1, source_target_pairs={{0,8},{4,12},{8,0},{12,4},{16,24},{20,28},{24,16},{28,20},{1,9},{5... | collective-permute-start | bytes 393224 | tf_op jit(solution)/shard_map/ppermute | solution.py:312
  245.2 12.9 %collective-permute-start.48 = (f32[7808]{0:T(1024)S(1)}, f32[7808]{0:T(1024)S(1)}, u32[]{:S(2)}, u32[]{:S(2)}) collective-permute-start(f32[7808]{0:T(1024)S(1)} %add.316), channel_id=1, source_target_pairs={{0,16},{4,20},{8,24},{12,28},{16,0},{20,4},{24,8},{28,12},{1,17},{... | collective-permute-start | bytes 93704 | tf_op jit(solution)/shard_map/ppermute | solution.py:312
  247.3 24.7 %collective-permute-start.49 = (bf16[512,1024]{1,0:T(8,128)(2,1)}, bf16[512,1024]{1,0:T(8,128)(2,1)}, u32[]{:S(2)}, u32[]{:S(2)}) collective-permute-start(bf16[512,1024]{1,0:T(8,128)(2,1)} %maximum_select_fusion.3), channel_id=1, source_target_pairs={{0,4},{4,0},{8,12},{12,8},{16,20},{20,16},{24,28},{28,24},{1,5},{5... | collective-permute-start | bytes 3145736 | tf_op jit(solution)/shard_map/ppermute | solution.py:312
  248.8 24.5 %collective-permute-start.50 = (bf16[512,1024]{1,0:T(8,128)(2,1)S(1)}, bf16[512,1024]{1,0:T(8,128)(2,1)}, u32[]{:S(2)}, u32[]{:S(2)}) collective-permute-start(bf16[512,1024]{1,0:T(8,128)(2,1)S(1)} %maximum_select_fusion.4), channel_id=1, source_target_pairs={{0,8},{4,12},{8,0},{12,4},{16,24},{20,28},{24,16},{28,20},{1,9},{5... | collective-permute-start | bytes 3145736 | tf_op jit(solution)/shard_map/ppermute | solution.py:312
  258.6 24.5 %collective-permute-start.51 = (bf16[512,768]{1,0:T(8,128)(2,1)S(1)}, bf16[512,768]{1,0:T(8,128)(2,1)S(1)}, u32[]{:S(2)}, u32[]{:S(2)}) collective-permute-start(bf16[512,768]{1,0:T(8,128)(2,1)S(1)} %maximum_select_fusion.5), channel_id=1, source_target_pairs={{0,4},{4,0},{8,12},{12,8},{16,20},{20,16},{24,28},{28,24},{1,5},{5... | collective-permute-start | bytes 2359304 | tf_op jit(solution)/shard_map/ppermute | solution.py:312
  262.8 20.4 %collective-permute-start.52 = (bf16[128,1024]{1,0:T(8,128)(2,1)S(1)}, bf16[128,1024]{1,0:T(8,128)(2,1)S(1)}, u32[]{:S(2)}, u32[]{:S(2)}) collective-permute-start(bf16[128,1024]{1,0:T(8,128)(2,1)S(1)} %maximum_select_fusion.10), channel_id=1, source_target_pairs={{0,4},{4,0},{8,12},{12,8},{16,20},{20,16},{24,28},{28,24},{1,5},{5... | collective-permute-start | bytes 786440 | tf_op jit(solution)/shard_map/ppermute | solution.py:312
  (99 other events, 525.8 us)
